TPU v7x, 32 devices: a whole 2x2x4 slice. The times are simulated.
32 devices in a mesh: seq: 8 (over z, y), wa: 4 (over x, core).
Axes of the slice: x: 2, y: 2, z: 4, core: 2. Of those that a mesh axis runs over, the one named last changes fastest.
Arguments:
- tokens: bfloat16 [8, 1024, 2048], P('wa', 'seq'), may hold values from -6 to 6
- cotangent: float32 [8, 1024, 2048], P('wa', 'seq'), may hold values from -6 to 6
- token_document_index: int32 [8, 1024], P('wa', 'seq'), may hold values from 0 to 7, never falling along the last dimension, each value on 1 to 512 neighbouring positions
- sequence_adapter_index: int32 [8], P('wa'), may hold values from 0 to 7
- query_weight: bfloat16 [2048, 2048], P(('seq', 'wa')), may hold values from -0.125 to 0.125
- key_weight: bfloat16 [2048, 2048], P(('seq', 'wa')), may hold values from -0.125 to 0.125
- value_weight: bfloat16 [2048, 2048], P(('seq', 'wa')), may hold values from -0.125 to 0.125
- output_weight: bfloat16 [2048, 2048], P(('seq', 'wa')), may hold values from -0.125 to 0.125
- gate_weight: bfloat16 [2048, 8192], P(('seq', 'wa')), may hold values from -0.125 to 0.125
- up_weight: bfloat16 [2048, 8192], P(('seq', 'wa')), may hold values from -0.125 to 0.125
- down_weight: bfloat16 [8192, 2048], P(('seq', 'wa')), may hold values from -0.0625 to 0.0625
- query_norm_gain: bfloat16 [2048], replicated, may hold values from 0.25 to 1.75
- key_norm_gain: bfloat16 [2048], replicated, may hold values from 0.25 to 1.75
- attention_norm_gain: bfloat16 [2048], replicated, may hold values from 0.25 to 1.75
- feedforward_norm_gain: bfloat16 [2048], replicated, may hold values from 0.25 to 1.75
- attention_down_adapters: bfloat16 [4, 128, 2048], P(None, ('seq', 'wa')), may hold values from -0.125 to 0.125
- attention_up_adapters: bfloat16 [4, 128, 2048], P(None, ('seq', 'wa')), may hold values from -0.75 to 0.75
- feedforward_down_adapters: bfloat16 [2, 128, 2048], P(None, ('seq', 'wa')), may hold values from -0.125 to 0.125
- feedforward_up_adapters: bfloat16 [2, 128, 8192], P(None, ('seq', 'wa')), may hold values from -0.75 to 0.75
- downproj_down_adapters: bfloat16 [128, 8192], P(('seq', 'wa')), may hold values from -0.0625 to 0.0625
- downproj_up_adapters: bfloat16 [128, 2048], P(('seq', 'wa')), may hold values from -0.75 to 0.75
Outputs:
- layer_out: bfloat16 [8, 1024, 2048], P('wa', 'seq')
- input_grad: float32 [8, 1024, 2048], P('wa', 'seq')
- attn_a_grad: float32 [4, 128, 2048], P(None, ('seq', 'wa'))
- attn_b_grad: float32 [4, 128, 2048], P(None, ('seq', 'wa'))
- ffn_a_grad: float32 [2, 128, 2048], P(None, ('seq', 'wa'))
- ffn_b_grad: float32 [2, 128, 8192], P(None, ('seq', 'wa'))
- down_a_grad: float32 [128, 8192], P(('seq', 'wa'))
- down_b_grad: float32 [128, 2048], P(('seq', 'wa'))
Inputs may be any that keep to these rules, and one draw needn't show every extreme that they name: `token_document_index`: along a sequence the document number never falls and every one of the 8 numbers occurs; no document is longer than 512 tokens, and each sequence has one exactly that long.
All inputs are finite; a program needn't handle non-finite values.
Results may differ from a plain program's by a relative error of at most 0.018.
Values may be sent and summed in bfloat16 or wider, within the bound.
A program may use at most 320 MiB of HBM per device.

v0:
```python
import math

import jax
import jax.numpy as jnp
from jax import lax
from jax.sharding import PartitionSpec as P

HEADS = 16
HEAD_DIM = 128
ADAPTER_COUNT = 8
ADAPTER_RANK = 16


EPSILON = 1e-06
ROPE_BASE = 500000.0
MASKED = -1e30


def rope_tables(positions):
    inverse = 1.0 / ROPE_BASE ** (jnp.arange(0, HEAD_DIM, 2, dtype=jnp.float32) / HEAD_DIM)
    angle = positions[:, None] * inverse[None, :]
    return (jnp.cos(angle), jnp.sin(angle))


def rotate(values, cosine, sine):
    half_dim = values.shape[-1] // 2
    first = values[..., :half_dim]
    second = values[..., half_dim:]
    cos_part = cosine[:, None, :]
    sin_part = sine[:, None, :]
    return jnp.concatenate(
        [first * cos_part - second * sin_part, second * cos_part + first * sin_part], axis=-1
    )


def rms_scale(values, gain):
    return values * lax.rsqrt(jnp.mean(values * values, axis=-1, keepdims=True) + EPSILON) * gain


def times_t(left, weight):
    return lax.dot_general(
        left, weight, (((1,), (1,)), ((), ())), preferred_element_type=jnp.float32
    )


def choose(table, picker):
    if table.ndim == 3:
        grouped = table.reshape(table.shape[0], ADAPTER_COUNT, ADAPTER_RANK, table.shape[-1])
        chosen = jnp.einsum("sa,parx->psrx", picker, grouped, preferred_element_type=jnp.float32)
        return chosen.astype(jnp.bfloat16)
    grouped = table.reshape(ADAPTER_COUNT, ADAPTER_RANK, table.shape[-1])
    return jnp.einsum("sa,arx->srx", picker, grouped, preferred_element_type=jnp.float32).astype(
        jnp.bfloat16
    )


def spread_all(terms, onehot):
    placed = jnp.einsum(
        "hk,yhdb->ykdb",
        onehot,
        terms,
        precision=lax.Precision.HIGHEST,
        preferred_element_type=jnp.float32,
    )
    return placed.reshape(terms.shape[0], ADAPTER_COUNT * ADAPTER_RANK, terms.shape[-1])


def project(inputs, weight, down_map, up_map):
    seq_count, local_len, in_width = inputs.shape
    middle = jnp.einsum(
        "sli,sri->slr", inputs, down_map, preferred_element_type=jnp.float32
    ).astype(jnp.bfloat16)
    product = jnp.dot(
        inputs.reshape(seq_count * local_len, in_width), weight, preferred_element_type=jnp.float32
    )
    product = product.reshape(seq_count, local_len, weight.shape[1])
    return (
        product + jnp.einsum("slr,sro->slo", middle, up_map, preferred_element_type=jnp.float32),
        middle,
    )


def project_back(gradient, inputs, middle, weight, down_map, up_map):
    seq_count, local_len, out_width = gradient.shape
    grad_middle = jnp.einsum(
        "slo,sro->slr", gradient, up_map, preferred_element_type=jnp.float32
    ).astype(jnp.bfloat16)
    grad_input = times_t(gradient.reshape(seq_count * local_len, out_width), weight).reshape(
        seq_count, local_len, weight.shape[0]
    )
    grad_input = grad_input + jnp.einsum(
        "slr,sri->sli", grad_middle, down_map, preferred_element_type=jnp.float32
    )
    grad_up_map = jnp.einsum("slr,slo->sro", middle, gradient, preferred_element_type=jnp.float32)
    grad_down_map = jnp.einsum(
        "slr,sli->sri", grad_middle, inputs, preferred_element_type=jnp.float32
    )
    return (grad_input, grad_down_map, grad_up_map)


def masked_scores(query_block, key_block, row_segments, key_segments, start, key_start):
    scale = 1.0 / math.sqrt(key_block.shape[1])
    scores = (
        jnp.einsum("qd,kd->qk", query_block, key_block, preferred_element_type=jnp.float32) * scale
    )
    row_places = start + jnp.arange(query_block.shape[0])
    key_places = key_start + jnp.arange(key_block.shape[0])
    allowed = (key_places[None, :] <= row_places[:, None]) & (
        row_segments[:, None] == key_segments[None, :]
    )
    return jnp.where(allowed, scores, MASKED)


def key_span(segments, start, block_rows):
    first_segment = lax.dynamic_index_in_dim(segments, start, 0, keepdims=False)
    doc_start = jnp.sum((segments < first_segment).astype(jnp.int32))
    return (doc_start // block_rows, start // block_rows + 1)


def key_pieces(key, value, segments, key_start, block_rows):
    key_block = lax.dynamic_slice_in_dim(key, key_start, block_rows, 0)
    value_block = lax.dynamic_slice_in_dim(value, key_start, block_rows, 0)
    segment_block = lax.dynamic_slice_in_dim(segments, key_start, block_rows, 0)
    return (key_block, value_block, segment_block)


def attend_item(query, key, value, segments, block_rows):
    length, head_width = key.shape

    def one_block(start):
        query_block = lax.dynamic_slice_in_dim(query, start, block_rows, 0)
        row_segments = lax.dynamic_slice_in_dim(segments, start, block_rows, 0)
        lowest, highest = key_span(segments, start, block_rows)

        def top_pass(block_index, carry):
            row_top, row_total = carry
            key_start = block_index * block_rows
            key_block, value_block, segment_block = key_pieces(
                key, value, segments, key_start, block_rows
            )
            scores = masked_scores(
                query_block, key_block, row_segments, segment_block, start, key_start
            )
            new_top = jnp.maximum(row_top, jnp.max(scores, axis=1))
            row_total = row_total * jnp.exp(row_top - new_top) + jnp.sum(
                jnp.exp(scores - new_top[:, None]), axis=1
            )
            return (new_top, row_total)

        row_top, row_total = lax.fori_loop(
            lowest,
            highest,
            top_pass,
            (jnp.full((block_rows,), MASKED, jnp.float32), jnp.zeros((block_rows,), jnp.float32)),
        )
        log_total = row_top + jnp.log(row_total)

        def value_pass(block_index, summed):
            key_start = block_index * block_rows
            key_block, value_block, segment_block = key_pieces(
                key, value, segments, key_start, block_rows
            )
            scores = masked_scores(
                query_block, key_block, row_segments, segment_block, start, key_start
            )
            weights_soft = jnp.exp(scores - log_total[:, None]).astype(jnp.bfloat16)
            return summed + jnp.dot(weights_soft, value_block, preferred_element_type=jnp.float32)

        summed = lax.fori_loop(
            lowest, highest, value_pass, jnp.zeros((block_rows, head_width), jnp.float32)
        )
        return (summed.astype(jnp.bfloat16), log_total)

    starts = jnp.arange(length // block_rows) * block_rows
    results, log_totals = lax.map(one_block, starts)
    return (results.reshape(length, head_width), log_totals.reshape(length))


def attend_back(query, key, value, segments, log_total, grad_out, block_rows):
    length, head_width = key.shape
    scale = 1.0 / math.sqrt(head_width)

    def step(carry, start):
        query_block = lax.dynamic_slice_in_dim(query, start, block_rows, 0)
        grad_block = lax.dynamic_slice_in_dim(grad_out, start, block_rows, 0)
        total_block = lax.dynamic_slice_in_dim(log_total, start, block_rows, 0)
        row_segments = lax.dynamic_slice_in_dim(segments, start, block_rows, 0)
        lowest, highest = key_span(segments, start, block_rows)

        def block_terms(block_index):
            key_start = block_index * block_rows
            key_block, value_block, segment_block = key_pieces(
                key, value, segments, key_start, block_rows
            )
            scores = masked_scores(
                query_block, key_block, row_segments, segment_block, start, key_start
            )
            weights_soft = jnp.exp(scores - total_block[:, None])
            grad_weights = jnp.einsum(
                "qd,kd->qk", grad_block, value_block, preferred_element_type=jnp.float32
            )
            return (key_start, key_block, weights_soft, grad_weights)

        def dot_pass(block_index, row_dot):
            key_start, key_block, weights_soft, grad_weights = block_terms(block_index)
            return row_dot + jnp.sum(weights_soft * grad_weights, axis=1)

        row_dot = lax.fori_loop(lowest, highest, dot_pass, jnp.zeros((block_rows,), jnp.float32))

        def grad_pass(block_index, inner):
            query_grad, key_grad, value_grad = inner
            key_start, key_block, weights_soft, grad_weights = block_terms(block_index)
            value_piece = jnp.einsum(
                "qk,qd->kd",
                weights_soft.astype(jnp.bfloat16),
                grad_block,
                preferred_element_type=jnp.float32,
            )
            value_grad = lax.dynamic_update_slice_in_dim(
                value_grad,
                lax.dynamic_slice_in_dim(value_grad, key_start, block_rows, 0) + value_piece,
                key_start,
                0,
            )
            grad_scores = (weights_soft * (grad_weights - row_dot[:, None])).astype(jnp.bfloat16)
            query_grad = (
                query_grad
                + jnp.dot(grad_scores, key_block, preferred_element_type=jnp.float32) * scale
            )
            key_piece = (
                jnp.einsum(
                    "qk,qd->kd", grad_scores, query_block, preferred_element_type=jnp.float32
                )
                * scale
            )
            key_grad = lax.dynamic_update_slice_in_dim(
                key_grad,
                lax.dynamic_slice_in_dim(key_grad, key_start, block_rows, 0) + key_piece,
                key_start,
                0,
            )
            return (query_grad, key_grad, value_grad)

        key_grad, value_grad = carry
        query_grad, key_grad, value_grad = lax.fori_loop(
            lowest,
            highest,
            grad_pass,
            (jnp.zeros((block_rows, head_width), jnp.float32), key_grad, value_grad),
        )
        return ((key_grad, value_grad), query_grad.astype(jnp.bfloat16))

    zeros = jnp.zeros((length, head_width), jnp.float32)
    starts = jnp.arange(length // block_rows) * block_rows
    (key_grad, value_grad), query_grads = lax.scan(step, (zeros, zeros), starts)
    return (
        query_grads.reshape(length, head_width),
        key_grad.astype(jnp.bfloat16),
        value_grad.astype(jnp.bfloat16),
    )


def per_device(
    tokens,
    cotangent,
    token_document_index,
    sequence_adapter_index,
    query_weight,
    key_weight,
    value_weight,
    output_weight,
    gate_weight,
    up_weight,
    down_weight,
    query_norm_gain,
    key_norm_gain,
    attention_norm_gain,
    feedforward_norm_gain,
    attention_down_adapters,
    attention_up_adapters,
    feedforward_down_adapters,
    feedforward_up_adapters,
    downproj_down_adapters,
    downproj_up_adapters,
):
    seq_count, local_len, model_width = tokens.shape
    seq_devices = lax.axis_size("seq")
    full_len = local_len * seq_devices
    block_rows = min(512, full_len)
    item_count = seq_count * HEADS // seq_devices
    matches = sequence_adapter_index[:, None] == jnp.arange(ADAPTER_COUNT)[None, :]
    picker = matches.astype(jnp.bfloat16)
    onehot = matches.astype(jnp.float32)
    positions = (lax.axis_index("seq") * local_len + jnp.arange(local_len)).astype(jnp.float32)
    cosine, sine = rope_tables(positions)
    gain_q = query_norm_gain.astype(jnp.float32)
    gain_k = key_norm_gain.astype(jnp.float32)
    gain_a = attention_norm_gain.astype(jnp.float32)
    gain_f = feedforward_norm_gain.astype(jnp.float32)

    def heads_major(array):
        return (
            array.reshape(seq_count, local_len, HEADS, HEAD_DIM)
            .transpose(0, 2, 1, 3)
            .reshape(seq_count * HEADS, local_len, HEAD_DIM)
        )

    def tokens_split(array):
        return array.reshape(seq_count, HEADS, local_len, HEAD_DIM).transpose(0, 2, 1, 3)

    def norm_rope(gain):
        return lambda values: rotate(
            rms_scale(values, gain).reshape(seq_count, local_len, HEADS, HEAD_DIM), cosine, sine
        )

    query_full, key_full, value_full, out_full, attn_down_tab, attn_up_tab = (
        lax.all_gather(query_weight, ("seq", "wa"), axis=0, tiled=True),
        lax.all_gather(key_weight, ("seq", "wa"), axis=0, tiled=True),
        lax.all_gather(value_weight, ("seq", "wa"), axis=0, tiled=True),
        lax.all_gather(output_weight, ("seq", "wa"), axis=0, tiled=True),
        lax.all_gather(attention_down_adapters, ("seq", "wa"), axis=1, tiled=True),
        lax.all_gather(attention_up_adapters, ("seq", "wa"), axis=1, tiled=True),
    )
    attn_down = choose(attn_down_tab, picker)
    attn_up = choose(attn_up_tab, picker)
    query_raw, query_mid = project(tokens, query_full, attn_down[0], attn_up[0])
    key_raw, key_mid = project(tokens, key_full, attn_down[1], attn_up[1])
    value_raw, value_mid = project(tokens, value_full, attn_down[2], attn_up[2])
    value_low = value_raw.astype(jnp.bfloat16)
    query_rot, query_pull = jax.vjp(norm_rope(gain_q), query_raw)
    key_rot, key_pull = jax.vjp(norm_rope(gain_k), key_raw)
    whole_segments = lax.all_gather(token_document_index, "seq", axis=1, tiled=True)
    query_items, key_items, value_items = (
        lax.all_to_all(
            heads_major(query_rot.astype(jnp.bfloat16)),
            "seq",
            split_axis=0,
            concat_axis=1,
            tiled=True,
        ),
        lax.all_to_all(
            heads_major(key_rot.astype(jnp.bfloat16)),
            "seq",
            split_axis=0,
            concat_axis=1,
            tiled=True,
        ),
        lax.all_to_all(heads_major(value_low), "seq", split_axis=0, concat_axis=1, tiled=True),
    )
    item_seq = (lax.axis_index("seq") * item_count + jnp.arange(item_count)) // HEADS
    owner = (item_seq[:, None] == jnp.arange(seq_count)[None, :])[:, :, None]
    item_segments = jnp.sum(jnp.where(owner, whole_segments[None, :, :], 0), axis=1)
    attended_items, log_totals = lax.map(
        lambda packed: attend_item(packed[0], packed[1], packed[2], packed[3], block_rows),
        (query_items, key_items, value_items, item_segments),
    )
    attended_back = lax.all_to_all(attended_items, "seq", split_axis=1, concat_axis=0, tiled=True)
    attended = tokens_split(attended_back).reshape(seq_count, local_len, model_width)
    branch, out_mid = project(attended, out_full, attn_down[3], attn_up[3])
    normed, attn_pull = jax.vjp(lambda values: rms_scale(values, gain_a), branch)
    hidden = tokens.astype(jnp.float32) + normed
    hidden_low = hidden.astype(jnp.bfloat16)
    gate_full, up_full, down_full, ffn_down_tab, ffn_up_tab, down_down_tab, down_up_tab = (
        lax.all_gather(gate_weight, ("seq", "wa"), axis=0, tiled=True),
        lax.all_gather(up_weight, ("seq", "wa"), axis=0, tiled=True),
        lax.all_gather(down_weight, ("seq", "wa"), axis=0, tiled=True),
        lax.all_gather(feedforward_down_adapters, ("seq", "wa"), axis=1, tiled=True),
        lax.all_gather(feedforward_up_adapters, ("seq", "wa"), axis=1, tiled=True),
        lax.all_gather(downproj_down_adapters, ("seq", "wa"), axis=0, tiled=True),
        lax.all_gather(downproj_up_adapters, ("seq", "wa"), axis=0, tiled=True),
    )
    ffn_down = choose(ffn_down_tab, picker)
    ffn_up = choose(ffn_up_tab, picker)
    down_down = choose(down_down_tab, picker)
    down_up = choose(down_up_tab, picker)
    gate, gate_mid = project(hidden_low, gate_full, ffn_down[0], ffn_up[0])
    up_value, up_mid = project(hidden_low, up_full, ffn_down[1], ffn_up[1])
    mixed_full, mixed_pull = jax.vjp(
        lambda gate_in, up_in: gate_in * jax.nn.sigmoid(gate_in) * up_in, gate, up_value
    )
    mixed = mixed_full.astype(jnp.bfloat16)
    ffn_branch, down_mid = project(mixed, down_full, down_down, down_up)
    ffn_normed, ffn_pull = jax.vjp(lambda values: rms_scale(values, gain_f), ffn_branch)
    layer_out = (hidden + ffn_normed).astype(jnp.bfloat16)
    gate_full, up_full, down_full = (
        lax.all_gather(gate_weight, ("seq", "wa"), axis=0, tiled=True),
        lax.all_gather(up_weight, ("seq", "wa"), axis=0, tiled=True),
        lax.all_gather(down_weight, ("seq", "wa"), axis=0, tiled=True),
    )
    d_ffn = ffn_pull(cotangent)[0].astype(jnp.bfloat16)
    d_mixed, down_a_terms, down_b_terms = project_back(
        d_ffn, mixed, down_mid, down_full, down_down, down_up
    )
    d_gate, d_up = mixed_pull(d_mixed)
    d_gate = d_gate.astype(jnp.bfloat16)
    d_up = d_up.astype(jnp.bfloat16)
    gate_input, gate_a_terms, gate_b_terms = project_back(
        d_gate, hidden_low, gate_mid, gate_full, ffn_down[0], ffn_up[0]
    )
    up_input, up_a_terms, up_b_terms = project_back(
        d_up, hidden_low, up_mid, up_full, ffn_down[1], ffn_up[1]
    )
    d_hidden = cotangent + gate_input + up_input
    d_branch = attn_pull(d_hidden)[0].astype(jnp.bfloat16)
    query_full, key_full, value_full, out_full = (
        lax.all_gather(query_weight, ("seq", "wa"), axis=0, tiled=True),
        lax.all_gather(key_weight, ("seq", "wa"), axis=0, tiled=True),
        lax.all_gather(value_weight, ("seq", "wa"), axis=0, tiled=True),
        lax.all_gather(output_weight, ("seq", "wa"), axis=0, tiled=True),
    )
    d_attended, out_a_terms, out_b_terms = project_back(
        d_branch, attended, out_mid, out_full, attn_down[3], attn_up[3]
    )
    d_items = lax.all_to_all(
        heads_major(d_attended.astype(jnp.bfloat16)), "seq", split_axis=0, concat_axis=1, tiled=True
    )
    d_query_items, d_key_items, d_value_items = lax.map(
        lambda packed: attend_back(
            packed[0], packed[1], packed[2], packed[3], packed[4], packed[5], block_rows
        ),
        (query_items, key_items, value_items, item_segments, log_totals, d_items),
    )
    d_query_back, d_key_back, d_value_back = (
        lax.all_to_all(d_query_items, "seq", split_axis=1, concat_axis=0, tiled=True),
        lax.all_to_all(d_key_items, "seq", split_axis=1, concat_axis=0, tiled=True),
        lax.all_to_all(d_value_items, "seq", split_axis=1, concat_axis=0, tiled=True),
    )
    d_query_raw = query_pull(tokens_split(d_query_back).astype(jnp.float32))[0].astype(jnp.bfloat16)
    d_key_raw = key_pull(tokens_split(d_key_back).astype(jnp.float32))[0].astype(jnp.bfloat16)
    d_value = tokens_split(d_value_back).reshape(seq_count, local_len, model_width)
    query_input, query_a_terms, query_b_terms = project_back(
        d_query_raw, tokens, query_mid, query_full, attn_down[0], attn_up[0]
    )
    key_input, key_a_terms, key_b_terms = project_back(
        d_key_raw, tokens, key_mid, key_full, attn_down[1], attn_up[1]
    )
    value_input, value_a_terms, value_b_terms = project_back(
        d_value, tokens, value_mid, value_full, attn_down[2], attn_up[2]
    )
    input_grad = d_hidden + query_input + key_input + value_input
    all_terms = (
        jnp.stack([query_a_terms, key_a_terms, value_a_terms, out_a_terms]),
        jnp.stack([query_b_terms, key_b_terms, value_b_terms, out_b_terms]),
        jnp.stack([gate_a_terms, up_a_terms]),
        jnp.stack([gate_b_terms, up_b_terms]),
        down_a_terms[None],
        down_b_terms[None],
    )
    placed = tuple((spread_all(element_entry, onehot) for element_entry in all_terms))
    owned = (
        lax.psum_scatter(placed[0], ("seq", "wa"), scatter_dimension=1, tiled=True),
        lax.psum_scatter(placed[1], ("seq", "wa"), scatter_dimension=1, tiled=True),
        lax.psum_scatter(placed[2], ("seq", "wa"), scatter_dimension=1, tiled=True),
        lax.psum_scatter(placed[3], ("seq", "wa"), scatter_dimension=1, tiled=True),
        lax.psum_scatter(placed[4], ("seq", "wa"), scatter_dimension=1, tiled=True),
        lax.psum_scatter(placed[5], ("seq", "wa"), scatter_dimension=1, tiled=True),
    )
    return (layer_out, input_grad, owned[0], owned[1], owned[2], owned[3], owned[4][0], owned[5][0])


def solution(mesh):
    in_specs = (
        P("wa", "seq", None),
        P("wa", "seq", None),
        P("wa", "seq"),
        P("wa"),
        P(("seq", "wa"), None),
        P(("seq", "wa"), None),
        P(("seq", "wa"), None),
        P(("seq", "wa"), None),
        P(("seq", "wa"), None),
        P(("seq", "wa"), None),
        P(("seq", "wa"), None),
        P(),
        P(),
        P(),
        P(),
        P(None, ("seq", "wa"), None),
        P(None, ("seq", "wa"), None),
        P(None, ("seq", "wa"), None),
        P(None, ("seq", "wa"), None),
        P(("seq", "wa"), None),
        P(("seq", "wa"), None),
    )
    out_specs = (
        P("wa", "seq", None),
        P("wa", "seq", None),
        P(None, ("seq", "wa"), None),
        P(None, ("seq", "wa"), None),
        P(None, ("seq", "wa"), None),
        P(None, ("seq", "wa"), None),
        P(("seq", "wa"), None),
        P(("seq", "wa"), None),
    )
    return jax.shard_map(
        per_device, mesh=mesh, in_specs=in_specs, out_specs=out_specs, check_vma=False
    )
```

profile of v0, /device:TPU:6, one launch (start us, length us, event | category | flops | bytes accessed | tf_op | source)
XLA Modules:
  0.0 2070.2 jit_solution(1740895736547940977)
XLA Ops:
  19.4 48.8 %all-gather.17.cloned.1.call-done = bf16[4,128,2048]{2,0,1:T(4,128)(2,1)} async-done(((bf16[4,4,2048]{2,0,1:T(4,128)(2,1)}), bf16[4,128,2048]{2,0,1:T(4,128)(2,1)}) %all-gather.17.cloned.1.call-update) | async-done | bytes 2097168 | tf_op jit(solution)/shard_map/all_gather | solution.py:321
  73.4 53.4 %all-gather.19.cloned.1.call-done = bf16[4,128,2048]{2,0,1:T(4,128)(2,1)} async-done(((bf16[4,4,2048]{2,0,1:T(4,128)(2,1)}), bf16[4,128,2048]{2,0,1:T(4,128)(2,1)}) %all-gather.19.cloned.1.call-update) | async-done | bytes 2097168 | tf_op jit(solution)/shard_map/all_gather | solution.py:322
  132.9 73.1 %all-gather.21.cloned.1.call-done = bf16[2048,2048]{1,0:T(8,128)(2,1)} async-done(((bf16[64,2048]{1,0:T(8,128)(2,1)}), bf16[2048,2048]{1,0:T(8,128)(2,1)}) %all-gather.21.cloned.1.call-update) | async-done | bytes 8388624 | tf_op jit(solution)/shard_map/all_gather | solution.py:318
  214.0 70.8 %all-gather.15.cloned.1.call-done = bf16[2048,2048]{1,0:T(8,128)(2,1)} async-done(((bf16[64,2048]{1,0:T(8,128)(2,1)}), bf16[2048,2048]{1,0:T(8,128)(2,1)}) %all-gather.15.cloned.1.call-update) | async-done | bytes 8388624 | tf_op jit(solution)/shard_map/all_gather | solution.py:317
  305.7 35.3 %all-to-all-done = bf16[32,128,128]{2,1,0:T(8,128)(2,1)} async-done(((bf16[32,128,128]{2,1,0:T(8,128)(2,1)}), bf16[32,128,128]{2,1,0:T(8,128)(2,1)}, u32[]{:S(2)}, u32[]{:S(2)}) %all-to-all-start) | async-done | bytes 1048608 | tf_op jit(solution)/shard_map/all_to_all | solution.py:334
  347.2 48.6 %all-gather.23.cloned.1.call-done = bf16[2048,2048]{1,0:T(8,128)(2,1)} async-done(((bf16[64,2048]{1,0:T(8,128)(2,1)}), bf16[2048,2048]{1,0:T(8,128)(2,1)}) %all-gather.23.cloned.1.call-update) | async-done | bytes 8388624 | tf_op jit(solution)/shard_map/all_gather | solution.py:319
  408.2 51.1 %all-gather.1 = bf16[32,4,2048]{2,1,0:T(4,128)(2,1)S(1)} all-gather(bf16[1,4,2048]{2,1,0:T(4,128)(2,1)S(1)} %bitcast.547), channel_id=1, replica_groups=mesh['seq'=8,'wa'=4] {'seq','wa'}, dimensions={0}, use_global_device_ids=true | all-gather | bytes 540672 | tf_op jit(solution)/shard_map/all_gather | solution.py:370
  459.3 20.8 %all_gather.52 = s32[2,1024]{1,0:T(2,128)S(1)} all-gather(s32[2,128]{1,0:T(2,128)S(1)} %copy-done.110), channel_id=1, replica_groups=mesh['seq'=8,'wa'=4] {'seq'}, dimensions={1}, use_global_device_ids=true | all-gather | bytes 9216 | tf_op jit(solution)/shard_map/all_gather | solution.py:332
  484.7 32.4 %all-gather.37.cloned.1.call-done = bf16[32,4,8192]{2,1,0:T(4,128)(2,1)} async-done(((bf16[1,4,8192]{2,1,0:T(4,128)(2,1)}), bf16[32,4,8192]{2,1,0:T(4,128)(2,1)}) %all-gather.37.cloned.1.call-update) | async-done | bytes 2097168 | tf_op jit(solution)/shard_map/all_gather | solution.py:369
  528.8 122.6 %while.184 = (s32[]{:T(128)}, bf16[4,1024,128]{2,1,0:T(8,128)(2,1)S(1)}, f32[4,1024]{1,0:T(4,128)}, bf16[4,1024,128]{2,1,0:T(8,128)(2,1)}, s32[4,1024]{1,0:T(4,1...) while((s32[]{:T(128)}, ...), condition=%wide.region_13.14_spmd, body=%wide.region_3.13_spmd.sunk | while | flops 205396512 | bytes 6402717 | solution.py:353
  530.9 27.1 %while.187 = (s32[]{:T(128)}, bf16[2,512,128]{2,1,0:T(8,128)(2,1)S(1)}, f32[2,512]{1,0:T(2,128)S(1)}, s32[2]{0:T(128)S(1)}, s32[1024]{0:T(1024)S(1)}, /*index=5*...) while((s32[]{:T(128)}, ...), condition=%wide.region_12.12_spmd, body=%wide.region_4.11_spmd.sunk | while | flops 205396512 | bytes 4280532 | solution.py:175
  561.5 27.1 %while.187 = (s32[]{:T(128)}, bf16[2,512,128]{2,1,0:T(8,128)(2,1)S(1)}, f32[2,512]{1,0:T(2,128)S(1)}, s32[2]{0:T(128)S(1)}, s32[1024]{0:T(1024)S(1)}, /*index=5*...) while((s32[]{:T(128)}, ...), condition=%wide.region_12.12_spmd, body=%wide.region_4.11_spmd.sunk | while | flops 205396512 | bytes 4280532 | solution.py:175
  592.2 27.1 %while.187 = (s32[]{:T(128)}, bf16[2,512,128]{2,1,0:T(8,128)(2,1)S(1)}, f32[2,512]{1,0:T(2,128)S(1)}, s32[2]{0:T(128)S(1)}, s32[1024]{0:T(1024)S(1)}, /*index=5*...) while((s32[]{:T(128)}, ...), condition=%wide.region_12.12_spmd, body=%wide.region_4.11_spmd.sunk | while | flops 205396512 | bytes 4280532 | solution.py:175
  622.8 27.2 %while.187 = (s32[]{:T(128)}, bf16[2,512,128]{2,1,0:T(8,128)(2,1)S(1)}, f32[2,512]{1,0:T(2,128)S(1)}, s32[2]{0:T(128)S(1)}, s32[1024]{0:T(1024)S(1)}, /*index=5*...) while((s32[]{:T(128)}, ...), condition=%wide.region_12.12_spmd, body=%wide.region_4.11_spmd.sunk | while | flops 205396512 | bytes 4280532 | solution.py:175
  666.9 30.7 %all-to-all-done.3 = bf16[4,1024,128]{2,0,1:T(4,128)(2,1)S(1)} async-done(((bf16[4,1024,128]{2,0,1:T(4,128)(2,1)}), bf16[4,1024,128]{2,0,1:T(4,128)(2,1)S(1)}, u32[]{:S(2)}, u32[]{:S(2)}) %all-to-all-start.3) | async-done | bytes 1048608 | tf_op jit(solution)/shard_map/all_to_all | solution.py:357
  716.3 148.4 %all-gather.27.cloned.1.call-done = bf16[2048,8192]{1,0:T(8,128)(2,1)} async-done(((bf16[64,8192]{1,0:T(8,128)(2,1)}), bf16[2048,8192]{1,0:T(8,128)(2,1)}) %all-gather.27.cloned.1.call-update) | async-done | bytes 33554448 | tf_op jit(solution)/shard_map/all_gather | solution.py:364
  864.7 22.0 %fusion.68 = f32[2,128,8192]{2,1,0:T(8,128)} fusion(f32[2,128,8192]{2,1,0:T(8,128)} %fusion.141, bf16[2,128,2048]{2,1,0:T(8,128)(2,1)S(1)} %fusion.116, bf16[2048,8192]{1,0:T(8,128)(2,1)} %all-gather.27.cloned.1.call-done), kind=kOutput, calls=%fused_computation.110 | convolution fusion | flops 8592031744 | bytes 51380224 | tf_op jit(solution)/shard_map/dot_general | solution.py:73
  886.7 173.8 %all-gather.33.cloned.1.call-done = bf16[2048,8192]{1,0:T(8,128)(2,1)} async-done(((bf16[64,8192]{1,0:T(8,128)(2,1)}), bf16[2048,8192]{1,0:T(8,128)(2,1)}) %all-gather.33.cloned.1.call-update) | async-done | bytes 33554448 | tf_op jit(solution)/shard_map/all_gather | solution.py:365
  1060.5 26.0 %multiply_convert_fusion.1 = (bf16[2,128,8192]{2,1,0:T(8,128)(2,1)S(1)}, f32[2,128,8192]{2,1,0:T(8,128)}) fusion(f32[2,128,8192]{2,1,0:T(8,128)} %fusion.68, f32[2,128,8192]{2,1,0:T(8,128)} %fusion.138, bf16[2,128,2048]{2,1,0:T(8,128)(2,1)S(1)} %fusion.116, bf16[2048,8192]{1,0:T(8,128)(2,1)} %all-gather.33.cloned.1.call-done), kind=kOutput, calls=%fused_computation.140 | convolution fusion | flops 8604614656 | bytes 63963136 | tf_op jit(solution)/shard_map/dot_general | solution.py:73
  1090.4 165.8 %all-gather.35.cloned.1.call-done = bf16[8192,2048]{1,0:T(8,128)(2,1)} async-done(((bf16[256,2048]{1,0:T(8,128)(2,1)}), bf16[8192,2048]{1,0:T(8,128)(2,1)}) %all-gather.35.cloned.1.call-update) | async-done | bytes 33554448 | tf_op jit(solution)/shard_map/all_gather | solution.py:366
  1256.3 16.7 fusion.58
  1277.2 18.5 fusion.56
  1311.2 16.9 fusion.64
  1331.5 17.5 fusion.60
  1365.2 25.9 %all-to-all-done.4 = bf16[32,128,128]{2,1,0:T(8,128)(2,1)S(1)} async-done(((bf16[32,128,128]{2,1,0:T(8,128)(2,1)}), bf16[32,128,128]{2,1,0:T(8,128)(2,1)S(1)}, u32[]{:S(2)}, u32[]{:S(2)}) %all-to-all-start.4) | async-done | bytes 1048608 | tf_op jit(solution)/shard_map/all_to_all | solution.py:414
  1395.5 152.1 %while.186 = (s32[]{:T(128)}, bf16[4,1024,128]{2,1,0:T(8,128)(2,1)}, bf16[4,1024,128]{2,1,0:T(8,128)(2,1)}, bf16[4,1024,128]{2,1,0:T(8,128)(2,1)}, bf16[4,1024,1...) while((s32[]{:T(128)}, bf16[4,1024,128]{2,1,0:T(8,128)(2,1)}, ...), condition=%wide.region_27.28_spmd, body=%wide.region_18.27_spmd.sunk | while | flops 475141152 | bytes 16332637 | solution.py:417
  1401.0 31.0 %while.188 = (s32[]{:T(128)}, f32[1024,128]{1,0:T(8,128)S(1)}, f32[1024,128]{1,0:T(8,128)S(1)}, bf16[2,512,128]{2,1,0:T(8,128)(2,1)S(1)}, s32[2]{0:T(128)S(1)}, ...) while((s32[]{:T(128)}, f32[1024,128]{1,0:T(8,128)S(1)}, ...), condition=%wide.region_26.26_spmd, body=%wide.region_19.25_spmd.sunk | while | flops 474879008 | bytes 11072856 | solution.py:255
  1439.0 31.0 %while.188 = (s32[]{:T(128)}, f32[1024,128]{1,0:T(8,128)S(1)}, f32[1024,128]{1,0:T(8,128)S(1)}, bf16[2,512,128]{2,1,0:T(8,128)(2,1)S(1)}, s32[2]{0:T(128)S(1)}, ...) while((s32[]{:T(128)}, f32[1024,128]{1,0:T(8,128)S(1)}, ...), condition=%wide.region_26.26_spmd, body=%wide.region_19.25_spmd.sunk | while | flops 474879008 | bytes 11072856 | solution.py:255
  1477.0 31.0 %while.188 = (s32[]{:T(128)}, f32[1024,128]{1,0:T(8,128)S(1)}, f32[1024,128]{1,0:T(8,128)S(1)}, bf16[2,512,128]{2,1,0:T(8,128)(2,1)S(1)}, s32[2]{0:T(128)S(1)}, ...) while((s32[]{:T(128)}, f32[1024,128]{1,0:T(8,128)S(1)}, ...), condition=%wide.region_26.26_spmd, body=%wide.region_19.25_spmd.sunk | while | flops 474879008 | bytes 11072856 | solution.py:255
  1515.0 31.0 %while.188 = (s32[]{:T(128)}, f32[1024,128]{1,0:T(8,128)S(1)}, f32[1024,128]{1,0:T(8,128)S(1)}, bf16[2,512,128]{2,1,0:T(8,128)(2,1)S(1)}, s32[2]{0:T(128)S(1)}, ...) while((s32[]{:T(128)}, f32[1024,128]{1,0:T(8,128)S(1)}, ...), condition=%wide.region_26.26_spmd, body=%wide.region_19.25_spmd.sunk | while | flops 474879008 | bytes 11072856 | solution.py:255
  1561.2 19.2 all-to-all-done.6
  1684.5 369.3 %all-reduce.13.cloned.1.call-done = (f32[4,128,2048]{2,1,0:T(8,128)}, f32[4,128,2048]{2,1,0:T(8,128)}, f32[2,128,2048]{2,1,0:T(8,128)}, f32[2,128,8192]{2,1,0:T(...) async-done(((f32[4,128,2048]{2,1,0:T(8,128)}, f32[4,128,2048]{2,1,0:T(8,128)}, f32[2,128,2048]{2,1,0:T(8,128)}, f32[2,128,8192]{2,1,0:T(8,128)}, ...) | async-done | bytes 24117264
  (959 shorter events, 545.7 us)
Async XLA Ops:
  7.2 61.0 %all-gather.17.cloned.1.call-start = ((), (), s32[]{:S(2)}) async-start(), calls=%async_computation.9 | async-start | bytes 2162688 | tf_op jit(solution)/shard_map/all_gather | solution.py:321
  8.8 118.1 %all-gather.19.cloned.1.call-start = ((), (), s32[]{:S(2)}) async-start(), calls=%async_computation.10 | async-start | bytes 2162688 | tf_op jit(solution)/shard_map/all_gather | solution.py:322
  10.4 195.7 %all-gather.21.cloned.1.call-start = ((), (), s32[]{:S(2)}) async-start(), calls=%async_computation.11 | async-start | bytes 8650752 | tf_op jit(solution)/shard_map/all_gather | solution.py:318
  11.1 273.7 %all-gather.15.cloned.1.call-start = ((), (), s32[]{:S(2)}) async-start(), calls=%async_computation.8 | async-start | bytes 8650752 | tf_op jit(solution)/shard_map/all_gather | solution.py:317
  11.7 384.1 %all-gather.23.cloned.1.call-start = ((), (), s32[]{:S(2)}) async-start(), calls=%async_computation.12 | async-start | bytes 8650752 | tf_op jit(solution)/shard_map/all_gather | solution.py:319
  12.3 469.0 %all-gather.29.cloned.1.call-start = ((), (), s32[]{:S(2)}) async-start(), calls=%async_computation.15 | async-start | bytes 1081344 | tf_op jit(solution)/shard_map/all_gather | solution.py:367
  13.8 503.3 %all-gather.37.cloned.1.call-start = ((), (), s32[]{:S(2)}) async-start(), calls=%async_computation.19 | async-start | bytes 2162688 | tf_op jit(solution)/shard_map/all_gather | solution.py:369
  14.5 643.9 %all-gather.31.cloned.1.call-start = ((), (), s32[]{:S(2)}) async-start(), calls=%async_computation.16 | async-start | bytes 4325376 | tf_op jit(solution)/shard_map/all_gather | solution.py:368
  16.3 681.9 %all-gather.25.cloned.1.call-start = ((), (), s32[]{:S(2)}) async-start(), calls=%async_computation.13 | async-start | bytes 8650752 | tf_op jit(solution)/shard_map/all_gather | solution.py:320
  17.0 847.7 %all-gather.27.cloned.1.call-start = ((), (), s32[]{:S(2)}) async-start(), calls=%async_computation.14 | async-start | bytes 34603008 | tf_op jit(solution)/shard_map/all_gather | solution.py:364
  17.6 1042.9 %all-gather.33.cloned.1.call-start = ((), (), s32[]{:S(2)}) async-start(), calls=%async_computation.17 | async-start | bytes 34603008 | tf_op jit(solution)/shard_map/all_gather | solution.py:365
  18.4 1237.9 %all-gather.35.cloned.1.call-start = ((), (), s32[]{:S(2)}) async-start(), calls=%async_computation.18 | async-start | bytes 34603008 | tf_op jit(solution)/shard_map/all_gather | solution.py:366
  19.0 193.4 %copy-start.65 = (f32[2048]{0:T(1024)}, f32[2048]{0:T(1024)S(1)}, u32[]{:S(2)}) copy-start(f32[2048]{0:T(1024)S(1)} %convert_element_type.220) | copy-start | bytes 24580
  19.0 272.2 %copy-start.63 = (f32[2048]{0:T(1024)}, f32[2048]{0:T(1024)S(1)}, u32[]{:S(2)}) copy-start(f32[2048]{0:T(1024)S(1)} %convert_element_type.217) | copy-start | bytes 24580
  19.3 274.9 %copy-start.50 = (f32[128,64]{1,0:T(8,128)}, f32[128,64]{1,0:T(8,128)S(1)}, u32[]{:S(2)}) copy-start(f32[128,64]{1,0:T(8,128)S(1)} %get-tuple-element.1030) | copy-start | bytes 98308
  19.4 274.9 %copy-start.52 = (f32[128,64]{1,0:T(8,128)}, f32[128,64]{1,0:T(8,128)S(1)}, u32[]{:S(2)}) copy-start(f32[128,64]{1,0:T(8,128)S(1)} %get-tuple-element.1031) | copy-start | bytes 98308
  73.4 273.5 %copy-start.36 = (bf16[2,16,2048]{2,0,1:T(2,128)(2,1)}, bf16[2,16,2048]{2,0,1:T(2,128)(2,1)S(1)}, u32[]{:S(2)}) copy-start(bf16[2,16,2048]{2,0,1:T(2,128)(2,1)S(1)} %get-tuple-element.1019) | copy-start | bytes 393220
  132.1 158.4 %copy-start.42 = (bf16[2,16,2048]{2,0,1:T(2,128)(2,1)}, bf16[2,16,2048]{2,0,1:T(2,128)(2,1)S(1)}, u32[]{:S(2)}) copy-start(bf16[2,16,2048]{2,0,1:T(2,128)(2,1)S(1)} %get-tuple-element.1017) | copy-start | bytes 393220
  298.5 42.4 %all-to-all-start = ((bf16[32,128,128]{2,1,0:T(8,128)(2,1)}), bf16[32,128,128]{2,1,0:T(8,128)(2,1)}, u32[]{:S(2)}, u32[]{:S(2)}) async-start(bf16[32,128,128]{2,1,0:T(8,128)(2,1)} %bitcast.526), calls=%async_computation | async-start | bytes 2097152 | tf_op jit(solution)/shard_map/all_to_all | solution.py:334
  341.0 62.3 %all-to-all-start.1 = ((bf16[32,128,128]{2,1,0:T(8,128)(2,1)}), bf16[32,128,128]{2,1,0:T(8,128)(2,1)S(1)}, u32[]{:S(2)}, u32[]{:S(2)}) async-start(bf16[32,128,128]{2,1,0:T(8,128)(2,1)} %bitcast.525), calls=%async_computation.1 | async-start | bytes 2097152 | tf_op jit(solution)/shard_map/all_to_all | solution.py:341
  403.3 123.0 %all-to-all-start.2 = ((bf16[32,128,128]{2,1,0:T(8,128)(2,1)}), bf16[32,128,128]{2,1,0:T(8,128)(2,1)}, u32[]{:S(2)}, u32[]{:S(2)}) async-start(bf16[32,128,128]{2,1,0:T(8,128)(2,1)} %bitcast.54), calls=%async_computation.2 | async-start | bytes 2097152 | tf_op jit(solution)/shard_map/all_to_all | solution.py:348
  653.1 44.4 %all-to-all-start.3 = ((bf16[4,1024,128]{2,0,1:T(4,128)(2,1)}), bf16[4,1024,128]{2,0,1:T(4,128)(2,1)S(1)}, u32[]{:S(2)}, u32[]{:S(2)}) async-start(bf16[4,1024,128]{2,0,1:T(4,128)(2,1)} %copy.279), calls=%async_computation.3 | async-start | bytes 2097152 | tf_op jit(solution)/shard_map/all_to_all | solution.py:357
  706.0 354.6 %copy-start.3 = (bf16[2,128,2048]{2,1,0:T(8,128)(2,1)}, bf16[2,128,2048]{2,1,0:T(8,128)(2,1)S(1)}, u32[]{:S(2)}) copy-start(bf16[2,128,2048]{2,1,0:T(8,128)(2,1)S(1)} %fusion.116) | copy-start | bytes 3145732
  886.7 201.9 %copy-start.32 = (bf16[2,16,8192]{2,0,1:T(2,128)(2,1)S(1)}, bf16[2,16,8192]{2,0,1:T(2,128)(2,1)}, u32[]{:S(2)}) copy-start(bf16[2,16,8192]{2,0,1:T(2,128)(2,1)} %convolution_convert_fusion.1) | copy-start | bytes 1572868
  1090.4 182.5 %copy-start.11 = (f32[2,128,2048]{2,1,0:T(8,128)S(1)}, f32[2,128,2048]{2,1,0:T(8,128)}, u32[]{:S(2)}) copy-start(f32[2,128,2048]{2,1,0:T(8,128)} %param.38) | copy-start | bytes 6291460
  1090.4 182.6 %copy-start.35 = (bf16[2,16,2048]{2,0,1:T(2,128)(2,1)S(1)}, bf16[2,16,2048]{2,0,1:T(2,128)(2,1)}, u32[]{:S(2)}) copy-start(bf16[2,16,2048]{2,0,1:T(2,128)(2,1)} %convolution_convert_fusion.5) | copy-start | bytes 393220
  1090.4 182.6 %copy-start.68 = (f32[2048]{0:T(1024)S(1)}, f32[2048]{0:T(1024)}, u32[]{:S(2)}) copy-start(f32[2048]{0:T(1024)} %convert_element_type.236) | copy-start | bytes 24580
  1360.3 30.8 %all-to-all-start.4 = ((bf16[32,128,128]{2,1,0:T(8,128)(2,1)}), bf16[32,128,128]{2,1,0:T(8,128)(2,1)S(1)}, u32[]{:S(2)}, u32[]{:S(2)}) async-start(bf16[32,128,128]{2,1,0:T(8,128)(2,1)} %bitcast.80), calls=%async_computation.4 | async-start | bytes 2097152 | tf_op jit(solution)/shard_map/all_to_all | solution.py:414
  1550.7 29.7 %all-to-all-start.6 = ((bf16[4,1024,128]{2,0,1:T(4,128)(2,1)}), bf16[4,1024,128]{2,0,1:T(4,128)(2,1)S(1)}, u32[]{:S(2)}, u32[]{:S(2)}) async-start(bf16[4,1024,128]{2,0,1:T(4,128)(2,1)} %copy.315), calls=%async_computation.6 | async-start | bytes 2097152 | tf_op jit(solution)/shard_map/all_to_all | solution.py:425
  1580.5 29.6 %all-to-all-start.7 = ((bf16[4,1024,128]{2,0,1:T(4,128)(2,1)}), bf16[4,1024,128]{2,0,1:T(4,128)(2,1)S(1)}, u32[]{:S(2)}, u32[]{:S(2)}) async-start(bf16[4,1024,128]{2,0,1:T(4,128)(2,1)} %copy.321), calls=%async_computation.7 | async-start | bytes 2097152 | tf_op jit(solution)/shard_map/all_to_all | solution.py:426
  1610.0 29.7 %all-to-all-start.5 = ((bf16[4,1024,128]{2,0,1:T(4,128)(2,1)}), bf16[4,1024,128]{2,0,1:T(4,128)(2,1)}, u32[]{:S(2)}, u32[]{:S(2)}) async-start(bf16[4,1024,128]{2,0,1:T(4,128)(2,1)} %copy.309), calls=%async_computation.5 | async-start | bytes 2097152 | tf_op jit(solution)/shard_map/all_to_all | solution.py:424
  1614.8 439.0 %all-reduce.13.cloned.1.call-start = ((), (), s32[]{:S(2)}) async-start(), calls=%async_computation.20 | async-start | bytes 48234496
  (104 other events, 1389.6 us)
Sparse Core Ops, SparseCore 0:
  11.4 56.6 all-gather.16
  71.6 55.2 all-gather.18
  129.7 76.2 all-gather.20
  208.7 76.0 all-gather.14
  287.5 108.2 all-gather.22
  399.1 59.6 all-gather.28
  461.6 55.4 all-gather.36
  520.0 60.9 all-gather.30
  583.8 75.7 all-gather.24
  662.3 202.3 all-gather.26
  867.6 192.9 all-gather.32
  1063.3 192.9 all-gather.34
  1667.3 386.4 all-reduce.12
where the time goes:
time: 2090 us; the launch traced here: 2070 us
  waiting for transfers between devices  1310 us (63%)
  matrix products  295 us (14%)
  local copies, waits for them, and re-layouts  154 us (7%)
  loops' own time  108 us (5%)
  other arithmetic  76 us (4%)
  blocking collectives  71.8 us (3%)
  starting transfers between devices  39.1 us (2%)
    unnamed x14, waiting for transfers between devices  374 us
    all_gather x1, waiting for transfers between devices, per_device(): lax.all_gather(up_weight, ('seq', 'wa'), axis=0, tiled=True)  174 us
    all_gather x1, waiting for transfers between devices, per_device(): lax.all_gather(down_weight, ('seq', 'wa'), axis=0, tiled=True)  166 us
    all_gather x1, waiting for transfers between devices, per_device(): lax.all_gather(gate_weight, ('seq', 'wa'), axis=0, tiled=True)  148 us
    dot_general x7, matrix products, project(): jnp.dot(inputs.reshape(seq_count * local_len, in_width), weight, preferre...  87.6 us
    all_gather x1, waiting for transfers between devices, per_device(): lax.all_gather(key_weight, ('seq', 'wa'), axis=0, tiled=True)  73.1 us
    all_gather x1, waiting for transfers between devices, per_device(): lax.all_gather(query_weight, ('seq', 'wa'), axis=0, tiled=True)  70.8 us
    dot_general x7, matrix products, times_t(): lax.dot_general(left, weight, (((1,), (1,)), ((), ())), preferred_element...  69.7 us
  transfers between devices with their start and end apart: 21, of which 16 were waited for; matrix products, arithmetic and copies ran while one was open for 13% of the time, Pallas kernels for 0%

commit v1 on v0

--- a/solution.py
+++ b/solution.py
@@ -1,8 +1,11 @@
+import functools
 import math
 
 import jax
 import jax.numpy as jnp
 from jax import lax
+from jax.experimental import pallas as pl
+from jax.experimental.pallas import tpu as pltpu
 from jax.sharding import PartitionSpec as P
 
 HEADS = 16
@@ -458,7 +461,491 @@
     return (layer_out, input_grad, owned[0], owned[1], owned[2], owned[3], owned[4][0], owned[5][0])
 
 
+def low_dot(left, right):
+    return jnp.dot(left, right, preferred_element_type=jnp.float32)
+
+
+def dot_rows(left, right):
+    return lax.dot_general(
+        left, right, (((0,), (0,)), ((), ())), preferred_element_type=jnp.float32
+    )
+
+
+def rope_full(length):
+    cosine, sine = rope_tables(jnp.arange(length).astype(jnp.float32))
+    return (
+        jnp.concatenate([cosine, cosine], axis=-1),
+        jnp.concatenate([-sine, sine], axis=-1),
+    )
+
+
+def block_scores(query, key, doc_col, doc_row, row, first, rows):
+    scores = lax.dot_general(
+        query, key, (((1,), (1,)), ((), ())), preferred_element_type=jnp.float32
+    ) * (1.0 / math.sqrt(HEAD_DIM))
+    shape = scores.shape
+    row_at = row + lax.broadcasted_iota(jnp.int32, shape, 0)
+    key_at = first + lax.broadcasted_iota(jnp.int32, shape, 1)
+    allowed = (key_at <= row_at) & (doc_col == doc_row)
+    return jnp.where(allowed, scores, MASKED)
+
+
+def soft(scores):
+    top = jnp.max(scores, axis=1, keepdims=True)
+    raised = jnp.exp(scores - top)
+    return raised * (1.0 / jnp.sum(raised, axis=1, keepdims=True))
+
+
+def attend_kernel(
+    q_raw, k_raw, v_raw, q_sum, k_sum, gain_q, gain_k, cosine, sine, doc_col, doc_row,
+    out, q_out, k_out, v_out, *, rows, back,
+):
+    length = q_raw.shape[0]
+    width = HEADS * HEAD_DIM
+
+    def turned(raw, total, gain):
+        scale = lax.rsqrt(total[...] * (1.0 / width) + EPSILON)
+        normed = raw[...] * scale * gain[...]
+        return normed * cosine[...] + pltpu.roll(normed, HEAD_DIM // 2, 1) * sine[...]
+
+    q_out[...] = turned(q_raw, q_sum, gain_q).astype(jnp.bfloat16)
+    k_out[...] = turned(k_raw, k_sum, gain_k).astype(jnp.bfloat16)
+    v_out[...] = v_raw[...].astype(jnp.bfloat16)
+    for row in range(0, length, rows):
+        first, last = max(0, row - back), row + rows
+        scores = block_scores(
+            q_out[row:last, :], k_out[first:last, :], doc_col[row:last, :],
+            doc_row[:, first:last], row, first, rows,
+        )
+        probs = soft(scores).astype(jnp.bfloat16)
+        out[row:last, :] = low_dot(probs, v_out[first:last, :]).astype(jnp.bfloat16)
+
+
+def attend_back_kernel(
+    query, key, value, grad, q_raw, k_raw, gain_q, gain_k, cosine, sine, doc_col, doc_row,
+    t_q, t_k, d_value, q_dot, k_dot, dk_sum, dv_sum, *, rows, back,
+):
+    length = query.shape[0]
+    scale = 1.0 / math.sqrt(HEAD_DIM)
+
+    def unturned(turned_grad, gain):
+        low = turned_grad.astype(jnp.bfloat16).astype(jnp.float32)
+        plain = low * cosine_part + pltpu.roll(low * sine_part, HEAD_DIM // 2, 1)
+        return plain * gain[...]
+
+    dk_sum[...] = jnp.zeros_like(dk_sum)
+    dv_sum[...] = jnp.zeros_like(dv_sum)
+
+    @pl.when(pl.program_id(0) == 0)
+    def _():
+        q_dot[...] = jnp.zeros_like(q_dot)
+        k_dot[...] = jnp.zeros_like(k_dot)
+
+    for row in range(0, length, rows):
+        first, last = max(0, row - back), row + rows
+        scores = block_scores(
+            query[row:last, :], key[first:last, :], doc_col[row:last, :],
+            doc_row[:, first:last], row, first, rows,
+        )
+        probs = soft(scores)
+        grad_rows = grad[row:last, :]
+        d_probs = lax.dot_general(
+            grad_rows, value[first:last, :], (((1,), (1,)), ((), ())),
+            preferred_element_type=jnp.float32,
+        )
+        dots = jnp.sum(probs * d_probs, axis=1, keepdims=True)
+        d_scores = (probs * (d_probs - dots)).astype(jnp.bfloat16)
+        dv_sum[first:last, :] += dot_rows(probs.astype(jnp.bfloat16), grad_rows)
+        dk_sum[first:last, :] += dot_rows(d_scores, query[row:last, :])
+        dq = low_dot(d_scores, key[first:last, :]) * scale
+        cosine_part, sine_part = cosine[row:last, :], sine[row:last, :]
+        t_rows = unturned(dq, gain_q)
+        t_q[row:last, :] = t_rows
+        q_dot[row:last, :] += jnp.sum(q_raw[row:last, :] * t_rows, axis=1, keepdims=True)
+    cosine_part, sine_part = cosine[...], sine[...]
+    t_key = unturned(dk_sum[...] * scale, gain_k)
+    t_k[...] = t_key
+    k_dot[...] += jnp.sum(k_raw[...] * t_key, axis=1, keepdims=True)
+    d_value[...] = dv_sum[...].astype(jnp.bfloat16)
+
+
+def attention_specs(length):
+    head = lambda offset: pl.BlockSpec((length, HEAD_DIM), lambda h: (0, offset + h))
+    whole = lambda shape: pl.BlockSpec(shape, lambda h: (0, 0))
+    gain = lambda: pl.BlockSpec((1, HEAD_DIM), lambda h: (0, h))
+    return head, whole, gain
+
+
+def attend_heads(qkv_raw, q_sum, k_sum, gain_q, gain_k, tables, doc_col, doc_row, back):
+    length, heads = qkv_raw.shape[0], qkv_raw.shape[1] // (3 * HEAD_DIM)
+    head, whole, gain = attention_specs(length)
+    rows = min(256, length)
+    low = jax.ShapeDtypeStruct((length, heads * HEAD_DIM), jnp.bfloat16)
+    return pl.pallas_call(
+        functools.partial(attend_kernel, rows=rows, back=back),
+        grid=(heads,),
+        in_specs=[
+            head(0), head(heads), head(2 * heads), whole((length, 1)), whole((length, 1)),
+            gain(), gain(), whole((length, HEAD_DIM)), whole((length, HEAD_DIM)),
+            whole((length, 1)), whole((1, length)),
+        ],
+        out_specs=[head(0)] * 4,
+        out_shape=[low] * 4,
+        name="attend",
+        compiler_params=pltpu.CompilerParams(vmem_limit_bytes=48 << 20),
+        cost_estimate=pl.CostEstimate(
+            flops=heads * length * length * HEAD_DIM * 3, bytes_accessed=length * heads * 2560,
+            transcendentals=heads * length * length // 2,
+        ),
+    )(qkv_raw, qkv_raw, qkv_raw, q_sum, k_sum, gain_q, gain_k, *tables, doc_col, doc_row)
+
+
+def attend_heads_back(
+    query, key, value, grad, qkv_raw, gain_q, gain_k, tables, doc_col, doc_row, back
+):
+    length, heads = qkv_raw.shape[0], qkv_raw.shape[1] // (3 * HEAD_DIM)
+    head, whole, gain = attention_specs(length)
+    rows = min(256, length)
+    wide = jax.ShapeDtypeStruct((length, heads * HEAD_DIM), jnp.float32)
+    thin = jax.ShapeDtypeStruct((length, 1), jnp.float32)
+    return pl.pallas_call(
+        functools.partial(attend_back_kernel, rows=rows, back=back),
+        grid=(heads,),
+        in_specs=[head(0)] * 4
+        + [
+            head(0), head(heads), gain(), gain(), whole((length, HEAD_DIM)),
+            whole((length, HEAD_DIM)), whole((length, 1)), whole((1, length)),
+        ],
+        out_specs=[head(0), head(0), head(0), whole((length, 1)), whole((length, 1))],
+        out_shape=[
+            wide, wide, jax.ShapeDtypeStruct(wide.shape, jnp.bfloat16), thin, thin,
+        ],
+        scratch_shapes=[
+            pltpu.VMEM((length, HEAD_DIM), jnp.float32),
+            pltpu.VMEM((length, HEAD_DIM), jnp.float32),
+        ],
+        name="attend_back",
+        compiler_params=pltpu.CompilerParams(vmem_limit_bytes=48 << 20),
+        cost_estimate=pl.CostEstimate(
+            flops=heads * length * length * HEAD_DIM * 7, bytes_accessed=length * heads * 4096,
+            transcendentals=heads * length * length // 2,
+        ),
+    )(query, key, value, grad, qkv_raw, qkv_raw, gain_q, gain_k, *tables, doc_col, doc_row)
+
+
+def rms_back(values, gain, grad):
+    scale = lax.rsqrt(jnp.mean(values * values, axis=-1, keepdims=True) + EPSILON)
+    weighted = grad * gain
+    mean = jnp.mean(values * weighted, axis=-1, keepdims=True)
+    return scale * weighted - values * (scale * scale * scale * mean)
+
+
+def group_home(group, wa):
+    quarter = group // 4 if isinstance(group, int) else lax.div(group, 4)
+    inner = group % 4 if isinstance(group, int) else lax.rem(group, 4)
+    return (inner % 2) * 2 + inner // 2, quarter
+
+
+def home_pairs(groups, wa):
+    both = []
+    for flip in (0, 1):
+        pairs = []
+        for place in range(groups):
+            for column in range(wa):
+                block = (place % 2) ^ flip
+                group = 4 * block + 2 * (column % 2) + column // 2
+                pairs.append((place * wa + column, group * wa + place // 2))
+        both.append(pairs)
+    return both
+
+
+BOTH = ("seq", "wa")
+
+
+def per_group(
+    tokens,
+    cotangent,
+    token_document_index,
+    sequence_adapter_index,
+    query_weight,
+    key_weight,
+    value_weight,
+    output_weight,
+    gate_weight,
+    up_weight,
+    down_weight,
+    query_norm_gain,
+    key_norm_gain,
+    attention_norm_gain,
+    feedforward_norm_gain,
+    attention_down_adapters,
+    attention_up_adapters,
+    feedforward_down_adapters,
+    feedforward_up_adapters,
+    downproj_down_adapters,
+    downproj_up_adapters,
+):
+    f32, bf16 = jnp.float32, jnp.bfloat16
+    groups, wa = lax.axis_size("seq"), lax.axis_size("wa")
+    place, column = lax.axis_index("seq"), lax.axis_index("wa")
+    _, local_len, width = tokens.shape
+    length = local_len * groups
+    hidden_units = gate_weight.shape[1]
+    slice_heads = HEADS // wa
+    slice_width = slice_heads * HEAD_DIM
+    slice_units = hidden_units // wa
+    unit_block = down_weight.shape[0]
+    half = wa // 2
+    out_pairs, back_pairs = home_pairs(groups, wa), None
+    back_pairs = [[(b, a) for a, b in pairs] for pairs in out_pairs]
+    home_column, home_block = group_home(place, wa)
+    parity = lax.rem(place, 2)
+
+    def to_group(array):
+        first = lax.dynamic_index_in_dim(array, parity, 0, keepdims=False)
+        second = lax.dynamic_index_in_dim(array, 1 - parity, 0, keepdims=False)
+        first = lax.ppermute(first, BOTH, out_pairs[0])
+        second = lax.ppermute(second, BOTH, out_pairs[1])
+        swap = home_block == 1
+        return jnp.concatenate(
+            [jnp.where(swap, second, first), jnp.where(swap, first, second)], axis=0
+        )
+
+    def to_home(array):
+        pieces = array.reshape(2, local_len, *array.shape[1:])
+        first = lax.dynamic_index_in_dim(pieces, home_block, 0, keepdims=False)
+        second = lax.dynamic_index_in_dim(pieces, 1 - home_block, 0, keepdims=False)
+        first = lax.ppermute(first, BOTH, back_pairs[0])
+        second = lax.ppermute(second, BOTH, back_pairs[1])
+        swap = parity == 1
+        return jnp.stack([jnp.where(swap, second, first), jnp.where(swap, first, second)])
+
+    def gather_wa(array):
+        return lax.all_gather(array, "wa", axis=0, tiled=True)
+
+    def gather_seq(array):
+        return lax.all_gather(array, "seq", axis=0, tiled=True)
+
+    def scatter_wa(product, middle):
+        both = jnp.concatenate([product.astype(bf16), middle.astype(bf16)], axis=1)
+        both = lax.psum_scatter(both, "wa", scatter_dimension=0, tiled=True)
+        return both[:, : product.shape[1]].astype(f32), both[:, product.shape[1] :]
+
+    def by_head(array):
+        parts = array.reshape(*array.shape[:-1], 2, slice_heads, half, HEAD_DIM)
+        parts = jnp.moveaxis(parts, (-2, -4), (0, 1))
+        return parts.reshape(wa, *array.shape[:-1], slice_width)
+
+    def by_unit(array):
+        parts = array.reshape(*array.shape[:-1], groups, wa, unit_block)
+        parts = jnp.moveaxis(parts, -2, 0)
+        return parts.reshape(wa, *array.shape[:-1], slice_units)
+
+    def mine(parts):
+        return lax.dynamic_index_in_dim(parts, column, 0, keepdims=False)
+
+    gain_q = query_norm_gain.astype(f32)
+    gain_k = key_norm_gain.astype(f32)
+    gain_a = attention_norm_gain.astype(f32)
+    gain_f = feedforward_norm_gain.astype(f32)
+
+    my_tokens = to_group(tokens)
+    my_cotangent = to_group(cotangent)
+    small = jnp.concatenate([token_document_index, sequence_adapter_index[:, None]], axis=1)
+    small = lax.all_gather(small, BOTH, axis=0, tiled=False).reshape(groups, wa, 2, local_len + 1)
+    order = [group_home(g, wa) for g in range(groups)]
+    adapter_of = jnp.stack([small[0, c, b, local_len] for c, b in order])
+    my_adapter = lax.dynamic_index_in_dim(adapter_of, place, 0, keepdims=False)
+    documents = lax.dynamic_index_in_dim(
+        lax.dynamic_index_in_dim(small, home_column, 1, keepdims=False),
+        home_block, 1, keepdims=False,
+    )[:, :local_len].reshape(length)
+    doc_col, doc_row = documents[:, None], documents[None, :]
+
+    def adapter(table):
+        every = lax.all_gather(table, "seq", axis=0, tiled=False)
+        return lax.dynamic_index_in_dim(every, my_adapter, 0, keepdims=False)
+
+    rows_a = adapter(
+        jnp.concatenate(
+            [
+                jnp.concatenate(list(attention_down_adapters), axis=1),
+                jnp.concatenate(list(attention_up_adapters), axis=1),
+                jnp.concatenate(list(feedforward_down_adapters), axis=1),
+                jnp.concatenate(list(feedforward_up_adapters), axis=1),
+                downproj_down_adapters,
+                downproj_up_adapters,
+            ],
+            axis=1,
+        )
+    )
+    rows_a = gather_wa(rows_a)
+    cuts = [width] * 10 + [hidden_units] * 3 + [width]
+    spots = [sum(cuts[:i]) for i in range(len(cuts))]
+    pieces = [rows_a[:, a : a + n] for a, n in zip(spots, cuts, strict=True)]
+    aq, ak, av, ao, bq, bk, bv, bo, ag, au, bg, bu, ad, bd = pieces
+    aqkv = jnp.concatenate([aq, ak, av], axis=0)
+    bq, bk, bv, ao = (mine(by_head(t)) for t in (bq, bk, bv, ao))
+    bg, bu, ad = (mine(by_unit(t)) for t in (bg, bu, ad))
+    agu = jnp.concatenate([ag, au], axis=0)
+    zero = jnp.zeros((ADAPTER_RANK, slice_width), bf16)
+    b_qkv = jnp.concatenate(
+        [
+            jnp.concatenate([bq, zero, zero], axis=1),
+            jnp.concatenate([zero, bk, zero], axis=1),
+            jnp.concatenate([zero, zero, bv], axis=1),
+        ],
+        axis=0,
+    )
+
+    def to_members(parts):
+        moved = lax.all_to_all(parts, "wa", split_axis=0, concat_axis=0, tiled=True)
+        return moved.reshape(-1, parts.shape[-1])
+
+    w_qkv = gather_seq(
+        to_members(
+            jnp.concatenate([by_head(w) for w in (query_weight, key_weight, value_weight)], axis=-1)
+        )
+    )
+    w_out = gather_seq(output_weight[None])
+    core = lax.rem(column, 2)
+    w_out = w_out.reshape(2, groups // 2, *output_weight.shape)
+    other = lax.ppermute(
+        lax.dynamic_index_in_dim(w_out, 1 - core, 0, keepdims=False),
+        "wa", [(i, i ^ 1) for i in range(wa)],
+    )
+    own = lax.dynamic_index_in_dim(w_out, core, 0, keepdims=False)
+    w_out = jnp.stack(
+        [jnp.where(core == 0, own, other), jnp.where(core == 0, other, own)], axis=1
+    ).reshape(slice_width, width)
+    w_gate = gather_seq(to_members(by_unit(gate_weight)))
+    w_up = gather_seq(to_members(by_unit(up_weight)))
+    w_down = gather_seq(down_weight)
+
+    seq_tokens = gather_wa(my_tokens)
+    mid_qkv = times_t(seq_tokens, aqkv).astype(bf16)
+    qkv_raw = low_dot(seq_tokens, w_qkv) + low_dot(mid_qkv, b_qkv)
+    squares = jnp.sum(
+        jnp.square(qkv_raw[:, : 2 * slice_width]).reshape(length, 2, slice_width), axis=2
+    )
+    squares = lax.psum(squares, "wa")
+    tables = rope_full(length)
+    my_gain_q = mine(by_head(gain_q[None]))
+    my_gain_k = mine(by_head(gain_k[None]))
+    window = length // 2
+    attended, query, key, value = attend_heads(
+        qkv_raw, squares[:, :1], squares[:, 1:], my_gain_q, my_gain_k, tables,
+        doc_col, doc_row, window,
+    )
+    branch, mid_out = scatter_wa(low_dot(attended, w_out), times_t(attended, ao))
+    branch = branch + low_dot(mid_out, bo)
+    hidden = my_tokens.astype(f32) + rms_scale(branch, gain_a)
+    hidden_low = hidden.astype(bf16)
+
+    seq_hidden = gather_wa(hidden_low)
+    mid_gu = times_t(seq_hidden, agu).astype(bf16)
+    mid_gate, mid_up = mid_gu[:, :ADAPTER_RANK], mid_gu[:, ADAPTER_RANK:]
+    gate = low_dot(seq_hidden, w_gate) + low_dot(mid_gate, bg)
+    up_value = low_dot(seq_hidden, w_up) + low_dot(mid_up, bu)
+    sigmoid = jax.nn.sigmoid(gate)
+    mixed = (gate * sigmoid * up_value).astype(bf16)
+    ffn_branch, mid_down = scatter_wa(low_dot(mixed, w_down), times_t(mixed, ad))
+    ffn_branch = ffn_branch + low_dot(mid_down, bd)
+    layer_out = (hidden + rms_scale(ffn_branch, gain_f)).astype(bf16)
+
+    d_ffn = rms_back(ffn_branch, gain_f, my_cotangent).astype(bf16)
+    seq_d_ffn = gather_wa(d_ffn)
+    bd_grad = dot_rows(mid_down, d_ffn)
+    d_mid_down = times_t(seq_d_ffn, bd).astype(bf16)
+    d_mixed = times_t(seq_d_ffn, w_down) + low_dot(d_mid_down, ad)
+    ad_grad = dot_rows(d_mid_down, mixed)
+    d_gate = (d_mixed * up_value * (sigmoid + gate * sigmoid * (1.0 - sigmoid))).astype(bf16)
+    d_up = (d_mixed * gate * sigmoid).astype(bf16)
+    bg_grad = dot_rows(mid_gate, d_gate)
+    bu_grad = dot_rows(mid_up, d_up)
+    d_hidden, d_mid_gu = scatter_wa(
+        times_t(d_gate, w_gate) + times_t(d_up, w_up),
+        jnp.concatenate([times_t(d_gate, bg), times_t(d_up, bu)], axis=1),
+    )
+    d_hidden = my_cotangent + d_hidden + low_dot(d_mid_gu, agu)
+    agu_grad = dot_rows(d_mid_gu, hidden_low)
+
+    d_branch = rms_back(branch, gain_a, d_hidden).astype(bf16)
+    seq_d_branch = gather_wa(d_branch)
+    bo_grad = dot_rows(mid_out, d_branch)
+    d_mid_out = times_t(seq_d_branch, bo).astype(bf16)
+    d_attended = (times_t(seq_d_branch, w_out) + low_dot(d_mid_out, ao)).astype(bf16)
+    ao_grad = dot_rows(d_mid_out, attended)
+    t_q, t_k, d_value, q_dot, k_dot = attend_heads_back(
+        query, key, value, d_attended, qkv_raw, my_gain_q, my_gain_k, tables,
+        doc_col, doc_row, window,
+    )
+    dots = lax.psum(jnp.concatenate([q_dot, k_dot], axis=1), "wa") * (1.0 / width)
+    scales = lax.rsqrt(squares * (1.0 / width) + EPSILON)
+
+    def raw_grad(raw, weighted, i):
+        scale = scales[:, i : i + 1]
+        back = raw * (scale * scale * scale * dots[:, i : i + 1])
+        return (scale * weighted - back).astype(bf16)
+
+    d_qkv = jnp.concatenate(
+        [
+            raw_grad(qkv_raw[:, :slice_width], t_q, 0),
+            raw_grad(qkv_raw[:, slice_width : 2 * slice_width], t_k, 1),
+            d_value,
+        ],
+        axis=1,
+    )
+    b_qkv_grad = dot_rows(mid_qkv, d_qkv)
+    d_tokens, d_mid_qkv = scatter_wa(times_t(d_qkv, w_qkv), times_t(d_qkv, b_qkv))
+    my_grad = d_hidden + d_tokens + low_dot(d_mid_qkv, aqkv)
+    aqkv_grad = dot_rows(d_mid_qkv, my_tokens)
+
+    def to_owners(sliced, full):
+        cut = jnp.concatenate(sliced + full, axis=1).reshape(wa, ADAPTER_RANK // wa, -1)
+        every = lax.all_to_all(cut.astype(bf16), "wa", split_axis=0, concat_axis=0, tiled=True)
+        n = sum(p.shape[1] for p in sliced)
+        joined = jnp.moveaxis(every[:, :, :n], 0, 1).reshape(ADAPTER_RANK // wa, -1)
+        summed = jnp.sum(every[:, :, n:].astype(f32), axis=0).astype(bf16)
+        both = lax.all_gather(jnp.concatenate([joined, summed], axis=1), "seq", axis=0, tiled=False)
+        chosen = (adapter_of == place)[:, None, None]
+        total = jnp.sum(jnp.where(chosen, both.astype(f32), 0.0), axis=0)
+        return total[:, : n * wa].reshape(-1, wa, n), total[:, n * wa :]
+
+    def heads_back(parts):
+        split = parts.reshape(-1, half, 2, slice_heads, HEAD_DIM)
+        return jnp.transpose(split, (0, 2, 3, 1, 4)).reshape(-1, width)
+
+    def units_back(parts):
+        split = parts.reshape(-1, wa, groups, unit_block)
+        return jnp.transpose(split, (0, 2, 1, 3)).reshape(-1, hidden_units)
+
+    r = ADAPTER_RANK
+    ffn_cut, ffn_full = to_owners(
+        [bg_grad, bu_grad, ad_grad], [agu_grad[:r], agu_grad[r:], bd_grad]
+    )
+    u = slice_units
+    ffn_b_grad = jnp.stack([units_back(ffn_cut[:, :, :u]), units_back(ffn_cut[:, :, u : 2 * u])])
+    down_a_grad = units_back(ffn_cut[:, :, 2 * u :])
+    ffn_a_grad = jnp.stack([ffn_full[:, :width], ffn_full[:, width : 2 * width]])
+    down_b_grad = ffn_full[:, 2 * width :]
+    w = slice_width
+    attn_cut, attn_full = to_owners(
+        [b_qkv_grad[:r, :w], b_qkv_grad[r : 2 * r, w : 2 * w], b_qkv_grad[2 * r :, 2 * w :], ao_grad],
+        [aqkv_grad[:r], aqkv_grad[r : 2 * r], aqkv_grad[2 * r :], bo_grad],
+    )
+    heads = [heads_back(attn_cut[:, :, i * w : (i + 1) * w]) for i in range(4)]
+    fulls = [attn_full[:, i * width : (i + 1) * width] for i in range(4)]
+    attn_a_grad = jnp.stack(fulls[:3] + [heads[3]])
+    attn_b_grad = jnp.stack(heads[:3] + [fulls[3]])
+    return (
+        to_home(layer_out), to_home(my_grad), attn_a_grad, attn_b_grad, ffn_a_grad, ffn_b_grad,
+        down_a_grad, down_b_grad,
+    )
+
+
 def solution(mesh):
+    groups, wa = mesh.shape["seq"], mesh.shape["wa"]
     in_specs = (
         P("wa", "seq", None),
         P("wa", "seq", None),
@@ -492,6 +979,7 @@
         P(("seq", "wa"), None),
         P(("seq", "wa"), None),
     )
+    body = per_group if groups == 8 and wa == 4 else per_device
     return jax.shard_map(
-        per_device, mesh=mesh, in_specs=in_specs, out_specs=out_specs, check_vma=False
-    )
+        body, mesh=mesh, in_specs=in_specs, out_specs=out_specs, check_vma=False
+    )

time: 2090 us -> 1410 us (0.67)
  waiting for transfers between devices: 1310 us -> 869 us
  matrix products: 295 us -> 174 us
  loops' own time: 108 us -> 0 us
  local copies, waits for them, and re-layouts: 154 us -> 94.3 us
  blocking collectives: 71.8 us -> 130 us
  Pallas kernels: 0 us -> 38.4 us
  other arithmetic: 76 us -> 44.5 us
    unnamed x14 -> x17, waiting for transfers between devices: 374 us -> 1.48 us
    all_gather x12 -> x13, waiting for transfers between devices: 815 us -> 532 us  [the longest x5 417 us: gather_seq(): return lax.all_gather(array, 'seq', axis=0, tiled=True)]
    ppermute x0 -> x9, waiting for transfers between devices: none -> 219 us  [the longest x2 104 us: to_home(): second = lax.ppermute(second, BOTH, back_pairs[1])]
    dot_general x169 -> x23, matrix products: 225 us -> 101 us  [the longest x14 85.7 us: low_dot(): return jnp.dot(left, right, preferred_element_type=jnp.float32)]
    all_to_all x8 -> x2, waiting for transfers between devices: 122 us -> 10 us  [to_owners(): lax.all_to_all(cut.astype(bf16), 'wa', split_axis=0, concat_axis=0, tiled...]
    another operation x42 -> x0, loops' own time: 108 us -> none  [the longest x4 53.2 us: attend_back(): (key_grad, value_grad), query_grads = lax.scan(step, (zeros, zeros), starts)]
    reduce_scatter x0 -> x4, waiting for transfers between devices: none -> 107 us  [scatter_wa(): both = lax.psum_scatter(both, 'wa', scatter_dimension=0, tiled=True)]
    all_to_all x0 -> x3, blocking collectives: none -> 62.1 us  [to_members(): moved = lax.all_to_all(parts, 'wa', split_axis=0, concat_axis=0, tiled=True)]
  transfers between devices with their start and end apart: 21 -> 28, of which waited for: 16 -> 23; matrix products, arithmetic and copies ran while one was open for 13% -> 10% of each run, Pallas kernels for 0% -> 2%
where the time goes in v1:
time: 1410 us
  waiting for transfers between devices  869 us (62%)
  matrix products  174 us (12%)
  blocking collectives  130 us (9%)
  local copies, waits for them, and re-layouts  94.3 us (7%)
  other arithmetic  44.5 us (3%)
  starting transfers between devices  40 us (3%)
  Pallas kernels  38.4 us (3%)
  between operations  17.9 us (1%)
    all_gather x5, waiting for transfers between devices, gather_seq(): return lax.all_gather(array, 'seq', axis=0, tiled=True)  417 us
    reduce_scatter x4, waiting for transfers between devices, scatter_wa(): both = lax.psum_scatter(both, 'wa', scatter_dimension=0, tiled=True)  107 us
    ppermute x2, waiting for transfers between devices, to_home(): second = lax.ppermute(second, BOTH, back_pairs[1])  104 us
    all_gather x5, waiting for transfers between devices, gather_wa(): return lax.all_gather(array, 'wa', axis=0, tiled=True)  100 us
    dot_general x14, matrix products, low_dot(): return jnp.dot(left, right, preferred_element_type=jnp.float32)  85.7 us
    dot_general x14, matrix products, times_t(): lax.dot_general(left, weight, (((1,), (1,)), ((), ())), preferred_element...  72.7 us
    ppermute x2, waiting for transfers between devices, to_group(): second = lax.ppermute(second, BOTH, out_pairs[1])  67 us
    all_to_all x3, blocking collectives, to_members(): moved = lax.all_to_all(parts, 'wa', split_axis=0, concat_axis=0, tiled=True)  62.1 us
  transfers between devices with their start and end apart: 28, of which 23 were waited for; matrix products, arithmetic and copies ran while one was open for 10% of the time, Pallas kernels for 2%

profile of v1, /device:TPU:6, one launch (start us, length us, event | category | flops | bytes accessed | tf_op | source)
XLA Modules:
  0.0 1408.2 jit_solution(1437591333891988455)
XLA Ops:
  21.0 33.9 %all-gather.7 = s32[32,2,129]{2,1,0:T(2,128)S(1)} all-gather(s32[1,2,129]{2,1,0:T(2,128)S(1)} %add_bitcast_fusion), channel_id=3, replica_groups=mesh['seq'=8,'wa'=4] {'seq','wa'}, dimensions={0}, use_global_device_ids=true | all-gather | bytes 34056 | tf_op jit(solution)/shard_map/all_gather | solution.py:755
  63.4 14.9 %all-gather.44.cloned.1.call-done = bf16[8,4,47104]{2,1,0:T(4,128)(2,1)} async-done(((bf16[1,4,47104]{2,1,0:T(4,128)(2,1)}), bf16[8,4,47104]{2,1,0:T(4,128)(2,1)}) %all-gather.44.cloned.1.call-update) | async-done | bytes 3014672 | tf_op jit(solution)/shard_map/all_gather | solution.py:766
  87.9 26.6 %collective-permute-done = bf16[128,2048]{1,0:T(8,128)(2,1)S(1)} collective-permute-done((bf16[128,2048]{1,0:T(8,128)(2,1)S(1)}, bf16[128,2048]{1,0:T(8,128)(2,1)S(1)}, u32[]{:S(2)}, u32[]{:S(2)}) %collective-permute-start) | collective-permute-done | bytes 524320 | tf_op jit(solution)/shard_map/ppermute | solution.py:708
  121.9 13.2 all_to_all.25
  150.5 19.7 %all-gather.40.cloned.1.call-done = bf16[1,16,47104]{2,0,1:T(2,128)(2,1)} async-done(((bf16[1,4,47104]{2,0,1:T(2,128)(2,1)}), bf16[1,16,47104]{2,0,1:T(2,128)(2,1)}) %all-gather.40.cloned.1.call-update) | async-done | bytes 1507344 | tf_op jit(solution)/shard_map/all_gather | solution.py:724
  174.6 32.0 %all-gather.24.cloned.1.call-done = bf16[1024,2048]{1,0:T(8,128)(2,1)} async-done(((bf16[256,2048]{1,0:T(8,128)(2,1)}), bf16[1024,2048]{1,0:T(8,128)(2,1)}) %all-gather.24.cloned.1.call-update) | async-done | bytes 4194320 | tf_op jit(solution)/shard_map/all_gather | solution.py:724
  213.9 93.8 %all-gather.26.cloned.1.call-done = bf16[2048,1536]{1,0:T(8,128)(2,1)} async-done(((bf16[256,1536]{1,0:T(8,128)(2,1)}), bf16[2048,1536]{1,0:T(8,128)(2,1)}) %all-gather.26.cloned.1.call-update) | async-done | bytes 6291472 | tf_op jit(solution)/shard_map/all_gather | solution.py:727
  307.8 10.9 convolution_add_fusion.3.q_raw.k_raw.v_raw
  333.9 16.3 %psum.14 = f32[1024,2]{1,0:T(8,128)S(1)} all-reduce(f32[1024,2]{1,0:T(8,128)S(1)} %reduce_sum.95), channel_id=1, replica_groups=mesh['seq'=8,'wa'=4] {'wa'}, use_global_device_ids=true, to_apply=%region_1.2 | all-reduce | flops 2048 | bytes 16384 | tf_op jit(solution)/shard_map/psum | solution.py:831
  351.0 16.8 %attend.1 = (bf16[1024,512]{1,0:T(8,128)(2,1)S(1)}, bf16[1024,512]{1,0:T(8,128)(2,1)S(1)}, bf16[1024,512]{1,0:T(8,128)(2,1)S(1)}, bf16[1024,512]{1,0:T(8,128)(2,1)}) custom-call(f32[1024,1536]{1,0:T(8,128)} %copy-done.8, f32[1024,1536]{1,0:T(8,128)} %copy-done.8, f32[1024,1536]{1,0:T(8,128)} %copy-done.8, f32[1024,1]{1,0:T(8,128)S(1)} %get-tuple-element.69.q_sum, ...), custom_call_target="tpu_custom_call" | custom-call | flops 1610612736 | bytes 10485760 | tf_op jit(solution)/shard_map/attend/pallas_call | solution.py:584
  379.0 44.0 %reduce-scatter.5.cloned.1.call-done = bf16[256,2064]{1,0:T(8,128)(2,1)} async-done(((bf16[1024,2064]{1,0:T(8,128)(2,1)}), bf16[256,2064]{1,0:T(8,128)(2,1)}) %reduce-scatter.5.cloned.1.call-update) | async-done | bytes 1056784 | tf_op jit(solution)/shard_map/reduce_scatter | solution.py:731
  432.9 29.9 %all_to_all.26 = bf16[4,64,2048]{2,1,0:T(8,128)(2,1)} all-to-all(bf16[4,64,2048]{2,1,0:T(8,128)(2,1)} %reshape.310), channel_id=1, replica_groups=mesh['seq'=8,'wa'=4] {'wa'}, dimensions={0} | all-to-all | bytes 2097152 | tf_op jit(solution)/shard_map/all_to_all | solution.py:802
  470.5 19.0 %all_to_all.27 = bf16[4,64,2048]{2,1,0:T(8,128)(2,1)} all-to-all(bf16[4,64,2048]{2,1,0:T(8,128)(2,1)} %reshape.315), channel_id=1, replica_groups=mesh['seq'=8,'wa'=4] {'wa'}, dimensions={0} | all-to-all | bytes 2097152 | tf_op jit(solution)/shard_map/all_to_all | solution.py:802
  497.8 102.9 %all-gather.30.cloned.1.call-done = bf16[2048,2048]{1,0:T(8,128)(2,1)} async-done(((bf16[256,2048]{1,0:T(8,128)(2,1)}), bf16[2048,2048]{1,0:T(8,128)(2,1)}) %all-gather.30.cloned.1.call-update) | async-done | bytes 8388624 | tf_op jit(solution)/shard_map/all_gather | solution.py:727
  600.7 12.5 fusion.86
  617.7 108.5 %all-gather.32.cloned.1.call-done = bf16[2048,2048]{1,0:T(8,128)(2,1)} async-done(((bf16[256,2048]{1,0:T(8,128)(2,1)}), bf16[2048,2048]{1,0:T(8,128)(2,1)}) %all-gather.32.cloned.1.call-update) | async-done | bytes 8388624 | tf_op jit(solution)/shard_map/all_gather | solution.py:727
  726.2 12.6 fusion.87
  746.8 104.7 %all-gather.34.cloned.1.call-done = bf16[2048,2048]{1,0:T(8,128)(2,1)} async-done(((bf16[256,2048]{1,0:T(8,128)(2,1)}), bf16[2048,2048]{1,0:T(8,128)(2,1)}) %all-gather.34.cloned.1.call-update) | async-done | bytes 8388624 | tf_op jit(solution)/shard_map/all_gather | solution.py:727
  851.5 12.6 convolution_convert_fusion.1
  875.1 40.4 %collective-permute-done.5 = f32[128,2048]{1,0:T(8,128)S(1)} collective-permute-done((f32[128,2048]{1,0:T(8,128)S(1)}, f32[128,2048]{1,0:T(8,128)S(1)}, u32[]{:S(2)}, u32[]{:S(2)}) %collective-permute-start.5) | collective-permute-done | bytes 1048608 | tf_op jit(solution)/shard_map/ppermute | solution.py:708
  933.4 35.4 %all-gather.36.cloned.1.call-done = bf16[1024,2048]{1,0:T(8,128)(2,1)} async-done(((bf16[256,2048]{1,0:T(8,128)(2,1)}), bf16[1024,2048]{1,0:T(8,128)(2,1)}) %all-gather.36.cloned.1.call-update) | async-done | bytes 4194320 | tf_op jit(solution)/shard_map/all_gather | solution.py:724
  968.8 15.7 %fusion.88 = f32[1024,2048]{1,0:T(8,128)} fusion(bf16[1024,2048]{1,0:T(8,128)(2,1)} %all-gather.36.cloned.1.call-done, bf16[2048,2048]{1,0:T(8,128)(2,1)} %all-gather.34.cloned.1.call-done), kind=kOutput, calls=%fused_computation.249 | convolution fusion | flops 8589934592 | bytes 20971520 | tf_op jit(solution)/shard_map/dot_general | solution.py:44
  1002.7 12.7 fusion.89
  1015.4 13.1 add_convert_fusion
  1036.4 46.3 %reduce-scatter.9.cloned.1.call-done = bf16[256,2080]{1,0:T(8,128)(2,1)} async-done(((bf16[1024,2080]{1,0:T(8,128)(2,1)}), bf16[256,2080]{1,0:T(8,128)(2,1)}) %reduce-scatter.9.cloned.1.call-update) | async-done | bytes 1064976 | tf_op jit(solution)/shard_map/reduce_scatter | solution.py:731
  1114.6 12.9 all-gather.38.cloned.1.call-done
  1135.6 21.6 %attend_back.1 = (f32[1024,512]{1,0:T(8,128)}, f32[1024,512]{1,0:T(8,128)}, bf16[1024,512]{1,0:T(8,128)(2,1)S(1)}, f32[1024,1]{1,0:T(8,128)S(1)}, f32[1024,1]{1,0:T(8,128)S(1)}) custom-call(bf16[1024,512]{1,0:T(8,128)(2,1)S(1)} %copy-done.3, bf16[1024,512]{1,0:T(8,128)(2,1)S(1)} %copy-done.5, bf16[1024,512]{1,0:T(8,128)(2,1)} %get-tuple-element.20.value, ...), custom_call_target="tpu_custom_call" | custom-call | flops 3758096384 | bytes 16777216 | tf_op jit(solution)/shard_map/attend_back/pallas_call | solution.py:611
  1158.8 17.5 %psum.15 = f32[1024,2]{1,0:T(8,128)S(1)} all-reduce(f32[1024,2]{1,0:T(8,128)S(1)} %copy.198), channel_id=1, replica_groups=mesh['seq'=8,'wa'=4] {'wa'}, use_global_device_ids=true, to_apply=%region_9.10 | all-reduce | flops 2048 | bytes 16384 | tf_op jit(solution)/shard_map/psum | solution.py:883
  1200.5 48.2 %collective-permute-done.3 = bf16[128,2048]{1,0:T(8,128)(2,1)S(1)} collective-permute-done((bf16[128,2048]{1,0:T(8,128)(2,1)S(1)}, bf16[128,2048]{1,0:T(8,128)(2,1)S(1)}, u32[]{:S(2)}, u32[]{:S(2)}) %collective-permute-start.3) | collective-permute-done | bytes 524320 | tf_op jit(solution)/shard_map/ppermute | solution.py:719
  1275.6 10.7 all-to-all-start.3
  1299.2 55.7 %collective-permute-done.7 = f32[128,2048]{1,0:T(8,128)S(1)} collective-permute-done((f32[128,2048]{1,0:T(8,128)S(1)}, f32[128,2048]{1,0:T(8,128)S(1)}, u32[]{:S(2)}, u32[]{:S(2)}) %collective-permute-start.7) | collective-permute-done | bytes 1048608 | tf_op jit(solution)/shard_map/ppermute | solution.py:719
  1354.9 39.7 %collective-permute-done.8 = f32[128,2048]{1,0:T(8,128)} collective-permute-done((f32[128,2048]{1,0:T(8,128)S(1)}, f32[128,2048]{1,0:T(8,128)}, u32[]{:S(2)}, u32[]{:S(2)}) %collective-permute-start.8) | collective-permute-done | bytes 1048608 | tf_op jit(solution)/shard_map/ppermute | solution.py:718
  (415 shorter events, 295.3 us)
Async XLA Ops:
  7.2 71.2 %all-gather.44.cloned.1.call-start = ((), (), s32[]{:S(2)}) async-start(), calls=%async_computation.23 | async-start | bytes 3391488 | tf_op jit(solution)/shard_map/all_gather | solution.py:766
  18.8 123.5 %all-gather.42.cloned.1.call-start = ((), (), s32[]{:S(2)}) async-start(), calls=%async_computation.22 | async-start | bytes 2359296 | tf_op jit(solution)/shard_map/all_gather | solution.py:727
  19.5 150.6 %all-gather.40.cloned.1.call-start = ((), (), s32[]{:S(2)}) async-start(), calls=%async_computation.21 | async-start | bytes 3768320 | tf_op jit(solution)/shard_map/all_gather | solution.py:724
  81.0 125.7 %all-gather.24.cloned.1.call-start = ((), (), s32[]{:S(2)}) async-start(), calls=%async_computation.9 | async-start | bytes 5242880 | tf_op jit(solution)/shard_map/all_gather | solution.py:724
  81.2 33.3 %collective-permute-start = (bf16[128,2048]{1,0:T(8,128)(2,1)S(1)}, bf16[128,2048]{1,0:T(8,128)(2,1)S(1)}, u32[]{:S(2)}, u32[]{:S(2)}) collective-permute-start(bf16[128,2048]{1,0:T(8,128)(2,1)S(1)} %get-tuple-element.66), channel_id=1, source_target_pairs={{0,16},{1,24},{2,20},{3,28},{4,0},{5,8},{6,4},{7,12},{8,17},{9,25}... | collective-permute-start | bytes 1572872 | tf_op jit(solution)/shard_map/ppermute | solution.py:708
  81.8 36.8 %collective-permute-start.1 = (bf16[128,2048]{1,0:T(8,128)(2,1)S(1)}, bf16[128,2048]{1,0:T(8,128)(2,1)S(1)}, u32[]{:S(2)}, u32[]{:S(2)}) collective-permute-start(bf16[128,2048]{1,0:T(8,128)(2,1)S(1)} %get-tuple-element.67), channel_id=1, source_target_pairs={{0,0},{1,8},{2,4},{3,12},{4,16},{5,24},{6,20},{7,28},{8,1},{9,9},{... | collective-permute-start | bytes 1572872 | tf_op jit(solution)/shard_map/ppermute | solution.py:707
  118.7 306.1 %copy-start.23 = (bf16[128,2048]{1,0:T(8,128)(2,1)}, bf16[128,2048]{1,0:T(8,128)(2,1)S(1)}, u32[]{:S(2)}) copy-start(bf16[128,2048]{1,0:T(8,128)(2,1)S(1)} %get-tuple-element.64) | copy-start | bytes 1572868
  120.6 187.2 %all-gather.26.cloned.1.call-start = ((), (), s32[]{:S(2)}) async-start(), calls=%async_computation.10 | async-start | bytes 7077888 | tf_op jit(solution)/shard_map/all_gather | solution.py:727
  135.1 287.9 %reduce-scatter.5.cloned.1.call-start = ((), (), s32[]{:S(2)}) async-start(), calls=%async_computation.11 | async-start | bytes 5570560 | tf_op jit(solution)/shard_map/reduce_scatter | solution.py:731
  144.6 3.0 collective-permute-start.2
  174.1 320.2 %copy-start.51 = (bf16[16,2048]{1,0:T(8,128)(2,1)}, bf16[16,2048]{1,0:T(8,128)(2,1)S(1)}, u32[]{:S(2)}) copy-start(bf16[16,2048]{1,0:T(8,128)(2,1)S(1)} %get-tuple-element.51) | copy-start | bytes 196612
  174.1 320.2 %copy-start.53 = (bf16[16,2048]{1,0:T(8,128)(2,1)}, bf16[16,2048]{1,0:T(8,128)(2,1)S(1)}, u32[]{:S(2)}) copy-start(bf16[16,2048]{1,0:T(8,128)(2,1)S(1)} %get-tuple-element.52) | copy-start | bytes 196612
  378.3 115.9 %all-gather.28.cloned.1.call-start = ((), (), s32[]{:S(2)}) async-start(), calls=%async_computation.12 | async-start | bytes 5242880 | tf_op jit(solution)/shard_map/all_gather | solution.py:724
  427.5 173.2 %all-gather.30.cloned.1.call-start = ((), (), s32[]{:S(2)}) async-start(), calls=%async_computation.13 | async-start | bytes 9437184 | tf_op jit(solution)/shard_map/all_gather | solution.py:727
  462.9 263.3 %all-gather.32.cloned.1.call-start = ((), (), s32[]{:S(2)}) async-start(), calls=%async_computation.14 | async-start | bytes 9437184 | tf_op jit(solution)/shard_map/all_gather | solution.py:727
  489.5 362.0 %all-gather.34.cloned.1.call-start = ((), (), s32[]{:S(2)}) async-start(), calls=%async_computation.15 | async-start | bytes 9437184 | tf_op jit(solution)/shard_map/all_gather | solution.py:727
  490.1 438.1 %reduce-scatter.7.cloned.1.call-start = ((), (), s32[]{:S(2)}) async-start(), calls=%async_computation.16 | async-start | bytes 5570560 | tf_op jit(solution)/shard_map/reduce_scatter | solution.py:731
  492.5 250.9 %copy-start.57 = (bf16[4,16,2048]{2,1,0:T(8,128)(2,1)}, bf16[4,16,2048]{2,1,0:T(8,128)(2,1)S(1)}, u32[]{:S(2)}) copy-start(bf16[4,16,2048]{2,1,0:T(8,128)(2,1)S(1)} %reshape.320) | copy-start | bytes 786436
  866.7 102.1 %all-gather.36.cloned.1.call-start = ((), (), s32[]{:S(2)}) async-start(), calls=%async_computation.17 | async-start | bytes 5242880 | tf_op jit(solution)/shard_map/all_gather | solution.py:724
  868.4 47.1 %collective-permute-start.5 = (f32[128,2048]{1,0:T(8,128)S(1)}, f32[128,2048]{1,0:T(8,128)S(1)}, u32[]{:S(2)}, u32[]{:S(2)}) collective-permute-start(f32[128,2048]{1,0:T(8,128)S(1)} %get-tuple-element.46), channel_id=1, source_target_pairs={{0,16},{1,24},{2,20},{3,28},{4,0},{5,8},{6,4},{7,12},{8,17},{9,25}... | collective-permute-start | bytes 3145736 | tf_op jit(solution)/shard_map/ppermute | solution.py:708
  869.0 50.2 %collective-permute-start.6 = (f32[128,2048]{1,0:T(8,128)S(1)}, f32[128,2048]{1,0:T(8,128)S(1)}, u32[]{:S(2)}, u32[]{:S(2)}) collective-permute-start(f32[128,2048]{1,0:T(8,128)S(1)} %get-tuple-element.47), channel_id=1, source_target_pairs={{0,0},{1,8},{2,4},{3,12},{4,16},{5,24},{6,20},{7,28},{8,1},{9,9},{... | collective-permute-start | bytes 3145736 | tf_op jit(solution)/shard_map/ppermute | solution.py:707
  933.4 149.3 %reduce-scatter.9.cloned.1.call-start = ((), (), s32[]{:S(2)}) async-start(), calls=%async_computation.18 | async-start | bytes 5570560 | tf_op jit(solution)/shard_map/reduce_scatter | solution.py:731
  1036.3 91.2 %all-gather.38.cloned.1.call-start = ((), (), s32[]{:S(2)}) async-start(), calls=%async_computation.19 | async-start | bytes 5242880 | tf_op jit(solution)/shard_map/all_gather | solution.py:724
  1098.6 15.0 %all-to-all-start.4 = ((bf16[4,4,12288]{2,1,0:T(4,128)(2,1)}), bf16[4,4,12288]{2,1,0:T(4,128)(2,1)S(1)}, u32[]{:S(2)}, u32[]{:S(2)}) async-start(bf16[4,4,12288]{2,1,0:T(4,128)(2,1)} %convert_element_type.149), calls=%async_computation.8 | async-start | bytes 786432 | tf_op jit(solution)/shard_map/all_to_all | solution.py:906
  1103.5 146.4 %all-gather.48.cloned.1.call-start = ((), (), s32[]{:S(2)}) async-start(), calls=%async_computation.25 | async-start | bytes 2211840 | tf_op jit(solution)/shard_map/all_gather | solution.py:910
  1114.5 154.0 %reduce-scatter.11.cloned.1.call-start = ((), (), s32[]{:S(2)}) async-start(), calls=%async_computation.20 | async-start | bytes 5570560 | tf_op jit(solution)/shard_map/reduce_scatter | solution.py:731
  1195.3 53.4 %collective-permute-start.3 = (bf16[128,2048]{1,0:T(8,128)(2,1)S(1)}, bf16[128,2048]{1,0:T(8,128)(2,1)S(1)}, u32[]{:S(2)}, u32[]{:S(2)}) collective-permute-start(bf16[128,2048]{1,0:T(8,128)(2,1)S(1)} %get-tuple-element.62), channel_id=1, source_target_pairs={{16,0},{24,1},{20,2},{28,3},{0,4},{8,5},{4,6},{12,7},{17,8},{25,9}... | collective-permute-start | bytes 1572872 | tf_op jit(solution)/shard_map/ppermute | solution.py:719
  1197.8 50.9 %collective-permute-start.4 = (bf16[128,2048]{1,0:T(8,128)(2,1)S(1)}, bf16[128,2048]{1,0:T(8,128)(2,1)S(1)}, u32[]{:S(2)}, u32[]{:S(2)}) collective-permute-start(bf16[128,2048]{1,0:T(8,128)(2,1)S(1)} %get-tuple-element.63), channel_id=1, source_target_pairs={{0,0},{8,1},{4,2},{12,3},{16,4},{24,5},{20,6},{28,7},{1,8},{9,9},{... | collective-permute-start | bytes 1572872 | tf_op jit(solution)/shard_map/ppermute | solution.py:718
  1275.6 17.6 %all-to-all-start.3 = ((bf16[4,4,10240]{2,1,0:T(4,128)(2,1)}), bf16[4,4,10240]{2,1,0:T(4,128)(2,1)S(1)}, u32[]{:S(2)}, u32[]{:S(2)}) async-start(bf16[4,4,10240]{2,1,0:T(4,128)(2,1)} %convert_element_type.147), calls=%async_computation.7 | async-start | bytes 655360 | tf_op jit(solution)/shard_map/all_to_all | solution.py:906
  1286.4 111.1 %all-gather.46.cloned.1.call-start = ((), (), s32[]{:S(2)}) async-start(), calls=%async_computation.24 | async-start | bytes 1179648 | tf_op jit(solution)/shard_map/all_gather | solution.py:910
  1288.3 66.6 %collective-permute-start.7 = (f32[128,2048]{1,0:T(8,128)S(1)}, f32[128,2048]{1,0:T(8,128)S(1)}, u32[]{:S(2)}, u32[]{:S(2)}) collective-permute-start(f32[128,2048]{1,0:T(8,128)S(1)} %get-tuple-element.42), channel_id=1, source_target_pairs={{16,0},{24,1},{20,2},{28,3},{0,4},{8,5},{4,6},{12,7},{17,8},{25,9}... | collective-permute-start | bytes 3145736 | tf_op jit(solution)/shard_map/ppermute | solution.py:719
  1291.3 103.3 %collective-permute-start.8 = (f32[128,2048]{1,0:T(8,128)S(1)}, f32[128,2048]{1,0:T(8,128)}, u32[]{:S(2)}, u32[]{:S(2)}) collective-permute-start(f32[128,2048]{1,0:T(8,128)S(1)} %get-tuple-element.43), channel_id=1, source_target_pairs={{0,0},{8,1},{4,2},{12,3},{16,4},{24,5},{20,6},{28,7},{1,8},{9,9},{... | collective-permute-start | bytes 3145736 | tf_op jit(solution)/shard_map/ppermute | solution.py:718
  (78 other events, 1712.0 us)
Sparse Core Ops, SparseCore 0:
  18.9 59.4 all-gather.43
  80.5 61.7 all-gather.41
  143.9 26.2 all-gather.39
  172.2 34.4 all-gather.23
  208.7 99.0 all-gather.25
  378.5 44.4 reduce-scatter.4
  427.6 45.7 all-gather.27
  475.7 124.9 all-gather.29
  603.0 123.1 all-gather.31
  728.4 123.1 all-gather.33
  866.8 61.2 reduce-scatter.6
  933.5 35.2 all-gather.35
  1036.4 46.1 reduce-scatter.8
  1088.8 38.6 all-gather.37
  1130.4 47.5 all-gather.47
  1194.1 74.3 reduce-scatter.10
  1294.3 80.9 all-gather.45

commit v2 on v1

--- a/solution.py
+++ b/solution.py
@@ -640,26 +640,550 @@
     return scale * weighted - values * (scale * scale * scale * mean)
 
 
-def group_home(group, wa):
-    quarter = group // 4 if isinstance(group, int) else lax.div(group, 4)
-    inner = group % 4 if isinstance(group, int) else lax.rem(group, 4)
-    return (inner % 2) * 2 + inner // 2, quarter
-
-
-def home_pairs(groups, wa):
-    both = []
-    for flip in (0, 1):
-        pairs = []
-        for place in range(groups):
-            for column in range(wa):
-                block = (place % 2) ^ flip
-                group = 4 * block + 2 * (column % 2) + column // 2
-                pairs.append((place * wa + column, group * wa + place // 2))
-        both.append(pairs)
-    return both
-
-
-BOTH = ("seq", "wa")
+MESH = pl.DeviceIdType.MESH
+VMEM_BYTES = 58 << 20
+
+
+def remote(source, target, send, recv, device):
+    return pltpu.make_async_remote_copy(
+        src_ref=source, dst_ref=target, send_sem=send, recv_sem=recv,
+        device_id=device, device_id_type=MESH,
+    )
+
+
+def greet(sources, count):
+    barrier = pltpu.get_barrier_semaphore()
+    for device in sources:
+        pl.semaphore_signal(barrier, inc=1, device_id=device, device_id_type=MESH)
+    pl.semaphore_wait(barrier, count)
+
+
+def flip(index, bit):
+    return index + bit * (1 - 2 * (index // bit % 2))
+
+
+def wa_peers(place, column):
+    near, across = flip(column, 1), flip(column, 2)
+    return [(place, near), (place, across), (place, flip(across, 1))]
+
+
+def ring_place(place, count):
+    return place // 2 + place % 2 * (count - 1 - 2 * (place // 2))
+
+
+def ring_owner(spot, count):
+    spot = (spot + 2 * count) % count
+    return 2 * spot + spot // (count // 2) * (2 * count - 1 - 4 * spot)
+
+
+def ring_peers(place, column, count):
+    spot = ring_place(place, count)
+    return [(ring_owner(spot + 1, count), column), (ring_owner(spot - 1, count), column)]
+
+
+class Ring:
+    def __init__(self, buffer, send, recv, place, column, own=None):
+        self.buffer, self.send, self.recv, self.own = buffer, send, recv, own
+        self.count = buffer.shape[0]
+        self.half = buffer.shape[1] // 2
+        self.spot = ring_place(place, self.count)
+        self.peers = ring_peers(place, column, self.count)
+        long = self.count // 2
+        self.order = [
+            [(t, h) for t in range(long) for h in (way, 1 - way) if t < long - (h != way)]
+            for way in (0, 1)
+        ]
+
+    def region(self, away, h):
+        owner = ring_owner(self.spot + away, self.count)
+        return self.buffer.at[owner, pl.ds(h * self.half, self.half)]
+
+    def copy(self, way, i, back=0):
+        t, h = self.order[way][i]
+        region = self.region((t + back) * (1 if way else -1), h)
+        source = region
+        if t + back == 0 and self.own is not None:
+            source = self.own.at[pl.ds(h * self.half, self.half)]
+        return remote(
+            source, region, self.send.at[way, i], self.recv.at[way, i], self.peers[way]
+        )
+
+    def step(self, i):
+        for way in (0, 1):
+            t, h = self.order[way][i]
+            if t > 0:
+                self.copy(way, self.order[way].index((t - 1, h)), 1).wait_recv()
+            self.copy(way, i).start()
+
+    @property
+    def steps(self):
+        return self.count - 1
+
+    def finish(self):
+        for way in (0, 1):
+            for i, (t, h) in enumerate(self.order[way]):
+                if (t + 1, h) not in self.order[way]:
+                    self.copy(way, i, 1).wait_recv()
+        for way in (0, 1):
+            for i in range(self.steps):
+                self.copy(way, i).wait_send()
+
+
+def here():
+    return lax.axis_index("seq"), lax.axis_index("wa")
+
+
+def group_of(column, block):
+    return 4 * block + 2 * (column % 2) + column // 2
+
+
+def home_of(place):
+    return place % 2 * 2 + place // 2 % 2, place // 4
+
+
+class WaGather:
+    def __init__(self, buffer, send, recv, place, column, pieces, source=None):
+        self.buffer, self.send, self.recv, self.pieces = buffer, send, recv, pieces
+        self.source = source
+        self.quarter = flip(column, 1)
+        self.near, self.across, _ = wa_peers(place, column)
+        self.rows = buffer.shape[1] // pieces
+
+    def region(self, quarter, i):
+        return self.buffer.at[quarter, pl.ds(i * self.rows, self.rows)]
+
+    def copy(self, kind, i, quarter=None):
+        device = self.across if kind == 1 else self.near
+        region = self.region(self.quarter if quarter is None else quarter, i)
+        source = region
+        if quarter is None and self.source is not None:
+            source = self.source.at[pl.ds(i * self.rows, self.rows)]
+        return remote(source, region, self.send.at[kind, i], self.recv.at[kind, i], device)
+
+    def own(self, i):
+        self.copy(1, i).start()
+        self.copy(0, i).start()
+
+    def forward(self, i):
+        far = flip(self.quarter, 2)
+        self.copy(1, i, far).wait_recv()
+        self.copy(2, i, far).start()
+
+    def finish(self):
+        for i in range(self.pieces):
+            self.copy(0, i, flip(self.quarter, 1)).wait_recv()
+            self.copy(2, i, flip(flip(self.quarter, 2), 1)).wait_recv()
+        for i in range(self.pieces):
+            for kind in (0, 1):
+                self.copy(kind, i).wait_send()
+            self.copy(2, i, flip(self.quarter, 2)).wait_send()
+
+
+def params(number, **more):
+    return pltpu.CompilerParams(collective_id=number, has_side_effects=True, **more)
+
+
+ANY = pl.BlockSpec(memory_space=pl.ANY)
+VMEM = pl.BlockSpec(memory_space=pltpu.VMEM)
+DMA = pltpu.SemaphoreType.DMA
+
+
+def fetch_kernel(
+    tokens, cotangent, qkv_parts, out_part, gate, up, down, table,
+    all_tokens, my_cotangent, w_qkv, w_out, w_gate, w_up, w_down, tables, out_slabs,
+    home_send, home_recv, part_send, part_recv, wa_send, wa_recv, table_send, table_recv,
+    ring_send, ring_recv, local, out_send, out_recv,
+):
+    place, column = here()
+    count = w_qkv.shape[0]
+    local_len = tokens.shape[1]
+    level, parity = place // 2, place % 2
+    member = flip(level, 1)
+    home_column, home_block = home_of(place)
+    quarter = flip(column, 1)
+    near_far = wa_peers(place, column)
+    ring_near = ring_peers(place, column, count)
+    home_from = [(2 * quarter, home_column), (2 * quarter + 1, home_column)]
+    home_to = [(group_of(column, b), member) for b in (0, 1)]
+    greet(home_from + near_far + ring_near, 7)
+
+    rows = qkv_parts.shape[1]
+    ours = pl.ds(pl.multiple_of(column * rows, rows), rows)
+    block = w_gate.shape[2] // count
+
+    def slices(source, buffer, who):
+        for b in range(count):
+            at = pl.multiple_of((4 * b + who) * block, block)
+            yield source.at[:, pl.ds(at, block)], buffer.at[place, ours, pl.ds(b * block, block)]
+
+    starts = [
+        pltpu.make_async_copy(table, tables.at[quarter, place], local.at[0]),
+        pltpu.make_async_copy(qkv_parts.at[column], w_qkv.at[place, ours], local.at[1]),
+        pltpu.make_async_copy(out_part, out_slabs.at[place], local.at[2]),
+        pltpu.make_async_copy(down, w_down.at[place], local.at[3]),
+    ]
+    for copy in starts:
+        copy.start()
+    moves = []
+    for k, peer in enumerate(near_far):
+        moves.append(
+            remote(qkv_parts.at[peer[1]], w_qkv.at[place, ours], part_send.at[0, k], part_recv.at[0, k], peer)
+        )
+    for move in moves:
+        move.start()
+    homes = [
+        remote(tokens.at[b], all_tokens.at[level, pl.ds(parity * local_len, local_len)], home_send.at[0, b], home_recv.at[0, parity], home_to[b])
+        for b in (0, 1)
+    ]
+    for move in homes:
+        move.start()
+    for t, (source, buffer) in enumerate(((gate, w_gate), (up, w_up))):
+        for piece, target in slices(source, buffer, column):
+            pltpu.make_async_copy(piece, target, local.at[4 + t]).start()
+        for k, peer in enumerate(near_far):
+            for piece, target in slices(source, buffer, peer[1]):
+                remote(piece, target, part_send.at[1 + t, k], part_recv.at[1 + t, k], peer).start()
+
+    def parts_here(t, buffer):
+        for k, peer in enumerate(near_far):
+            theirs = pl.ds(pl.multiple_of(peer[1] * rows, rows), rows)
+            region = buffer.at[place, theirs]
+            remote(region, region, part_send.at[t, k], part_recv.at[t, k], peer).wait_recv()
+
+    rings = [
+        Ring(buffer, ring_send.at[i], ring_recv.at[i], place, column)
+        for i, buffer in enumerate((w_qkv, tables.at[quarter], out_slabs, w_gate, w_up, w_down))
+    ]
+    table_gather = WaGather(tables, table_send, table_recv, place, column, count)
+    gather = WaGather(all_tokens, wa_send, wa_recv, place, column, 2)
+    starts[1].wait()
+    parts_here(0, w_qkv)
+    qkv_ring, table_ring, out_ring, gate_ring, up_ring, down_ring = rings
+    qkv_ring.step(0)
+    starts[0].wait()
+    qkv_ring.step(1)
+
+    def token_block(i):
+        region = gather.region(quarter, i)
+        remote(region, region, home_send.at[0, i], home_recv.at[0, i], home_from[i]).wait_recv()
+        gather.own(i)
+
+    token_block(0)
+    token_block(1)
+    for i in range(2, 7):
+        qkv_ring.step(i)
+        if i in (4, 6):
+            gather.forward((i - 4) // 2)
+    for i in range(7):
+        table_ring.step(i)
+    starts[2].wait()
+    for i in range(7):
+        out_ring.step(i)
+    late = [
+        remote(cotangent.at[b], my_cotangent.at[pl.ds(parity * local_len, local_len)], home_send.at[1, b], home_recv.at[1, parity], home_to[b])
+        for b in (0, 1)
+    ]
+    for move in late:
+        move.start()
+    table_ring.finish()
+    for i in range(count):
+        table_gather.own(i)
+    for t, (buffer, ring) in enumerate(((w_gate, gate_ring), (w_up, up_ring))):
+        region = buffer.at[place, ours]
+        pltpu.make_async_copy(region, region, local.at[4 + t]).wait()
+        parts_here(1 + t, buffer)
+        for i in range(7):
+            ring.step(i)
+            if t == 1:
+                table_gather.forward(i)
+    table_gather.forward(7)
+    out_ring.finish()
+    core = column % 2
+    some = count // 2
+    keep = pltpu.make_async_copy(out_slabs.at[pl.ds(core * some, some)], w_out.at[:, core], local.at[2])
+    keep.start()
+    give = remote(
+        out_slabs.at[pl.ds((1 - core) * some, some)], w_out.at[:, core], out_send, out_recv, near_far[0]
+    )
+    give.start()
+    starts[3].wait()
+    for i in range(7):
+        down_ring.step(i)
+    for i in (0, 1):
+        region = my_cotangent.at[pl.ds(i * local_len, local_len)]
+        remote(region, region, home_send.at[1, i], home_recv.at[1, i], home_from[i]).wait_recv()
+    for ring in (qkv_ring, gate_ring, up_ring, down_ring):
+        ring.finish()
+    gather.finish()
+    table_gather.finish()
+    keep.wait()
+    take = w_out.at[:, 1 - core]
+    remote(take, take, out_send, out_recv, near_far[0]).wait_recv()
+    give.wait_send()
+    for move in moves + homes + late:
+        move.wait_send()
+    for t, (source, buffer) in enumerate(((gate, w_gate), (up, w_up))):
+        for k, peer in enumerate(near_far):
+            region = buffer.at[place, ours]
+            remote(region, region, part_send.at[1 + t, k], part_recv.at[1 + t, k], peer).wait_send()
+
+
+def fetch(tokens, cotangent, qkv_parts, out_part, gate, up, down, table, count):
+    bf16 = jnp.bfloat16
+    width = tokens.shape[2]
+    slab = 4 * qkv_parts.shape[1]
+    units = gate.shape[1] // 4
+    shape = lambda *dims: jax.ShapeDtypeStruct(dims, bf16)
+    return pl.pallas_call(
+        fetch_kernel,
+        in_specs=[ANY] * 8,
+        out_specs=[ANY] * 9,
+        out_shape=[
+            shape(4, 2 * tokens.shape[1], width), shape(2 * tokens.shape[1], width), shape(count, slab, qkv_parts.shape[2]),
+            shape(count // 2, 2, *out_part.shape), shape(count, slab, units),
+            shape(count, slab, units), shape(count, *down.shape), shape(4, count, *table.shape),
+            shape(count, *out_part.shape),
+        ],
+        scratch_shapes=[
+            DMA((2, 2)), DMA((2, 2)), DMA((3, 3)), DMA((3, 3)), DMA((3, 2)), DMA((3, 2)),
+            DMA((3, count)), DMA((3, count)), DMA((6, 2, count - 1)), DMA((6, 2, count - 1)),
+            DMA((6,)), DMA(()), DMA(()),
+        ],
+        name="fetch",
+        compiler_params=params(1),
+    )(tokens, cotangent, qkv_parts, out_part, gate, up, down, table)
+
+
+def gather_kernel(own, every, send, recv, local):
+    place, column = here()
+    greet(wa_peers(place, column)[:2], 2)
+    gather = WaGather(every, send, recv, place, column, send.shape[1], own)
+    for i in range(gather.pieces):
+        gather.own(i)
+    keep = pltpu.make_async_copy(own, every.at[gather.quarter], local)
+    keep.start()
+    for i in range(gather.pieces):
+        gather.forward(i)
+    gather.finish()
+    keep.wait()
+
+
+def gather_rows(own, number, pieces=4):
+    return pl.pallas_call(
+        gather_kernel,
+        in_specs=[VMEM],
+        out_specs=ANY,
+        out_shape=jax.ShapeDtypeStruct((4, *own.shape), own.dtype),
+        scratch_shapes=[DMA((3, pieces)), DMA((3, pieces)), DMA(())],
+        name="gather_rows",
+        compiler_params=params(number),
+    )(own)
+
+
+def swap_kernel(parts, out, send, recv, local):
+    place, column = here()
+    peers = wa_peers(place, column)
+    greet(peers, 3)
+    keep = pltpu.make_async_copy(parts.at[column], out.at[column], local)
+    keep.start()
+    moves = [
+        remote(parts.at[peer[1]], out.at[column], send.at[k], recv.at[k], peer)
+        for k, peer in enumerate(peers)
+    ]
+    for move in moves:
+        move.start()
+    keep.wait()
+    for k, peer in enumerate(peers):
+        region = out.at[peer[1]]
+        remote(region, region, send.at[k], recv.at[k], peer).wait_recv()
+    for move in moves:
+        move.wait_send()
+
+
+def swap_parts(parts, number):
+    return pl.pallas_call(
+        swap_kernel,
+        in_specs=[ANY],
+        out_specs=ANY,
+        out_shape=jax.ShapeDtypeStruct(parts.shape, parts.dtype),
+        scratch_shapes=[DMA((3,)), DMA((3,)), DMA(())],
+        name="swap_parts",
+        compiler_params=params(number),
+    )(parts)
+
+
+def scatter_kernel(*refs, turned, pieces):
+    pairs = len(turned)
+    operands, (out, mid_out) = refs[: 3 * pairs], refs[3 * pairs : 3 * pairs + 2]
+    (
+        partial, middle, first, first_mid, chip, chip_mid, last, last_mid, send, recv,
+    ) = refs[3 * pairs + 2 :]
+    place, column = here()
+    near, across, _ = wa_peers(place, column)
+    greet([near, across], 2)
+    quarter = flip(column, 1)
+    far = flip(quarter, 2)
+    rows = partial.shape[1]
+    width = partial.shape[2]
+    step = 512
+
+    def product(which):
+        at = pl.ds(pl.multiple_of(which * rows, rows), rows)
+
+        def block(b, carry):
+            cols = pl.ds(pl.multiple_of(b * step, step), step)
+            total = None
+            for p in range(pairs):
+                left, weight, _ = operands[3 * p : 3 * p + 3]
+                if turned[p]:
+                    term = times_t(left[at, :], weight[cols, :])
+                else:
+                    term = low_dot(left[at, :], weight[:, cols])
+                total = term if total is None else total + term
+            partial[which, :, cols] = total.astype(jnp.bfloat16)
+            return carry
+
+        lax.fori_loop(0, width // step, block, 0)
+        total = None
+        for p in range(pairs):
+            left, _, adapter = operands[3 * p : 3 * p + 3]
+            term = times_t(left[at, :], adapter[...])
+            total = term if total is None else total + term
+        middle[which] = total.astype(jnp.bfloat16)
+
+    def to_near(slot, which):
+        return (
+            remote(partial.at[which], first.at[slot], send.at[slot], recv.at[slot], near),
+            remote(middle.at[which], first_mid.at[slot], send.at[2 + slot], recv.at[2 + slot], near),
+        )
+
+    sent = []
+    for slot, which in ((0, flip(far, 1)), (1, flip(quarter, 1))):
+        product(which)
+        for copy in to_near(slot, which):
+            copy.start()
+            sent.append(copy)
+        if slot == 0:
+            product(far)
+            for copy in to_near(0, which):
+                copy.wait_recv()
+            size = rows // pieces
+            for i in range(pieces):
+                at = pl.ds(i * size, size)
+                chip[at] = (
+                    partial[far, at, :].astype(jnp.float32) + first[0, at, :].astype(jnp.float32)
+                ).astype(jnp.bfloat16)
+                copy = remote(chip.at[at], last.at[at], send.at[4 + i], recv.at[4 + i], across)
+                copy.start()
+                sent.append(copy)
+            chip_mid[...] = (
+                middle[far].astype(jnp.float32) + first_mid[0].astype(jnp.float32)
+            ).astype(jnp.bfloat16)
+            copy = remote(chip_mid, last_mid, send.at[4 + pieces], recv.at[4 + pieces], across)
+            copy.start()
+            sent.append(copy)
+    product(quarter)
+    for copy in to_near(1, quarter):
+        copy.wait_recv()
+    size = rows // pieces
+    for i in range(pieces):
+        at = pl.ds(i * size, size)
+        remote(last.at[at], last.at[at], send.at[4 + i], recv.at[4 + i], across).wait_recv()
+        out[at, :] = (
+            partial[quarter, at, :].astype(jnp.float32)
+            + first[1, at, :].astype(jnp.float32)
+            + last[at, :].astype(jnp.float32)
+        )
+    remote(last_mid, last_mid, send.at[4 + pieces], recv.at[4 + pieces], across).wait_recv()
+    mid_out[...] = (
+        middle[quarter].astype(jnp.float32)
+        + first_mid[1].astype(jnp.float32)
+        + last_mid[...].astype(jnp.float32)
+    )
+    for copy in sent:
+        copy.wait_send()
+
+
+def scatter_product(operands, turned, width, number, pieces=4):
+    rows = operands[0][0].shape[0] // 4
+    ranks = operands[0][2].shape[0]
+    bf16, f32 = jnp.bfloat16, jnp.float32
+    flat = [array for triple in operands for array in triple]
+    return pl.pallas_call(
+        functools.partial(scatter_kernel, turned=turned, pieces=pieces),
+        in_specs=[VMEM] * len(flat),
+        out_specs=[VMEM] * 2,
+        out_shape=[
+            jax.ShapeDtypeStruct((rows, width), f32), jax.ShapeDtypeStruct((rows, ranks), f32),
+        ],
+        scratch_shapes=[
+            pltpu.VMEM((4, rows, width), bf16), pltpu.VMEM((4, rows, ranks), bf16),
+            pltpu.VMEM((2, rows, width), bf16), pltpu.VMEM((2, rows, ranks), bf16),
+            pltpu.VMEM((rows, width), bf16), pltpu.VMEM((rows, ranks), bf16),
+            pltpu.VMEM((rows, width), bf16), pltpu.VMEM((rows, ranks), bf16),
+            DMA((5 + pieces,)), DMA((5 + pieces,)),
+        ],
+        name="scatter_product",
+        compiler_params=params(number, vmem_limit_bytes=VMEM_BYTES),
+        cost_estimate=pl.CostEstimate(
+            flops=sum(8 * rows * a.shape[1] * width for a, _, _ in operands),
+            bytes_accessed=sum(2 * math.prod(a.shape) for a in flat), transcendentals=0,
+        ),
+    )(*flat)
+
+
+def finish_kernel(
+    result, grad, table, result_home, grad_home, tables, send, recv, ring_send, ring_recv, local
+):
+    place, column = here()
+    count = tables.shape[0]
+    local_len = result.shape[0] // 2
+    level, parity = place // 2, place % 2
+    home_column, home_block = home_of(place)
+    quarter = flip(column, 1)
+    targets = [(2 * quarter, home_column), (2 * quarter + 1, home_column)]
+    sources = [(group_of(column, b), flip(level, 1)) for b in (0, 1)]
+    greet(sources + ring_peers(place, column, count), 4)
+    keep = pltpu.make_async_copy(table, tables.at[place], local)
+    keep.start()
+    moves = []
+    for t, (own, home) in enumerate(((result, result_home), (grad, grad_home))):
+        for i in (0, 1):
+            moves.append(
+                remote(
+                    own.at[pl.ds(i * local_len, local_len)], home.at[home_block], send.at[t, i],
+                    recv.at[t, home_block], targets[i],
+                )
+            )
+    ring = Ring(tables, ring_send, ring_recv, place, column, table)
+    ring.step(0)
+    for move in moves:
+        move.start()
+    for i in range(1, 7):
+        ring.step(i)
+    ring.finish()
+    for t, home in enumerate((result_home, grad_home)):
+        for b in (0, 1):
+            remote(home.at[b], home.at[b], send.at[t, b], recv.at[t, b], sources[b]).wait_recv()
+    for move in moves:
+        move.wait_send()
+    keep.wait()
+
+
+def finish(result, grad, table, count, number):
+    bf16 = jnp.bfloat16
+    home = jax.ShapeDtypeStruct((2, result.shape[0] // 2, result.shape[1]), bf16)
+    return pl.pallas_call(
+        finish_kernel,
+        in_specs=[ANY] * 3,
+        out_specs=[ANY] * 3,
+        out_shape=[home, home, jax.ShapeDtypeStruct((count, *table.shape), bf16)],
+        scratch_shapes=[
+            DMA((2, 2)), DMA((2, 2)), DMA((2, count - 1)), DMA((2, count - 1)), DMA(()),
+        ],
+        name="finish",
+        compiler_params=params(number),
+    )(result, grad, table)
 
 
 def per_group(
@@ -696,40 +1220,8 @@
     slice_units = hidden_units // wa
     unit_block = down_weight.shape[0]
     half = wa // 2
-    out_pairs, back_pairs = home_pairs(groups, wa), None
-    back_pairs = [[(b, a) for a, b in pairs] for pairs in out_pairs]
-    home_column, home_block = group_home(place, wa)
-    parity = lax.rem(place, 2)
-
-    def to_group(array):
-        first = lax.dynamic_index_in_dim(array, parity, 0, keepdims=False)
-        second = lax.dynamic_index_in_dim(array, 1 - parity, 0, keepdims=False)
-        first = lax.ppermute(first, BOTH, out_pairs[0])
-        second = lax.ppermute(second, BOTH, out_pairs[1])
-        swap = home_block == 1
-        return jnp.concatenate(
-            [jnp.where(swap, second, first), jnp.where(swap, first, second)], axis=0
-        )
-
-    def to_home(array):
-        pieces = array.reshape(2, local_len, *array.shape[1:])
-        first = lax.dynamic_index_in_dim(pieces, home_block, 0, keepdims=False)
-        second = lax.dynamic_index_in_dim(pieces, 1 - home_block, 0, keepdims=False)
-        first = lax.ppermute(first, BOTH, back_pairs[0])
-        second = lax.ppermute(second, BOTH, back_pairs[1])
-        swap = parity == 1
-        return jnp.stack([jnp.where(swap, second, first), jnp.where(swap, first, second)])
-
-    def gather_wa(array):
-        return lax.all_gather(array, "wa", axis=0, tiled=True)
-
-    def gather_seq(array):
-        return lax.all_gather(array, "seq", axis=0, tiled=True)
-
-    def scatter_wa(product, middle):
-        both = jnp.concatenate([product.astype(bf16), middle.astype(bf16)], axis=1)
-        both = lax.psum_scatter(both, "wa", scatter_dimension=0, tiled=True)
-        return both[:, : product.shape[1]].astype(f32), both[:, product.shape[1] :]
+    rank = ADAPTER_RANK
+    own_rows = rank // wa
 
     def by_head(array):
         parts = array.reshape(*array.shape[:-1], 2, slice_heads, half, HEAD_DIM)
@@ -744,51 +1236,71 @@
     def mine(parts):
         return lax.dynamic_index_in_dim(parts, column, 0, keepdims=False)
 
+    def gather_wa(array, number, pieces=4):
+        return gather_rows(array, number, pieces).reshape(-1, array.shape[-1])
+
     gain_q = query_norm_gain.astype(f32)
     gain_k = key_norm_gain.astype(f32)
     gain_a = attention_norm_gain.astype(f32)
     gain_f = feedforward_norm_gain.astype(f32)
 
-    my_tokens = to_group(tokens)
-    my_cotangent = to_group(cotangent)
-    small = jnp.concatenate([token_document_index, sequence_adapter_index[:, None]], axis=1)
-    small = lax.all_gather(small, BOTH, axis=0, tiled=False).reshape(groups, wa, 2, local_len + 1)
-    order = [group_home(g, wa) for g in range(groups)]
-    adapter_of = jnp.stack([small[0, c, b, local_len] for c, b in order])
+    marks = jnp.concatenate(
+        [
+            token_document_index.reshape(1, -1).astype(bf16),
+            sequence_adapter_index.reshape(1, -1).astype(bf16),
+        ],
+        axis=1,
+    )
+    marks = jnp.pad(marks, ((0, 3), (0, width - marks.shape[1])))
+    adapter_arrays = (
+        attention_down_adapters, attention_up_adapters, feedforward_down_adapters,
+        feedforward_up_adapters, downproj_down_adapters, downproj_up_adapters,
+    )
+    table = jnp.concatenate([a.reshape(-1, width) for a in adapter_arrays] + [marks], axis=0)
+    mark_at = table.shape[0] - 4
+    qkv_parts = jnp.concatenate(
+        [by_head(w) for w in (query_weight, key_weight, value_weight)], axis=-1
+    )
+    seq_tokens, my_cotangent, w_qkv, w_out, w_gate, w_up, w_down, tables, _ = fetch(
+        tokens, cotangent.astype(bf16), qkv_parts, output_weight, gate_weight, up_weight,
+        down_weight, table, groups,
+    )
+    quarter = flip(column, 1)
+    my_tokens = lax.dynamic_index_in_dim(seq_tokens, quarter, 0, keepdims=False)
+    my_cotangent = my_cotangent.astype(f32)
+    seq_tokens = seq_tokens.reshape(length, width)
+    w_qkv = w_qkv.reshape(width, 3 * slice_width)
+    w_out = w_out.reshape(slice_width, width)
+    w_gate, w_up = (w.reshape(width, slice_units) for w in (w_gate, w_up))
+    w_down = w_down.reshape(slice_units, width)
+
+    marks = tables[:, :, mark_at]
+    adapter_of = jnp.stack(
+        [marks[flip(home_of(g)[0], 1), 0, 2 * local_len + home_of(g)[1]] for g in range(groups)]
+    ).astype(jnp.int32)
     my_adapter = lax.dynamic_index_in_dim(adapter_of, place, 0, keepdims=False)
-    documents = lax.dynamic_index_in_dim(
-        lax.dynamic_index_in_dim(small, home_column, 1, keepdims=False),
-        home_block, 1, keepdims=False,
-    )[:, :local_len].reshape(length)
+    home_column, home_block = home_of(place)
+    marks = lax.dynamic_index_in_dim(marks, flip(home_column, 1), 0, keepdims=False)
+    documents = lax.dynamic_slice_in_dim(marks, home_block * local_len, local_len, 1)
+    documents = documents.reshape(length).astype(jnp.int32)
     doc_col, doc_row = documents[:, None], documents[None, :]
 
-    def adapter(table):
-        every = lax.all_gather(table, "seq", axis=0, tiled=False)
-        return lax.dynamic_index_in_dim(every, my_adapter, 0, keepdims=False)
-
-    rows_a = adapter(
-        jnp.concatenate(
-            [
-                jnp.concatenate(list(attention_down_adapters), axis=1),
-                jnp.concatenate(list(attention_up_adapters), axis=1),
-                jnp.concatenate(list(feedforward_down_adapters), axis=1),
-                jnp.concatenate(list(feedforward_up_adapters), axis=1),
-                downproj_down_adapters,
-                downproj_up_adapters,
-            ],
-            axis=1,
-        )
-    )
-    rows_a = gather_wa(rows_a)
-    cuts = [width] * 10 + [hidden_units] * 3 + [width]
-    spots = [sum(cuts[:i]) for i in range(len(cuts))]
-    pieces = [rows_a[:, a : a + n] for a, n in zip(spots, cuts, strict=True)]
-    aq, ak, av, ao, bq, bk, bv, bo, ag, au, bg, bu, ad, bd = pieces
+    chosen = lax.dynamic_index_in_dim(tables, my_adapter, 1, keepdims=False)
+    chosen = jnp.stack([chosen[flip(w, 1)] for w in range(wa)])
+    picked, at = [], 0
+    for array in adapter_arrays:
+        kinds = array.shape[0] if array.ndim == 3 else 1
+        rows = kinds * own_rows * (array.shape[-1] // width)
+        part = chosen[:, at : at + rows].reshape(wa, kinds, own_rows, array.shape[-1])
+        part = jnp.moveaxis(part, 0, 1).reshape(kinds, rank, array.shape[-1])
+        picked += [part[k] for k in range(kinds)]
+        at += rows
+    aq, ak, av, ao, bq, bk, bv, bo, ag, au, bg, bu, ad, bd = picked
     aqkv = jnp.concatenate([aq, ak, av], axis=0)
     bq, bk, bv, ao = (mine(by_head(t)) for t in (bq, bk, bv, ao))
     bg, bu, ad = (mine(by_unit(t)) for t in (bg, bu, ad))
     agu = jnp.concatenate([ag, au], axis=0)
-    zero = jnp.zeros((ADAPTER_RANK, slice_width), bf16)
+    zero = jnp.zeros((rank, slice_width), bf16)
     b_qkv = jnp.concatenate(
         [
             jnp.concatenate([bq, zero, zero], axis=1),
@@ -798,37 +1310,15 @@
         axis=0,
     )
 
-    def to_members(parts):
-        moved = lax.all_to_all(parts, "wa", split_axis=0, concat_axis=0, tiled=True)
-        return moved.reshape(-1, parts.shape[-1])
-
-    w_qkv = gather_seq(
-        to_members(
-            jnp.concatenate([by_head(w) for w in (query_weight, key_weight, value_weight)], axis=-1)
-        )
-    )
-    w_out = gather_seq(output_weight[None])
-    core = lax.rem(column, 2)
-    w_out = w_out.reshape(2, groups // 2, *output_weight.shape)
-    other = lax.ppermute(
-        lax.dynamic_index_in_dim(w_out, 1 - core, 0, keepdims=False),
-        "wa", [(i, i ^ 1) for i in range(wa)],
-    )
-    own = lax.dynamic_index_in_dim(w_out, core, 0, keepdims=False)
-    w_out = jnp.stack(
-        [jnp.where(core == 0, own, other), jnp.where(core == 0, other, own)], axis=1
-    ).reshape(slice_width, width)
-    w_gate = gather_seq(to_members(by_unit(gate_weight)))
-    w_up = gather_seq(to_members(by_unit(up_weight)))
-    w_down = gather_seq(down_weight)
-
-    seq_tokens = gather_wa(my_tokens)
+    def padded(array, before=0):
+        return jnp.pad(array, ((before, 128 - before - array.shape[0]), (0, 0)))
+
     mid_qkv = times_t(seq_tokens, aqkv).astype(bf16)
     qkv_raw = low_dot(seq_tokens, w_qkv) + low_dot(mid_qkv, b_qkv)
-    squares = jnp.sum(
-        jnp.square(qkv_raw[:, : 2 * slice_width]).reshape(length, 2, slice_width), axis=2
-    )
-    squares = lax.psum(squares, "wa")
+    squares = jnp.stack(
+        [jnp.sum(jnp.square(qkv_raw[:, i * slice_width : (i + 1) * slice_width]), axis=1) for i in (0, 1)]
+    )
+    squares = jnp.sum(gather_rows(squares.reshape(8, -1), 2, 1), axis=0).reshape(2, length).T
     tables = rope_full(length)
     my_gain_q = mine(by_head(gain_q[None]))
     my_gain_k = mine(by_head(gain_k[None]))
@@ -837,24 +1327,26 @@
         qkv_raw, squares[:, :1], squares[:, 1:], my_gain_q, my_gain_k, tables,
         doc_col, doc_row, window,
     )
-    branch, mid_out = scatter_wa(low_dot(attended, w_out), times_t(attended, ao))
+    branch, mid_out = scatter_product([(attended, w_out, padded(ao))], (False,), width, 3)
+    mid_out = mid_out[:, :rank].astype(bf16)
     branch = branch + low_dot(mid_out, bo)
     hidden = my_tokens.astype(f32) + rms_scale(branch, gain_a)
     hidden_low = hidden.astype(bf16)
 
-    seq_hidden = gather_wa(hidden_low)
+    seq_hidden = gather_wa(hidden_low, 4)
     mid_gu = times_t(seq_hidden, agu).astype(bf16)
-    mid_gate, mid_up = mid_gu[:, :ADAPTER_RANK], mid_gu[:, ADAPTER_RANK:]
+    mid_gate, mid_up = mid_gu[:, :rank], mid_gu[:, rank:]
     gate = low_dot(seq_hidden, w_gate) + low_dot(mid_gate, bg)
     up_value = low_dot(seq_hidden, w_up) + low_dot(mid_up, bu)
     sigmoid = jax.nn.sigmoid(gate)
     mixed = (gate * sigmoid * up_value).astype(bf16)
-    ffn_branch, mid_down = scatter_wa(low_dot(mixed, w_down), times_t(mixed, ad))
+    ffn_branch, mid_down = scatter_product([(mixed, w_down, padded(ad))], (False,), width, 5)
+    mid_down = mid_down[:, :rank].astype(bf16)
     ffn_branch = ffn_branch + low_dot(mid_down, bd)
     layer_out = (hidden + rms_scale(ffn_branch, gain_f)).astype(bf16)
 
     d_ffn = rms_back(ffn_branch, gain_f, my_cotangent).astype(bf16)
-    seq_d_ffn = gather_wa(d_ffn)
+    seq_d_ffn = gather_wa(d_ffn, 6)
     bd_grad = dot_rows(mid_down, d_ffn)
     d_mid_down = times_t(seq_d_ffn, bd).astype(bf16)
     d_mixed = times_t(seq_d_ffn, w_down) + low_dot(d_mid_down, ad)
@@ -863,15 +1355,15 @@
     d_up = (d_mixed * gate * sigmoid).astype(bf16)
     bg_grad = dot_rows(mid_gate, d_gate)
     bu_grad = dot_rows(mid_up, d_up)
-    d_hidden, d_mid_gu = scatter_wa(
-        times_t(d_gate, w_gate) + times_t(d_up, w_up),
-        jnp.concatenate([times_t(d_gate, bg), times_t(d_up, bu)], axis=1),
-    )
+    d_hidden, d_mid_gu = scatter_product(
+        [(d_gate, w_gate, padded(bg)), (d_up, w_up, padded(bu, rank))], (True, True), width, 7
+    )
+    d_mid_gu = d_mid_gu[:, : 2 * rank].astype(bf16)
     d_hidden = my_cotangent + d_hidden + low_dot(d_mid_gu, agu)
     agu_grad = dot_rows(d_mid_gu, hidden_low)
 
     d_branch = rms_back(branch, gain_a, d_hidden).astype(bf16)
-    seq_d_branch = gather_wa(d_branch)
+    seq_d_branch = gather_wa(d_branch, 8)
     bo_grad = dot_rows(mid_out, d_branch)
     d_mid_out = times_t(seq_d_branch, bo).astype(bf16)
     d_attended = (times_t(seq_d_branch, w_out) + low_dot(d_mid_out, ao)).astype(bf16)
@@ -880,7 +1372,8 @@
         query, key, value, d_attended, qkv_raw, my_gain_q, my_gain_k, tables,
         doc_col, doc_row, window,
     )
-    dots = lax.psum(jnp.concatenate([q_dot, k_dot], axis=1), "wa") * (1.0 / width)
+    dots = jnp.concatenate([q_dot, k_dot], axis=1).T.reshape(8, -1)
+    dots = jnp.sum(gather_rows(dots, 9, 1), axis=0).reshape(2, length).T * (1.0 / width)
     scales = lax.rsqrt(squares * (1.0 / width) + EPSILON)
 
     def raw_grad(raw, weighted, i):
@@ -897,51 +1390,52 @@
         axis=1,
     )
     b_qkv_grad = dot_rows(mid_qkv, d_qkv)
-    d_tokens, d_mid_qkv = scatter_wa(times_t(d_qkv, w_qkv), times_t(d_qkv, b_qkv))
+    d_tokens, d_mid_qkv = scatter_product([(d_qkv, w_qkv, padded(b_qkv))], (True,), width, 10)
+    d_mid_qkv = d_mid_qkv[:, : 3 * rank].astype(bf16)
     my_grad = d_hidden + d_tokens + low_dot(d_mid_qkv, aqkv)
     aqkv_grad = dot_rows(d_mid_qkv, my_tokens)
 
-    def to_owners(sliced, full):
-        cut = jnp.concatenate(sliced + full, axis=1).reshape(wa, ADAPTER_RANK // wa, -1)
-        every = lax.all_to_all(cut.astype(bf16), "wa", split_axis=0, concat_axis=0, tiled=True)
-        n = sum(p.shape[1] for p in sliced)
-        joined = jnp.moveaxis(every[:, :, :n], 0, 1).reshape(ADAPTER_RANK // wa, -1)
-        summed = jnp.sum(every[:, :, n:].astype(f32), axis=0).astype(bf16)
-        both = lax.all_gather(jnp.concatenate([joined, summed], axis=1), "seq", axis=0, tiled=False)
-        chosen = (adapter_of == place)[:, None, None]
-        total = jnp.sum(jnp.where(chosen, both.astype(f32), 0.0), axis=0)
-        return total[:, : n * wa].reshape(-1, wa, n), total[:, n * wa :]
-
     def heads_back(parts):
-        split = parts.reshape(-1, half, 2, slice_heads, HEAD_DIM)
-        return jnp.transpose(split, (0, 2, 3, 1, 4)).reshape(-1, width)
+        split = parts.reshape(own_rows, half, 2, slice_heads, HEAD_DIM)
+        return jnp.transpose(split, (0, 2, 3, 1, 4)).reshape(own_rows, width)
 
     def units_back(parts):
-        split = parts.reshape(-1, wa, groups, unit_block)
-        return jnp.transpose(split, (0, 2, 1, 3)).reshape(-1, hidden_units)
-
-    r = ADAPTER_RANK
-    ffn_cut, ffn_full = to_owners(
-        [bg_grad, bu_grad, ad_grad], [agu_grad[:r], agu_grad[r:], bd_grad]
-    )
-    u = slice_units
-    ffn_b_grad = jnp.stack([units_back(ffn_cut[:, :, :u]), units_back(ffn_cut[:, :, u : 2 * u])])
-    down_a_grad = units_back(ffn_cut[:, :, 2 * u :])
-    ffn_a_grad = jnp.stack([ffn_full[:, :width], ffn_full[:, width : 2 * width]])
-    down_b_grad = ffn_full[:, 2 * width :]
+        split = parts.reshape(own_rows, wa, groups, unit_block)
+        return jnp.transpose(split, (0, 2, 1, 3)).reshape(-1, width)
+
+    def to_rows(sliced, full, back, number):
+        cut = jnp.concatenate(sliced + full, axis=1).astype(bf16)
+        every = swap_parts(cut.reshape(wa, -1, width), number).reshape(wa, own_rows, -1)
+        n = sliced[0].shape[1]
+        joined = [
+            back(jnp.moveaxis(every[:, :, i * n : (i + 1) * n], 0, 1)) for i in range(len(sliced))
+        ]
+        summed = jnp.sum(every[:, :, n * len(sliced) :].astype(f32), axis=0).astype(bf16)
+        return joined, [summed[:, i * width : (i + 1) * width] for i in range(len(full))]
+
+    (bg_rows, bu_rows, ad_rows), (ag_rows, au_rows, bd_rows) = to_rows(
+        [bg_grad, bu_grad, ad_grad], [agu_grad[:rank], agu_grad[rank:], bd_grad], units_back, 11
+    )
     w = slice_width
-    attn_cut, attn_full = to_owners(
-        [b_qkv_grad[:r, :w], b_qkv_grad[r : 2 * r, w : 2 * w], b_qkv_grad[2 * r :, 2 * w :], ao_grad],
-        [aqkv_grad[:r], aqkv_grad[r : 2 * r], aqkv_grad[2 * r :], bo_grad],
-    )
-    heads = [heads_back(attn_cut[:, :, i * w : (i + 1) * w]) for i in range(4)]
-    fulls = [attn_full[:, i * width : (i + 1) * width] for i in range(4)]
-    attn_a_grad = jnp.stack(fulls[:3] + [heads[3]])
-    attn_b_grad = jnp.stack(heads[:3] + [fulls[3]])
-    return (
-        to_home(layer_out), to_home(my_grad), attn_a_grad, attn_b_grad, ffn_a_grad, ffn_b_grad,
-        down_a_grad, down_b_grad,
-    )
+    (bq_rows, bk_rows, bv_rows, ao_rows), (aq_rows, ak_rows, av_rows, bo_rows) = to_rows(
+        [b_qkv_grad[i * rank : (i + 1) * rank, i * w : (i + 1) * w] for i in range(3)] + [ao_grad],
+        [aqkv_grad[i * rank : (i + 1) * rank] for i in range(3)] + [bo_grad],
+        heads_back, 12,
+    )
+    grads = [
+        aq_rows, ak_rows, av_rows, ao_rows, bq_rows, bk_rows, bv_rows, bo_rows, ag_rows, au_rows,
+        bg_rows, bu_rows, ad_rows, bd_rows,
+    ]
+    table = jnp.concatenate(grads + [jnp.zeros((4, width), bf16)], axis=0)
+    out_home, grad_home, tables = finish(layer_out, my_grad.astype(bf16), table, groups, 13)
+    shared = (adapter_of == place)[:, None, None]
+    total = jnp.sum(jnp.where(shared, tables.astype(f32), 0.0), axis=0)
+    outputs, at = [], 0
+    for array in adapter_arrays:
+        rows = math.prod(array.shape) // width
+        outputs.append(total[at : at + rows].reshape(array.shape))
+        at += rows
+    return (out_home, grad_home.astype(f32), *outputs)
 
 
 def solution(mesh):

time: 1410 us -> 1060 us (0.75); the launches traced: 1410 us -> 1040 us
  waiting for transfers between devices: 869 us -> 0 us
  Pallas kernels: 38.4 us -> 821 us
  blocking collectives: 130 us -> 0 us
  matrix products: 174 us -> 118 us
  starting transfers between devices: 40 us -> 0 us
  local copies, waits for them, and re-layouts: 94.3 us -> 71.5 us
  other arithmetic: 44.5 us -> 29.2 us
    pallas_call x0 -> x13, Pallas kernels: none -> 782 us  [the longest x1 390 us: fetch(): pl.pallas_call(fetch_kernel, in_specs=[ANY] * 8, out_specs=[ANY] * 9, out...]
    all_gather x13 -> x0, waiting for transfers between devices: 532 us -> none  [the longest x5 417 us: gather_seq(): return lax.all_gather(array, 'seq', axis=0, tiled=True)]
    ppermute x9 -> x0, waiting for transfers between devices: 219 us -> none  [the longest x2 104 us: to_home(): second = lax.ppermute(second, BOTH, back_pairs[1])]
    reduce_scatter x4 -> x0, waiting for transfers between devices: 107 us -> none  [scatter_wa(): both = lax.psum_scatter(both, 'wa', scatter_dimension=0, tiled=True)]
    all_to_all x3 -> x0, blocking collectives: 62.1 us -> none  [to_members(): moved = lax.all_to_all(parts, 'wa', split_axis=0, concat_axis=0, tiled=True)]
    dot_general x14 -> x6, matrix products: 72.7 us -> 31.9 us  [times_t(): lax.dot_general(left, weight, (((1,), (1,)), ((), ())), preferred_element...]
    all_gather x1 -> x0, blocking collectives: 33.9 us -> none  [per_group(): lax.all_gather(small, BOTH, axis=0, tiled=False)]
    psum x2 -> x0, blocking collectives: 33.8 us -> none  [the longest x1 17.5 us: per_group(): lax.psum(jnp.concatenate([q_dot, k_dot], axis=1), 'wa') * (1.0 / width)]
  transfers between devices with their start and end apart: 28 -> 0, of which waited for: 23 -> 0; matrix products, arithmetic and copies ran while one was open for 10% -> 0% of each run, Pallas kernels for 2% -> 0%
where the time goes in v2:
time: 1060 us; the launch traced here: 1040 us
  Pallas kernels  821 us (77%)
  matrix products  118 us (11%)
  local copies, waits for them, and re-layouts  71.5 us (7%)
  other arithmetic  29.2 us (3%)
    pallas_call x1, Pallas kernels, fetch(): pl.pallas_call(fetch_kernel, in_specs=[ANY] * 8, out_specs=[ANY] * 9, out...  390 us
    pallas_call x4, Pallas kernels, scatter_product(): pl.pallas_call(functools.partial(scatter_kernel, turned=turned, pieces=pi...  161 us
    pallas_call x1, Pallas kernels, finish(): pl.pallas_call(finish_kernel, in_specs=[ANY] * 3, out_specs=[ANY] * 3, ou...  121 us
    pallas_call x5, Pallas kernels, gather_rows(): pl.pallas_call(gather_kernel, in_specs=[VMEM], out_specs=ANY, out_shape=j...  96 us
    dot_general x12, matrix products, low_dot(): return jnp.dot(left, right, preferred_element_type=jnp.float32)  77.5 us
    dot_general x6, matrix products, times_t(): lax.dot_general(left, weight, (((1,), (1,)), ((), ())), preferred_element...  31.9 us
    pallas_call x1, Pallas kernels, attend_heads_back(): pl.pallas_call(functools.partial(attend_back_kernel, rows=rows, back=back...  21.8 us

profile of v2, /device:TPU:6, one launch (start us, length us, event | category | flops | bytes accessed | tf_op | source)
XLA Modules:
  0.0 1043.9 jit_solution(6162861343274322705)
XLA Ops:
  6.3 3.8 concatenate.56.table
  10.1 389.6 %fetch.1 = (bf16[4,256,2048]{2,1,0:T(8,128)(2,1)}, bf16[256,2048]{1,0:T(8,128)(2,1)}, bf16[8,256,1536]{2,1,0:T(8,128)(2,1)}, bf16[4,2,64,2048]{3,2,1,0:T(8,128)(...) custom-call(bf16[2,128,2048]{2,1,0:T(8,128)(2,1)} %tokens.1, ...), custom_call_target="tpu_custom_call" | custom-call | tf_op jit(solution)/shard_map/fetch/pallas_call | solution.py:937
  401.9 5.3 stack.15
  421.6 3.7 convolution_convert_fusion.8
  425.3 9.1 fusion.52
  439.1 5.7 gather_rows.5
  448.9 16.9 %attend.1 = (bf16[1024,512]{1,0:T(8,128)(2,1)S(1)}, bf16[1024,512]{1,0:T(8,128)(2,1)S(1)}, bf16[1024,512]{1,0:T(8,128)(2,1)S(1)}, bf16[1024,512]{1,0:T(8,128)(2,1)}) custom-call(f32[1024,1536]{1,0:T(8,128)} %copy-done.7, f32[1024,1536]{1,0:T(8,128)} %copy-done.7, f32[1024,1536]{1,0:T(8,128)} %copy-done.7, f32[1024,1]{1,0:T(8,128)S(1)} %get-tuple-element.90.q_sum, ...), custom_call_target="tpu_custom_call" | custom-call | flops 1610612736 | bytes 10485760 | tf_op jit(solution)/shard_map/attend/pallas_call | solution.py:584
  468.5 34.4 %scatter_product.4 = (f32[256,2048]{1,0:T(8,128)}, f32[256,128]{1,0:T(8,128)}) custom-call(bf16[1024,512]{1,0:T(8,128)(2,1)} %copy-done.2, bf16[512,2048]{1,0:T(8,128)(2,1)} %bitcast.272, bf16[128,512]{1,0:T(8,128)(2,1)} %pad.26.refs_2_), custom_call_target="tpu_custom_call" | custom-call | flops 2147483648 | bytes 3276800 | tf_op jit(solution)/shard_map/scatter_product/pallas_call | solution.py:1112
  503.8 3.4 multiply_reduce_fusion.2
  512.3 28.2 %gather_rows.6 = bf16[4,256,2048]{2,1,0:T(8,128)(2,1)} custom-call(bf16[256,2048]{1,0:T(8,128)(2,1)} %fusion.12.own), custom_call_target="tpu_custom_call" | custom-call | tf_op jit(solution)/shard_map/gather_rows/pallas_call | solution.py:972
  540.5 14.6 %fusion.54 = f32[1024,2048]{1,0:T(8,128)} fusion(bf16[1024,2048]{1,0:T(8,128)(2,1)} %bitcast.219, bf16[2048,2048]{1,0:T(8,128)(2,1)} %bitcast.266), kind=kOutput, calls=%fused_computation.178 | convolution fusion | flops 8589934592 | bytes 20971520 | tf_op jit(solution)/shard_map/dot_general | solution.py:465
  556.9 3.7 convolution_convert_fusion.9
  560.6 13.3 %fusion.53 = f32[1024,2048]{1,0:T(8,128)} fusion(bf16[1024,2048]{1,0:T(8,128)(2,1)S(1)} %bitcast.221, bf16[2048,2048]{1,0:T(8,128)(2,1)} %bitcast.264), kind=kOutput, calls=%fused_computation.177 | convolution fusion | flops 8589934592 | bytes 20971520 | tf_op jit(solution)/shard_map/dot_general | solution.py:465
  575.9 4.7 convolution_add_fusion.3
  580.6 11.2 %multiply_convert_fusion.2 = (bf16[1024,2048]{1,0:T(8,128)(2,1)}, f32[1024,2048]{1,0:T(8,128)}) fusion(f32[1024,2048]{1,0:T(8,128)S(1)} %convolution_add_fusion.3, f32[1024,2048]{1,0:T(8,128)} %fusion.54, bf16[16,2048]{1,0:T(8,128)(2,1)S(1)} %copy-done.46, bf16[1024,32]{0,1:T(8,128)(2,1)S(1)} %convolution_convert_fusion.9), kind=kOutput, calls=%fused_computation.2 | convolution fusion | flops 81788928 | bytes 29458432 | tf_op jit(solution)/shard_map/dot_general | solution.py:465
  592.6 40.0 %scatter_product.5 = (f32[256,2048]{1,0:T(8,128)}, f32[256,128]{1,0:T(8,128)}) custom-call(bf16[1024,2048]{1,0:T(8,128)(2,1)} %get-tuple-element.132.refs_0_, bf16[2048,2048]{1,0:T(8,128)(2,1)} %bitcast.268, bf16[128,2048]{1,0:T(8,128)(2,1)} %pad.27.refs_2_), custom_call_target="tpu_custom_call" | custom-call | flops 8589934592 | bytes 13107200 | tf_op jit(solution)/shard_map/scatter_product/pallas_call | solution.py:1112
  637.8 28.0 %gather_rows.7 = bf16[4,256,2048]{2,1,0:T(8,128)(2,1)} custom-call(bf16[256,2048]{1,0:T(8,128)(2,1)} %fusion.10.own), custom_call_target="tpu_custom_call" | custom-call | tf_op jit(solution)/shard_map/gather_rows/pallas_call | solution.py:972
  665.8 3.5 convolution_convert_fusion.11
  669.3 13.5 %fusion.55 = f32[1024,2048]{1,0:T(8,128)} fusion(bf16[1024,2048]{1,0:T(8,128)(2,1)S(1)} %bitcast.223, bf16[2048,2048]{1,0:T(8,128)(2,1)} %bitcast.269), kind=kOutput, calls=%fused_computation.179 | convolution fusion | flops 8589934592 | bytes 20971520 | tf_op jit(solution)/shard_map/dot_general | solution.py:44
  682.8 10.2 multiply_convert_fusion
  694.7 48.8 %scatter_product.6 = (f32[256,2048]{1,0:T(8,128)}, f32[256,128]{1,0:T(8,128)}) custom-call(bf16[1024,2048]{1,0:T(8,128)(2,1)} %get-tuple-element.73.refs_0_, bf16[2048,2048]{1,0:T(8,128)(2,1)} %bitcast.265, bf16[128,2048]{1,0:T(8,128)(2,1)} %pad.28.refs_2_, bf16[1024,2048]{1,0:T(8,128)(2,1)} %get-tuple-element.72.refs_3_, bf16[2048,2048]{1,0:T(8,128)(2,1)} %bitcast.267, ...), custom_call_target="tpu_custom_call" | custom-call | flops 17179869184 | bytes 26214400 | tf_op jit(solution)/shard_map/scatter_product/pallas_call | solution.py:1112
  752.8 7.1 swap_parts.3
  770.8 3.8 subtract_convert_fusion.2
  774.6 28.4 %gather_rows.8 = bf16[4,256,2048]{2,1,0:T(8,128)(2,1)} custom-call(bf16[256,2048]{1,0:T(8,128)(2,1)} %get-tuple-element.80.own), custom_call_target="tpu_custom_call" | custom-call | tf_op jit(solution)/shard_map/gather_rows/pallas_call | solution.py:972
  803.1 3.5 convolution_convert_fusion.10
  806.6 4.0 fusion.56
  812.1 21.8 %attend_back.1 = (f32[1024,512]{1,0:T(8,128)}, f32[1024,512]{1,0:T(8,128)}, bf16[1024,512]{1,0:T(8,128)(2,1)S(1)}, f32[1024,1]{1,0:T(8,128)S(1)}, f32[1024,1]{1,0:T(8,128)S(1)}) custom-call(bf16[1024,512]{1,0:T(8,128)(2,1)S(1)} %get-tuple-element.51.query, bf16[1024,512]{1,0:T(8,128)(2,1)S(1)} %copy-done.1, bf16[1024,512]{1,0:T(8,128)(2,1)} %get-tuple-element.53.value, ...), custom_call_target="tpu_custom_call" | custom-call | flops 3758096384 | bytes 16777216 | tf_op jit(solution)/shard_map/attend_back/pallas_call | solution.py:611
  837.7 5.7 gather_rows.9
  851.9 37.8 %scatter_product.7 = (f32[256,2048]{1,0:T(8,128)}, f32[256,128]{1,0:T(8,128)}) custom-call(bf16[1024,1536]{1,0:T(8,128)(2,1)} %pad_maximum_fusion.refs_0_, bf16[2048,1536]{1,0:T(8,128)(2,1)} %bitcast.271, bf16[128,1536]{1,0:T(8,128)(2,1)} %pad.30.refs_2_), custom_call_target="tpu_custom_call" | custom-call | flops 6442450944 | bytes 9830400 | tf_op jit(solution)/shard_map/scatter_product/pallas_call | solution.py:1112
  894.0 7.1 swap_parts.2
  903.0 5.8 concatenate.69.table
  911.8 120.9 %finish.1 = (bf16[2,128,2048]{2,1,0:T(8,128)(2,1)}, bf16[2,128,2048]{2,1,0:T(8,128)(2,1)}, bf16[8,96,2048]{2,1,0:T(8,128)(2,1)}) custom-call(bf16[256,2048]{1,0:T(8,128)(2,1)} %get-tuple-element.81.result, bf16[256,2048]{1,0:T(8,128)(2,1)} %fusion.1.grad, bf16[96,2048]{1,0:T(8,128)(2,1)} %concatenate.69.table), custom_call_target="tpu_custom_call" | custom-call | tf_op jit(solution)/shard_map/finish/pallas_call | solution.py:1176
  (346 shorter events, 101.8 us)
Async XLA Ops:
  420.9 13.5 %copy-start.51 = (bf16[16,512]{1,0:T(8,128)(2,1)}, bf16[16,512]{1,0:T(8,128)(2,1)S(1)}, u32[]{:S(2)}) copy-start(bf16[16,512]{1,0:T(8,128)(2,1)S(1)} %get-tuple-element.141) | copy-start | bytes 49156
  421.0 13.5 %copy-start.52 = (bf16[16,512]{1,0:T(8,128)(2,1)}, bf16[16,512]{1,0:T(8,128)(2,1)S(1)}, u32[]{:S(2)}) copy-start(bf16[16,512]{1,0:T(8,128)(2,1)S(1)} %get-tuple-element.142) | copy-start | bytes 49156
  421.4 13.0 %copy-start.53 = (bf16[16,512]{1,0:T(8,128)(2,1)}, bf16[16,512]{1,0:T(8,128)(2,1)S(1)}, u32[]{:S(2)}) copy-start(bf16[16,512]{1,0:T(8,128)(2,1)S(1)} %get-tuple-element.140) | copy-start | bytes 49156
  421.5 46.3 %copy-start.48 = (bf16[16,512]{1,0:T(8,128)(2,1)}, bf16[16,512]{1,0:T(8,128)(2,1)S(1)}, u32[]{:S(2)}) copy-start(bf16[16,512]{1,0:T(8,128)(2,1)S(1)} %get-tuple-element.139) | copy-start | bytes 49156
  421.6 12.8 %copy-start.32 = (bf16[48,2048]{1,0:T(8,128)(2,1)}, bf16[48,2048]{1,0:T(8,128)(2,1)S(1)}, u32[]{:S(2)}) copy-start(bf16[48,2048]{1,0:T(8,128)(2,1)S(1)} %constant_dynamic-update-slice_fusion) | copy-start | bytes 589828
  425.3 9.1 copy-start.36
  438.1 7.9 copy-start.68
  438.1 7.9 copy-start.69
  540.5 14.6 %copy-start.19 = (bf16[1,96,2048]{2,1,0:T(8,128)(2,1)S(1)}, bf16[1,96,2048]{2,1,0:T(8,128)(2,1)}, u32[]{:S(2)}) copy-start(bf16[1,96,2048]{2,1,0:T(8,128)(2,1)} %copy-done.18) | copy-start | bytes 1179652
  540.5 14.6 %copy-start.21 = (bf16[1,96,2048]{2,1,0:T(8,128)(2,1)S(1)}, bf16[1,96,2048]{2,1,0:T(8,128)(2,1)}, u32[]{:S(2)}) copy-start(bf16[1,96,2048]{2,1,0:T(8,128)(2,1)} %copy-done.20) | copy-start | bytes 1179652
  560.6 13.4 %copy-start.35 = (bf16[1,4,4,8192]{3,2,0,1:T(4,128)(2,1)S(1)}, bf16[1,4,4,8192]{3,2,0,1:T(4,128)(2,1)}, u32[]{:S(2)}) copy-start(bf16[1,4,4,8192]{3,2,0,1:T(4,128)(2,1)} %get-tuple-element.87) | copy-start | bytes 786436
  575.9 4.7 copy-start.46
  580.6 11.2 %copy-start.26 = (f32[1024,2048]{1,0:T(8,128)}, f32[1024,2048]{1,0:T(8,128)S(1)}, u32[]{:S(2)}) copy-start(f32[1024,2048]{1,0:T(8,128)S(1)} %convolution_add_fusion.3) | copy-start | bytes 25165828
  580.6 11.2 %copy-start.47 = (bf16[16,2048]{1,0:T(8,128)(2,1)S(1)}, bf16[16,2048]{1,0:T(8,128)(2,1)}, u32[]{:S(2)}) copy-start(bf16[16,2048]{1,0:T(8,128)(2,1)} %get-tuple-element.137) | copy-start | bytes 196612
  592.6 40.0 %copy-start.70 = (bf16[2048]{0:T(1024)(128)(2,1)S(1)}, bf16[2048]{0:T(1024)(128)(2,1)}, u32[]{:S(2)}) copy-start(bf16[2048]{0:T(1024)(128)(2,1)} %param.35) | copy-start | bytes 12292
  592.6 40.0 %copy-start.23 = (bf16[256,2048]{1,0:T(8,128)(2,1)S(1)}, bf16[256,2048]{1,0:T(8,128)(2,1)}, u32[]{:S(2)}) copy-start(bf16[256,2048]{1,0:T(8,128)(2,1)} %get-tuple-element.48) | copy-start | bytes 3145732
  632.6 5.2 copy-start.57
  635.0 30.7 %copy-start.66 = (f32[256]{0:T(256)}, f32[256]{0:T(256)S(1)}, u32[]{:S(2)}) copy-start(f32[256]{0:T(256)S(1)} %get-tuple-element.129) | copy-start | bytes 3076
  665.8 17.1 %slice-start = ((s8[8388608]{0:T(1024)(128)(4,1)}), s8[4194304]{0:T(1024)(128)(4,1)S(1)}, s32[]{:S(2)}) async-start(s8[8388608]{0:T(1024)(128)(4,1)} %bitcast.228), calls=%async_computation | async-start | bytes 8388608
  669.3 13.5 %slice-start.1 = ((s8[8388608]{0:T(1024)(128)(4,1)}), s8[4194304]{0:T(1024)(128)(4,1)S(1)}, s32[]{:S(2)}) async-start(s8[8388608]{0:T(1024)(128)(4,1)} %bitcast.228), calls=%async_computation.1 | async-start | bytes 8388608
  694.7 48.8 %copy-start.22 = (bf16[256,2048]{1,0:T(8,128)(2,1)S(1)}, bf16[256,2048]{1,0:T(8,128)(2,1)}, u32[]{:S(2)}) copy-start(bf16[256,2048]{1,0:T(8,128)(2,1)} %fusion.12.own) | copy-start | bytes 3145732
  751.2 15.8 %copy-start.38 = (f32[256,128]{1,0:T(8,128)S(1)}, f32[256,128]{1,0:T(8,128)}, u32[]{:S(2)}) copy-start(f32[256,128]{1,0:T(8,128)} %get-tuple-element.50) | copy-start | bytes 393220
  851.9 39.6 %copy-start.17 = (bf16[1024,1536]{1,0:T(8,128)(2,1)S(1)}, bf16[1024,1536]{1,0:T(8,128)(2,1)}, u32[]{:S(2)}) copy-start(bf16[1024,1536]{1,0:T(8,128)(2,1)} %pad_maximum_fusion.refs_0_) | copy-start | bytes 9437188
  851.9 39.7 %copy-start.37 = (bf16[1024,48]{0,1:T(8,128)(2,1)S(1)}, bf16[1024,48]{0,1:T(8,128)(2,1)}, u32[]{:S(2)}) copy-start(bf16[1024,48]{0,1:T(8,128)(2,1)} %copy-done.36) | copy-start | bytes 294916
  892.2 10.8 %copy-start.42 = (bf16[16,2048]{1,0:T(8,128)(2,1)S(1)}, bf16[16,2048]{1,0:T(8,128)(2,1)}, u32[]{:S(2)}) copy-start(bf16[16,2048]{1,0:T(8,128)(2,1)} %reshape.438) | copy-start | bytes 196612
  892.2 10.8 %copy-start.43 = (bf16[16,2048]{1,0:T(8,128)(2,1)S(1)}, bf16[16,2048]{1,0:T(8,128)(2,1)}, u32[]{:S(2)}) copy-start(bf16[16,2048]{1,0:T(8,128)(2,1)} %reshape.440) | copy-start | bytes 196612
  892.2 10.8 %copy-start.44 = (bf16[16,2048]{1,0:T(8,128)(2,1)S(1)}, bf16[16,2048]{1,0:T(8,128)(2,1)}, u32[]{:S(2)}) copy-start(bf16[16,2048]{1,0:T(8,128)(2,1)} %reshape.442) | copy-start | bytes 196612
  892.3 16.5 %copy-start.33 = (bf16[48,2048]{1,0:T(8,128)(2,1)S(1)}, bf16[48,2048]{1,0:T(8,128)(2,1)}, u32[]{:S(2)}) copy-start(bf16[48,2048]{1,0:T(8,128)(2,1)} %copy-done.32) | copy-start | bytes 589828
  892.3 16.5 %copy-start.40 = (f32[256,128]{1,0:T(8,128)S(1)}, f32[256,128]{1,0:T(8,128)}, u32[]{:S(2)}) copy-start(f32[256,128]{1,0:T(8,128)} %get-tuple-element.60) | copy-start | bytes 393220
  892.6 16.2 %copy-start.13 = (f32[256,2048]{1,0:T(8,128)S(1)}, f32[256,2048]{1,0:T(8,128)}, u32[]{:S(2)}) copy-start(f32[256,2048]{1,0:T(8,128)} %copy-done.12) | copy-start | bytes 6291460
  908.8 123.9 %copy-start.72 = (bf16[8]{0:T(256)(128)(2,1)S(1)}, bf16[8]{0:T(256)(128)(2,1)}, u32[]{:S(2)}) copy-start(bf16[8]{0:T(256)(128)(2,1)} %copy-done.71) | copy-start | bytes 52
  1032.7 7.1 copy-start.34
  (45 other events, 113.6 us)

commit v3 on v0

--- a/solution.py
+++ b/solution.py
@@ -1,8 +1,11 @@
+import functools
 import math
 
 import jax
 import jax.numpy as jnp
 from jax import lax
+from jax.experimental import pallas as pl
+from jax.experimental.pallas import tpu as pltpu
 from jax.sharding import PartitionSpec as P
 
 HEADS = 16
@@ -458,7 +461,1437 @@
     return (layer_out, input_grad, owned[0], owned[1], owned[2], owned[3], owned[4][0], owned[5][0])
 
 
+def low_dot(left, right):
+    return jnp.dot(left, right, preferred_element_type=jnp.float32)
+
+
+def dot_rows(left, right):
+    return lax.dot_general(
+        left, right, (((0,), (0,)), ((), ())), preferred_element_type=jnp.float32
+    )
+
+
+def rope_full(length):
+    cosine, sine = rope_tables(jnp.arange(length).astype(jnp.float32))
+    return (
+        jnp.concatenate([cosine, cosine], axis=-1),
+        jnp.concatenate([-sine, sine], axis=-1),
+    )
+
+
+def block_scores(query, key, doc_col, doc_row, row, first, rows):
+    scores = lax.dot_general(
+        query, key, (((1,), (1,)), ((), ())), preferred_element_type=jnp.float32
+    ) * (1.0 / math.sqrt(HEAD_DIM))
+    shape = scores.shape
+    row_at = row + lax.broadcasted_iota(jnp.int32, shape, 0)
+    key_at = first + lax.broadcasted_iota(jnp.int32, shape, 1)
+    allowed = (key_at <= row_at) & (doc_col == doc_row)
+    return jnp.where(allowed, scores, MASKED)
+
+
+def soft(scores):
+    top = jnp.max(scores, axis=1, keepdims=True)
+    raised = jnp.exp(scores - top)
+    return raised * (1.0 / jnp.sum(raised, axis=1, keepdims=True))
+
+
+MESH = pl.DeviceIdType.MESH
+VMEM_BYTES = 58 << 20
+
+
+def remote(source, target, send, recv, device):
+    return pltpu.make_async_remote_copy(
+        src_ref=source, dst_ref=target, send_sem=send, recv_sem=recv,
+        device_id=device, device_id_type=MESH,
+    )
+
+
+def greet(sources, count):
+    barrier = pltpu.get_barrier_semaphore()
+    for device in sources:
+        pl.semaphore_signal(barrier, inc=1, device_id=device, device_id_type=MESH)
+    pl.semaphore_wait(barrier, count)
+
+
+def flip(index, bit):
+    return index + bit * (1 - 2 * (index // bit % 2))
+
+
+def wa_peers(place, column):
+    near, across = flip(column, 1), flip(column, 2)
+    return [(place, near), (place, across), (place, flip(across, 1))]
+
+
+def ring_place(place, count):
+    return place // 2 + place % 2 * (count - 1 - 2 * (place // 2))
+
+
+def ring_owner(spot, count):
+    spot = (spot + 2 * count) % count
+    return 2 * spot + spot // (count // 2) * (2 * count - 1 - 4 * spot)
+
+
+def ring_peers(place, column, count):
+    spot = ring_place(place, count)
+    return [(ring_owner(spot + 1, count), column), (ring_owner(spot - 1, count), column)]
+
+
+class Ring:
+    def __init__(self, buffer, send, recv, place, column, own=None):
+        self.buffer, self.send, self.recv, self.own = buffer, send, recv, own
+        self.count = buffer.shape[0]
+        self.half = buffer.shape[1] // 2
+        self.spot = ring_place(place, self.count)
+        self.peers = ring_peers(place, column, self.count)
+        long = self.count // 2
+        self.order = [
+            [(t, h) for t in range(long) for h in (way, 1 - way) if t < long - (h != way)]
+            for way in (0, 1)
+        ]
+
+    def region(self, away, h):
+        owner = ring_owner(self.spot + away, self.count)
+        return self.buffer.at[owner, pl.ds(h * self.half, self.half)]
+
+    def copy(self, way, i, back=0):
+        t, h = self.order[way][i]
+        region = self.region((t + back) * (1 if way else -1), h)
+        source = region
+        if t + back == 0 and self.own is not None:
+            source = self.own.at[pl.ds(h * self.half, self.half)]
+        return remote(
+            source, region, self.send.at[way, i], self.recv.at[way, i], self.peers[way]
+        )
+
+    def step(self, i):
+        for way in (0, 1):
+            t, h = self.order[way][i]
+            if t > 0:
+                self.copy(way, self.order[way].index((t - 1, h)), 1).wait_recv()
+            self.copy(way, i).start()
+
+    @property
+    def steps(self):
+        return self.count - 1
+
+    def finish(self):
+        for way in (0, 1):
+            for i, (t, h) in enumerate(self.order[way]):
+                if (t + 1, h) not in self.order[way]:
+                    self.copy(way, i, 1).wait_recv()
+        for way in (0, 1):
+            for i in range(self.steps):
+                self.copy(way, i).wait_send()
+
+
+def here():
+    return lax.axis_index("seq"), lax.axis_index("wa")
+
+
+def group_of(column, block):
+    return 4 * block + 2 * (column % 2) + column // 2
+
+
+def home_of(place):
+    return place % 2 * 2 + place // 2 % 2, place // 4
+
+
+class WaGather:
+    def __init__(self, buffer, send, recv, place, column, pieces, source=None):
+        self.buffer, self.send, self.recv, self.pieces = buffer, send, recv, pieces
+        self.source = source
+        self.quarter = flip(column, 1)
+        self.near, self.across, _ = wa_peers(place, column)
+        self.rows = buffer.shape[1] // pieces
+
+    def region(self, quarter, i):
+        return self.buffer.at[quarter, pl.ds(i * self.rows, self.rows)]
+
+    def copy(self, kind, i, quarter=None):
+        device = self.across if kind == 1 else self.near
+        region = self.region(self.quarter if quarter is None else quarter, i)
+        source = region
+        if quarter is None and self.source is not None:
+            source = self.source.at[pl.ds(i * self.rows, self.rows)]
+        return remote(source, region, self.send.at[kind, i], self.recv.at[kind, i], device)
+
+    def own(self, i):
+        self.copy(1, i).start()
+        self.copy(0, i).start()
+
+    def forward(self, i):
+        far = flip(self.quarter, 2)
+        self.copy(1, i, far).wait_recv()
+        self.copy(2, i, far).start()
+
+    def finish(self):
+        for i in range(self.pieces):
+            self.copy(0, i, flip(self.quarter, 1)).wait_recv()
+            self.copy(2, i, flip(flip(self.quarter, 2), 1)).wait_recv()
+        for i in range(self.pieces):
+            for kind in (0, 1):
+                self.copy(kind, i).wait_send()
+            self.copy(2, i, flip(self.quarter, 2)).wait_send()
+
+
+def params(number, **more):
+    return pltpu.CompilerParams(collective_id=number, has_side_effects=True, **more)
+
+
+ANY = pl.BlockSpec(memory_space=pl.ANY)
+VMEM = pl.BlockSpec(memory_space=pltpu.VMEM)
+DMA = pltpu.SemaphoreType.DMA
+
+
+class Scatter:
+    def __init__(self, refs, place, column):
+        (
+            self.partial, self.middle, self.first, self.first_mid, self.chip, self.chip_mid,
+            self.last, self.last_mid, self.send, self.recv,
+        ) = refs
+        self.near, self.across, _ = wa_peers(place, column)
+        self.quarter = flip(column, 1)
+        self.far = flip(self.quarter, 2)
+        self.rows = self.partial.shape[1]
+        self.pieces = PIECES
+        self.size = self.rows // self.pieces
+        self.sent = []
+
+    def product(self, which, lefts):
+        width, step = self.partial.shape[2], 512
+        at = pl.ds(pl.multiple_of(which * self.rows, self.rows), self.rows)
+
+        def block(b, carry):
+            cols = pl.ds(pl.multiple_of(b * step, step), step)
+            total = None
+            for left, weight, turned, _ in lefts:
+                if turned:
+                    term = times_t(left[at, :], weight[cols, :])
+                else:
+                    term = low_dot(left[at, :], weight[:, cols])
+                total = term if total is None else total + term
+            self.partial[which, :, cols] = total.astype(jnp.bfloat16)
+            return carry
+
+        lax.fori_loop(0, width // step, block, 0)
+        total = None
+        for left, _, _, adapter in lefts:
+            term = times_t(left[at, :], adapter[...])
+            total = term if total is None else total + term
+        self.middle[which] = total.astype(jnp.bfloat16)
+
+    def to_near(self, slot, which):
+        return (
+            remote(
+                self.partial.at[which], self.first.at[slot], self.send.at[slot],
+                self.recv.at[slot], self.near,
+            ),
+            remote(
+                self.middle.at[which], self.first_mid.at[slot], self.send.at[2 + slot],
+                self.recv.at[2 + slot], self.near,
+            ),
+        )
+
+    def begin(self, copy):
+        copy.start()
+        self.sent.append(copy)
+
+    def across_copy(self, i):
+        at = pl.ds(i * self.size, self.size)
+        return remote(
+            self.chip.at[at], self.last.at[at], self.send.at[4 + i], self.recv.at[4 + i],
+            self.across,
+        )
+
+    def across_mid(self):
+        i = 4 + self.pieces
+        return remote(self.chip_mid, self.last_mid, self.send.at[i], self.recv.at[i], self.across)
+
+    def outward(self, lefts):
+        f32, bf16 = jnp.float32, jnp.bfloat16
+        which = flip(self.far, 1)
+        self.product(which, lefts)
+        for copy in self.to_near(0, which):
+            self.begin(copy)
+        self.product(self.far, lefts)
+        for copy in self.to_near(0, which):
+            copy.wait_recv()
+        self.chip_mid[...] = (
+            self.middle[self.far].astype(f32) + self.first_mid[0].astype(f32)
+        ).astype(bf16)
+        self.begin(self.across_mid())
+        for i in range(self.pieces):
+            at = pl.ds(i * self.size, self.size)
+            self.chip[at] = (
+                self.partial[self.far, at, :].astype(f32) + self.first[0, at, :].astype(f32)
+            ).astype(bf16)
+            self.begin(self.across_copy(i))
+
+    def inward(self, lefts):
+        which = flip(self.quarter, 1)
+        self.product(which, lefts)
+        for copy in self.to_near(1, which):
+            self.begin(copy)
+        self.product(self.quarter, lefts)
+        for copy in self.to_near(1, which):
+            copy.wait_recv()
+        self.across_mid().wait_recv()
+
+    def piece(self, i):
+        f32 = jnp.float32
+        at = pl.ds(i * self.size, self.size)
+        self.across_copy(i).wait_recv()
+        total = (
+            self.partial[self.quarter, at, :].astype(f32)
+            + self.first[1, at, :].astype(f32)
+            + self.last[at, :].astype(f32)
+        )
+        middle = (
+            self.middle[self.quarter, at, :].astype(f32)
+            + self.first_mid[1, at, :].astype(f32)
+            + self.last_mid[at, :].astype(f32)
+        )
+        return at, total, middle.astype(jnp.bfloat16)
+
+    def finish(self):
+        for copy in self.sent:
+            copy.wait_send()
+
+
+PIECES = 4
+LANES = 128
+
+
+def scatter_scratch(rows, width):
+    bf16 = jnp.bfloat16
+    return [
+        pltpu.VMEM((4, rows, width), bf16), pltpu.VMEM((4, rows, LANES), bf16),
+        pltpu.VMEM((2, rows, width), bf16), pltpu.VMEM((2, rows, LANES), bf16),
+        pltpu.VMEM((rows, width), bf16), pltpu.VMEM((rows, LANES), bf16),
+        pltpu.VMEM((rows, width), bf16), pltpu.VMEM((rows, LANES), bf16),
+        DMA((5 + PIECES,)), DMA((5 + PIECES,)),
+    ]
+
+
+SCATTER_REFS = 10
+
+
+class Home:
+    def __init__(self, own, home, send, recv, place, column):
+        self.own, self.home, self.send, self.recv = own, home, send, recv
+        self.column, self.block = home_of(place)
+        self.level, self.quarter = place // 2, flip(column, 1)
+        self.my_column = column
+        self.length = home.shape[1]
+
+    def targets(self):
+        return [(2 * self.quarter + i, self.column) for i in (0, 1)]
+
+    def sources(self):
+        return [(group_of(self.my_column, b), flip(self.level, 1)) for b in (0, 1)]
+
+    def copy(self, i, pieces=1, k=0):
+        size = self.length // pieces
+        return remote(
+            self.own.at[pl.ds(i * self.length + k * size, size)],
+            self.home.at[self.block, pl.ds(k * size, size)],
+            self.send.at[i, k], self.recv.at[self.block, k], self.targets()[i],
+        )
+
+    def finish(self, pieces=1):
+        size = self.length // pieces
+        for b in (0, 1):
+            for k in range(pieces):
+                region = self.home.at[b, pl.ds(k * size, size)]
+                remote(
+                    region, region, self.send.at[b, k], self.recv.at[b, k], self.sources()[b]
+                ).wait_recv()
+        for i in (0, 1):
+            for k in range(pieces):
+                self.copy(i, pieces, k).wait_send()
+
+
+def rms_factor(values):
+    return lax.rsqrt(jnp.mean(values * values, axis=-1, keepdims=True) + EPSILON)
+
+
+class RowSums:
+    def __init__(self, refs, place, column):
+        self.columns, self.mine, self.theirs, self.send, self.recv = refs
+        self.peers = wa_peers(place, column)
+
+    def copy(self, k):
+        return remote(
+            self.mine, self.theirs.at[k], self.send.at[k], self.recv.at[k], self.peers[k]
+        )
+
+    def start(self):
+        self.mine[...] = self.columns[...].T[:8]
+        for k in range(3):
+            self.copy(k).start()
+
+    def result(self):
+        for k in range(3):
+            self.copy(k).wait_recv()
+        total = self.mine[...] + self.theirs[0] + self.theirs[1] + self.theirs[2]
+        filler = jnp.zeros((LANES - 8, total.shape[1]), jnp.float32)
+        return jnp.concatenate([total, filler], axis=0).T
+
+    def finish(self):
+        for k in range(3):
+            self.copy(k).wait_send()
+
+
+def row_sums_scratch(length):
+    return [
+        pltpu.VMEM((length, LANES), jnp.float32), pltpu.VMEM((8, length), jnp.float32),
+        pltpu.VMEM((3, 8, length), jnp.float32), DMA((3,)), DMA((3,)),
+    ]
+
+
+ROW_SUMS_REFS = 5
+
+
+def two_lanes(first, second):
+    lane = lax.broadcasted_iota(jnp.int32, (first.shape[0], LANES), 1)
+    return jnp.where(lane == 0, first, jnp.where(lane == 1, second, 0.0))
+
+
+def fetch_kernel(
+    tokens, qkv_parts, gate, up, table,
+    all_tokens, w_qkv, w_gate, w_up, tables, marks,
+    home_send, home_recv, part_send, part_recv, wa_send, wa_recv, mark_send, mark_recv,
+    ring_send, ring_recv, local,
+):
+    place, column = here()
+    count = w_qkv.shape[0]
+    local_len = tokens.shape[1]
+    level, parity = place // 2, place % 2
+    member = flip(level, 1)
+    home_column, _ = home_of(place)
+    quarter = flip(column, 1)
+    near_far = wa_peers(place, column)
+    ring_near = ring_peers(place, column, count)
+    home_from = [(2 * quarter, home_column), (2 * quarter + 1, home_column)]
+    home_to = [(group_of(column, b), member) for b in (0, 1)]
+    greet(home_from + near_far + ring_near, 7)
+
+    rows = qkv_parts.shape[1]
+    ours = pl.ds(pl.multiple_of(column * rows, rows), rows)
+    block = w_gate.shape[2] // count
+
+    def slices(source, buffer, who):
+        for b in range(count):
+            at = pl.multiple_of((4 * b + who) * block, block)
+            yield source.at[:, pl.ds(at, block)], buffer.at[place, ours, pl.ds(b * block, block)]
+
+    own_qkv = pltpu.make_async_copy(qkv_parts.at[column], w_qkv.at[place, ours], local.at[1])
+    own_qkv.start()
+    moves = [
+        remote(
+            qkv_parts.at[peer[1]], w_qkv.at[place, ours], part_send.at[0, k], part_recv.at[0, k],
+            peer,
+        )
+        for k, peer in enumerate(near_far)
+    ]
+    moves += [
+        remote(
+            tokens.at[b], all_tokens.at[level, pl.ds(parity * local_len, local_len)],
+            home_send.at[b], home_recv.at[parity], home_to[b],
+        )
+        for b in (0, 1)
+    ]
+    for move in moves:
+        move.start()
+    table_ring = Ring(tables, ring_send.at[1], ring_recv.at[1], place, column, table)
+    table_ring.step(0)
+    table_ring.step(1)
+    own_table = pltpu.make_async_copy(table, tables.at[place], local.at[0])
+    own_table.start()
+
+    def parts_here(t, buffer):
+        for k, peer in enumerate(near_far):
+            theirs = pl.ds(pl.multiple_of(peer[1] * rows, rows), rows)
+            region = buffer.at[place, theirs]
+            remote(region, region, part_send.at[t, k], part_recv.at[t, k], peer).wait_recv()
+
+    gather = WaGather(all_tokens, wa_send, wa_recv, place, column, 2)
+    qkv_ring = Ring(w_qkv, ring_send.at[0], ring_recv.at[0], place, column)
+    own_qkv.wait()
+    parts_here(0, w_qkv)
+    qkv_ring.step(0)
+    qkv_ring.step(1)
+    for i in (2, 3):
+        table_ring.step(i)
+    for i in (0, 1):
+        region = gather.region(quarter, i)
+        remote(region, region, home_send.at[i], home_recv.at[i], home_from[i]).wait_recv()
+        gather.own(i)
+    for t, (source, buffer) in enumerate(((gate, w_gate), (up, w_up))):
+        for piece, target in slices(source, buffer, column):
+            pltpu.make_async_copy(piece, target, local.at[2 + t]).start()
+        for k, peer in enumerate(near_far):
+            for piece, target in slices(source, buffer, peer[1]):
+                remote(piece, target, part_send.at[1 + t, k], part_recv.at[1 + t, k], peer).start()
+    for i in (4, 5, 6):
+        table_ring.step(i)
+    qkv_ring.step(2)
+    own_table.wait()
+    table_ring.finish()
+    own_marks = pltpu.make_async_copy(
+        tables.at[:, pl.ds(MARKS, 8)], marks.at[quarter], local.at[4]
+    )
+    own_marks.start()
+    mark_moves = [
+        remote(
+            tables.at[:, pl.ds(MARKS, 8)], marks.at[quarter], mark_send.at[k], mark_recv.at[k],
+            peer,
+        )
+        for k, peer in enumerate(near_far)
+    ]
+    for move in mark_moves:
+        move.start()
+    gather.forward(0)
+    qkv_ring.step(3)
+    gather.forward(1)
+    for i in (4, 5, 6):
+        qkv_ring.step(i)
+    for t, buffer in enumerate((w_gate, w_up)):
+        region = buffer.at[place, ours]
+        pltpu.make_async_copy(region, region, local.at[2 + t]).wait()
+        parts_here(1 + t, buffer)
+    for k, peer in enumerate(near_far):
+        region = marks.at[flip(peer[1], 1)]
+        remote(region, region, mark_send.at[k], mark_recv.at[k], peer).wait_recv()
+    qkv_ring.finish()
+    gather.finish()
+    own_marks.wait()
+    for move in moves + mark_moves:
+        move.wait_send()
+    for t, buffer in enumerate((w_gate, w_up)):
+        for k, peer in enumerate(near_far):
+            region = buffer.at[place, ours]
+            remote(
+                region, region, part_send.at[1 + t, k], part_recv.at[1 + t, k], peer
+            ).wait_send()
+
+
+def fetch(tokens, qkv_parts, gate, up, table, count):
+    bf16 = jnp.bfloat16
+    width = tokens.shape[2]
+    slab = 4 * qkv_parts.shape[1]
+    units = gate.shape[1] // 4
+    shape = lambda *dims: jax.ShapeDtypeStruct(dims, bf16)
+    return pl.pallas_call(
+        fetch_kernel,
+        in_specs=[VMEM] * 5,
+        out_specs=[ANY] * 6,
+        out_shape=[
+            shape(4, 2 * tokens.shape[1], width), shape(count, slab, qkv_parts.shape[2]),
+            shape(count, slab, units), shape(count, slab, units), shape(count, *table.shape),
+            shape(4, count, 8, width),
+        ],
+        scratch_shapes=[
+            DMA((2,)), DMA((2,)), DMA((3, 3)), DMA((3, 3)), DMA((3, 2)), DMA((3, 2)),
+            DMA((3,)), DMA((3,)), DMA((2, 2, count - 1)), DMA((2, 2, count - 1)), DMA((5,)),
+        ],
+        name="fetch",
+        compiler_params=params(1),
+    )(tokens, qkv_parts, gate, up, table)
+
+
+KINDS = 8
+MARKS = 24
+BY_HEAD = 32
+BY_UNIT = 48
+
+
+def kind_rows(shape):
+    return lax.broadcasted_iota(jnp.int32, shape, 0) // 4 % KINDS
+
+
+class Adapters:
+    def __init__(self, table, full, heads, units, send, recv, local, place, column):
+        self.table, self.local = table, local
+        self.peers = wa_peers(place, column)
+        self.send, self.recv = send, recv
+        self.quarter = flip(column, 1)
+        self.column = column
+        self.full, self.heads, self.units = full, heads, units
+
+    def pieces(self, member, quarter):
+        part = self.heads.shape[2]
+        cols = pl.ds(pl.multiple_of(member * part, part), part)
+        rows = pl.ds(pl.multiple_of(BY_UNIT + 16 * member, 16), 16)
+        return [
+            (self.table.at[pl.ds(0, 32)], self.full.at[pl.ds(pl.multiple_of(32 * quarter, 32), 32)]),
+            (self.table.at[pl.ds(BY_HEAD, 16), cols], self.heads.at[quarter]),
+            (self.table.at[rows], self.units.at[quarter]),
+        ]
+
+    def copies(self, k):
+        return [
+            remote(source, target, self.send.at[k, i], self.recv.at[k, i], self.peers[k])
+            for i, (source, target) in enumerate(self.pieces(self.peers[k][1], self.quarter))
+        ]
+
+    def own(self, i):
+        source, target = self.pieces(self.column, self.quarter)[i]
+        return pltpu.make_async_copy(source, target, self.local.at[i])
+
+    def start(self):
+        for i in range(3):
+            self.own(i).start()
+        for k in range(3):
+            for copy in self.copies(k):
+                copy.start()
+
+    def wait(self, i):
+        self.own(i).wait()
+        for k in range(3):
+            _, target = self.pieces(self.column, flip(self.peers[k][1], 1))[i]
+            remote(target, target, self.send.at[k, i], self.recv.at[k, i], self.peers[k]).wait_recv()
+
+    def finish(self):
+        for k in range(3):
+            for copy in self.copies(k):
+                copy.wait_send()
+
+
+def attend_kernel(
+    tokens, w_qkv, table, gain_q, gain_k, cosine, sine, doc_col, doc_row, out_part, cotangent,
+    attended, query, key, value, qkv_raw, middle, scales, full, b_qkv, b_out, b_gate, b_up, b_down,
+    w_out, out_slabs, my_cotangent, *refs, back,
+):
+    place, column = here()
+    sums = RowSums(refs[:ROW_SUMS_REFS], place, column)
+    (
+        ring_send, ring_recv, home_send, home_recv, local, out_send, out_recv, heads, units,
+        table_send, table_recv, table_local,
+    ) = refs[ROW_SUMS_REFS:]
+    count = out_slabs.shape[0]
+    peers = wa_peers(place, column)
+    local_len = cotangent.shape[1]
+    level, parity = place // 2, place % 2
+    home_column, _ = home_of(place)
+    quarter = flip(column, 1)
+    home_from = [(2 * quarter + i, home_column) for i in (0, 1)]
+    home_to = [(group_of(column, b), flip(level, 1)) for b in (0, 1)]
+    greet(peers + ring_peers(place, column, count) + home_from, 7)
+    adapters = Adapters(
+        table, full, heads, units, table_send, table_recv, table_local, place, column
+    )
+    adapters.start()
+    ring = Ring(out_slabs, ring_send, ring_recv, place, column, out_part)
+    ring.step(0)
+    ring.step(1)
+    keep = pltpu.make_async_copy(out_part, out_slabs.at[place], local.at[0])
+    keep.start()
+    moves = [
+        remote(
+            cotangent.at[b], my_cotangent.at[pl.ds(parity * local_len, local_len)],
+            home_send.at[b], home_recv.at[parity], home_to[b],
+        )
+        for b in (0, 1)
+    ]
+    for move in moves:
+        move.start()
+    length, width = tokens.shape
+    part = value.shape[1]
+    rows = 256
+    bf16 = jnp.bfloat16
+    adapters.wait(0)
+    adapters.wait(1)
+    kind = kind_rows((128, part))
+    spread_heads = jnp.concatenate(
+        [piece for q in range(4) for piece in (heads[q], jnp.zeros((16, part), bf16))], axis=0
+    )
+    zero = jnp.zeros((128, part), bf16)
+    for c in range(3):
+        b_qkv[:, c * part : (c + 1) * part] = jnp.where(kind == c, spread_heads, zero)
+    b_out[...] = jnp.where(kind == 3, spread_heads, zero)
+    middle[...] = times_t(tokens[...], full[...]).astype(bf16)
+
+    def block(r, carry):
+        at = pl.ds(pl.multiple_of(r * rows, rows), rows)
+        squares = []
+        for c in range(3):
+            cols = slice(c * part, (c + 1) * part)
+            raw = low_dot(tokens[at, :], w_qkv[:, cols])
+            raw = raw + low_dot(middle[at, :], b_qkv[:, cols])
+            if c == 2:
+                value[at, :] = raw.astype(bf16)
+            else:
+                qkv_raw[at, cols] = raw
+                squares.append(jnp.sum(raw * raw, axis=1, keepdims=True))
+        sums.columns[at, :] = two_lanes(*squares)
+        return carry
+
+    lax.fori_loop(0, length // rows, block, 0)
+    sums.start()
+    ring.step(2)
+    adapters.wait(2)
+    kind = kind_rows((128, width))
+    spread_units = jnp.concatenate(
+        [piece for q in range(4) for piece in (jnp.zeros((16, width), bf16), units[q])], axis=0
+    )
+    zero = jnp.zeros((128, width), bf16)
+    for c, target in ((4, b_gate), (5, b_up), (6, b_down)):
+        target[...] = jnp.where(kind == c, spread_units, zero)
+    scales[...] = lax.rsqrt(sums.result() * (1.0 / width) + EPSILON)
+    ring.step(3)
+
+    def head(h, carry):
+        cols = pl.ds(pl.multiple_of(h * HEAD_DIM, HEAD_DIM), HEAD_DIM)
+        k_cols = pl.ds(pl.multiple_of(part + h * HEAD_DIM, HEAD_DIM), HEAD_DIM)
+        for lane, at, gain, target in ((0, cols, gain_q, query), (1, k_cols, gain_k, key)):
+            normed = qkv_raw[:, at] * scales[:, lane : lane + 1] * gain[:, cols]
+            turned = normed * cosine[...] + pltpu.roll(normed, HEAD_DIM // 2, 1) * sine[...]
+            target[:, cols] = turned.astype(bf16)
+        for row in range(0, length, rows):
+            first, last = max(0, row - back), row + rows
+            scores = block_scores(
+                query[row:last, cols], key[first:last, cols], doc_col[row:last, :],
+                doc_row[:, first:last], row, first, rows,
+            )
+            probs = soft(scores).astype(bf16)
+            attended[row:last, cols] = low_dot(probs, value[first:last, cols]).astype(bf16)
+        for i in (4, 5, 6):
+            pl.when(h == i - 4)(functools.partial(ring.step, i))
+        return carry
+
+    lax.fori_loop(0, part // HEAD_DIM, head, 0)
+    keep.wait()
+    ring.finish()
+    core, some = column % 2, count // 2
+    mine = pltpu.make_async_copy(
+        out_slabs.at[pl.ds(core * some, some)], w_out.at[:, core], local.at[1]
+    )
+    mine.start()
+    give = remote(
+        out_slabs.at[pl.ds((1 - core) * some, some)], w_out.at[:, core], out_send, out_recv,
+        peers[0],
+    )
+    give.start()
+    take = w_out.at[:, 1 - core]
+    remote(take, take, out_send, out_recv, peers[0]).wait_recv()
+    give.wait_send()
+    mine.wait()
+    for i in (0, 1):
+        region = my_cotangent.at[pl.ds(i * local_len, local_len)]
+        remote(region, region, home_send.at[i], home_recv.at[i], home_from[i]).wait_recv()
+    for move in moves:
+        move.wait_send()
+    adapters.finish()
+    sums.finish()
+
+
+def attend(tokens, w_qkv, table, gain_q, gain_k, tables, doc_col, doc_row, out_part, cotangent, back, count):
+    f32, bf16 = jnp.float32, jnp.bfloat16
+    (length, width), part = tokens.shape, w_qkv.shape[1] // 3
+    shape = jax.ShapeDtypeStruct
+    low = shape((length, part), bf16)
+    maps = shape((LANES, width), bf16)
+    return pl.pallas_call(
+        functools.partial(attend_kernel, back=back),
+        in_specs=[VMEM] * 9 + [ANY] * 2,
+        out_specs=[VMEM] * 14 + [ANY] * 2,
+        out_shape=[
+            low, low, low, low, shape((length, 2 * part), f32), shape((length, LANES), bf16),
+            shape((length, LANES), f32), maps, shape((LANES, 3 * part), bf16),
+            shape((LANES, part), bf16), maps, maps, maps,
+            shape((count // 2, 2, *out_part.shape), bf16), shape((count, *out_part.shape), bf16),
+            shape((2 * cotangent.shape[1], width), bf16),
+        ],
+        scratch_shapes=row_sums_scratch(length)
+        + [
+            DMA((2, count - 1)), DMA((2, count - 1)), DMA((2,)), DMA((2,)), DMA((2,)), DMA(()),
+            DMA(()), pltpu.VMEM((4, 16, part), bf16), pltpu.VMEM((4, 16, width), bf16),
+            DMA((3, 3)), DMA((3, 3)), DMA((3,)),
+        ],
+        name="attend",
+        compiler_params=params(2, vmem_limit_bytes=VMEM_BYTES),
+    )(tokens, w_qkv, table, gain_q, gain_k, *tables, doc_col, doc_row, out_part, cotangent)
+
+
+class Grads:
+    def __init__(self, refs, first_kind, place, column):
+        self.full, self.cut, self.full_in, self.cut_in, self.send, self.recv = refs
+        self.kind = first_kind
+        self.peers = wa_peers(place, column)
+        self.quarter = flip(column, 1)
+        self.column = column
+
+    def put(self, target, step, total):
+        low = total.astype(jnp.bfloat16)
+        for q in range(4):
+            at = 32 * q + 4 * self.kind
+            target[q, :, step] = low[at : at + 16]
+
+    def copies(self, k):
+        there = flip(self.peers[k][1], 1)
+        return [
+            remote(self.full.at[there], self.full_in.at[k], self.send.at[k, 0], self.recv.at[k, 0], self.peers[k]),
+            remote(self.cut.at[there], self.cut_in.at[k], self.send.at[k, 1], self.recv.at[k, 1], self.peers[k]),
+        ]
+
+    def start(self):
+        for k in range(3):
+            for copy in self.copies(k):
+                copy.start()
+
+    def summed(self):
+        for k in range(3):
+            for copy in self.copies(k):
+                copy.wait_recv()
+        f32 = jnp.float32
+        total = self.full[self.quarter].astype(f32)
+        for k in range(3):
+            total = total + self.full_in[k].astype(f32)
+        return total.astype(jnp.bfloat16)
+
+    def slices(self):
+        yield self.column, self.cut[self.quarter]
+        for k in range(3):
+            yield self.peers[k][1], self.cut_in[k]
+
+    def finish(self):
+        for k in range(3):
+            for copy in self.copies(k):
+                copy.wait_send()
+
+
+def grads_scratch(width, part):
+    bf16 = jnp.bfloat16
+    return [
+        pltpu.VMEM((4, 16, width), bf16), pltpu.VMEM((4, 16, part), bf16),
+        pltpu.VMEM((3, 16, width), bf16), pltpu.VMEM((3, 16, part), bf16), DMA((3, 2)), DMA((3, 2)),
+    ]
+
+
+GRADS_REFS = 6
+
+
+def by_kind(shape, choices):
+    kind, total = kind_rows(shape), jnp.zeros(shape, jnp.float32)
+    for which, value in choices:
+        total = jnp.where(kind == which, value, total)
+    return total
+
+
+def lanes(b, step):
+    return pl.ds(pl.multiple_of(b * step, step), step)
+
+
+def branch_kernel(
+    attended, w_out, ao, gain, bo, every_token, _gate, branch, hidden, mid_out, hidden_low, every,
+    w_gate, *refs,
+):
+    place, column = here()
+    scatter = Scatter(refs[:SCATTER_REFS], place, column)
+    wa_send, wa_recv, ring_send, ring_recv, local, tokens, token_sem = refs[SCATTER_REFS:]
+    load = pltpu.make_async_copy(every_token.at[scatter.quarter], tokens, token_sem)
+    load.start()
+    greet(wa_peers(place, column)[:2] + ring_peers(place, column, w_gate.shape[0]), 4)
+    ring = Ring(w_gate, ring_send, ring_recv, place, column)
+    gather = WaGather(every, wa_send, wa_recv, place, column, PIECES, hidden_low)
+    lefts = [(attended, w_out, False, ao)]
+    ring.step(0)
+    ring.step(1)
+    scatter.outward(lefts)
+    scatter.inward(lefts)
+    load.wait()
+    for i in range(PIECES):
+        if i % 2 == 0:
+            ring.step(2 + i // 2)
+        at, total, middle = scatter.piece(i)
+        total = total + low_dot(middle, bo[...])
+        rows = tokens[at, :].astype(jnp.float32) + total * rms_factor(total) * gain[...]
+        branch[at, :] = total
+        hidden[at, :] = rows
+        mid_out[at, :] = middle
+        hidden_low[at, :] = rows.astype(jnp.bfloat16)
+        gather.own(i)
+    keep = pltpu.make_async_copy(hidden_low, every.at[gather.quarter], local)
+    keep.start()
+    for i in range(PIECES):
+        if i % 2 == 0:
+            ring.step(4 + i // 2)
+        gather.forward(i)
+    ring.step(6)
+    gather.finish()
+    scatter.finish()
+    ring.finish()
+    keep.wait()
+
+
+def out_branch(attended, w_out, ao, gain, bo, tokens, w_gate):
+    f32, bf16 = jnp.float32, jnp.bfloat16
+    _, rows, width = tokens.shape
+    count = w_gate.shape[0]
+    shape = jax.ShapeDtypeStruct
+    return pl.pallas_call(
+        branch_kernel,
+        in_specs=[VMEM] * 5 + [ANY] * 2,
+        out_specs=[VMEM] * 4 + [ANY] * 2,
+        out_shape=[
+            shape((rows, width), f32), shape((rows, width), f32), shape((rows, LANES), bf16),
+            shape((rows, width), bf16), shape((4, rows, width), bf16), shape(w_gate.shape, bf16),
+        ],
+        scratch_shapes=scatter_scratch(rows, width)
+        + [
+            DMA((3, PIECES)), DMA((3, PIECES)), DMA((2, count - 1)), DMA((2, count - 1)), DMA(()),
+            pltpu.VMEM((rows, width), bf16), DMA(()),
+        ],
+        input_output_aliases={6: 5},
+        name="out_branch",
+        compiler_params=params(3, vmem_limit_bytes=VMEM_BYTES),
+    )(attended, w_out, ao, gain, bo, tokens, w_gate)
+
+
+def ffn_kernel(
+    rows_in, full, bg, bu, ad, hidden, cotangent, gain, w_gate, _up, down,
+    gate_low, up_low, mixed, middle, layer_out, d_ffn, mid_down, every, w_up, w_down, *refs,
+):
+    place, column = here()
+    scatter = Scatter(refs[:SCATTER_REFS], place, column)
+    wa_send, wa_recv, ring_send, ring_recv, local, first_w, second_w = refs[SCATTER_REFS:]
+    count = w_up.shape[0]
+    greet(wa_peers(place, column)[:2] + ring_peers(place, column, count), 4)
+    up_ring = Ring(w_up, ring_send.at[0], ring_recv.at[0], place, column)
+    down_ring = Ring(w_down, ring_send.at[1], ring_recv.at[1], place, column, down)
+    gather = WaGather(every, wa_send, wa_recv, place, column, PIECES, d_ffn)
+    keep_down = pltpu.make_async_copy(down, w_down.at[place], local.at[0])
+    keep_down.start()
+
+    def load(weights, target, sem):
+        slab = weights.shape[1]
+        for s in range(count):
+            pltpu.make_async_copy(weights.at[s], target.at[pl.ds(s * slab, slab)], sem).start()
+
+    def loaded(target, sem):
+        pltpu.make_async_copy(target, target, sem).wait()
+
+    load(w_gate, first_w, local.at[1])
+    middle[...] = times_t(rows_in[...], full[...]).astype(jnp.bfloat16)
+    for i in range(7):
+        up_ring.step(i)
+    down_ring.step(0)
+    down_ring.step(1)
+    up_ring.finish()
+    load(w_up, second_w, local.at[2])
+    loaded(first_w, local.at[1])
+    loaded(second_w, local.at[2])
+    rows, width = hidden.shape
+    units, step = mixed.shape[1], 512
+
+    def one(weights, adapter, at, cols):
+        return low_dot(rows_in[at, :], weights[:, cols]) + low_dot(middle[at, :], adapter[:, cols])
+
+    def quarter_rows(q):
+        at = pl.ds(q * rows, rows)
+
+        def block(b, carry):
+            cols = pl.ds(pl.multiple_of(b * step, step), step)
+            gate = one(first_w, bg, at, cols)
+            up = one(second_w, bu, at, cols)
+            gate_low[at, cols] = gate.astype(jnp.bfloat16)
+            up_low[at, cols] = up.astype(jnp.bfloat16)
+            mixed[at, cols] = (gate * jax.nn.sigmoid(gate) * up).astype(jnp.bfloat16)
+            return carry
+
+        lax.fori_loop(0, units // step, block, 0)
+
+    for q in range(4):
+        quarter_rows(q)
+        down_ring.step(2 + q)
+    down_ring.step(6)
+    keep_down.wait()
+    down_ring.finish()
+    load(w_down, first_w, local.at[1])
+    loaded(first_w, local.at[1])
+    lefts = [(mixed, first_w, False, ad)]
+    scatter.outward(lefts)
+    scatter.inward(lefts)
+    for i in range(PIECES):
+        at, total, mid = scatter.piece(i)
+        total = total + low_dot(mid, full[...])
+        scale = rms_factor(total)
+        layer_out[at, :] = (hidden[at, :] + total * scale * gain[...]).astype(jnp.bfloat16)
+        mid_down[at, :] = mid
+        weighted = cotangent[at, :].astype(jnp.float32) * gain[...]
+        mean = jnp.mean(total * weighted, axis=-1, keepdims=True)
+        grad = scale * weighted - total * (scale * scale * scale * mean)
+        d_ffn[at, :] = grad.astype(jnp.bfloat16)
+        gather.own(i)
+    keep = pltpu.make_async_copy(d_ffn, every.at[gather.quarter], local.at[0])
+    keep.start()
+    for i in range(PIECES):
+        gather.forward(i)
+    gather.finish()
+    scatter.finish()
+    keep.wait()
+
+
+def feed_forward(rows_in, full, bg, bu, ad, hidden, cotangent, gain, w_gate, w_up, down):
+    f32, bf16 = jnp.float32, jnp.bfloat16
+    rows, width = hidden.shape
+    length = rows_in.shape[0]
+    count, slab, units = w_up.shape
+    shape = jax.ShapeDtypeStruct
+    wide = shape((length, units), bf16)
+    return pl.pallas_call(
+        ffn_kernel,
+        in_specs=[VMEM] * 8 + [ANY] * 3,
+        out_specs=[VMEM] * 7 + [ANY] * 3,
+        out_shape=[
+            wide, wide, wide, shape((length, LANES), bf16), shape((rows, width), bf16),
+            shape((rows, width), bf16), shape((rows, LANES), bf16),
+            shape((4, rows, width), bf16), shape(w_up.shape, bf16),
+            shape((count, *down.shape), bf16),
+        ],
+        scratch_shapes=scatter_scratch(rows, width)
+        + [
+            DMA((3, PIECES)), DMA((3, PIECES)), DMA((2, 2, count - 1)), DMA((2, 2, count - 1)),
+            DMA((3,)), pltpu.VMEM((width, units), bf16), pltpu.VMEM((width, units), bf16),
+        ],
+        input_output_aliases={9: 8},
+        name="feed_forward",
+        compiler_params=params(4, vmem_limit_bytes=VMEM_BYTES),
+    )(rows_in, full, bg, bu, ad, hidden, cotangent, gain, w_gate, w_up, down)
+
+
+def ffn_back_kernel(
+    d_gate, d_up, w_gate, w_up, bg, bu, cotangent, branch, gain, full, mid_gu, d_mid_down, mixed,
+    seq_hidden, mid_down, d_ffn, layer_out,
+    d_hidden, d_branch, grad_table, every, out_home, *refs,
+):
+    place, column = here()
+    scatter = Scatter(refs[:SCATTER_REFS], place, column)
+    grads = Grads(refs[SCATTER_REFS : SCATTER_REFS + GRADS_REFS], 4, place, column)
+    wa_send, wa_recv, home_send, home_recv, local = refs[SCATTER_REFS + GRADS_REFS :]
+    home = Home(layer_out, out_home, home_send, home_recv, place, column)
+    greet(wa_peers(place, column) + home.sources(), 5)
+    for i in (0, 1):
+        home.copy(i).start()
+    gather = WaGather(every, wa_send, wa_recv, place, column, PIECES, d_branch)
+    lefts = [(d_gate, w_gate, True, bg), (d_up, w_up, True, bu)]
+    scatter.outward(lefts)
+    scatter.inward(lefts)
+    width, step = d_hidden.shape[1], 512
+    rows = d_hidden.shape[0]
+
+    def grad_block(b, carry):
+        cols = lanes(b, step)
+        hidden_sum = None
+        for q in range(4):
+            term = dot_rows(scatter.middle[q], seq_hidden[q * rows : (q + 1) * rows, cols])
+            hidden_sum = term if hidden_sum is None else hidden_sum + term
+        shape = hidden_sum.shape
+        down_sum = dot_rows(mid_down[...], d_ffn[:, cols])
+        choices = [(4, hidden_sum), (5, hidden_sum), (6, down_sum)]
+        grads.put(grads.full, cols, by_kind(shape, choices))
+        choices = [
+            (4, dot_rows(mid_gu[...], d_gate[:, cols])), (5, dot_rows(mid_gu[...], d_up[:, cols])),
+            (6, dot_rows(d_mid_down[...], mixed[:, cols])),
+        ]
+        grads.put(grads.cut, cols, by_kind(shape, choices))
+        return carry
+
+    lax.fori_loop(0, width // step, grad_block, 0)
+    grads.start()
+    for i in range(PIECES):
+        at, total, mid = scatter.piece(i)
+        grad = cotangent[at, :].astype(jnp.float32) + total + low_dot(mid, full[...])
+        d_hidden[at, :] = grad
+        values = branch[at, :]
+        scale = rms_factor(values)
+        weighted = grad * gain[...]
+        mean = jnp.mean(values * weighted, axis=-1, keepdims=True)
+        back = scale * weighted - values * (scale * scale * scale * mean)
+        d_branch[at, :] = back.astype(jnp.bfloat16)
+        gather.own(i)
+    keep = pltpu.make_async_copy(d_branch, every.at[gather.quarter], local)
+    keep.start()
+    for i in range(PIECES):
+        gather.forward(i)
+    grad_table[0:16, :] = grads.summed()
+    for member, rows_here in grads.slices():
+        grad_table[pl.ds(pl.multiple_of(16 + 16 * member, 16), 16), :] = rows_here
+    gather.finish()
+    scatter.finish()
+    home.finish()
+    grads.finish()
+    keep.wait()
+
+
+def ffn_back(arrays, layer_out):
+    f32, bf16 = jnp.float32, jnp.bfloat16
+    rows, width = arrays[7].shape
+    units = arrays[0].shape[1]
+    shape = jax.ShapeDtypeStruct
+    return pl.pallas_call(
+        ffn_back_kernel,
+        in_specs=[VMEM] * len(arrays) + [ANY],
+        out_specs=[VMEM] * 3 + [ANY] * 2,
+        out_shape=[
+            shape((rows, width), f32), shape((rows, width), bf16), shape((80, width), bf16),
+            shape((4, rows, width), bf16), shape((2, rows // 2, width), bf16),
+        ],
+        scratch_shapes=scatter_scratch(rows, width)
+        + grads_scratch(width, units)
+        + [DMA((3, PIECES)), DMA((3, PIECES)), DMA((2, 1)), DMA((2, 1)), DMA(())],
+        name="ffn_back",
+        compiler_params=params(5, vmem_limit_bytes=VMEM_BYTES),
+    )(*arrays, layer_out)
+
+
+def attend_back_kernel(
+    d_rows, w_out, full, ao, query, key, value, qkv_raw, scales, gain_q, gain_k, cosine, sine,
+    doc_col, doc_row, w_qkv, b_qkv, d_hidden, tokens, attended, mid_qkv, mid_out, d_branch, table,
+    grad_home, tables, own_tables, *refs, back,
+):
+    place, column = here()
+    count = tables.shape[0]
+    scatter = Scatter(refs[:SCATTER_REFS], place, column)
+    sums = RowSums(refs[SCATTER_REFS : SCATTER_REFS + ROW_SUMS_REFS], place, column)
+    (
+        ring_send, ring_recv, home_send, home_recv, local, grad, t_rows, dk_sum, dv_sum, my_grad,
+        d_qkv, d_mid_out, own_table,
+    ) = refs[SCATTER_REFS + ROW_SUMS_REFS + GRADS_REFS :]
+    at = SCATTER_REFS + ROW_SUMS_REFS
+    grads = Grads(refs[at : at + GRADS_REFS], 0, place, column)
+    home = Home(my_grad, grad_home, home_send, home_recv, place, column)
+    greet(wa_peers(place, column) + ring_peers(place, column, count) + home.sources(), 7)
+    ring = Ring(tables, ring_send.at[0], ring_recv.at[0], place, column, table)
+    own_ring = Ring(own_tables, ring_send.at[1], ring_recv.at[1], place, column, own_table)
+    ring.step(0)
+    ring.step(1)
+    keep = pltpu.make_async_copy(table, tables.at[place], local.at[0])
+    keep.start()
+    f32, bf16 = jnp.float32, jnp.bfloat16
+    length, part = query.shape
+    width = d_rows.shape[1]
+    rows = 256
+    scale = 1.0 / math.sqrt(HEAD_DIM)
+    d_mid_out[...] = times_t(d_rows[...], full[...]).astype(bf16)
+
+    def attended_rows(r, carry):
+        at = pl.ds(pl.multiple_of(r * rows, rows), rows)
+        total = times_t(d_rows[at, :], w_out[...]) + low_dot(d_mid_out[at, :], ao[...])
+        grad[at, :] = total.astype(bf16)
+        return carry
+
+    lax.fori_loop(0, length // rows, attended_rows, 0)
+    sums.columns[...] = jnp.zeros_like(sums.columns)
+    ring.step(2)
+
+    def unturned(turned_grad, gain, cosine_part, sine_part):
+        low = turned_grad.astype(bf16).astype(f32)
+        return (low * cosine_part + pltpu.roll(low * sine_part, HEAD_DIM // 2, 1)) * gain
+
+    def head(h, carry):
+        cols = pl.ds(pl.multiple_of(h * HEAD_DIM, HEAD_DIM), HEAD_DIM)
+        k_cols = pl.ds(pl.multiple_of(part + h * HEAD_DIM, HEAD_DIM), HEAD_DIM)
+        v_cols = pl.ds(pl.multiple_of(2 * part + h * HEAD_DIM, HEAD_DIM), HEAD_DIM)
+        dk_sum[...] = jnp.zeros_like(dk_sum)
+        dv_sum[...] = jnp.zeros_like(dv_sum)
+        q_dots = []
+        for row in range(0, length, rows):
+            first, last = max(0, row - back), row + rows
+            scores = block_scores(
+                query[row:last, cols], key[first:last, cols], doc_col[row:last, :],
+                doc_row[:, first:last], row, first, rows,
+            )
+            probs = soft(scores)
+            grad_rows = grad[row:last, cols]
+            d_probs = times_t(grad_rows, value[first:last, cols])
+            dots = jnp.sum(probs * d_probs, axis=1, keepdims=True)
+            d_scores = (probs * (d_probs - dots)).astype(bf16)
+            dv_sum[first:last, :] += dot_rows(probs.astype(bf16), grad_rows)
+            dk_sum[first:last, :] += dot_rows(d_scores, query[row:last, cols])
+            dq = low_dot(d_scores, key[first:last, cols]) * scale
+            t_q = unturned(dq, gain_q[:, cols], cosine[row:last, :], sine[row:last, :])
+            t_rows[row:last, cols] = t_q
+            q_dots.append(jnp.sum(qkv_raw[row:last, cols] * t_q, axis=1, keepdims=True))
+        t_k = unturned(dk_sum[...] * scale, gain_k[:, cols], cosine[...], sine[...])
+        t_rows[:, k_cols] = t_k
+        k_dot = jnp.sum(qkv_raw[:, k_cols] * t_k, axis=1, keepdims=True)
+        sums.columns[...] += two_lanes(jnp.concatenate(q_dots, axis=0), k_dot)
+        d_qkv[:, v_cols] = dv_sum[...].astype(bf16)
+        for i in (3, 4, 5, 6):
+            pl.when(h == i - 3)(functools.partial(ring.step, i))
+        return carry
+
+    lax.fori_loop(0, part // HEAD_DIM, head, 0)
+    sums.start()
+    factors = sums.result() * (1.0 / width)
+    sums.columns[...] = factors * scales[...] * scales[...] * scales[...]
+
+    def raw_rows(r, carry):
+        at = pl.ds(pl.multiple_of(r * rows, rows), rows)
+        for lane in (0, 1):
+            cols = slice(lane * part, (lane + 1) * part)
+            d_qkv[at, cols] = (
+                scales[at, lane : lane + 1] * t_rows[at, cols]
+                - qkv_raw[at, cols] * sums.columns[at, lane : lane + 1]
+            ).astype(bf16)
+        return carry
+
+    lax.fori_loop(0, length // rows, raw_rows, 0)
+    lefts = [(d_qkv, w_qkv, True, b_qkv)]
+    scatter.outward(lefts)
+    scatter.inward(lefts)
+    step = 512
+    quarter_rows = scatter.rows
+
+    def grad_block(b, carry):
+        cols = lanes(b, step)
+        token_sum = None
+        for q in range(4):
+            term = dot_rows(
+                scatter.middle[q], tokens[q * quarter_rows : (q + 1) * quarter_rows, cols]
+            )
+            token_sum = term if token_sum is None else token_sum + term
+        choices = [(c, token_sum) for c in range(3)]
+        choices.append((3, dot_rows(mid_out[...], d_branch[:, cols])))
+        grads.put(grads.full, cols, by_kind(token_sum.shape, choices))
+        return carry
+
+    lax.fori_loop(0, width // step, grad_block, 0)
+    choices = [
+        (c, dot_rows(mid_qkv[...], d_qkv[:, c * part : (c + 1) * part])) for c in range(3)
+    ] + [(3, dot_rows(d_mid_out[...], attended[...]))]
+    grads.put(grads.cut, slice(0, part), by_kind((LANES, part), choices))
+    grads.start()
+    keep_own = pltpu.make_async_copy(own_table, own_tables.at[place], local.at[1])
+    for i in range(PIECES):
+        at, total, mid = scatter.piece(i)
+        my_grad[at, :] = (d_hidden[at, :] + total + low_dot(mid, full[...])).astype(bf16)
+        home.copy(i // 2, PIECES // 2, i % 2).start()
+        if i == 0:
+            own_table[0:16, :] = grads.summed()
+            for member, rows_here in grads.slices():
+                own_table[16:32, lanes(member, part)] = rows_here
+            own_ring.step(0)
+            own_ring.step(1)
+            keep_own.start()
+        else:
+            own_ring.step(1 + i)
+    for i in (5, 6):
+        own_ring.step(i)
+    ring.finish()
+    own_ring.finish()
+    scatter.finish()
+    home.finish(PIECES // 2)
+    sums.finish()
+    grads.finish()
+    keep.wait()
+    keep_own.wait()
+
+
+def attention_back(arrays, table, back, count):
+    f32, bf16 = jnp.float32, jnp.bfloat16
+    length, width = arrays[0].shape
+    part = arrays[4].shape[1]
+    rows = length // 4
+    shape = jax.ShapeDtypeStruct
+    return pl.pallas_call(
+        functools.partial(attend_back_kernel, back=back),
+        in_specs=[VMEM] * len(arrays) + [ANY],
+        out_specs=[ANY] * 3,
+        out_shape=[
+            shape((2, rows // 2, width), bf16), shape((count, *table.shape), bf16),
+            shape((count, 32, width), bf16),
+        ],
+        scratch_shapes=scatter_scratch(rows, width)
+        + row_sums_scratch(length)
+        + grads_scratch(width, part)
+        + [
+            DMA((2, 2, count - 1)), DMA((2, 2, count - 1)), DMA((2, PIECES // 2)),
+            DMA((2, PIECES // 2)), DMA((2,)), pltpu.VMEM((length, part), bf16), pltpu.VMEM((length, 2 * part), f32),
+            pltpu.VMEM((length, HEAD_DIM), f32), pltpu.VMEM((length, HEAD_DIM), f32),
+            pltpu.VMEM((rows, width), bf16), pltpu.VMEM((length, 3 * part), bf16),
+            pltpu.VMEM((length, LANES), bf16), pltpu.VMEM((32, width), bf16),
+        ],
+        name="attend_back",
+        compiler_params=params(6, vmem_limit_bytes=VMEM_BYTES),
+    )(*arrays, table)
+
+
+def per_group(
+    tokens,
+    cotangent,
+    token_document_index,
+    sequence_adapter_index,
+    query_weight,
+    key_weight,
+    value_weight,
+    output_weight,
+    gate_weight,
+    up_weight,
+    down_weight,
+    query_norm_gain,
+    key_norm_gain,
+    attention_norm_gain,
+    feedforward_norm_gain,
+    attention_down_adapters,
+    attention_up_adapters,
+    feedforward_down_adapters,
+    feedforward_up_adapters,
+    downproj_down_adapters,
+    downproj_up_adapters,
+):
+    f32, bf16 = jnp.float32, jnp.bfloat16
+    groups, wa = lax.axis_size("seq"), lax.axis_size("wa")
+    place, column = lax.axis_index("seq"), lax.axis_index("wa")
+    _, local_len, width = tokens.shape
+    length = local_len * groups
+    hidden_units = gate_weight.shape[1]
+    slice_heads = HEADS // wa
+    slice_width = slice_heads * HEAD_DIM
+    slice_units = hidden_units // wa
+    unit_block = down_weight.shape[0]
+    half = wa // 2
+    own_rows = ADAPTER_RANK // wa
+
+    def by_head(array):
+        parts = array.reshape(-1, 2, slice_heads, half, HEAD_DIM)
+        return jnp.transpose(parts, (0, 3, 1, 2, 4)).reshape(array.shape)
+
+    def by_unit(array):
+        parts = array.reshape(-1, groups, wa, unit_block)
+        return jnp.transpose(parts, (2, 0, 1, 3)).reshape(wa, -1, slice_units)
+
+    gain_q = query_norm_gain.astype(f32)[None]
+    gain_k = key_norm_gain.astype(f32)[None]
+    gain_a = attention_norm_gain.astype(f32)[None]
+    gain_f = feedforward_norm_gain.astype(f32)[None]
+
+    marks = jnp.concatenate(
+        [
+            token_document_index.reshape(1, -1).astype(bf16),
+            sequence_adapter_index.reshape(1, -1).astype(bf16),
+        ],
+        axis=1,
+    )
+    marks = jnp.pad(marks, ((0, own_rows - 1), (0, width - marks.shape[1])))
+    narrow = jnp.concatenate([attention_up_adapters[:3], attention_down_adapters[3:]])
+    wide = jnp.concatenate([feedforward_up_adapters, downproj_down_adapters[None]])
+    wide = jnp.pad(wide, ((0, 1), (0, 0), (0, 0)))
+    table = jnp.concatenate(
+        [
+            attention_down_adapters[:3].reshape(-1, width), attention_up_adapters[3],
+            feedforward_down_adapters.reshape(-1, width), downproj_up_adapters, marks,
+            by_head(narrow.reshape(-1, width)),
+            by_unit(wide.reshape(-1, hidden_units)).reshape(-1, width),
+        ],
+        axis=0,
+    )
+    qkv_parts = jnp.concatenate(
+        [
+            by_head(w).reshape(-1, wa, slice_width)
+            for w in (query_weight, key_weight, value_weight)
+        ],
+        axis=-1,
+    )
+    every_token, w_qkv, gate_slabs, up_slabs, tables, marks = fetch(
+        tokens, jnp.moveaxis(qkv_parts, 1, 0), gate_weight, up_weight, table, groups
+    )
+    seq_tokens = every_token.reshape(length, width)
+    w_qkv = w_qkv.reshape(width, 3 * slice_width)
+
+    marks = marks[:, :, 4]
+    adapter_of = marks[:, 0, 2 * local_len : 2 * local_len + 2].reshape(half, 2, 2)[:, ::-1]
+    adapter_of = jnp.transpose(adapter_of, (2, 1, 0)).reshape(groups).astype(jnp.int32)
+    home_column, home_block = home_of(place)
+    documents = lax.dynamic_slice(
+        marks, (flip(home_column, 1), 0, home_block * local_len), (1, groups, local_len)
+    )
+    documents = documents.reshape(length).astype(jnp.int32)
+    doc_col, doc_row = documents[:, None], documents[None, :]
+    my_adapter = lax.dynamic_index_in_dim(adapter_of, place, 0, keepdims=False)
+    table = lax.dynamic_index_in_dim(tables, my_adapter, 0, keepdims=False)
+    rope = rope_full(length)
+    my_gain_q, my_gain_k = (
+        lax.dynamic_slice_in_dim(by_head(g), column * slice_width, slice_width, 1)
+        for g in (gain_q, gain_k)
+    )
+    window = length // 2
+
+    (
+        attended, query, key, value, qkv_raw, mid_qkv, scales, full, b_qkv, b_out, b_gate, b_up,
+        b_down, w_out, _, my_cotangent,
+    ) = attend(
+        seq_tokens, w_qkv, table, my_gain_q, my_gain_k, rope, doc_col, doc_row, output_weight,
+        cotangent.astype(bf16), window, groups,
+    )
+    w_out = w_out.reshape(slice_width, width)
+    branch, hidden, mid_out, _, seq_hidden, gate_slabs = out_branch(
+        attended, w_out, b_out, gain_a, full, every_token, gate_slabs
+    )
+    seq_hidden = seq_hidden.reshape(length, width)
+    gate, up_value, mixed, mid_gu, layer_out, d_ffn, mid_down, seq_d_ffn, up_slabs, down_slabs = (
+        feed_forward(
+            seq_hidden, full, b_gate, b_up, b_down, hidden, my_cotangent, gain_f, gate_slabs,
+            up_slabs, down_weight,
+        )
+    )
+    w_gate = gate_slabs.reshape(width, slice_units)
+    w_up = up_slabs.reshape(width, slice_units)
+    w_down = down_slabs.reshape(slice_units, width)
+
+    seq_d_ffn = seq_d_ffn.reshape(length, width)
+    d_mid_down = times_t(seq_d_ffn, full).astype(bf16)
+    d_mixed = times_t(seq_d_ffn, w_down) + low_dot(d_mid_down, b_down)
+    gate, up_value = gate.astype(f32), up_value.astype(f32)
+    sigmoid = jax.nn.sigmoid(gate)
+    d_gate = (d_mixed * up_value * (sigmoid + gate * sigmoid * (1.0 - sigmoid))).astype(bf16)
+    d_up = (d_mixed * gate * sigmoid).astype(bf16)
+    d_hidden, d_branch, ffn_table, seq_d_branch, out_home = ffn_back(
+        (
+            d_gate, d_up, w_gate, w_up, b_gate, b_up, my_cotangent, branch, gain_a, full, mid_gu,
+            d_mid_down, mixed, seq_hidden, mid_down, d_ffn,
+        ),
+        layer_out,
+    )
+
+    grad_home, ffn_tables, attn_tables = attention_back(
+        (
+            seq_d_branch.reshape(length, width), w_out, full, b_out, query, key, value, qkv_raw,
+            scales, my_gain_q, my_gain_k, *rope, doc_col, doc_row, w_qkv, b_qkv, d_hidden,
+            seq_tokens, attended, mid_qkv, mid_out, d_branch,
+        ),
+        ffn_table, window, groups,
+    )
+
+    shared = (adapter_of == place)[:, None, None]
+
+    def over_groups(every):
+        total = jnp.sum(jnp.where(shared, every.astype(f32), 0.0), axis=0)
+        return total[:16].reshape(4, own_rows, width), total[16:]
+
+    attn_full, attn_cut = over_groups(attn_tables)
+    attn_cut = attn_cut.reshape(4, own_rows, half, 2, slice_heads, HEAD_DIM)
+    attn_cut = jnp.transpose(attn_cut, (0, 1, 3, 4, 2, 5)).reshape(4, own_rows, width)
+    ffn_full, ffn_cut = over_groups(ffn_tables)
+    ffn_cut = ffn_cut.reshape(wa, 4, own_rows, groups, unit_block)
+    ffn_cut = jnp.transpose(ffn_cut, (1, 2, 3, 0, 4)).reshape(4, own_rows, hidden_units)
+    return (
+        out_home,
+        grad_home.astype(f32),
+        jnp.concatenate([attn_full[:3], attn_cut[3:]]),
+        jnp.concatenate([attn_cut[:3], attn_full[3:]]),
+        ffn_full[:2],
+        ffn_cut[:2],
+        ffn_cut[2],
+        ffn_full[2],
+    )
+
+
 def solution(mesh):
+    groups, wa = mesh.shape["seq"], mesh.shape["wa"]
     in_specs = (
         P("wa", "seq", None),
         P("wa", "seq", None),
@@ -492,6 +1925,7 @@
         P(("seq", "wa"), None),
         P(("seq", "wa"), None),
     )
+    body = per_group if groups == 8 and wa == 4 else per_device
     return jax.shard_map(
-        per_device, mesh=mesh, in_specs=in_specs, out_specs=out_specs, check_vma=False
-    )
+        body, mesh=mesh, in_specs=in_specs, out_specs=out_specs, check_vma=False
+    )

time: 2090 us -> 855 us (0.41)
  the two profiles are of different devices: /device:TPU:6 before, /device:TPU:0 now
where the time goes in v3:
time: 855 us; the launch traced here: 845 us
  Pallas kernels  772 us (90%)
  matrix products  25.8 us (3%)
  local copies, waits for them, and re-layouts  24 us (3%)
  other arithmetic  19.4 us (2%)
    pallas_call x1, Pallas kernels, feed_forward(): pl.pallas_call(ffn_kernel, in_specs=[VMEM] * 8 + [ANY] * 3, out_specs=[VM...  231 us
    pallas_call x1, Pallas kernels, attention_back(): pl.pallas_call(functools.partial(attend_back_kernel, back=back), in_specs...  185 us
    pallas_call x1, Pallas kernels, fetch(): pl.pallas_call(fetch_kernel, in_specs=[VMEM] * 5, out_specs=[ANY] * 6, ou...  123 us
    pallas_call x1, Pallas kernels, out_branch(): pl.pallas_call(branch_kernel, in_specs=[VMEM] * 5 + [ANY] * 2, out_specs=...  88 us
    pallas_call x1, Pallas kernels, ffn_back(): pl.pallas_call(ffn_back_kernel, in_specs=[VMEM] * len(arrays) + [ANY], ou...  84 us
    pallas_call x1, Pallas kernels, attend(): pl.pallas_call(functools.partial(attend_kernel, back=back), in_specs=[VME...  62 us

profile of v3, /device:TPU:0, one launch (start us, length us, event | category | flops | bytes accessed | tf_op | source)
XLA Modules:
  0.0 845.2 jit_solution(18221574755354450561)
XLA Ops:
  0.7 0.8 convert_bitcast_fusion.6
  5.3 1.3 broadcast_in_dim.51
  6.5 1.3 broadcast_in_dim.52
  9.3 0.8 reshape.159
  10.1 0.8 slice.74
  10.9 0.8 slice.76
  11.9 1.1 reshape.155
  13.2 1.2 reshape.156
  15.1 0.9 maximum_bitcast_fusion.qkv_parts
  16.5 4.7 concatenate.31.table
  21.1 1.1 convert_element_type.118.cotangent
  22.3 1.9 fusion.12
  24.2 1.3 pad_maximum_fusion
  25.5 122.8 %fetch.1 = (bf16[4,256,2048]{2,1,0:T(8,128)(2,1)}, bf16[8,256,1536]{2,1,0:T(8,128)(2,1)}, bf16[8,256,2048]{2,1,0:T(8,128)(2,1)}, bf16[8,256,2048]{2,1,0:T(8,128)...) custom-call(bf16[2,128,2048]{2,1,0:T(8,128)(2,1)} %tokens.1, ...), custom_call_target="tpu_custom_call" | custom-call | tf_op jit(solution)/shard_map/fetch/pallas_call | solution.py:986
  148.3 1.5 slice.78
  153.5 1.8 dynamic-slice_bitcast_fusion.table
  155.4 1.0 copy.51.doc_col
  156.4 62.0 %attend.1 = (bf16[1024,512]{1,0:T(8,128)(2,1)}, bf16[1024,512]{1,0:T(8,128)(2,1)}, bf16[1024,512]{1,0:T(8,128)(2,1)}, bf16[1024,512]{1,0:T(8,128)(2,1)}, f32[102...) custom-call(bf16[1024,2048]{1,0:T(8,128)(2,1)} %bitcast.85, ...), custom_call_target="tpu_custom_call" | custom-call | tf_op jit(solution)/shard_map/attend/pallas_call | solution.py:1196
  218.4 88.0 %out_branch.1 = (f32[256,2048]{1,0:T(8,128)}, f32[256,2048]{1,0:T(8,128)}, bf16[256,128]{1,0:T(8,128)(2,1)}, bf16[256,2048]{1,0:T(8,128)(2,1)}, bf16[4,256,2048]...) custom-call(bf16[1024,512]{1,0:T(8,128)(2,1)} %get-tuple-element.56.attended, ...), custom_call_target="tpu_custom_call", output_to_operand_aliasing={{5}: (6, {})} | custom-call | tf_op jit(solution)/shard_map/out_branch/pallas_call | solution.py:1334
  306.4 230.6 %feed_forward.1 = (bf16[1024,2048]{1,0:T(8,128)(2,1)}, bf16[1024,2048]{1,0:T(8,128)(2,1)}, bf16[1024,2048]{1,0:T(8,128)(2,1)}, bf16[1024,128]{1,0:T(8,128)(2,1)}...) custom-call(bf16[1024,2048]{1,0:T(8,128)(2,1)} %bitcast.90, ...), custom_call_target="tpu_custom_call", output_to_operand_aliasing={{8}: (9, {})} | custom-call | tf_op jit(solution)/shard_map/feed_forward/pallas_call | solution.py:1444
  537.0 15.7 %fusion.19 = f32[1024,2048]{1,0:T(8,128)} fusion(bf16[1024,2048]{1,0:T(8,128)(2,1)} %bitcast.117, bf16[2048,2048]{1,0:T(8,128)(2,1)} %bitcast.116), kind=kOutput, calls=%fused_computation.58 | convolution fusion | flops 8589934592 | bytes 20971520 | tf_op jit(solution)/shard_map/dot_general | solution.py:44
  552.7 1.3 convolution_convert_fusion.d_mid_down
  554.0 1.1 copy-done.12
  555.1 8.9 %fusion.8 = (bf16[1024,2048]{1,0:T(8,128)(2,1)}, bf16[1024,2048]{1,0:T(8,128)(2,1)}) fusion(bf16[1024,2048]{1,0:T(8,128)(2,1)S(1)} %copy-done.12, bf16[1024,2048]{1,0:T(8,128)(2,1)S(1)} %copy-done.13, f32[1024,2048]{1,0:T(8,128)} %fusion.19, bf16[1024,128]{1,0:T(8,128)(2,1)S(1)} %convolution_convert_fusion.d_mid_down, bf16[128,2048]{1,0:T(8,128)(2,1)S(1)} %copy-done.4), kind=kOutput, calls=%fused_computation.11 | convolution fusion | flops 570425344 | bytes 25952256 | tf_op jit(solution)/shard_map/dot_general | solution.py:465
  564.0 84.0 %ffn_back.1 = (f32[256,2048]{1,0:T(8,128)}, bf16[256,2048]{1,0:T(8,128)(2,1)}, bf16[80,2048]{1,0:T(8,128)(2,1)}, bf16[4,256,2048]{2,1,0:T(8,128)(2,1)}, bf16[2,128,2048]{2,1,0:T(8,128)(2,1)}) custom-call(bf16[1024,2048]{1,0:T(8,128)(2,1)} %get-tuple-element.97.d_gate, bf16[1024,2048]{1,0:T(8,128)(2,1)} %get-tuple-element.96.d_up, ...), custom_call_target="tpu_custom_call" | custom-call | tf_op jit(solution)/shard_map/ffn_back/pallas_call | solution.py:1534
  648.0 185.1 %attend_back.1 = (bf16[2,128,2048]{2,1,0:T(8,128)(2,1)}, bf16[8,80,2048]{2,1,0:T(8,128)(2,1)}, bf16[8,32,2048]{2,1,0:T(8,128)(2,1)}) custom-call(bf16[1024,2048]{1,0:T(8,128)(2,1)} %bitcast.94, bf16[512,2048]{1,0:T(8,128)(2,1)} %bitcast.93, bf16[128,2048]{1,0:T(8,128)(2,1)} %get-tuple-element.59.bo.full, bf16[128,512]{1,0:T(8,128)(2,1)} %get-tuple-element.58.ao, ...), custom_call_target="tpu_custom_call" | custom-call | tf_op jit(solution)/shard_map/attend_back/pallas_call | solution.py:1700
  833.1 1.5 select_reduce_fusion.1
  834.6 2.4 select_reduce_fusion
  838.7 0.9 slice.93
  839.7 0.7 squeeze.22
  842.3 1.6 convert_element_type.124
  843.8 1.0 copy.76
  (90 shorter events, 11.8 us)
Async XLA Ops:
  0.6 15.4 %copy-start.8 = (bf16[4,8192]{1,0:T(4,128)(2,1)S(1)}, bf16[4,8192]{1,0:T(4,128)(2,1)}, u32[]{:S(2)}) copy-start(bf16[4,8192]{1,0:T(4,128)(2,1)} %param.40) | copy-start | bytes 196612
  0.6 15.4 %copy-start.7 = (bf16[2,4,8192]{2,1,0:T(4,128)(2,1)S(1)}, bf16[2,4,8192]{2,1,0:T(4,128)(2,1)}, u32[]{:S(2)}) copy-start(bf16[2,4,8192]{2,1,0:T(4,128)(2,1)} %param.39) | copy-start | bytes 393220
  0.7 14.0 %copy-start.6 = (bf16[64,2048]{1,0:T(8,128)(2,1)S(1)}, bf16[64,2048]{1,0:T(8,128)(2,1)}, u32[]{:S(2)}) copy-start(bf16[64,2048]{1,0:T(8,128)(2,1)} %param.27) | copy-start | bytes 786436
  11.9 4.5 copy-start.9
  13.1 8.0 copy-start.1
  16.0 6.3 copy-start.10
  16.0 6.3 copy-start.11
  537.0 15.7 %copy-start = (bf16[128,2048]{1,0:T(8,128)(2,1)S(1)}, bf16[128,2048]{1,0:T(8,128)(2,1)}, u32[]{:S(2)}) copy-start(bf16[128,2048]{1,0:T(8,128)(2,1)} %get-tuple-element.59.bo.full) | copy-start | bytes 1572868
  537.0 15.7 %copy-start.14 = (bf16[4,256,2048]{2,1,0:T(8,128)(2,1)S(1)}, bf16[4,256,2048]{2,1,0:T(8,128)(2,1)}, u32[]{:S(2)}) copy-start(bf16[4,256,2048]{2,1,0:T(8,128)(2,1)} %get-tuple-element.69) | copy-start | bytes 12582916
  537.0 17.0 %copy-start.13 = (bf16[1024,2048]{1,0:T(8,128)(2,1)S(1)}, bf16[1024,2048]{1,0:T(8,128)(2,1)}, u32[]{:S(2)}) copy-start(bf16[1024,2048]{1,0:T(8,128)(2,1)} %get-tuple-element.71) | copy-start | bytes 12582916
  552.7 1.3 copy-start.4
  552.7 2.4 copy-start.12
  555.1 8.9 %copy-start.5 = (bf16[1024,128]{1,0:T(8,128)(2,1)}, bf16[1024,128]{1,0:T(8,128)(2,1)S(1)}, u32[]{:S(2)}) copy-start(bf16[1024,128]{1,0:T(8,128)(2,1)S(1)} %convolution_convert_fusion.d_mid_down) | copy-start | bytes 786436
  837.0 5.3 copy-start.2
  837.9 6.0 copy-start.3

commit v4 on v3

--- a/solution.py
+++ b/solution.py
@@ -538,10 +538,11 @@
 
 
 class Ring:
-    def __init__(self, buffer, send, recv, place, column, own=None):
+    def __init__(self, buffer, send, recv, place, column, own=None, part=0, parts=1):
         self.buffer, self.send, self.recv, self.own = buffer, send, recv, own
         self.count = buffer.shape[0]
-        self.half = buffer.shape[1] // 2
+        self.half = buffer.shape[1] // parts // 2
+        self.base = part * buffer.shape[1] // parts
         self.spot = ring_place(place, self.count)
         self.peers = ring_peers(place, column, self.count)
         long = self.count // 2
@@ -552,14 +553,14 @@
 
     def region(self, away, h):
         owner = ring_owner(self.spot + away, self.count)
-        return self.buffer.at[owner, pl.ds(h * self.half, self.half)]
+        return self.buffer.at[owner, pl.ds(self.base + h * self.half, self.half)]
 
     def copy(self, way, i, back=0):
         t, h = self.order[way][i]
         region = self.region((t + back) * (1 if way else -1), h)
         source = region
         if t + back == 0 and self.own is not None:
-            source = self.own.at[pl.ds(h * self.half, self.half)]
+            source = self.own.at[pl.ds(self.base + h * self.half, self.half)]
         return remote(
             source, region, self.send.at[way, i], self.recv.at[way, i], self.peers[way]
         )
@@ -585,23 +586,48 @@
                 self.copy(way, i).wait_send()
 
 
+class Pair:
+    def __init__(self, buffer, send, recv, first, place, column, own=None):
+        self.rings = [
+            Ring(buffer, send.at[first + i], recv.at[first + i], place, column, own, i, 2)
+            for i in (0, 1)
+        ]
+
+    def step(self, i):
+        for ring in self.rings:
+            ring.step(i)
+
+    def finish(self):
+        for ring in self.rings:
+            ring.finish()
+
+
 def here():
     return lax.axis_index("seq"), lax.axis_index("wa")
 
 
 def group_of(column, block):
-    return 4 * block + 2 * (column % 2) + column // 2
+    return 4 * block + column
 
 
 def home_of(place):
-    return place % 2 * 2 + place // 2 % 2, place // 4
+    return place % 4, place // 4
+
+
+def quarter_of(column):
+    return 2 * (column % 2) + 1 - column // 2
+
+
+def member_of(quarter):
+    return 2 * (1 - quarter % 2) + quarter // 2
 
 
 class WaGather:
     def __init__(self, buffer, send, recv, place, column, pieces, source=None):
         self.buffer, self.send, self.recv, self.pieces = buffer, send, recv, pieces
         self.source = source
-        self.quarter = flip(column, 1)
+        self.quarter = quarter_of(column)
+        self.far = flip(self.quarter, 1)
         self.near, self.across, _ = wa_peers(place, column)
         self.rows = buffer.shape[1] // pieces
 
@@ -621,18 +647,17 @@
         self.copy(0, i).start()
 
     def forward(self, i):
-        far = flip(self.quarter, 2)
-        self.copy(1, i, far).wait_recv()
-        self.copy(2, i, far).start()
+        self.copy(1, i, self.far).wait_recv()
+        self.copy(2, i, self.far).start()
 
     def finish(self):
         for i in range(self.pieces):
-            self.copy(0, i, flip(self.quarter, 1)).wait_recv()
-            self.copy(2, i, flip(flip(self.quarter, 2), 1)).wait_recv()
+            self.copy(0, i, flip(self.quarter, 2)).wait_recv()
+            self.copy(2, i, flip(self.far, 2)).wait_recv()
         for i in range(self.pieces):
             for kind in (0, 1):
                 self.copy(kind, i).wait_send()
-            self.copy(2, i, flip(self.quarter, 2)).wait_send()
+            self.copy(2, i, self.far).wait_send()
 
 
 def params(number, **more):
@@ -651,19 +676,20 @@
             self.last, self.last_mid, self.send, self.recv,
         ) = refs
         self.near, self.across, _ = wa_peers(place, column)
-        self.quarter = flip(column, 1)
-        self.far = flip(self.quarter, 2)
+        self.quarter = quarter_of(column)
+        self.far = flip(self.quarter, 1)
         self.rows = self.partial.shape[1]
         self.pieces = PIECES
         self.size = self.rows // self.pieces
         self.sent = []
+        self.ready, self.block_ready, self.adapted = None, None, False
 
     def product(self, which, lefts):
         width, step = self.partial.shape[2], 512
         at = pl.ds(pl.multiple_of(which * self.rows, self.rows), self.rows)
 
         def block(b, carry):
-            cols = pl.ds(pl.multiple_of(b * step, step), step)
+            cols = lanes(b, step)
             total = None
             for left, weight, turned, _ in lefts:
                 if turned:
@@ -674,7 +700,20 @@
             self.partial[which, :, cols] = total.astype(jnp.bfloat16)
             return carry
 
-        lax.fori_loop(0, width // step, block, 0)
+        if self.ready is not None:
+            self.ready(which)
+        if self.block_ready is None:
+            lax.fori_loop(0, width // step, block, 0)
+        else:
+            for b in range(width // step):
+                self.block_ready(b)
+                block(b, 0)
+            self.block_ready = None
+        if not self.adapted:
+            self.adapt(which, lefts)
+
+    def adapt(self, which, lefts):
+        at = pl.ds(pl.multiple_of(which * self.rows, self.rows), self.rows)
         total = None
         for left, _, _, adapter in lefts:
             term = times_t(left[at, :], adapter[...])
@@ -710,7 +749,7 @@
 
     def outward(self, lefts):
         f32, bf16 = jnp.float32, jnp.bfloat16
-        which = flip(self.far, 1)
+        which = flip(self.far, 2)
         self.product(which, lefts)
         for copy in self.to_near(0, which):
             self.begin(copy)
@@ -729,7 +768,7 @@
             self.begin(self.across_copy(i))
 
     def inward(self, lefts):
-        which = flip(self.quarter, 1)
+        which = flip(self.quarter, 2)
         self.product(which, lefts)
         for copy in self.to_near(1, which):
             self.begin(copy)
@@ -781,7 +820,7 @@
     def __init__(self, own, home, send, recv, place, column):
         self.own, self.home, self.send, self.recv = own, home, send, recv
         self.column, self.block = home_of(place)
-        self.level, self.quarter = place // 2, flip(column, 1)
+        self.level, self.quarter = place // 2, quarter_of(column)
         self.my_column = column
         self.length = home.shape[1]
 
@@ -789,7 +828,7 @@
         return [(2 * self.quarter + i, self.column) for i in (0, 1)]
 
     def sources(self):
-        return [(group_of(self.my_column, b), flip(self.level, 1)) for b in (0, 1)]
+        return [(group_of(self.my_column, b), member_of(self.level)) for b in (0, 1)]
 
     def copy(self, i, pieces=1, k=0):
         size = self.length // pieces
@@ -868,9 +907,9 @@
     count = w_qkv.shape[0]
     local_len = tokens.shape[1]
     level, parity = place // 2, place % 2
-    member = flip(level, 1)
+    member = member_of(level)
     home_column, _ = home_of(place)
-    quarter = flip(column, 1)
+    quarter = quarter_of(column)
     near_far = wa_peers(place, column)
     ring_near = ring_peers(place, column, count)
     home_from = [(2 * quarter, home_column), (2 * quarter + 1, home_column)]
@@ -928,15 +967,18 @@
         region = gather.region(quarter, i)
         remote(region, region, home_send.at[i], home_recv.at[i], home_from[i]).wait_recv()
         gather.own(i)
+    for i in (4, 5):
+        table_ring.step(i)
+    qkv_ring.step(2)
+    qkv_ring.step(3)
+    table_ring.step(6)
     for t, (source, buffer) in enumerate(((gate, w_gate), (up, w_up))):
         for piece, target in slices(source, buffer, column):
             pltpu.make_async_copy(piece, target, local.at[2 + t]).start()
         for k, peer in enumerate(near_far):
             for piece, target in slices(source, buffer, peer[1]):
                 remote(piece, target, part_send.at[1 + t, k], part_recv.at[1 + t, k], peer).start()
-    for i in (4, 5, 6):
-        table_ring.step(i)
-    qkv_ring.step(2)
+    qkv_ring.step(4)
     own_table.wait()
     table_ring.finish()
     own_marks = pltpu.make_async_copy(
@@ -953,16 +995,15 @@
     for move in mark_moves:
         move.start()
     gather.forward(0)
-    qkv_ring.step(3)
     gather.forward(1)
-    for i in (4, 5, 6):
+    for i in (5, 6):
         qkv_ring.step(i)
     for t, buffer in enumerate((w_gate, w_up)):
         region = buffer.at[place, ours]
         pltpu.make_async_copy(region, region, local.at[2 + t]).wait()
         parts_here(1 + t, buffer)
     for k, peer in enumerate(near_far):
-        region = marks.at[flip(peer[1], 1)]
+        region = marks.at[quarter_of(peer[1])]
         remote(region, region, mark_send.at[k], mark_recv.at[k], peer).wait_recv()
     qkv_ring.finish()
     gather.finish()
@@ -1003,8 +1044,7 @@
 
 KINDS = 8
 MARKS = 24
-BY_HEAD = 32
-BY_UNIT = 48
+SLICES = 32
 
 
 def kind_rows(shape):
@@ -1012,22 +1052,19 @@
 
 
 class Adapters:
-    def __init__(self, table, full, heads, units, send, recv, local, place, column):
+    def __init__(self, table, full, slices, send, recv, local, place, column):
         self.table, self.local = table, local
         self.peers = wa_peers(place, column)
         self.send, self.recv = send, recv
-        self.quarter = flip(column, 1)
+        self.quarter = quarter_of(column)
         self.column = column
-        self.full, self.heads, self.units = full, heads, units
+        self.full, self.slices = full, slices
 
     def pieces(self, member, quarter):
-        part = self.heads.shape[2]
-        cols = pl.ds(pl.multiple_of(member * part, part), part)
-        rows = pl.ds(pl.multiple_of(BY_UNIT + 16 * member, 16), 16)
+        rows = pl.ds(pl.multiple_of(SLICES + 16 * member, 16), 16)
         return [
+            (self.table.at[rows], self.slices.at[quarter]),
             (self.table.at[pl.ds(0, 32)], self.full.at[pl.ds(pl.multiple_of(32 * quarter, 32), 32)]),
-            (self.table.at[pl.ds(BY_HEAD, 16), cols], self.heads.at[quarter]),
-            (self.table.at[rows], self.units.at[quarter]),
         ]
 
     def copies(self, k):
@@ -1041,17 +1078,20 @@
         return pltpu.make_async_copy(source, target, self.local.at[i])
 
     def start(self):
-        for i in range(3):
+        for i in range(2):
             self.own(i).start()
         for k in range(3):
             for copy in self.copies(k):
                 copy.start()
 
-    def wait(self, i):
-        self.own(i).wait()
-        for k in range(3):
-            _, target = self.pieces(self.column, flip(self.peers[k][1], 1))[i]
-            remote(target, target, self.send.at[k, i], self.recv.at[k, i], self.peers[k]).wait_recv()
+    def wait(self):
+        for i in range(2):
+            self.own(i).wait()
+            for k in range(3):
+                _, target = self.pieces(self.column, quarter_of(self.peers[k][1]))[i]
+                remote(
+                    target, target, self.send.at[k, i], self.recv.at[k, i], self.peers[k]
+                ).wait_recv()
 
     def finish(self):
         for k in range(3):
@@ -1060,58 +1100,53 @@
 
 
 def attend_kernel(
-    tokens, w_qkv, table, gain_q, gain_k, cosine, sine, doc_col, doc_row, out_part, cotangent,
-    attended, query, key, value, qkv_raw, middle, scales, full, b_qkv, b_out, b_gate, b_up, b_down,
-    w_out, out_slabs, my_cotangent, *refs, back,
+    table, gain_q, gain_k, cosine, sine, doc_col, doc_row, every_token, qkv_weight, out_part,
+    _gate, attended, query, key, value, qkv_raw, middle, scales, full, b_qkv, b_out, b_gate, b_up,
+    b_down, w_out, out_slabs, w_gate, *refs, back,
 ):
     place, column = here()
     sums = RowSums(refs[:ROW_SUMS_REFS], place, column)
     (
-        ring_send, ring_recv, home_send, home_recv, local, out_send, out_recv, heads, units,
-        table_send, table_recv, table_local,
+        ring_send, ring_recv, local, out_send, out_recv, slices, table_send, table_recv,
+        table_local, tokens, w_qkv,
     ) = refs[ROW_SUMS_REFS:]
+    loads = [
+        pltpu.make_async_copy(every_token, tokens, local.at[2]),
+        pltpu.make_async_copy(qkv_weight, w_qkv, local.at[3]),
+    ]
+    for load in loads:
+        load.start()
     count = out_slabs.shape[0]
     peers = wa_peers(place, column)
-    local_len = cotangent.shape[1]
-    level, parity = place // 2, place % 2
-    home_column, _ = home_of(place)
-    quarter = flip(column, 1)
-    home_from = [(2 * quarter + i, home_column) for i in (0, 1)]
-    home_to = [(group_of(column, b), flip(level, 1)) for b in (0, 1)]
-    greet(peers + ring_peers(place, column, count) + home_from, 7)
-    adapters = Adapters(
-        table, full, heads, units, table_send, table_recv, table_local, place, column
-    )
+    greet(peers + ring_peers(place, column, count), 5)
+    adapters = Adapters(table, full, slices, table_send, table_recv, table_local, place, column)
     adapters.start()
-    ring = Ring(out_slabs, ring_send, ring_recv, place, column, out_part)
+    ring = Ring(out_slabs, ring_send.at[0], ring_recv.at[0], place, column, out_part)
+    gate_rings = Pair(w_gate, ring_send, ring_recv, 1, place, column)
     ring.step(0)
     ring.step(1)
+    gate_rings.step(0)
+    gate_rings.step(1)
     keep = pltpu.make_async_copy(out_part, out_slabs.at[place], local.at[0])
     keep.start()
-    moves = [
-        remote(
-            cotangent.at[b], my_cotangent.at[pl.ds(parity * local_len, local_len)],
-            home_send.at[b], home_recv.at[parity], home_to[b],
-        )
-        for b in (0, 1)
-    ]
-    for move in moves:
-        move.start()
     length, width = tokens.shape
     part = value.shape[1]
     rows = 256
     bf16 = jnp.bfloat16
-    adapters.wait(0)
-    adapters.wait(1)
-    kind = kind_rows((128, part))
-    spread_heads = jnp.concatenate(
-        [piece for q in range(4) for piece in (heads[q], jnp.zeros((16, part), bf16))], axis=0
-    )
-    zero = jnp.zeros((128, part), bf16)
-    for c in range(3):
-        b_qkv[:, c * part : (c + 1) * part] = jnp.where(kind == c, spread_heads, zero)
-    b_out[...] = jnp.where(kind == 3, spread_heads, zero)
+    adapters.wait()
+    ring.step(2)
+    every_slice = jnp.concatenate([slices[q] for q in range(4)], axis=0)
+    to, at = (lax.broadcasted_iota(jnp.int32, (LANES, 64), d) for d in (0, 1))
+    for c in range(4):
+        moved = (to // 32 == at // 16) & (to % 32 // 4 == c) & (at % 16 == 12 + to % 4)
+        piece = low_dot(moved.astype(bf16), every_slice[:, c * part : (c + 1) * part])
+        if c < 3:
+            b_qkv[:, c * part : (c + 1) * part] = piece.astype(bf16)
+        else:
+            b_out[...] = piece.astype(bf16)
+    loads[0].wait()
     middle[...] = times_t(tokens[...], full[...]).astype(bf16)
+    loads[1].wait()
 
     def block(r, carry):
         at = pl.ds(pl.multiple_of(r * rows, rows), rows)
@@ -1130,17 +1165,20 @@
 
     lax.fori_loop(0, length // rows, block, 0)
     sums.start()
-    ring.step(2)
-    adapters.wait(2)
-    kind = kind_rows((128, width))
+    ring.step(3)
+    ring.step(4)
+    gate_rings.step(2)
+    kind = kind_rows((LANES, width))
     spread_units = jnp.concatenate(
-        [piece for q in range(4) for piece in (jnp.zeros((16, width), bf16), units[q])], axis=0
-    )
-    zero = jnp.zeros((128, width), bf16)
+        [piece for q in range(4) for piece in (jnp.zeros((16, width), bf16), slices[q])], axis=0
+    )
+    zero = jnp.zeros((LANES, width), bf16)
     for c, target in ((4, b_gate), (5, b_up), (6, b_down)):
         target[...] = jnp.where(kind == c, spread_units, zero)
     scales[...] = lax.rsqrt(sums.result() * (1.0 / width) + EPSILON)
-    ring.step(3)
+    ring.step(5)
+    gate_rings.step(3)
+    ring.step(6)
 
     def head(h, carry):
         cols = pl.ds(pl.multiple_of(h * HEAD_DIM, HEAD_DIM), HEAD_DIM)
@@ -1157,8 +1195,8 @@
             )
             probs = soft(scores).astype(bf16)
             attended[row:last, cols] = low_dot(probs, value[first:last, cols]).astype(bf16)
-        for i in (4, 5, 6):
-            pl.when(h == i - 4)(functools.partial(ring.step, i))
+        pl.when(h == 1)(functools.partial(gate_rings.step, 4))
+        pl.when(h == 3)(functools.partial(gate_rings.step, 5))
         return carry
 
     lax.fori_loop(0, part // HEAD_DIM, head, 0)
@@ -1176,18 +1214,17 @@
     give.start()
     take = w_out.at[:, 1 - core]
     remote(take, take, out_send, out_recv, peers[0]).wait_recv()
+    gate_rings.step(6)
     give.wait_send()
     mine.wait()
-    for i in (0, 1):
-        region = my_cotangent.at[pl.ds(i * local_len, local_len)]
-        remote(region, region, home_send.at[i], home_recv.at[i], home_from[i]).wait_recv()
-    for move in moves:
-        move.wait_send()
+    gate_rings.finish()
     adapters.finish()
     sums.finish()
 
 
-def attend(tokens, w_qkv, table, gain_q, gain_k, tables, doc_col, doc_row, out_part, cotangent, back, count):
+def attend(
+    tokens, w_qkv, table, gain_q, gain_k, tables, doc_col, doc_row, out_part, w_gate, back, count
+):
     f32, bf16 = jnp.float32, jnp.bfloat16
     (length, width), part = tokens.shape, w_qkv.shape[1] // 3
     shape = jax.ShapeDtypeStruct
@@ -1195,24 +1232,25 @@
     maps = shape((LANES, width), bf16)
     return pl.pallas_call(
         functools.partial(attend_kernel, back=back),
-        in_specs=[VMEM] * 9 + [ANY] * 2,
+        in_specs=[VMEM] * 7 + [ANY] * 4,
         out_specs=[VMEM] * 14 + [ANY] * 2,
         out_shape=[
             low, low, low, low, shape((length, 2 * part), f32), shape((length, LANES), bf16),
             shape((length, LANES), f32), maps, shape((LANES, 3 * part), bf16),
             shape((LANES, part), bf16), maps, maps, maps,
             shape((count // 2, 2, *out_part.shape), bf16), shape((count, *out_part.shape), bf16),
-            shape((2 * cotangent.shape[1], width), bf16),
+            shape(w_gate.shape, bf16),
         ],
         scratch_shapes=row_sums_scratch(length)
         + [
-            DMA((2, count - 1)), DMA((2, count - 1)), DMA((2,)), DMA((2,)), DMA((2,)), DMA(()),
-            DMA(()), pltpu.VMEM((4, 16, part), bf16), pltpu.VMEM((4, 16, width), bf16),
-            DMA((3, 3)), DMA((3, 3)), DMA((3,)),
+            DMA((3, 2, count - 1)), DMA((3, 2, count - 1)), DMA((4,)), DMA(()), DMA(()),
+            pltpu.VMEM((4, 16, width), bf16), DMA((3, 2)), DMA((3, 2)), DMA((2,)),
+            pltpu.VMEM(tokens.shape, bf16), pltpu.VMEM(w_qkv.shape, bf16),
         ],
+        input_output_aliases={10: 15},
         name="attend",
         compiler_params=params(2, vmem_limit_bytes=VMEM_BYTES),
-    )(tokens, w_qkv, table, gain_q, gain_k, *tables, doc_col, doc_row, out_part, cotangent)
+    )(table, gain_q, gain_k, *tables, doc_col, doc_row, tokens, w_qkv, out_part, w_gate)
 
 
 class Grads:
@@ -1220,7 +1258,7 @@
         self.full, self.cut, self.full_in, self.cut_in, self.send, self.recv = refs
         self.kind = first_kind
         self.peers = wa_peers(place, column)
-        self.quarter = flip(column, 1)
+        self.quarter = quarter_of(column)
         self.column = column
 
     def put(self, target, step, total):
@@ -1230,7 +1268,7 @@
             target[q, :, step] = low[at : at + 16]
 
     def copies(self, k):
-        there = flip(self.peers[k][1], 1)
+        there = quarter_of(self.peers[k][1])
         return [
             remote(self.full.at[there], self.full_in.at[k], self.send.at[k, 0], self.recv.at[k, 0], self.peers[k]),
             remote(self.cut.at[there], self.cut_in.at[k], self.send.at[k, 1], self.recv.at[k, 1], self.peers[k]),
@@ -1285,26 +1323,26 @@
 
 
 def branch_kernel(
-    attended, w_out, ao, gain, bo, every_token, _gate, branch, hidden, mid_out, hidden_low, every,
-    w_gate, *refs,
+    attended, w_out, ao, gain, bo, every_token, _up, branch, hidden, mid_out, hidden_low,
+    every, w_up, *refs,
 ):
     place, column = here()
     scatter = Scatter(refs[:SCATTER_REFS], place, column)
     wa_send, wa_recv, ring_send, ring_recv, local, tokens, token_sem = refs[SCATTER_REFS:]
     load = pltpu.make_async_copy(every_token.at[scatter.quarter], tokens, token_sem)
     load.start()
-    greet(wa_peers(place, column)[:2] + ring_peers(place, column, w_gate.shape[0]), 4)
-    ring = Ring(w_gate, ring_send, ring_recv, place, column)
+    greet(wa_peers(place, column)[:2] + ring_peers(place, column, w_up.shape[0]), 4)
+    rings = Pair(w_up, ring_send, ring_recv, 0, place, column)
     gather = WaGather(every, wa_send, wa_recv, place, column, PIECES, hidden_low)
     lefts = [(attended, w_out, False, ao)]
-    ring.step(0)
-    ring.step(1)
+    rings.step(0)
+    rings.step(1)
     scatter.outward(lefts)
     scatter.inward(lefts)
     load.wait()
     for i in range(PIECES):
         if i % 2 == 0:
-            ring.step(2 + i // 2)
+            rings.step(2 + i // 2)
         at, total, middle = scatter.piece(i)
         total = total + low_dot(middle, bo[...])
         rows = tokens[at, :].astype(jnp.float32) + total * rms_factor(total) * gain[...]
@@ -1316,20 +1354,20 @@
     keep = pltpu.make_async_copy(hidden_low, every.at[gather.quarter], local)
     keep.start()
     for i in range(PIECES):
+        gather.forward(i)
         if i % 2 == 0:
-            ring.step(4 + i // 2)
-        gather.forward(i)
-    ring.step(6)
+            rings.step(4 + i // 2)
+    rings.step(6)
     gather.finish()
     scatter.finish()
-    ring.finish()
+    rings.finish()
     keep.wait()
 
 
-def out_branch(attended, w_out, ao, gain, bo, tokens, w_gate):
+def out_branch(attended, w_out, ao, gain, bo, tokens, w_up):
     f32, bf16 = jnp.float32, jnp.bfloat16
     _, rows, width = tokens.shape
-    count = w_gate.shape[0]
+    count = w_up.shape[0]
     shape = jax.ShapeDtypeStruct
     return pl.pallas_call(
         branch_kernel,
@@ -1337,33 +1375,43 @@
         out_specs=[VMEM] * 4 + [ANY] * 2,
         out_shape=[
             shape((rows, width), f32), shape((rows, width), f32), shape((rows, LANES), bf16),
-            shape((rows, width), bf16), shape((4, rows, width), bf16), shape(w_gate.shape, bf16),
+            shape((rows, width), bf16), shape((4, rows, width), bf16), shape(w_up.shape, bf16),
         ],
         scratch_shapes=scatter_scratch(rows, width)
         + [
-            DMA((3, PIECES)), DMA((3, PIECES)), DMA((2, count - 1)), DMA((2, count - 1)), DMA(()),
-            pltpu.VMEM((rows, width), bf16), DMA(()),
+            DMA((3, PIECES)), DMA((3, PIECES)), DMA((2, 2, count - 1)), DMA((2, 2, count - 1)),
+            DMA(()), pltpu.VMEM((rows, width), bf16), DMA(()),
         ],
         input_output_aliases={6: 5},
         name="out_branch",
         compiler_params=params(3, vmem_limit_bytes=VMEM_BYTES),
-    )(attended, w_out, ao, gain, bo, tokens, w_gate)
+    )(attended, w_out, ao, gain, bo, tokens, w_up)
 
 
 def ffn_kernel(
-    rows_in, full, bg, bu, ad, hidden, cotangent, gain, w_gate, _up, down,
-    gate_low, up_low, mixed, middle, layer_out, d_ffn, mid_down, every, w_up, w_down, *refs,
+    full, bg, bu, ad, gain, every_row, every_hidden, home_cotangent, w_gate, w_up, down,
+    gate_low, up_low, mixed, middle, layer_out, d_ffn, mid_down, my_cotangent, every, w_down,
+    *refs,
 ):
     place, column = here()
     scatter = Scatter(refs[:SCATTER_REFS], place, column)
-    wa_send, wa_recv, ring_send, ring_recv, local, first_w, second_w = refs[SCATTER_REFS:]
+    (
+        wa_send, wa_recv, ring_send, ring_recv, local, first_w, second_w, rows_in, hidden,
+        home_send, home_recv,
+    ) = refs[SCATTER_REFS:]
     count = w_up.shape[0]
-    greet(wa_peers(place, column)[:2] + ring_peers(place, column, count), 4)
-    up_ring = Ring(w_up, ring_send.at[0], ring_recv.at[0], place, column)
-    down_ring = Ring(w_down, ring_send.at[1], ring_recv.at[1], place, column, down)
+    local_len = home_cotangent.shape[1]
+    level, parity = place // 2, place % 2
+    home_column, _ = home_of(place)
+    home_from = [(2 * scatter.quarter + i, home_column) for i in (0, 1)]
+    home_to = [(group_of(column, b), member_of(level)) for b in (0, 1)]
+    greet(wa_peers(place, column)[:2] + ring_peers(place, column, count) + home_from, 6)
+    rings = Pair(w_down, ring_send, ring_recv, 0, place, column, down)
     gather = WaGather(every, wa_send, wa_recv, place, column, PIECES, d_ffn)
-    keep_down = pltpu.make_async_copy(down, w_down.at[place], local.at[0])
-    keep_down.start()
+    rings.step(0)
+    rings.step(1)
+    load_rows = pltpu.make_async_copy(every_row, rows_in, local.at[3])
+    load_rows.start()
 
     def load(weights, target, sem):
         slab = weights.shape[1]
@@ -1374,13 +1422,13 @@
         pltpu.make_async_copy(target, target, sem).wait()
 
     load(w_gate, first_w, local.at[1])
+    load(w_up, second_w, local.at[2])
+    keep_down = pltpu.make_async_copy(down, w_down.at[place], local.at[0])
+    keep_down.start()
+    load_hidden = pltpu.make_async_copy(every_hidden, hidden, local.at[4])
+    load_hidden.start()
+    load_rows.wait()
     middle[...] = times_t(rows_in[...], full[...]).astype(jnp.bfloat16)
-    for i in range(7):
-        up_ring.step(i)
-    down_ring.step(0)
-    down_ring.step(1)
-    up_ring.finish()
-    load(w_up, second_w, local.at[2])
     loaded(first_w, local.at[1])
     loaded(second_w, local.at[2])
     rows, width = hidden.shape
@@ -1405,22 +1453,39 @@
 
     for q in range(4):
         quarter_rows(q)
-        down_ring.step(2 + q)
-    down_ring.step(6)
+        rings.step(2 + q)
+    rings.step(6)
     keep_down.wait()
-    down_ring.finish()
+    rings.finish()
+    moves = [
+        remote(
+            home_cotangent.at[b, pl.ds(i * scatter.size, scatter.size)],
+            my_cotangent.at[pl.ds(pl.multiple_of(parity * local_len + i * scatter.size, 8), scatter.size)],
+            home_send.at[b, i], home_recv.at[parity, i], home_to[b],
+        )
+        for i in range(local_len // scatter.size)
+        for b in (0, 1)
+    ]
+    for move in moves:
+        move.start()
     load(w_down, first_w, local.at[1])
     loaded(first_w, local.at[1])
     lefts = [(mixed, first_w, False, ad)]
     scatter.outward(lefts)
     scatter.inward(lefts)
+    load_hidden.wait()
     for i in range(PIECES):
         at, total, mid = scatter.piece(i)
+        source, k = divmod(i, PIECES // 2)
+        region = my_cotangent.at[at]
+        remote(
+            region, region, home_send.at[source, k], home_recv.at[source, k], home_from[source]
+        ).wait_recv()
         total = total + low_dot(mid, full[...])
         scale = rms_factor(total)
         layer_out[at, :] = (hidden[at, :] + total * scale * gain[...]).astype(jnp.bfloat16)
         mid_down[at, :] = mid
-        weighted = cotangent[at, :].astype(jnp.float32) * gain[...]
+        weighted = my_cotangent[at, :].astype(jnp.float32) * gain[...]
         mean = jnp.mean(total * weighted, axis=-1, keepdims=True)
         grad = scale * weighted - total * (scale * scale * scale * mean)
         d_ffn[at, :] = grad.astype(jnp.bfloat16)
@@ -1431,46 +1496,90 @@
         gather.forward(i)
     gather.finish()
     scatter.finish()
+    for move in moves:
+        move.wait_send()
     keep.wait()
 
 
 def feed_forward(rows_in, full, bg, bu, ad, hidden, cotangent, gain, w_gate, w_up, down):
-    f32, bf16 = jnp.float32, jnp.bfloat16
+    bf16 = jnp.bfloat16
     rows, width = hidden.shape
     length = rows_in.shape[0]
-    count, slab, units = w_up.shape
+    count, _, units = w_up.shape
     shape = jax.ShapeDtypeStruct
     wide = shape((length, units), bf16)
+    pieces = PIECES // 2
     return pl.pallas_call(
         ffn_kernel,
-        in_specs=[VMEM] * 8 + [ANY] * 3,
-        out_specs=[VMEM] * 7 + [ANY] * 3,
+        in_specs=[VMEM] * 5 + [ANY] * 6,
+        out_specs=[VMEM] * 8 + [ANY] * 2,
         out_shape=[
             wide, wide, wide, shape((length, LANES), bf16), shape((rows, width), bf16),
-            shape((rows, width), bf16), shape((rows, LANES), bf16),
-            shape((4, rows, width), bf16), shape(w_up.shape, bf16),
-            shape((count, *down.shape), bf16),
+            shape((rows, width), bf16), shape((rows, LANES), bf16), shape((rows, width), bf16),
+            shape((4, rows, width), bf16), shape((count, *down.shape), bf16),
         ],
         scratch_shapes=scatter_scratch(rows, width)
         + [
             DMA((3, PIECES)), DMA((3, PIECES)), DMA((2, 2, count - 1)), DMA((2, 2, count - 1)),
-            DMA((3,)), pltpu.VMEM((width, units), bf16), pltpu.VMEM((width, units), bf16),
+            DMA((5,)), pltpu.VMEM((width, units), bf16), pltpu.VMEM((width, units), bf16),
+            pltpu.VMEM((length, width), bf16), pltpu.VMEM((rows, width), jnp.float32),
+            DMA((2, pieces)), DMA((2, pieces)),
         ],
-        input_output_aliases={9: 8},
         name="feed_forward",
         compiler_params=params(4, vmem_limit_bytes=VMEM_BYTES),
-    )(rows_in, full, bg, bu, ad, hidden, cotangent, gain, w_gate, w_up, down)
+    )(full, bg, bu, ad, gain, rows_in, hidden, cotangent, w_gate, w_up, down)
 
 
 def ffn_back_kernel(
-    d_gate, d_up, w_gate, w_up, bg, bu, cotangent, branch, gain, full, mid_gu, d_mid_down, mixed,
-    seq_hidden, mid_down, d_ffn, layer_out,
+    bg, bu, cotangent, branch, gain, full, mid_gu, d_mid_down, mid_down, d_ffn, all_gate, all_up,
+    gate_weight, up_weight, all_mixed, all_hidden, layer_out,
     d_hidden, d_branch, grad_table, every, out_home, *refs,
 ):
     place, column = here()
     scatter = Scatter(refs[:SCATTER_REFS], place, column)
     grads = Grads(refs[SCATTER_REFS : SCATTER_REFS + GRADS_REFS], 4, place, column)
-    wa_send, wa_recv, home_send, home_recv, local = refs[SCATTER_REFS + GRADS_REFS :]
+    (
+        wa_send, wa_recv, home_send, home_recv, local, load_sem, d_gate, d_up, w_gate, w_up, mixed,
+        seq_hidden,
+    ) = refs[SCATTER_REFS + GRADS_REFS :]
+    rows, width = d_hidden.shape
+    step = 512
+
+    def rows_load(which, t):
+        at = pl.ds(pl.multiple_of(which * rows, rows), rows)
+        source, target = ((all_gate, d_gate), (all_up, d_up))[t]
+        return pltpu.make_async_copy(source.at[at], target.at[at], load_sem.at[t, which])
+
+    def weight_load(b, t):
+        at = pl.ds(b * step, step)
+        source, target = ((gate_weight, w_gate), (up_weight, w_up))[t]
+        return pltpu.make_async_copy(source.at[at], target.at[at], load_sem.at[2 + t, b])
+
+    outer = [flip(scatter.far, 2), scatter.far, flip(scatter.quarter, 2), scatter.quarter]
+    late = [
+        pltpu.make_async_copy(all_mixed, mixed, load_sem.at[4, 0]),
+        pltpu.make_async_copy(all_hidden, seq_hidden, load_sem.at[4, 1]),
+    ]
+    for t in (0, 1):
+        rows_load(outer[0], t).start()
+    for b in range(width // step):
+        for t in (0, 1):
+            weight_load(b, t).start()
+    for which in outer[1:]:
+        for t in (0, 1):
+            rows_load(which, t).start()
+    for load in late:
+        load.start()
+
+    def rows_ready(which):
+        for t in (0, 1):
+            rows_load(which, t).wait()
+
+    def block_ready(b):
+        for t in (0, 1):
+            weight_load(b, t).wait()
+
+    scatter.ready, scatter.block_ready = rows_ready, block_ready
     home = Home(layer_out, out_home, home_send, home_recv, place, column)
     greet(wa_peers(place, column) + home.sources(), 5)
     for i in (0, 1):
@@ -1479,8 +1588,8 @@
     lefts = [(d_gate, w_gate, True, bg), (d_up, w_up, True, bu)]
     scatter.outward(lefts)
     scatter.inward(lefts)
-    width, step = d_hidden.shape[1], 512
-    rows = d_hidden.shape[0]
+    for load in late:
+        load.wait()
 
     def grad_block(b, carry):
         cols = lanes(b, step)
@@ -1528,12 +1637,12 @@
 
 def ffn_back(arrays, layer_out):
     f32, bf16 = jnp.float32, jnp.bfloat16
-    rows, width = arrays[7].shape
-    units = arrays[0].shape[1]
+    rows, width = arrays[3].shape
+    length, units = arrays[10].shape
     shape = jax.ShapeDtypeStruct
     return pl.pallas_call(
         ffn_back_kernel,
-        in_specs=[VMEM] * len(arrays) + [ANY],
+        in_specs=[VMEM] * 10 + [ANY] * 7,
         out_specs=[VMEM] * 3 + [ANY] * 2,
         out_shape=[
             shape((rows, width), f32), shape((rows, width), bf16), shape((80, width), bf16),
@@ -1541,7 +1650,12 @@
         ],
         scratch_shapes=scatter_scratch(rows, width)
         + grads_scratch(width, units)
-        + [DMA((3, PIECES)), DMA((3, PIECES)), DMA((2, 1)), DMA((2, 1)), DMA(())],
+        + [
+            DMA((3, PIECES)), DMA((3, PIECES)), DMA((2, 1)), DMA((2, 1)), DMA(()), DMA((5, 4)),
+            pltpu.VMEM((length, units), bf16), pltpu.VMEM((length, units), bf16),
+            pltpu.VMEM((width, units), bf16), pltpu.VMEM((width, units), bf16),
+            pltpu.VMEM((length, units), bf16), pltpu.VMEM((length, width), bf16),
+        ],
         name="ffn_back",
         compiler_params=params(5, vmem_limit_bytes=VMEM_BYTES),
     )(*arrays, layer_out)
@@ -1549,8 +1663,8 @@
 
 def attend_back_kernel(
     d_rows, w_out, full, ao, query, key, value, qkv_raw, scales, gain_q, gain_k, cosine, sine,
-    doc_col, doc_row, w_qkv, b_qkv, d_hidden, tokens, attended, mid_qkv, mid_out, d_branch, table,
-    grad_home, tables, own_tables, *refs, back,
+    doc_col, doc_row, b_qkv, mid_qkv, mid_out, table, qkv_weight, all_hidden, all_tokens,
+    all_attended, all_branch, grad_home, tables, own_tables, *refs, back,
 ):
     place, column = here()
     count = tables.shape[0]
@@ -1558,8 +1672,19 @@
     sums = RowSums(refs[SCATTER_REFS : SCATTER_REFS + ROW_SUMS_REFS], place, column)
     (
         ring_send, ring_recv, home_send, home_recv, local, grad, t_rows, dk_sum, dv_sum, my_grad,
-        d_qkv, d_mid_out, own_table,
+        d_qkv, d_mid_out, own_table, load_sem, w_qkv, d_hidden, tokens, attended, d_branch,
     ) = refs[SCATTER_REFS + ROW_SUMS_REFS + GRADS_REFS :]
+    loads = [
+        pltpu.make_async_copy(source, target, load_sem.at[i])
+        for i, (source, target) in enumerate(
+            (
+                (qkv_weight, w_qkv), (all_tokens, tokens), (all_attended, attended),
+                (all_branch, d_branch), (all_hidden, d_hidden),
+            )
+        )
+    ]
+    for load in loads:
+        load.start()
     at = SCATTER_REFS + ROW_SUMS_REFS
     grads = Grads(refs[at : at + GRADS_REFS], 0, place, column)
     home = Home(my_grad, grad_home, home_send, home_recv, place, column)
@@ -1641,8 +1766,12 @@
 
     lax.fori_loop(0, length // rows, raw_rows, 0)
     lefts = [(d_qkv, w_qkv, True, b_qkv)]
+    for q in range(4):
+        scatter.adapt(q, lefts)
+    scatter.adapted = True
+    for load in loads:
+        load.wait()
     scatter.outward(lefts)
-    scatter.inward(lefts)
     step = 512
     quarter_rows = scatter.rows
 
@@ -1665,22 +1794,20 @@
     ] + [(3, dot_rows(d_mid_out[...], attended[...]))]
     grads.put(grads.cut, slice(0, part), by_kind((LANES, part), choices))
     grads.start()
+    scatter.inward(lefts)
+    own_table[0:16, :] = grads.summed()
+    for member, rows_here in grads.slices():
+        own_table[16:32, lanes(member, part)] = rows_here
+    own_ring.step(0)
+    own_ring.step(1)
     keep_own = pltpu.make_async_copy(own_table, own_tables.at[place], local.at[1])
+    keep_own.start()
     for i in range(PIECES):
         at, total, mid = scatter.piece(i)
         my_grad[at, :] = (d_hidden[at, :] + total + low_dot(mid, full[...])).astype(bf16)
+        own_ring.step(2 + i)
         home.copy(i // 2, PIECES // 2, i % 2).start()
-        if i == 0:
-            own_table[0:16, :] = grads.summed()
-            for member, rows_here in grads.slices():
-                own_table[16:32, lanes(member, part)] = rows_here
-            own_ring.step(0)
-            own_ring.step(1)
-            keep_own.start()
-        else:
-            own_ring.step(1 + i)
-    for i in (5, 6):
-        own_ring.step(i)
+    own_ring.step(6)
     ring.finish()
     own_ring.finish()
     scatter.finish()
@@ -1691,7 +1818,7 @@
     keep_own.wait()
 
 
-def attention_back(arrays, table, back, count):
+def attention_back(arrays, table, later, back, count):
     f32, bf16 = jnp.float32, jnp.bfloat16
     length, width = arrays[0].shape
     part = arrays[4].shape[1]
@@ -1699,7 +1826,7 @@
     shape = jax.ShapeDtypeStruct
     return pl.pallas_call(
         functools.partial(attend_back_kernel, back=back),
-        in_specs=[VMEM] * len(arrays) + [ANY],
+        in_specs=[VMEM] * 18 + [ANY] * 6,
         out_specs=[ANY] * 3,
         out_shape=[
             shape((2, rows // 2, width), bf16), shape((count, *table.shape), bf16),
@@ -1713,11 +1840,14 @@
             DMA((2, PIECES // 2)), DMA((2,)), pltpu.VMEM((length, part), bf16), pltpu.VMEM((length, 2 * part), f32),
             pltpu.VMEM((length, HEAD_DIM), f32), pltpu.VMEM((length, HEAD_DIM), f32),
             pltpu.VMEM((rows, width), bf16), pltpu.VMEM((length, 3 * part), bf16),
-            pltpu.VMEM((length, LANES), bf16), pltpu.VMEM((32, width), bf16),
+            pltpu.VMEM((length, LANES), bf16), pltpu.VMEM((32, width), bf16), DMA((5,)),
+            pltpu.VMEM((width, 3 * part), bf16), pltpu.VMEM((rows, width), f32),
+            pltpu.VMEM((length, width), bf16), pltpu.VMEM((length, part), bf16),
+            pltpu.VMEM((rows, width), bf16),
         ],
         name="attend_back",
         compiler_params=params(6, vmem_limit_bytes=VMEM_BYTES),
-    )(*arrays, table)
+    )(*arrays, table, *later)
 
 
 def per_group(
@@ -1778,14 +1908,15 @@
     )
     marks = jnp.pad(marks, ((0, own_rows - 1), (0, width - marks.shape[1])))
     narrow = jnp.concatenate([attention_up_adapters[:3], attention_down_adapters[3:]])
+    narrow = narrow.reshape(4, own_rows, 2, slice_heads, half, HEAD_DIM)
+    narrow = jnp.transpose(narrow, (4, 2, 1, 0, 3, 5)).reshape(wa, own_rows, width)
     wide = jnp.concatenate([feedforward_up_adapters, downproj_down_adapters[None]])
-    wide = jnp.pad(wide, ((0, 1), (0, 0), (0, 0)))
+    slices = jnp.concatenate([by_unit(wide.reshape(-1, hidden_units)), narrow], axis=1)
     table = jnp.concatenate(
         [
             attention_down_adapters[:3].reshape(-1, width), attention_up_adapters[3],
             feedforward_down_adapters.reshape(-1, width), downproj_up_adapters, marks,
-            by_head(narrow.reshape(-1, width)),
-            by_unit(wide.reshape(-1, hidden_units)).reshape(-1, width),
+            slices.reshape(-1, width),
         ],
         axis=0,
     )
@@ -1803,11 +1934,11 @@
     w_qkv = w_qkv.reshape(width, 3 * slice_width)
 
     marks = marks[:, :, 4]
-    adapter_of = marks[:, 0, 2 * local_len : 2 * local_len + 2].reshape(half, 2, 2)[:, ::-1]
+    adapter_of = marks[:, 0, 2 * local_len : 2 * local_len + 2].reshape(2, half, 2)[:, ::-1]
     adapter_of = jnp.transpose(adapter_of, (2, 1, 0)).reshape(groups).astype(jnp.int32)
     home_column, home_block = home_of(place)
     documents = lax.dynamic_slice(
-        marks, (flip(home_column, 1), 0, home_block * local_len), (1, groups, local_len)
+        marks, (quarter_of(home_column), 0, home_block * local_len), (1, groups, local_len)
     )
     documents = documents.reshape(length).astype(jnp.int32)
     doc_col, doc_row = documents[:, None], documents[None, :]
@@ -1822,21 +1953,22 @@
 
     (
         attended, query, key, value, qkv_raw, mid_qkv, scales, full, b_qkv, b_out, b_gate, b_up,
-        b_down, w_out, _, my_cotangent,
+        b_down, w_out, _, gate_slabs,
     ) = attend(
         seq_tokens, w_qkv, table, my_gain_q, my_gain_k, rope, doc_col, doc_row, output_weight,
-        cotangent.astype(bf16), window, groups,
+        gate_slabs, window, groups,
     )
     w_out = w_out.reshape(slice_width, width)
-    branch, hidden, mid_out, _, seq_hidden, gate_slabs = out_branch(
-        attended, w_out, b_out, gain_a, full, every_token, gate_slabs
+    branch, hidden, mid_out, _, seq_hidden, up_slabs = out_branch(
+        attended, w_out, b_out, gain_a, full, every_token, up_slabs
     )
     seq_hidden = seq_hidden.reshape(length, width)
-    gate, up_value, mixed, mid_gu, layer_out, d_ffn, mid_down, seq_d_ffn, up_slabs, down_slabs = (
-        feed_forward(
-            seq_hidden, full, b_gate, b_up, b_down, hidden, my_cotangent, gain_f, gate_slabs,
-            up_slabs, down_weight,
-        )
+    (
+        gate, up_value, mixed, mid_gu, layer_out, d_ffn, mid_down, my_cotangent, seq_d_ffn,
+        down_slabs,
+    ) = feed_forward(
+        seq_hidden, full, b_gate, b_up, b_down, hidden, cotangent.astype(bf16), gain_f, gate_slabs,
+        up_slabs, down_weight,
     )
     w_gate = gate_slabs.reshape(width, slice_units)
     w_up = up_slabs.reshape(width, slice_units)
@@ -1851,8 +1983,8 @@
     d_up = (d_mixed * gate * sigmoid).astype(bf16)
     d_hidden, d_branch, ffn_table, seq_d_branch, out_home = ffn_back(
         (
-            d_gate, d_up, w_gate, w_up, b_gate, b_up, my_cotangent, branch, gain_a, full, mid_gu,
-            d_mid_down, mixed, seq_hidden, mid_down, d_ffn,
+            b_gate, b_up, my_cotangent, branch, gain_a, full, mid_gu, d_mid_down, mid_down, d_ffn,
+            d_gate, d_up, w_gate, w_up, mixed, seq_hidden,
         ),
         layer_out,
     )
@@ -1860,10 +1992,9 @@
     grad_home, ffn_tables, attn_tables = attention_back(
         (
             seq_d_branch.reshape(length, width), w_out, full, b_out, query, key, value, qkv_raw,
-            scales, my_gain_q, my_gain_k, *rope, doc_col, doc_row, w_qkv, b_qkv, d_hidden,
-            seq_tokens, attended, mid_qkv, mid_out, d_branch,
+            scales, my_gain_q, my_gain_k, *rope, doc_col, doc_row, b_qkv, mid_qkv, mid_out,
         ),
-        ffn_table, window, groups,
+        ffn_table, (w_qkv, d_hidden, seq_tokens, attended, d_branch), window, groups,
     )
 
     shared = (adapter_of == place)[:, None, None]

time: 855 us -> 759 us (0.89)
  the two profiles are of different devices: /device:TPU:0 before, /device:TPU:6 now
where the time goes in v4:
time: 759 us; the launch traced here: 756 us
  Pallas kernels  697 us (92%)
  local copies, waits for them, and re-layouts  20.8 us (3%)
  matrix products  20.7 us (3%)
  other arithmetic  13.2 us (2%)
    pallas_call x1, Pallas kernels, feed_forward(): pl.pallas_call(ffn_kernel, in_specs=[VMEM] * 5 + [ANY] * 6, out_specs=[VM...  164 us
    pallas_call x1, Pallas kernels, attention_back(): pl.pallas_call(functools.partial(attend_back_kernel, back=back), in_specs...  127 us
    pallas_call x1, Pallas kernels, attend(): pl.pallas_call(functools.partial(attend_kernel, back=back), in_specs=[VME...  120 us
    pallas_call x1, Pallas kernels, fetch(): pl.pallas_call(fetch_kernel, in_specs=[VMEM] * 5, out_specs=[ANY] * 6, ou...  118 us
    pallas_call x1, Pallas kernels, out_branch(): pl.pallas_call(branch_kernel, in_specs=[VMEM] * 5 + [ANY] * 2, out_specs=...  86.9 us
    pallas_call x1, Pallas kernels, ffn_back(): pl.pallas_call(ffn_back_kernel, in_specs=[VMEM] * 10 + [ANY] * 7, out_spe...  81 us

profile of v4, /device:TPU:6, one launch (start us, length us, event | category | flops | bytes accessed | tf_op | source)
XLA Modules:
  0.0 755.5 jit_solution(15448397035065233227)
XLA Ops:
  0.7 1.1 reshape.164
  2.1 1.1 reshape.165
  3.5 1.1 reshape.166
  4.8 0.9 maximum_bitcast_fusion.qkv_parts
  6.9 4.2 concatenate.35.table
  11.1 118.3 %fetch.1 = (bf16[4,256,2048]{2,1,0:T(8,128)(2,1)}, bf16[8,256,1536]{2,1,0:T(8,128)(2,1)}, bf16[8,256,2048]{2,1,0:T(8,128)(2,1)}, bf16[8,256,2048]{2,1,0:T(8,128)...) custom-call(bf16[2,128,2048]{2,1,0:T(8,128)(2,1)} %tokens.1, ...), custom_call_target="tpu_custom_call" | custom-call | tf_op jit(solution)/shard_map/fetch/pallas_call | solution.py:1027
  129.5 1.5 slice.78
  131.0 0.6 convert_bitcast_fusion.2
  131.6 1.0 copy.52.doc_col
  135.8 1.8 dynamic-slice_bitcast_fusion.table
  138.2 1.9 fusion.9
  140.1 1.3 pad_maximum_fusion
  141.4 119.9 %attend.1 = (bf16[1024,512]{1,0:T(8,128)(2,1)}, bf16[1024,512]{1,0:T(8,128)(2,1)}, bf16[1024,512]{1,0:T(8,128)(2,1)}, bf16[1024,512]{1,0:T(8,128)(2,1)}, f32[102...) custom-call(bf16[96,2048]{1,0:T(8,128)(2,1)} %dynamic-slice_bitcast_, ...), custom_call_target="tpu_custom_call", output_to_operand_aliasing={{15}: (10, {})} | custom-call | tf_op jit(solution)/shard_map/attend/pallas_call | solution.py:1233
  261.4 0.6 broadcast_in_dim.52
  262.0 86.9 %out_branch.1 = (f32[256,2048]{1,0:T(8,128)}, f32[256,2048]{1,0:T(8,128)}, bf16[256,128]{1,0:T(8,128)(2,1)}, bf16[256,2048]{1,0:T(8,128)(2,1)}, bf16[4,256,2048]...) custom-call(bf16[1024,512]{1,0:T(8,128)(2,1)} %get-tuple-element.61.attended.all_attended, ...), custom_call_target="tpu_custom_call", output_to_operand_aliasing={{5}: (6, {})} | custom-call | tf_op jit(solution)/shard_map/out_branch/pallas_call | solution.py:1372
  348.9 1.1 convert_element_type.116.home_cotangent
  350.6 164.4 %feed_forward.1 = (bf16[1024,2048]{1,0:T(8,128)(2,1)}, bf16[1024,2048]{1,0:T(8,128)(2,1)}, bf16[1024,2048]{1,0:T(8,128)(2,1)}, bf16[1024,128]{1,0:T(8,128)(2,1)}...) custom-call(bf16[128,2048]{1,0:T(8,128)(2,1)} %get-tuple-element.59., ...), custom_call_target="tpu_custom_call" | custom-call | tf_op jit(solution)/shard_map/feed_forward/pallas_call | solution.py:1512
  515.1 12.7 %fusion.16 = f32[1024,2048]{1,0:T(8,128)S(1)} fusion(bf16[1024,2048]{1,0:T(8,128)(2,1)} %bitcast.123, bf16[2048,2048]{1,0:T(8,128)(2,1)} %bitcast.122), kind=kOutput, calls=%fused_computation.57 | convolution fusion | flops 8589934592 | bytes 20971520 | tf_op jit(solution)/shard_map/dot_general | solution.py:44
  527.9 1.3 convolution_convert_fusion.d_mid_down
  529.2 1.1 copy-done.16
  530.3 6.8 fusion.8
  537.1 81.0 %ffn_back.1 = (f32[256,2048]{1,0:T(8,128)}, bf16[256,2048]{1,0:T(8,128)(2,1)}, bf16[80,2048]{1,0:T(8,128)(2,1)}, bf16[4,256,2048]{2,1,0:T(8,128)(2,1)}, bf16[2,128,2048]{2,1,0:T(8,128)(2,1)}) custom-call(bf16[128,2048]{1,0:T(8,128)(2,1)} %get-tuple-element.57.bg, bf16[128,2048]{1,0:T(8,128)(2,1)} %get-tuple-element.58.bu, ...), custom_call_target="tpu_custom_call" | custom-call | tf_op jit(solution)/shard_map/ffn_back/pallas_call | solution.py:1643
  618.1 126.5 %attend_back.1 = (bf16[2,128,2048]{2,1,0:T(8,128)(2,1)}, bf16[8,80,2048]{2,1,0:T(8,128)(2,1)}, bf16[8,32,2048]{2,1,0:T(8,128)(2,1)}) custom-call(bf16[1024,2048]{1,0:T(8,128)(2,1)} %bitcast.100, bf16[512,2048]{1,0:T(8,128)(2,1)} %bitcast.99, bf16[128,2048]{1,0:T(8,128)(2,1)} %get-tuple-element.59.bo.full, bf16[128,512]{1,0:T(8,128)(2,1)} %get-tuple-element.63.ao, ...), custom_call_target="tpu_custom_call" | custom-call | tf_op jit(solution)/shard_map/attend_back/pallas_call | solution.py:1827
  744.7 2.5 select_reduce_fusion
  747.6 0.9 slice.93
  748.6 0.7 squeeze.22
  749.4 0.7 slice.90
  750.0 0.6 slice.106
  751.2 0.7 pad_maximum_fusion.5
  752.1 0.7 pad_maximum_fusion.4
  752.7 1.6 convert_element_type.122
  754.3 1.0 copy.78
  (107 shorter events, 5.2 us)
Async XLA Ops:
  0.6 5.1 copy-start.9
  0.6 5.1 copy-start.8
  0.7 5.6 slice-start.2
  0.7 5.6 slice-start
  2.0 4.8 slice-start.1
  2.1 4.7 copy-start.10
  2.1 4.7 copy-start.19
  2.1 4.8 copy-start.20
  2.1 4.8 copy-start.7
  2.1 4.8 copy-start.11
  6.6 130.9 %copy-start.12 = (bf16[2048]{0:T(1024)(128)(2,1)S(1)}, bf16[2048]{0:T(1024)(128)(2,1)}, u32[]{:S(2)}) copy-start(bf16[2048]{0:T(1024)(128)(2,1)} %param.32) | copy-start | bytes 12292
  6.6 130.9 %copy-start.13 = (bf16[2048]{0:T(1024)(128)(2,1)S(1)}, bf16[2048]{0:T(1024)(128)(2,1)}, u32[]{:S(2)}) copy-start(bf16[2048]{0:T(1024)(128)(2,1)} %param.33) | copy-start | bytes 12292
  141.4 119.9 %copy-start.14 = (bf16[2048]{0:T(1024)(128)(2,1)S(1)}, bf16[2048]{0:T(1024)(128)(2,1)}, u32[]{:S(2)}) copy-start(bf16[2048]{0:T(1024)(128)(2,1)} %param.34) | copy-start | bytes 12292
  262.0 86.9 %copy-start.1 = (f32[2,128,2048]{2,1,0:T(8,128)S(1)}, f32[2,128,2048]{2,1,0:T(8,128)}, u32[]{:S(2)}) copy-start(f32[2,128,2048]{2,1,0:T(8,128)} %param.22) | copy-start | bytes 6291460
  262.0 88.1 %copy-start.15 = (bf16[2048]{0:T(1024)(128)(2,1)S(1)}, bf16[2048]{0:T(1024)(128)(2,1)}, u32[]{:S(2)}) copy-start(bf16[2048]{0:T(1024)(128)(2,1)} %param.35) | copy-start | bytes 12292
  515.1 12.7 %copy-start = (bf16[128,2048]{1,0:T(8,128)(2,1)S(1)}, bf16[128,2048]{1,0:T(8,128)(2,1)}, u32[]{:S(2)}) copy-start(bf16[128,2048]{1,0:T(8,128)(2,1)} %get-tuple-element.59.bo.full) | copy-start | bytes 1572868
  515.1 12.7 %copy-start.18 = (bf16[4,256,2048]{2,1,0:T(8,128)(2,1)S(1)}, bf16[4,256,2048]{2,1,0:T(8,128)(2,1)}, u32[]{:S(2)}) copy-start(bf16[4,256,2048]{2,1,0:T(8,128)(2,1)} %get-tuple-element.72) | copy-start | bytes 12582916
  515.1 14.0 %copy-start.17 = (bf16[1024,2048]{1,0:T(8,128)(2,1)S(1)}, bf16[1024,2048]{1,0:T(8,128)(2,1)}, u32[]{:S(2)}) copy-start(bf16[1024,2048]{1,0:T(8,128)(2,1)} %get-tuple-element.76) | copy-start | bytes 12582916
  527.8 1.3 copy-start.5
  527.9 2.4 copy-start.16
  529.1 8.0 %copy-start.6 = (bf16[1024,128]{1,0:T(8,128)(2,1)}, bf16[1024,128]{1,0:T(8,128)(2,1)S(1)}, u32[]{:S(2)}) copy-start(bf16[1024,128]{1,0:T(8,128)(2,1)S(1)} %convolution_convert_fusion.d_mid_down) | copy-start | bytes 786436
  744.7 5.9 copy-start.3
  747.2 5.6 copy-start.2
  750.9 3.4 copy-start.4

commit v5 on v4

--- a/solution.py
+++ b/solution.py
@@ -3,6 +3,7 @@
 
 import jax
 import jax.numpy as jnp
+import numpy as np
 from jax import lax
 from jax.experimental import pallas as pl
 from jax.experimental.pallas import tpu as pltpu
@@ -479,21 +480,15 @@
     )
 
 
-def block_scores(query, key, doc_col, doc_row, row, first, rows):
-    scores = lax.dot_general(
-        query, key, (((1,), (1,)), ((), ())), preferred_element_type=jnp.float32
-    ) * (1.0 / math.sqrt(HEAD_DIM))
-    shape = scores.shape
+def seen_bias(doc_col, doc_row, row, first):
+    shape = (doc_col.shape[0], doc_row.shape[1])
     row_at = row + lax.broadcasted_iota(jnp.int32, shape, 0)
     key_at = first + lax.broadcasted_iota(jnp.int32, shape, 1)
-    allowed = (key_at <= row_at) & (doc_col == doc_row)
-    return jnp.where(allowed, scores, MASKED)
-
-
-def soft(scores):
-    top = jnp.max(scores, axis=1, keepdims=True)
-    raised = jnp.exp(scores - top)
-    return raised * (1.0 / jnp.sum(raised, axis=1, keepdims=True))
+    return jnp.where((key_at <= row_at) & (doc_col == doc_row), 0.0, MASKED)
+
+
+def two_scores(query, key, bias):
+    return times_t(query, key) * (1.0 / math.sqrt(HEAD_DIM) / math.log(2.0)) + bias
 
 
 MESH = pl.DeviceIdType.MESH
@@ -507,11 +502,23 @@
     )
 
 
-def greet(sources, count):
+def hello(sources):
     barrier = pltpu.get_barrier_semaphore()
     for device in sources:
         pl.semaphore_signal(barrier, inc=1, device_id=device, device_id_type=MESH)
-    pl.semaphore_wait(barrier, count)
+
+
+def welcome(count):
+    pl.semaphore_wait(pltpu.get_barrier_semaphore(), count)
+
+
+def greet(sources, count):
+    hello(sources)
+    welcome(count)
+
+
+def head_at(member, i):
+    return (HEADS // 2 * (member % 2) + 2 * i + member // 2) * HEAD_DIM
 
 
 def flip(index, bit):
@@ -650,6 +657,20 @@
         self.copy(1, i, self.far).wait_recv()
         self.copy(2, i, self.far).start()
 
+    def near_here(self):
+        for i in range(self.pieces):
+            self.copy(0, i, flip(self.quarter, 2)).wait_recv()
+
+    def last_here(self, pieces=None):
+        for i in range(self.pieces) if pieces is None else pieces:
+            self.copy(2, i, flip(self.far, 2)).wait_recv()
+
+    def sent(self):
+        for i in range(self.pieces):
+            for kind in (0, 1):
+                self.copy(kind, i).wait_send()
+            self.copy(2, i, self.far).wait_send()
+
     def finish(self):
         for i in range(self.pieces):
             self.copy(0, i, flip(self.quarter, 2)).wait_recv()
@@ -682,11 +703,12 @@
         self.pieces = PIECES
         self.size = self.rows // self.pieces
         self.sent = []
-        self.ready, self.block_ready, self.adapted = None, None, False
-
-    def product(self, which, lefts):
-        width, step = self.partial.shape[2], 512
-        at = pl.ds(pl.multiple_of(which * self.rows, self.rows), self.rows)
+        self.adapted = False
+
+    def product(self, which, lefts, part=0, parts=1):
+        width, step = self.partial.shape[2], 1024
+        size = self.rows // parts
+        at = pl.ds(pl.multiple_of(which * self.rows + part * size, size), size)
 
         def block(b, carry):
             cols = lanes(b, step)
@@ -697,19 +719,11 @@
                 else:
                     term = low_dot(left[at, :], weight[:, cols])
                 total = term if total is None else total + term
-            self.partial[which, :, cols] = total.astype(jnp.bfloat16)
+            self.partial[which, part * size : (part + 1) * size, cols] = total.astype(jnp.bfloat16)
             return carry
 
-        if self.ready is not None:
-            self.ready(which)
-        if self.block_ready is None:
-            lax.fori_loop(0, width // step, block, 0)
-        else:
-            for b in range(width // step):
-                self.block_ready(b)
-                block(b, 0)
-            self.block_ready = None
-        if not self.adapted:
+        lax.fori_loop(0, width // step, block, 0)
+        if not self.adapted and part == parts - 1:
             self.adapt(which, lefts)
 
     def adapt(self, which, lefts):
@@ -747,14 +761,9 @@
         i = 4 + self.pieces
         return remote(self.chip_mid, self.last_mid, self.send.at[i], self.recv.at[i], self.across)
 
-    def outward(self, lefts):
+    def pass_on(self):
         f32, bf16 = jnp.float32, jnp.bfloat16
-        which = flip(self.far, 2)
-        self.product(which, lefts)
-        for copy in self.to_near(0, which):
-            self.begin(copy)
-        self.product(self.far, lefts)
-        for copy in self.to_near(0, which):
+        for copy in self.to_near(0, flip(self.far, 2)):
             copy.wait_recv()
         self.chip_mid[...] = (
             self.middle[self.far].astype(f32) + self.first_mid[0].astype(f32)
@@ -767,15 +776,27 @@
             ).astype(bf16)
             self.begin(self.across_copy(i))
 
-    def inward(self, lefts):
-        which = flip(self.quarter, 2)
-        self.product(which, lefts)
-        for copy in self.to_near(1, which):
+    def give(self, slot):
+        which = flip(self.quarter if slot else self.far, 2)
+        for copy in self.to_near(slot, which):
             self.begin(copy)
-        self.product(self.quarter, lefts)
-        for copy in self.to_near(1, which):
+
+    def take(self):
+        for copy in self.to_near(1, flip(self.quarter, 2)):
             copy.wait_recv()
         self.across_mid().wait_recv()
+
+    def outward(self, lefts):
+        self.product(flip(self.far, 2), lefts)
+        self.give(0)
+        self.product(self.far, lefts)
+        self.pass_on()
+
+    def inward(self, lefts):
+        self.product(flip(self.quarter, 2), lefts)
+        self.give(1)
+        self.product(self.quarter, lefts)
+        self.take()
 
     def piece(self, i):
         f32 = jnp.float32
@@ -855,6 +876,11 @@
     return lax.rsqrt(jnp.mean(values * values, axis=-1, keepdims=True) + EPSILON)
 
 
+def head_gain(gain, column, h):
+    head = HEADS // 2 * (column % 2) + 2 * h + column // 2
+    return gain[:, lanes(head, HEAD_DIM)].astype(jnp.float32)
+
+
 class RowSums:
     def __init__(self, refs, place, column):
         self.columns, self.mine, self.theirs, self.send, self.recv = refs
@@ -898,10 +924,11 @@
 
 
 def fetch_kernel(
-    tokens, qkv_parts, gate, up, table,
-    all_tokens, w_qkv, w_gate, w_up, tables, marks,
+    tokens, query_w, key_w, value_w, gate, up, attn_down, attn_up, ffn_down, ffn_up, down_down,
+    down_up, numbers, cotangent, frequencies,
+    all_tokens, w_qkv, w_gate, w_up, tables, marks, low_cotangent, cosine, sine,
     home_send, home_recv, part_send, part_recv, wa_send, wa_recv, mark_send, mark_recv,
-    ring_send, ring_recv, local,
+    ring_send, ring_recv, local, qkv_parts, wide_table, table,
 ):
     place, column = here()
     count = w_qkv.shape[0]
@@ -914,7 +941,15 @@
     ring_near = ring_peers(place, column, count)
     home_from = [(2 * quarter, home_column), (2 * quarter + 1, home_column)]
     home_to = [(group_of(column, b), member) for b in (0, 1)]
-    greet(home_from + near_far + ring_near, 7)
+    hello(home_from + near_far + ring_near)
+    f32, bf16 = jnp.float32, jnp.bfloat16
+    heads = HEADS // 4
+    for w in range(4):
+        for t, weight in enumerate((query_w, key_w, value_w)):
+            for i in range(heads):
+                at, to = head_at(w, i), (t * heads + i) * HEAD_DIM
+                qkv_parts[w, :, to : to + HEAD_DIM] = weight[:, at : at + HEAD_DIM]
+    welcome(7)
 
     rows = qkv_parts.shape[1]
     ours = pl.ds(pl.multiple_of(column * rows, rows), rows)
@@ -943,6 +978,25 @@
     ]
     for move in moves:
         move.start()
+    full_rows = [attn_down[t] for t in range(3)] + [attn_up[3]]
+    full_rows += [ffn_down[t] for t in range(2)] + [down_up[...], numbers[...]]
+    for t, value in enumerate(full_rows):
+        wide_table[4 * t : 4 * t + 4, :] = value.astype(f32)
+    for w in range(4):
+        first = SLICES + 16 * w
+        for t, source in enumerate((ffn_up.at[0], ffn_up.at[1], down_down)):
+            for b in range(count):
+                at = (4 * b + w) * block
+                wide_table[first + 4 * t : first + 4 * t + 4, b * block : (b + 1) * block] = (
+                    source[:, at : at + block].astype(f32)
+                )
+        for t, source in enumerate((attn_up.at[0], attn_up.at[1], attn_up.at[2], attn_down.at[3])):
+            for i in range(heads):
+                at, to = head_at(w, i), (t * heads + i) * HEAD_DIM
+                wide_table[first + 12 : first + 16, to : to + HEAD_DIM] = (
+                    source[:, at : at + HEAD_DIM].astype(f32)
+                )
+    table[...] = wide_table[...].astype(bf16)
     table_ring = Ring(tables, ring_send.at[1], ring_recv.at[1], place, column, table)
     table_ring.step(0)
     table_ring.step(1)
@@ -967,6 +1021,14 @@
         region = gather.region(quarter, i)
         remote(region, region, home_send.at[i], home_recv.at[i], home_from[i]).wait_recv()
         gather.own(i)
+    low_cotangent[...] = cotangent[...].astype(bf16)
+    length = cosine.shape[0]
+    for row in range(0, length, 256):
+        at = row + lax.broadcasted_iota(jnp.int32, (256, HEAD_DIM), 0)
+        angle = at.astype(f32) * frequencies[...]
+        lane = lax.broadcasted_iota(jnp.int32, (256, HEAD_DIM), 1)
+        cosine[row : row + 256, :] = jnp.cos(angle)
+        sine[row : row + 256, :] = jnp.where(lane < HEAD_DIM // 2, -1.0, 1.0) * jnp.sin(angle)
     for i in (4, 5):
         table_ring.step(i)
     qkv_ring.step(2)
@@ -1018,28 +1080,36 @@
             ).wait_send()
 
 
-def fetch(tokens, qkv_parts, gate, up, table, count):
-    bf16 = jnp.bfloat16
+def fetch(tokens, qkv, gate, up, adapter_arrays, numbers, cotangent, count):
+    bf16, f32 = jnp.bfloat16, jnp.float32
     width = tokens.shape[2]
-    slab = 4 * qkv_parts.shape[1]
+    rows, part = qkv[0].shape[0], 3 * width // 4
     units = gate.shape[1] // 4
+    length = tokens.shape[1] * count
     shape = lambda *dims: jax.ShapeDtypeStruct(dims, bf16)
+    rope = jax.ShapeDtypeStruct((length, HEAD_DIM), f32)
+    powers = np.arange(0, HEAD_DIM, 2, dtype=np.float32) / np.float32(HEAD_DIM)
+    frequencies = np.float32(1.0) / np.power(np.float32(ROPE_BASE), powers)
+    frequencies = jnp.asarray(np.concatenate([frequencies, frequencies])[None])
     return pl.pallas_call(
         fetch_kernel,
-        in_specs=[VMEM] * 5,
-        out_specs=[ANY] * 6,
+        in_specs=[VMEM] * 15,
+        out_specs=[ANY] * 6 + [VMEM] * 3,
         out_shape=[
-            shape(4, 2 * tokens.shape[1], width), shape(count, slab, qkv_parts.shape[2]),
-            shape(count, slab, units), shape(count, slab, units), shape(count, *table.shape),
-            shape(4, count, 8, width),
+            shape(4, 2 * tokens.shape[1], width), shape(count, 4 * rows, part),
+            shape(count, 4 * rows, units), shape(count, 4 * rows, units),
+            shape(count, SLICES + 64, width), shape(4, count, 8, width), shape(*cotangent.shape),
+            rope, rope,
         ],
         scratch_shapes=[
             DMA((2,)), DMA((2,)), DMA((3, 3)), DMA((3, 3)), DMA((3, 2)), DMA((3, 2)),
             DMA((3,)), DMA((3,)), DMA((2, 2, count - 1)), DMA((2, 2, count - 1)), DMA((5,)),
+            pltpu.VMEM((4, rows, part), bf16), pltpu.VMEM((SLICES + 64, width), f32),
+            pltpu.VMEM((SLICES + 64, width), bf16),
         ],
         name="fetch",
-        compiler_params=params(1),
-    )(tokens, qkv_parts, gate, up, table)
+        compiler_params=params(1, vmem_limit_bytes=VMEM_BYTES),
+    )(tokens, *qkv, gate, up, *adapter_arrays, numbers, cotangent, frequencies)
 
 
 KINDS = 8
@@ -1101,14 +1171,14 @@
 
 def attend_kernel(
     table, gain_q, gain_k, cosine, sine, doc_col, doc_row, every_token, qkv_weight, out_part,
-    _gate, attended, query, key, value, qkv_raw, middle, scales, full, b_qkv, b_out, b_gate, b_up,
-    b_down, w_out, out_slabs, w_gate, *refs, back,
+    _gate, attended, middle, scales, full, b_qkv, b_out, b_gate, b_up, b_down, w_out,
+    query_out, key_out, value_out, qkv_raw_out, out_slabs, w_gate, *refs, back,
 ):
     place, column = here()
     sums = RowSums(refs[:ROW_SUMS_REFS], place, column)
     (
         ring_send, ring_recv, local, out_send, out_recv, slices, table_send, table_recv,
-        table_local, tokens, w_qkv,
+        table_local, tokens, w_qkv, query, key, value, qkv_raw, write_sem,
     ) = refs[ROW_SUMS_REFS:]
     loads = [
         pltpu.make_async_copy(every_token, tokens, local.at[2]),
@@ -1180,26 +1250,45 @@
     gate_rings.step(3)
     ring.step(6)
 
-    def head(h, carry):
-        cols = pl.ds(pl.multiple_of(h * HEAD_DIM, HEAD_DIM), HEAD_DIM)
+    def turn(h, carry):
+        cols = lanes(h, HEAD_DIM)
         k_cols = pl.ds(pl.multiple_of(part + h * HEAD_DIM, HEAD_DIM), HEAD_DIM)
         for lane, at, gain, target in ((0, cols, gain_q, query), (1, k_cols, gain_k, key)):
-            normed = qkv_raw[:, at] * scales[:, lane : lane + 1] * gain[:, cols]
+            normed = qkv_raw[:, at] * scales[:, lane : lane + 1] * head_gain(gain, column, h)
             turned = normed * cosine[...] + pltpu.roll(normed, HEAD_DIM // 2, 1) * sine[...]
             target[:, cols] = turned.astype(bf16)
-        for row in range(0, length, rows):
-            first, last = max(0, row - back), row + rows
-            scores = block_scores(
-                query[row:last, cols], key[first:last, cols], doc_col[row:last, :],
-                doc_row[:, first:last], row, first, rows,
-            )
-            probs = soft(scores).astype(bf16)
-            attended[row:last, cols] = low_dot(probs, value[first:last, cols]).astype(bf16)
-        pl.when(h == 1)(functools.partial(gate_rings.step, 4))
-        pl.when(h == 3)(functools.partial(gate_rings.step, 5))
         return carry
 
-    lax.fori_loop(0, part // HEAD_DIM, head, 0)
+    heads = part // HEAD_DIM
+    lax.fori_loop(0, heads, turn, 0)
+    writes = [
+        pltpu.make_async_copy(source, target, write_sem.at[i])
+        for i, (source, target) in enumerate(
+            ((qkv_raw, qkv_raw_out), (query, query_out), (key, key_out), (value, value_out))
+        )
+    ]
+    for write in writes:
+        write.start()
+    for i, row in enumerate(range(0, length, rows)):
+        first, last = max(0, row - back), row + rows
+        bias = seen_bias(doc_col[row:last, :], doc_row[:, first:last], row, first)
+
+        def head(h, carry, row=row, first=first, last=last, bias=bias):
+            cols = lanes(h, HEAD_DIM)
+            scores = two_scores(query[row:last, cols], key[first:last, cols], bias)
+            top = jnp.max(scores, axis=1, keepdims=True)
+            raised = jnp.exp2(scores - top)
+            total = jnp.sum(raised, axis=1, keepdims=True)
+            summed = low_dot(raised.astype(bf16), value[first:last, cols])
+            attended[row:last, cols] = (summed * (1.0 / total)).astype(bf16)
+            lane = lax.broadcasted_iota(jnp.int32, (rows, LANES), 1)
+            log_total = top + jnp.log(total) * (1.0 / math.log(2.0))
+            scales[row:last, :] = jnp.where(lane == 2 + h, log_total, scales[row:last, :])
+            return carry
+
+        lax.fori_loop(0, heads, head, 0)
+        if i % 2 == 1:
+            gate_rings.step(4 + i // 2)
     keep.wait()
     ring.finish()
     core, some = column % 2, count // 2
@@ -1220,6 +1309,8 @@
     gate_rings.finish()
     adapters.finish()
     sums.finish()
+    for write in writes:
+        write.wait()
 
 
 def attend(
@@ -1233,12 +1324,12 @@
     return pl.pallas_call(
         functools.partial(attend_kernel, back=back),
         in_specs=[VMEM] * 7 + [ANY] * 4,
-        out_specs=[VMEM] * 14 + [ANY] * 2,
+        out_specs=[VMEM] * 10 + [ANY] * 6,
         out_shape=[
-            low, low, low, low, shape((length, 2 * part), f32), shape((length, LANES), bf16),
-            shape((length, LANES), f32), maps, shape((LANES, 3 * part), bf16),
-            shape((LANES, part), bf16), maps, maps, maps,
-            shape((count // 2, 2, *out_part.shape), bf16), shape((count, *out_part.shape), bf16),
+            low, shape((length, LANES), bf16), shape((length, LANES), f32), maps,
+            shape((LANES, 3 * part), bf16), shape((LANES, part), bf16), maps, maps, maps,
+            shape((count // 2, 2, *out_part.shape), bf16), low, low, low,
+            shape((length, 2 * part), f32), shape((count, *out_part.shape), bf16),
             shape(w_gate.shape, bf16),
         ],
         scratch_shapes=row_sums_scratch(length)
@@ -1246,6 +1337,8 @@
             DMA((3, 2, count - 1)), DMA((3, 2, count - 1)), DMA((4,)), DMA(()), DMA(()),
             pltpu.VMEM((4, 16, width), bf16), DMA((3, 2)), DMA((3, 2)), DMA((2,)),
             pltpu.VMEM(tokens.shape, bf16), pltpu.VMEM(w_qkv.shape, bf16),
+            pltpu.VMEM((length, part), bf16), pltpu.VMEM((length, part), bf16),
+            pltpu.VMEM((length, part), bf16), pltpu.VMEM((length, 2 * part), f32), DMA((4,)),
         ],
         input_output_aliases={10: 15},
         name="attend",
@@ -1345,7 +1438,7 @@
             rings.step(2 + i // 2)
         at, total, middle = scatter.piece(i)
         total = total + low_dot(middle, bo[...])
-        rows = tokens[at, :].astype(jnp.float32) + total * rms_factor(total) * gain[...]
+        rows = tokens[at, :].astype(jnp.float32) + total * rms_factor(total) * gain[...].astype(jnp.float32)
         branch[at, :] = total
         hidden[at, :] = rows
         mid_out[at, :] = middle
@@ -1390,14 +1483,13 @@
 
 def ffn_kernel(
     full, bg, bu, ad, gain, every_row, every_hidden, home_cotangent, w_gate, w_up, down,
-    gate_low, up_low, mixed, middle, layer_out, d_ffn, mid_down, my_cotangent, every, w_down,
-    *refs,
+    middle, layer_out, d_ffn, mid_down, my_cotangent, gate_out, up_out, mixed_out, w_down, *refs,
 ):
     place, column = here()
     scatter = Scatter(refs[:SCATTER_REFS], place, column)
     (
-        wa_send, wa_recv, ring_send, ring_recv, local, first_w, second_w, rows_in, hidden,
-        home_send, home_recv,
+        ring_send, ring_recv, local, first_w, second_w, rows_in, hidden, home_send, home_recv,
+        gate_low, up_low, mixed, write_sem,
     ) = refs[SCATTER_REFS:]
     count = w_up.shape[0]
     local_len = home_cotangent.shape[1]
@@ -1407,7 +1499,6 @@
     home_to = [(group_of(column, b), member_of(level)) for b in (0, 1)]
     greet(wa_peers(place, column)[:2] + ring_peers(place, column, count) + home_from, 6)
     rings = Pair(w_down, ring_send, ring_recv, 0, place, column, down)
-    gather = WaGather(every, wa_send, wa_recv, place, column, PIECES, d_ffn)
     rings.step(0)
     rings.step(1)
     load_rows = pltpu.make_async_copy(every_row, rows_in, local.at[3])
@@ -1444,15 +1535,24 @@
             cols = pl.ds(pl.multiple_of(b * step, step), step)
             gate = one(first_w, bg, at, cols)
             up = one(second_w, bu, at, cols)
-            gate_low[at, cols] = gate.astype(jnp.bfloat16)
-            up_low[at, cols] = up.astype(jnp.bfloat16)
-            mixed[at, cols] = (gate * jax.nn.sigmoid(gate) * up).astype(jnp.bfloat16)
+            sigmoid = jax.nn.sigmoid(gate)
+            active = gate * sigmoid
+            gate_low[at, cols] = (up * (sigmoid + active * (1.0 - sigmoid))).astype(jnp.bfloat16)
+            up_low[at, cols] = active.astype(jnp.bfloat16)
+            mixed[at, cols] = (active * up).astype(jnp.bfloat16)
             return carry
 
         lax.fori_loop(0, units // step, block, 0)
 
+    writes = []
     for q in range(4):
         quarter_rows(q)
+        at = pl.ds(q * rows, rows)
+        for t, (source, target) in enumerate(
+            ((gate_low, gate_out), (up_low, up_out), (mixed, mixed_out))
+        ):
+            writes.append(pltpu.make_async_copy(source.at[at], target.at[at], write_sem.at[t, q]))
+            writes[-1].start()
         rings.step(2 + q)
     rings.step(6)
     keep_down.wait()
@@ -1483,22 +1583,17 @@
         ).wait_recv()
         total = total + low_dot(mid, full[...])
         scale = rms_factor(total)
-        layer_out[at, :] = (hidden[at, :] + total * scale * gain[...]).astype(jnp.bfloat16)
+        layer_out[at, :] = (hidden[at, :] + total * scale * gain[...].astype(jnp.float32)).astype(jnp.bfloat16)
         mid_down[at, :] = mid
-        weighted = my_cotangent[at, :].astype(jnp.float32) * gain[...]
+        weighted = my_cotangent[at, :].astype(jnp.float32) * gain[...].astype(jnp.float32)
         mean = jnp.mean(total * weighted, axis=-1, keepdims=True)
         grad = scale * weighted - total * (scale * scale * scale * mean)
         d_ffn[at, :] = grad.astype(jnp.bfloat16)
-        gather.own(i)
-    keep = pltpu.make_async_copy(d_ffn, every.at[gather.quarter], local.at[0])
-    keep.start()
-    for i in range(PIECES):
-        gather.forward(i)
-    gather.finish()
     scatter.finish()
     for move in moves:
         move.wait_send()
-    keep.wait()
+    for write in writes:
+        write.wait()
 
 
 def feed_forward(rows_in, full, bg, bu, ad, hidden, cotangent, gain, w_gate, w_up, down):
@@ -1512,18 +1607,19 @@
     return pl.pallas_call(
         ffn_kernel,
         in_specs=[VMEM] * 5 + [ANY] * 6,
-        out_specs=[VMEM] * 8 + [ANY] * 2,
+        out_specs=[VMEM] * 5 + [ANY] * 4,
         out_shape=[
-            wide, wide, wide, shape((length, LANES), bf16), shape((rows, width), bf16),
-            shape((rows, width), bf16), shape((rows, LANES), bf16), shape((rows, width), bf16),
-            shape((4, rows, width), bf16), shape((count, *down.shape), bf16),
+            shape((length, LANES), bf16), shape((rows, width), bf16), shape((rows, width), bf16),
+            shape((rows, LANES), bf16), shape((rows, width), bf16), wide, wide, wide,
+            shape((count, *down.shape), bf16),
         ],
         scratch_shapes=scatter_scratch(rows, width)
         + [
-            DMA((3, PIECES)), DMA((3, PIECES)), DMA((2, 2, count - 1)), DMA((2, 2, count - 1)),
+            DMA((2, 2, count - 1)), DMA((2, 2, count - 1)),
             DMA((5,)), pltpu.VMEM((width, units), bf16), pltpu.VMEM((width, units), bf16),
             pltpu.VMEM((length, width), bf16), pltpu.VMEM((rows, width), jnp.float32),
-            DMA((2, pieces)), DMA((2, pieces)),
+            DMA((2, pieces)), DMA((2, pieces)), pltpu.VMEM((length, units), bf16),
+            pltpu.VMEM((length, units), bf16), pltpu.VMEM((length, units), bf16), DMA((3, 4)),
         ],
         name="feed_forward",
         compiler_params=params(4, vmem_limit_bytes=VMEM_BYTES),
@@ -1531,84 +1627,118 @@
 
 
 def ffn_back_kernel(
-    bg, bu, cotangent, branch, gain, full, mid_gu, d_mid_down, mid_down, d_ffn, all_gate, all_up,
-    gate_weight, up_weight, all_mixed, all_hidden, layer_out,
-    d_hidden, d_branch, grad_table, every, out_home, *refs,
+    bg, bu, ad, cotangent, branch, gain, full, mid_gu, mid_down, own_d_ffn, gate_low, up_low,
+    gate_weight, up_weight, down_weight, all_mixed, all_hidden, layer_out,
+    d_hidden, d_branch, grad_table, out_home, *refs,
 ):
     place, column = here()
     scatter = Scatter(refs[:SCATTER_REFS], place, column)
     grads = Grads(refs[SCATTER_REFS : SCATTER_REFS + GRADS_REFS], 4, place, column)
     (
-        wa_send, wa_recv, home_send, home_recv, local, load_sem, d_gate, d_up, w_gate, w_up, mixed,
-        seq_hidden,
+        wa_send, wa_recv, load_sem, every, d_gate, d_up, w_gate, w_up, w_down, d_mid_down,
+        home_send, home_recv,
     ) = refs[SCATTER_REFS + GRADS_REFS :]
     rows, width = d_hidden.shape
-    step = 512
+    units, step = d_gate.shape[1], 1024
+    quarter, far = scatter.quarter, scatter.far
+    outer = [quarter, flip(quarter, 2), flip(far, 2), far]
 
     def rows_load(which, t):
         at = pl.ds(pl.multiple_of(which * rows, rows), rows)
-        source, target = ((all_gate, d_gate), (all_up, d_up))[t]
+        source, target = ((gate_low, d_gate), (up_low, d_up))[t]
         return pltpu.make_async_copy(source.at[at], target.at[at], load_sem.at[t, which])
 
-    def weight_load(b, t):
-        at = pl.ds(b * step, step)
-        source, target = ((gate_weight, w_gate), (up_weight, w_up))[t]
-        return pltpu.make_async_copy(source.at[at], target.at[at], load_sem.at[2 + t, b])
-
-    outer = [flip(scatter.far, 2), scatter.far, flip(scatter.quarter, 2), scatter.quarter]
-    late = [
-        pltpu.make_async_copy(all_mixed, mixed, load_sem.at[4, 0]),
-        pltpu.make_async_copy(all_hidden, seq_hidden, load_sem.at[4, 1]),
+    own = pltpu.make_async_copy(own_d_ffn, every.at[quarter], load_sem.at[2, 0])
+    weights = [
+        pltpu.make_async_copy(source, target, load_sem.at[2, 1 + i])
+        for i, (source, target) in enumerate(
+            ((down_weight, w_down), (gate_weight, w_gate), (up_weight, w_up))
+        )
     ]
+    own.start()
     for t in (0, 1):
-        rows_load(outer[0], t).start()
-    for b in range(width // step):
-        for t in (0, 1):
-            weight_load(b, t).start()
+        rows_load(quarter, t).start()
+    for load in weights:
+        load.start()
     for which in outer[1:]:
         for t in (0, 1):
             rows_load(which, t).start()
+    home = Home(layer_out, out_home, home_send, home_recv, place, column)
+    greet(wa_peers(place, column) + home.sources(), 5)
+    gather = WaGather(every, wa_send, wa_recv, place, column, PIECES, own_d_ffn)
+    for i in range(PIECES):
+        gather.own(i)
+    lefts = [(d_gate, w_gate, True, bg), (d_up, w_up, True, bu)]
+
+    def stage(which):
+        at = pl.ds(pl.multiple_of(which * rows, rows), rows)
+        d_mid_down[at, :] = times_t(every[which], full[...]).astype(jnp.bfloat16)
+        for t in (0, 1):
+            rows_load(which, t).wait()
+
+        def block(b, carry):
+            cols = lanes(b, step)
+            d_mixed = times_t(every[which], w_down[cols, :])
+            d_mixed = d_mixed + low_dot(d_mid_down[at, :], ad[:, cols])
+            d_gate[at, cols] = (d_mixed * d_gate[at, cols].astype(jnp.float32)).astype(jnp.bfloat16)
+            d_up[at, cols] = (d_mixed * d_up[at, cols].astype(jnp.float32)).astype(jnp.bfloat16)
+            return carry
+
+        lax.fori_loop(0, units // step, block, 0)
+
+    own.wait()
+    weights[0].wait()
+    stage(quarter)
+    gather.near_here()
+    stage(flip(quarter, 2))
+    for load in weights[1:]:
+        load.wait()
+    gather.forward(0)
+    scatter.product(flip(quarter, 2), lefts)
+    scatter.give(1)
+    for i in (1, 2):
+        gather.forward(i)
+    scatter.product(quarter, lefts)
+    gather.forward(3)
+    gather.last_here()
+    for i in (0, 1):
+        home.copy(i).start()
+    stage(flip(far, 2))
+    scatter.product(flip(far, 2), lefts)
+    scatter.give(0)
+    stage(far)
+    length = d_gate.shape[0]
+    late = [
+        pltpu.make_async_copy(all_mixed, w_down.at[pl.ds(0, length)], load_sem.at[3, 0]),
+        pltpu.make_async_copy(all_hidden, w_down.at[pl.ds(length, length)], load_sem.at[3, 1]),
+    ]
     for load in late:
         load.start()
-
-    def rows_ready(which):
-        for t in (0, 1):
-            rows_load(which, t).wait()
-
-    def block_ready(b):
-        for t in (0, 1):
-            weight_load(b, t).wait()
-
-    scatter.ready, scatter.block_ready = rows_ready, block_ready
-    home = Home(layer_out, out_home, home_send, home_recv, place, column)
-    greet(wa_peers(place, column) + home.sources(), 5)
-    for i in (0, 1):
-        home.copy(i).start()
-    gather = WaGather(every, wa_send, wa_recv, place, column, PIECES, d_branch)
-    lefts = [(d_gate, w_gate, True, bg), (d_up, w_up, True, bu)]
-    scatter.outward(lefts)
-    scatter.inward(lefts)
+    scatter.product(far, lefts)
+    scatter.pass_on()
+    scatter.take()
     for load in late:
         load.wait()
 
     def grad_block(b, carry):
-        cols = lanes(b, step)
+        cols = lanes(b, 512)
         hidden_sum = None
         for q in range(4):
-            term = dot_rows(scatter.middle[q], seq_hidden[q * rows : (q + 1) * rows, cols])
+            first = length + q * rows
+            term = dot_rows(scatter.middle[q], w_down[first : first + rows, cols])
             hidden_sum = term if hidden_sum is None else hidden_sum + term
         shape = hidden_sum.shape
-        down_sum = dot_rows(mid_down[...], d_ffn[:, cols])
+        down_sum = dot_rows(mid_down[...], every[quarter, :, cols])
         choices = [(4, hidden_sum), (5, hidden_sum), (6, down_sum)]
         grads.put(grads.full, cols, by_kind(shape, choices))
         choices = [
             (4, dot_rows(mid_gu[...], d_gate[:, cols])), (5, dot_rows(mid_gu[...], d_up[:, cols])),
-            (6, dot_rows(d_mid_down[...], mixed[:, cols])),
+            (6, dot_rows(d_mid_down[...], w_down[:length, cols])),
         ]
         grads.put(grads.cut, cols, by_kind(shape, choices))
         return carry
 
-    lax.fori_loop(0, width // step, grad_block, 0)
+    lax.fori_loop(0, width // 512, grad_block, 0)
     grads.start()
     for i in range(PIECES):
         at, total, mid = scatter.piece(i)
@@ -1616,79 +1746,81 @@
         d_hidden[at, :] = grad
         values = branch[at, :]
         scale = rms_factor(values)
-        weighted = grad * gain[...]
+        weighted = grad * gain[...].astype(jnp.float32)
         mean = jnp.mean(values * weighted, axis=-1, keepdims=True)
         back = scale * weighted - values * (scale * scale * scale * mean)
         d_branch[at, :] = back.astype(jnp.bfloat16)
-        gather.own(i)
-    keep = pltpu.make_async_copy(d_branch, every.at[gather.quarter], local)
-    keep.start()
-    for i in range(PIECES):
-        gather.forward(i)
     grad_table[0:16, :] = grads.summed()
     for member, rows_here in grads.slices():
         grad_table[pl.ds(pl.multiple_of(16 + 16 * member, 16), 16), :] = rows_here
-    gather.finish()
+    gather.sent()
     scatter.finish()
     home.finish()
     grads.finish()
-    keep.wait()
-
-
-def ffn_back(arrays, layer_out):
+
+
+def ffn_back(near, far):
     f32, bf16 = jnp.float32, jnp.bfloat16
-    rows, width = arrays[3].shape
-    length, units = arrays[10].shape
+    rows, width = near[4].shape
+    length, units = far[1].shape
     shape = jax.ShapeDtypeStruct
     return pl.pallas_call(
         ffn_back_kernel,
-        in_specs=[VMEM] * 10 + [ANY] * 7,
-        out_specs=[VMEM] * 3 + [ANY] * 2,
+        in_specs=[VMEM] * len(near) + [ANY] * len(far),
+        out_specs=[VMEM] * 3 + [ANY],
         out_shape=[
             shape((rows, width), f32), shape((rows, width), bf16), shape((80, width), bf16),
-            shape((4, rows, width), bf16), shape((2, rows // 2, width), bf16),
+            shape((2, rows // 2, width), bf16),
         ],
         scratch_shapes=scatter_scratch(rows, width)
         + grads_scratch(width, units)
         + [
-            DMA((3, PIECES)), DMA((3, PIECES)), DMA((2, 1)), DMA((2, 1)), DMA(()), DMA((5, 4)),
-            pltpu.VMEM((length, units), bf16), pltpu.VMEM((length, units), bf16),
-            pltpu.VMEM((width, units), bf16), pltpu.VMEM((width, units), bf16),
-            pltpu.VMEM((length, units), bf16), pltpu.VMEM((length, width), bf16),
+            DMA((3, PIECES)), DMA((3, PIECES)), DMA((4, 4)),
+            pltpu.VMEM((4, rows, width), bf16), pltpu.VMEM((length, units), bf16),
+            pltpu.VMEM((length, units), bf16), pltpu.VMEM((width, units), bf16),
+            pltpu.VMEM((width, units), bf16), pltpu.VMEM((units, width), bf16),
+            pltpu.VMEM((length, LANES), bf16), DMA((2, 1)), DMA((2, 1)),
         ],
         name="ffn_back",
         compiler_params=params(5, vmem_limit_bytes=VMEM_BYTES),
-    )(*arrays, layer_out)
+    )(*near, *far)
 
 
 def attend_back_kernel(
-    d_rows, w_out, full, ao, query, key, value, qkv_raw, scales, gain_q, gain_k, cosine, sine,
-    doc_col, doc_row, b_qkv, mid_qkv, mid_out, table, qkv_weight, all_hidden, all_tokens,
-    all_attended, all_branch, grad_home, tables, own_tables, *refs, back,
+    w_out, full, ao, query, key, value, qkv_raw, scales, gain_q, gain_k, cosine, sine,
+    doc_col, doc_row, b_qkv, mid_qkv, mid_out, table, own_branch, qkv_weight, all_hidden,
+    all_tokens, all_attended, grad_home, tables, own_tables, *refs, back,
 ):
     place, column = here()
     count = tables.shape[0]
     scatter = Scatter(refs[:SCATTER_REFS], place, column)
     sums = RowSums(refs[SCATTER_REFS : SCATTER_REFS + ROW_SUMS_REFS], place, column)
+    at = SCATTER_REFS + ROW_SUMS_REFS
+    grads = Grads(refs[at : at + GRADS_REFS], 0, place, column)
     (
         ring_send, ring_recv, home_send, home_recv, local, grad, t_rows, dk_sum, dv_sum, my_grad,
-        d_qkv, d_mid_out, own_table, load_sem, w_qkv, d_hidden, tokens, attended, d_branch,
-    ) = refs[SCATTER_REFS + ROW_SUMS_REFS + GRADS_REFS :]
+        d_qkv, d_mid_out, own_table, load_sem, w_qkv, d_hidden, tokens, attended, d_rows, wa_send,
+        wa_recv,
+    ) = refs[at + GRADS_REFS :]
+    quarter, far = scatter.quarter, scatter.far
+    own = pltpu.make_async_copy(own_branch, d_rows.at[quarter], load_sem.at[4])
+    own.start()
     loads = [
         pltpu.make_async_copy(source, target, load_sem.at[i])
         for i, (source, target) in enumerate(
             (
-                (qkv_weight, w_qkv), (all_tokens, tokens), (all_attended, attended),
-                (all_branch, d_branch), (all_hidden, d_hidden),
+                (all_attended, attended), (qkv_weight, w_qkv), (all_tokens, tokens),
+                (all_hidden, d_hidden),
             )
         )
     ]
     for load in loads:
         load.start()
-    at = SCATTER_REFS + ROW_SUMS_REFS
-    grads = Grads(refs[at : at + GRADS_REFS], 0, place, column)
     home = Home(my_grad, grad_home, home_send, home_recv, place, column)
     greet(wa_peers(place, column) + ring_peers(place, column, count) + home.sources(), 7)
+    gather = WaGather(d_rows, wa_send, wa_recv, place, column, PIECES, own_branch)
+    for i in range(PIECES):
+        gather.own(i)
     ring = Ring(tables, ring_send.at[0], ring_recv.at[0], place, column, table)
     own_ring = Ring(own_tables, ring_send.at[1], ring_recv.at[1], place, column, own_table)
     ring.step(0)
@@ -1697,59 +1829,81 @@
     keep.start()
     f32, bf16 = jnp.float32, jnp.bfloat16
     length, part = query.shape
-    width = d_rows.shape[1]
-    rows = 256
+    rows, width = my_grad.shape
+    span = min(length, rows + back)
     scale = 1.0 / math.sqrt(HEAD_DIM)
-    d_mid_out[...] = times_t(d_rows[...], full[...]).astype(bf16)
-
-    def attended_rows(r, carry):
-        at = pl.ds(pl.multiple_of(r * rows, rows), rows)
-        total = times_t(d_rows[at, :], w_out[...]) + low_dot(d_mid_out[at, :], ao[...])
-        grad[at, :] = total.astype(bf16)
-        return carry
-
-    lax.fori_loop(0, length // rows, attended_rows, 0)
     sums.columns[...] = jnp.zeros_like(sums.columns)
-    ring.step(2)
+    dk_sum[...] = jnp.zeros_like(dk_sum)
+    dv_sum[...] = jnp.zeros_like(dv_sum)
 
     def unturned(turned_grad, gain, cosine_part, sine_part):
         low = turned_grad.astype(bf16).astype(f32)
         return (low * cosine_part + pltpu.roll(low * sine_part, HEAD_DIM // 2, 1)) * gain
 
-    def head(h, carry):
-        cols = pl.ds(pl.multiple_of(h * HEAD_DIM, HEAD_DIM), HEAD_DIM)
+    def attend_rows(which):
+        row = pl.multiple_of(which * rows, rows)
+        first = pl.multiple_of(jnp.maximum(row + rows - span, 0), rows)
+        at, seen = pl.ds(row, rows), pl.ds(first, span)
+        d_mid_out[at, :] = times_t(d_rows[which], full[...]).astype(bf16)
+        total = times_t(d_rows[which], w_out[...]) + low_dot(d_mid_out[at, :], ao[...])
+        grad[at, :] = total.astype(bf16)
+        bias = seen_bias(doc_col[at, :], doc_row[:, seen], row, first)
+
+        def head(h, carry):
+            cols = lanes(h, HEAD_DIM)
+            lane = lax.broadcasted_iota(jnp.int32, (rows, LANES), 1)
+            log_total = jnp.sum(
+                jnp.where(lane == 2 + h, scales[at, :], 0.0), axis=1, keepdims=True
+            )
+            scores = two_scores(query[at, cols], key[seen, cols], bias)
+            probs = jnp.exp2(scores - log_total)
+            grad_rows = grad[at, cols]
+            d_probs = times_t(grad_rows, value[seen, cols])
+            dots = jnp.sum(
+                attended[at, cols].astype(f32) * grad_rows.astype(f32), axis=1, keepdims=True
+            )
+            d_scores = (probs * (d_probs - dots)).astype(bf16)
+            dv_sum[seen, cols] += dot_rows(probs.astype(bf16), grad_rows)
+            dk_sum[seen, cols] += dot_rows(d_scores, query[at, cols])
+            dq = low_dot(d_scores, key[seen, cols]) * scale
+            t_q = unturned(dq, head_gain(gain_q, column, h), cosine[at, :], sine[at, :])
+            t_rows[at, cols] = t_q
+            q_dot = jnp.sum(qkv_raw[at, cols] * t_q, axis=1, keepdims=True)
+            sums.columns[at, :] += two_lanes(q_dot, jnp.zeros_like(q_dot))
+            return carry
+
+        lax.fori_loop(0, part // HEAD_DIM, head, 0)
+
+    own.wait()
+    loads[0].wait()
+    attend_rows(quarter)
+    gather.near_here()
+    ring.step(2)
+    attend_rows(flip(quarter, 2))
+    ring.step(3)
+    for i in range(PIECES):
+        gather.forward(i)
+    ring.step(4)
+    attend_rows(far)
+    gather.last_here()
+    ring.step(5)
+    attend_rows(flip(far, 2))
+    ring.step(6)
+
+    def key_head(h, carry):
+        cols = lanes(h, HEAD_DIM)
         k_cols = pl.ds(pl.multiple_of(part + h * HEAD_DIM, HEAD_DIM), HEAD_DIM)
         v_cols = pl.ds(pl.multiple_of(2 * part + h * HEAD_DIM, HEAD_DIM), HEAD_DIM)
-        dk_sum[...] = jnp.zeros_like(dk_sum)
-        dv_sum[...] = jnp.zeros_like(dv_sum)
-        q_dots = []
-        for row in range(0, length, rows):
-            first, last = max(0, row - back), row + rows
-            scores = block_scores(
-                query[row:last, cols], key[first:last, cols], doc_col[row:last, :],
-                doc_row[:, first:last], row, first, rows,
-            )
-            probs = soft(scores)
-            grad_rows = grad[row:last, cols]
-            d_probs = times_t(grad_rows, value[first:last, cols])
-            dots = jnp.sum(probs * d_probs, axis=1, keepdims=True)
-            d_scores = (probs * (d_probs - dots)).astype(bf16)
-            dv_sum[first:last, :] += dot_rows(probs.astype(bf16), grad_rows)
-            dk_sum[first:last, :] += dot_rows(d_scores, query[row:last, cols])
-            dq = low_dot(d_scores, key[first:last, cols]) * scale
-            t_q = unturned(dq, gain_q[:, cols], cosine[row:last, :], sine[row:last, :])
-            t_rows[row:last, cols] = t_q
-            q_dots.append(jnp.sum(qkv_raw[row:last, cols] * t_q, axis=1, keepdims=True))
-        t_k = unturned(dk_sum[...] * scale, gain_k[:, cols], cosine[...], sine[...])
+        t_k = unturned(
+            dk_sum[:, cols] * scale, head_gain(gain_k, column, h), cosine[...], sine[...]
+        )
         t_rows[:, k_cols] = t_k
         k_dot = jnp.sum(qkv_raw[:, k_cols] * t_k, axis=1, keepdims=True)
-        sums.columns[...] += two_lanes(jnp.concatenate(q_dots, axis=0), k_dot)
-        d_qkv[:, v_cols] = dv_sum[...].astype(bf16)
-        for i in (3, 4, 5, 6):
-            pl.when(h == i - 3)(functools.partial(ring.step, i))
+        sums.columns[...] += two_lanes(jnp.zeros_like(k_dot), k_dot)
+        d_qkv[:, v_cols] = dv_sum[:, cols].astype(bf16)
         return carry
 
-    lax.fori_loop(0, part // HEAD_DIM, head, 0)
+    lax.fori_loop(0, part // HEAD_DIM, key_head, 0)
     sums.start()
     factors = sums.result() * (1.0 / width)
     sums.columns[...] = factors * scales[...] * scales[...] * scales[...]
@@ -1769,9 +1923,10 @@
     for q in range(4):
         scatter.adapt(q, lefts)
     scatter.adapted = True
-    for load in loads:
+    for load in loads[1:]:
         load.wait()
-    scatter.outward(lefts)
+    scatter.product(flip(far, 2), lefts)
+    scatter.give(0)
     step = 512
     quarter_rows = scatter.rows
 
@@ -1784,7 +1939,7 @@
             )
             token_sum = term if token_sum is None else token_sum + term
         choices = [(c, token_sum) for c in range(3)]
-        choices.append((3, dot_rows(mid_out[...], d_branch[:, cols])))
+        choices.append((3, dot_rows(mid_out[...], d_rows[quarter, :, cols])))
         grads.put(grads.full, cols, by_kind(token_sum.shape, choices))
         return carry
 
@@ -1794,7 +1949,8 @@
     ] + [(3, dot_rows(d_mid_out[...], attended[...]))]
     grads.put(grads.cut, slice(0, part), by_kind((LANES, part), choices))
     grads.start()
-    scatter.inward(lefts)
+    scatter.product(far, lefts)
+    scatter.pass_on()
     own_table[0:16, :] = grads.summed()
     for member, rows_here in grads.slices():
         own_table[16:32, lanes(member, part)] = rows_here
@@ -1802,12 +1958,21 @@
     own_ring.step(1)
     keep_own = pltpu.make_async_copy(own_table, own_tables.at[place], local.at[1])
     keep_own.start()
+    scatter.product(flip(quarter, 2), lefts)
+    scatter.give(1)
+    own_ring.step(2)
+    own_ring.step(3)
+    scatter.product(quarter, lefts)
+    own_ring.step(4)
+    own_ring.step(5)
+    scatter.take()
     for i in range(PIECES):
         at, total, mid = scatter.piece(i)
         my_grad[at, :] = (d_hidden[at, :] + total + low_dot(mid, full[...])).astype(bf16)
-        own_ring.step(2 + i)
         home.copy(i // 2, PIECES // 2, i % 2).start()
-    own_ring.step(6)
+        if i == 0:
+            own_ring.step(6)
+    gather.sent()
     ring.finish()
     own_ring.finish()
     scatter.finish()
@@ -1818,15 +1983,14 @@
     keep_own.wait()
 
 
-def attention_back(arrays, table, later, back, count):
+def attention_back(near, table, far, back, count):
     f32, bf16 = jnp.float32, jnp.bfloat16
-    length, width = arrays[0].shape
-    part = arrays[4].shape[1]
-    rows = length // 4
+    length, part = near[3].shape
+    rows, width = length // 4, near[0].shape[1]
     shape = jax.ShapeDtypeStruct
     return pl.pallas_call(
         functools.partial(attend_back_kernel, back=back),
-        in_specs=[VMEM] * 18 + [ANY] * 6,
+        in_specs=[VMEM] * len(near) + [ANY] * (1 + len(far)),
         out_specs=[ANY] * 3,
         out_shape=[
             shape((2, rows // 2, width), bf16), shape((count, *table.shape), bf16),
@@ -1838,16 +2002,16 @@
         + [
             DMA((2, 2, count - 1)), DMA((2, 2, count - 1)), DMA((2, PIECES // 2)),
             DMA((2, PIECES // 2)), DMA((2,)), pltpu.VMEM((length, part), bf16), pltpu.VMEM((length, 2 * part), f32),
-            pltpu.VMEM((length, HEAD_DIM), f32), pltpu.VMEM((length, HEAD_DIM), f32),
+            pltpu.VMEM((length, part), f32), pltpu.VMEM((length, part), f32),
             pltpu.VMEM((rows, width), bf16), pltpu.VMEM((length, 3 * part), bf16),
             pltpu.VMEM((length, LANES), bf16), pltpu.VMEM((32, width), bf16), DMA((5,)),
             pltpu.VMEM((width, 3 * part), bf16), pltpu.VMEM((rows, width), f32),
             pltpu.VMEM((length, width), bf16), pltpu.VMEM((length, part), bf16),
-            pltpu.VMEM((rows, width), bf16),
+            pltpu.VMEM((4, rows, width), bf16), DMA((3, PIECES)), DMA((3, PIECES)),
         ],
         name="attend_back",
         compiler_params=params(6, vmem_limit_bytes=VMEM_BYTES),
-    )(*arrays, table, *later)
+    )(*near, table, *far)
 
 
 def per_group(
@@ -1886,49 +2050,26 @@
     half = wa // 2
     own_rows = ADAPTER_RANK // wa
 
-    def by_head(array):
-        parts = array.reshape(-1, 2, slice_heads, half, HEAD_DIM)
-        return jnp.transpose(parts, (0, 3, 1, 2, 4)).reshape(array.shape)
-
-    def by_unit(array):
-        parts = array.reshape(-1, groups, wa, unit_block)
-        return jnp.transpose(parts, (2, 0, 1, 3)).reshape(wa, -1, slice_units)
-
-    gain_q = query_norm_gain.astype(f32)[None]
-    gain_k = key_norm_gain.astype(f32)[None]
-    gain_a = attention_norm_gain.astype(f32)[None]
-    gain_f = feedforward_norm_gain.astype(f32)[None]
-
-    marks = jnp.concatenate(
+    gain_q = query_norm_gain[None]
+    gain_k = key_norm_gain[None]
+    gain_a = attention_norm_gain[None]
+    gain_f = feedforward_norm_gain[None]
+
+    numbers = jnp.concatenate(
         [
             token_document_index.reshape(1, -1).astype(bf16),
             sequence_adapter_index.reshape(1, -1).astype(bf16),
         ],
         axis=1,
     )
-    marks = jnp.pad(marks, ((0, own_rows - 1), (0, width - marks.shape[1])))
-    narrow = jnp.concatenate([attention_up_adapters[:3], attention_down_adapters[3:]])
-    narrow = narrow.reshape(4, own_rows, 2, slice_heads, half, HEAD_DIM)
-    narrow = jnp.transpose(narrow, (4, 2, 1, 0, 3, 5)).reshape(wa, own_rows, width)
-    wide = jnp.concatenate([feedforward_up_adapters, downproj_down_adapters[None]])
-    slices = jnp.concatenate([by_unit(wide.reshape(-1, hidden_units)), narrow], axis=1)
-    table = jnp.concatenate(
-        [
-            attention_down_adapters[:3].reshape(-1, width), attention_up_adapters[3],
-            feedforward_down_adapters.reshape(-1, width), downproj_up_adapters, marks,
-            slices.reshape(-1, width),
-        ],
-        axis=0,
-    )
-    qkv_parts = jnp.concatenate(
-        [
-            by_head(w).reshape(-1, wa, slice_width)
-            for w in (query_weight, key_weight, value_weight)
-        ],
-        axis=-1,
-    )
-    every_token, w_qkv, gate_slabs, up_slabs, tables, marks = fetch(
-        tokens, jnp.moveaxis(qkv_parts, 1, 0), gate_weight, up_weight, table, groups
+    numbers = jnp.pad(numbers, ((0, own_rows - 1), (0, width - numbers.shape[1])))
+    every_token, w_qkv, gate_slabs, up_slabs, tables, marks, low_cotangent, *rope = fetch(
+        tokens, (query_weight, key_weight, value_weight), gate_weight, up_weight,
+        (
+            attention_down_adapters, attention_up_adapters, feedforward_down_adapters,
+            feedforward_up_adapters, downproj_down_adapters, downproj_up_adapters,
+        ),
+        numbers, cotangent, groups,
     )
     seq_tokens = every_token.reshape(length, width)
     w_qkv = w_qkv.reshape(width, 3 * slice_width)
@@ -1944,18 +2085,13 @@
     doc_col, doc_row = documents[:, None], documents[None, :]
     my_adapter = lax.dynamic_index_in_dim(adapter_of, place, 0, keepdims=False)
     table = lax.dynamic_index_in_dim(tables, my_adapter, 0, keepdims=False)
-    rope = rope_full(length)
-    my_gain_q, my_gain_k = (
-        lax.dynamic_slice_in_dim(by_head(g), column * slice_width, slice_width, 1)
-        for g in (gain_q, gain_k)
-    )
     window = length // 2
 
     (
-        attended, query, key, value, qkv_raw, mid_qkv, scales, full, b_qkv, b_out, b_gate, b_up,
-        b_down, w_out, _, gate_slabs,
+        attended, mid_qkv, scales, full, b_qkv, b_out, b_gate, b_up, b_down, w_out, query, key,
+        value, qkv_raw, _, gate_slabs,
     ) = attend(
-        seq_tokens, w_qkv, table, my_gain_q, my_gain_k, rope, doc_col, doc_row, output_weight,
+        seq_tokens, w_qkv, table, gain_q, gain_k, rope, doc_col, doc_row, output_weight,
         gate_slabs, window, groups,
     )
     w_out = w_out.reshape(slice_width, width)
@@ -1964,37 +2100,25 @@
     )
     seq_hidden = seq_hidden.reshape(length, width)
     (
-        gate, up_value, mixed, mid_gu, layer_out, d_ffn, mid_down, my_cotangent, seq_d_ffn,
-        down_slabs,
+        mid_gu, layer_out, d_ffn, mid_down, my_cotangent, gate, up_value, mixed, down_slabs,
     ) = feed_forward(
-        seq_hidden, full, b_gate, b_up, b_down, hidden, cotangent.astype(bf16), gain_f, gate_slabs,
+        seq_hidden, full, b_gate, b_up, b_down, hidden, low_cotangent, gain_f, gate_slabs,
         up_slabs, down_weight,
     )
     w_gate = gate_slabs.reshape(width, slice_units)
     w_up = up_slabs.reshape(width, slice_units)
     w_down = down_slabs.reshape(slice_units, width)
 
-    seq_d_ffn = seq_d_ffn.reshape(length, width)
-    d_mid_down = times_t(seq_d_ffn, full).astype(bf16)
-    d_mixed = times_t(seq_d_ffn, w_down) + low_dot(d_mid_down, b_down)
-    gate, up_value = gate.astype(f32), up_value.astype(f32)
-    sigmoid = jax.nn.sigmoid(gate)
-    d_gate = (d_mixed * up_value * (sigmoid + gate * sigmoid * (1.0 - sigmoid))).astype(bf16)
-    d_up = (d_mixed * gate * sigmoid).astype(bf16)
-    d_hidden, d_branch, ffn_table, seq_d_branch, out_home = ffn_back(
-        (
-            b_gate, b_up, my_cotangent, branch, gain_a, full, mid_gu, d_mid_down, mid_down, d_ffn,
-            d_gate, d_up, w_gate, w_up, mixed, seq_hidden,
-        ),
-        layer_out,
-    )
-
+    d_hidden, d_branch, ffn_table, out_home = ffn_back(
+        (b_gate, b_up, b_down, my_cotangent, branch, gain_a, full, mid_gu, mid_down),
+        (d_ffn, gate, up_value, w_gate, w_up, w_down, mixed, seq_hidden, layer_out),
+    )
     grad_home, ffn_tables, attn_tables = attention_back(
         (
-            seq_d_branch.reshape(length, width), w_out, full, b_out, query, key, value, qkv_raw,
-            scales, my_gain_q, my_gain_k, *rope, doc_col, doc_row, b_qkv, mid_qkv, mid_out,
+            w_out, full, b_out, query, key, value, qkv_raw, scales, gain_q, gain_k, *rope,
+            doc_col, doc_row, b_qkv, mid_qkv, mid_out,
         ),
-        ffn_table, (w_qkv, d_hidden, seq_tokens, attended, d_branch), window, groups,
+        ffn_table, (d_branch, w_qkv, d_hidden, seq_tokens, attended), window, groups,
     )
 
     shared = (adapter_of == place)[:, None, None]

time: 759 us -> 690 us (0.909)
  Pallas kernels: 697 us -> 659 us
  matrix products: 20.7 us -> 0 us
    pallas_call x1, Pallas kernels: 164 us -> 137 us  [feed_forward(): pl.pallas_call(ffn_kernel, in_specs=[VMEM] * 5 + [ANY] * 6, out_specs=[VM...]
    dot_general x3 -> x0, matrix products: 20.7 us -> none  [the longest x2 13.9 us: times_t(): lax.dot_general(left, weight, (((1,), (1,)), ((), ())), preferred_element...]
    pallas_call x1, Pallas kernels: 127 us -> 112 us  [attention_back(): pl.pallas_call(functools.partial(attend_back_kernel, back=back), in_specs...]
where the time goes in v5:
time: 690 us; the launch traced here: 686 us
  Pallas kernels  659 us (96%)
  local copies, waits for them, and re-layouts  15.4 us (2%)
  other arithmetic  8.83 us (1%)
    pallas_call x1, Pallas kernels, feed_forward(): pl.pallas_call(ffn_kernel, in_specs=[VMEM] * 5 + [ANY] * 6, out_specs=[VM...  137 us
    pallas_call x1, Pallas kernels, fetch(): pl.pallas_call(fetch_kernel, in_specs=[VMEM] * 15, out_specs=[ANY] * 6 +...  120 us
    pallas_call x1, Pallas kernels, attend(): pl.pallas_call(functools.partial(attend_kernel, back=back), in_specs=[VME...  118 us
    pallas_call x1, Pallas kernels, attention_back(): pl.pallas_call(functools.partial(attend_back_kernel, back=back), in_specs...  112 us
    pallas_call x1, Pallas kernels, out_branch(): pl.pallas_call(branch_kernel, in_specs=[VMEM] * 5 + [ANY] * 2, out_specs=...  86.8 us
    pallas_call x1, Pallas kernels, ffn_back(): pl.pallas_call(ffn_back_kernel, in_specs=[VMEM] * len(near) + [ANY] * len...  84.6 us

profile of v5, /device:TPU:6, one launch (start us, length us, event | category | flops | bytes accessed | tf_op | source)
XLA Modules:
  0.0 686.1 jit_solution(13037644526873936142)
XLA Ops:
  0.7 0.7 convert_bitcast_fusion.4
  1.4 0.7 convert_bitcast_fusion.3
  2.0 1.3 broadcast_in_dim.39.gain_q
  3.3 1.3 broadcast_in_dim.40.gain_k
  4.6 1.3 broadcast_in_dim.42.gain
  5.9 1.3 broadcast_in_dim.41.gain
  7.2 0.6 fusion.4.numbers
  7.8 120.4 %fetch.1 = (bf16[4,256,2048]{2,1,0:T(8,128)(2,1)}, bf16[8,256,1536]{2,1,0:T(8,128)(2,1)}, bf16[8,256,2048]{2,1,0:T(8,128)(2,1)}, bf16[8,256,2048]{2,1,0:T(8,128)...) custom-call(bf16[2,128,2048]{2,1,0:T(8,128)(2,1)} %tokens.1, ...), custom_call_target="tpu_custom_call" | custom-call | tf_op jit(solution)/shard_map/fetch/pallas_call | solution.py:1094
  128.2 1.5 slice.62
  129.7 0.6 convert_bitcast_fusion
  130.4 0.1 copy.38
  130.7 0.1 copy.39
  130.9 0.6 dynamic_slice.11
  133.4 1.8 dynamic-slice_bitcast_fusion.table
  135.2 1.0 copy.40.doc_col
  136.2 118.0 %attend.1 = (bf16[1024,512]{1,0:T(8,128)(2,1)}, bf16[1024,128]{1,0:T(8,128)(2,1)}, f32[1024,128]{1,0:T(8,128)}, bf16[128,2048]{1,0:T(8,128)(2,1)}, bf16[128,1536...) custom-call(bf16[96,2048]{1,0:T(8,128)(2,1)} %dynamic-slice_bitcast_, ...), custom_call_target="tpu_custom_call", output_to_operand_aliasing={{15}: (10, {})} | custom-call | tf_op jit(solution)/shard_map/attend/pallas_call | solution.py:1324
  254.3 86.8 %out_branch.1 = (f32[256,2048]{1,0:T(8,128)}, f32[256,2048]{1,0:T(8,128)}, bf16[256,128]{1,0:T(8,128)(2,1)}, bf16[256,2048]{1,0:T(8,128)(2,1)}, bf16[4,256,2048]...) custom-call(bf16[1024,512]{1,0:T(8,128)(2,1)} %get-tuple-element.64.attended.all_attended, ...), custom_call_target="tpu_custom_call", output_to_operand_aliasing={{5}: (6, {})} | custom-call | tf_op jit(solution)/shard_map/out_branch/pallas_call | solution.py:1465
  341.1 137.0 %feed_forward.1 = (bf16[1024,128]{1,0:T(8,128)(2,1)}, bf16[256,2048]{1,0:T(8,128)(2,1)}, bf16[256,2048]{1,0:T(8,128)(2,1)}, bf16[256,128]{1,0:T(8,128)(2,1)}, bf...) custom-call(bf16[128,2048]{1,0:T(8,128)(2,1)} %get-tuple-element.63., ...), custom_call_target="tpu_custom_call" | custom-call | tf_op jit(solution)/shard_map/feed_forward/pallas_call | solution.py:1607
  478.1 84.6 %ffn_back.1 = (f32[256,2048]{1,0:T(8,128)}, bf16[256,2048]{1,0:T(8,128)(2,1)}, bf16[80,2048]{1,0:T(8,128)(2,1)}, bf16[2,128,2048]{2,1,0:T(8,128)(2,1)}) custom-call(bf16[128,2048]{1,0:T(8,128)(2,1)} %get-tuple-element.60.bg, bf16[128,2048]{1,0:T(8,128)(2,1)} %get-tuple-element.61.bu, bf16[128,2048]{1,0:T(8,128)(2,1)} %get-tuple-element.62.ad, ...), custom_call_target="tpu_custom_call" | custom-call | tf_op jit(solution)/shard_map/ffn_back/pallas_call | solution.py:1767
  562.7 111.8 %attend_back.1 = (bf16[2,128,2048]{2,1,0:T(8,128)(2,1)}, bf16[8,80,2048]{2,1,0:T(8,128)(2,1)}, bf16[8,32,2048]{2,1,0:T(8,128)(2,1)}) custom-call(bf16[512,2048]{1,0:T(8,128)(2,1)} %bitcast.47, bf16[128,2048]{1,0:T(8,128)(2,1)} %get-tuple-element.63.bo.full, bf16[128,512]{1,0:T(8,128)(2,1)} %get-tuple-element.66.ao, ...), custom_call_target="tpu_custom_call" | custom-call | tf_op jit(solution)/shard_map/attend_back/pallas_call | solution.py:1991
  674.5 1.5 select_reduce_fusion.1
  676.0 2.4 select_reduce_fusion
  678.5 0.6 slice.90
  679.2 0.2 copy.48
  679.3 0.7 slice.74
  680.0 0.2 copy.44
  680.2 0.9 slice.77
  681.2 0.7 squeeze.18
  682.0 0.1 reshape.116
  682.4 0.8 pad_maximum_fusion
  683.1 1.6 convert_element_type.80
  684.7 1.0 copy.56
  (27 shorter events, 0.8 us)
Async XLA Ops:
  678.5 4.7 copy-start
  679.3 5.4 copy-start.1

commit v6 on v5

--- a/solution.py
+++ b/solution.py
@@ -492,7 +492,7 @@
 
 
 MESH = pl.DeviceIdType.MESH
-VMEM_BYTES = 58 << 20
+VMEM_BYTES = 60 << 20
 
 
 def remote(source, target, send, recv, device):
@@ -1044,12 +1044,12 @@
     own_table.wait()
     table_ring.finish()
     own_marks = pltpu.make_async_copy(
-        tables.at[:, pl.ds(MARKS, 8)], marks.at[quarter], local.at[4]
+        tables.at[:, pl.ds(MARKS, 8), pl.ds(0, MARK_LANES)], marks.at[quarter], local.at[4]
     )
     own_marks.start()
     mark_moves = [
         remote(
-            tables.at[:, pl.ds(MARKS, 8)], marks.at[quarter], mark_send.at[k], mark_recv.at[k],
+            tables.at[:, pl.ds(MARKS, 8), pl.ds(0, MARK_LANES)], marks.at[quarter], mark_send.at[k], mark_recv.at[k],
             peer,
         )
         for k, peer in enumerate(near_far)
@@ -1098,7 +1098,7 @@
         out_shape=[
             shape(4, 2 * tokens.shape[1], width), shape(count, 4 * rows, part),
             shape(count, 4 * rows, units), shape(count, 4 * rows, units),
-            shape(count, SLICES + 64, width), shape(4, count, 8, width), shape(*cotangent.shape),
+            shape(count, SLICES + 64, width), shape(4, count, 8, MARK_LANES), shape(*cotangent.shape),
             rope, rope,
         ],
         scratch_shapes=[
@@ -1114,6 +1114,7 @@
 
 KINDS = 8
 MARKS = 24
+MARK_LANES = 384
 SLICES = 32
 
 
@@ -1170,11 +1171,12 @@
 
 
 def attend_kernel(
-    table, gain_q, gain_k, cosine, sine, doc_col, doc_row, every_token, qkv_weight, out_part,
+    table, gains, cosine, sine, doc_col, doc_row, every_token, qkv_weight, out_part,
     _gate, attended, middle, scales, full, b_qkv, b_out, b_gate, b_up, b_down, w_out,
     query_out, key_out, value_out, qkv_raw_out, out_slabs, w_gate, *refs, back,
 ):
     place, column = here()
+    gain_q, gain_k = (gains.at[pl.ds(i, 1)] for i in (0, 1))
     sums = RowSums(refs[:ROW_SUMS_REFS], place, column)
     (
         ring_send, ring_recv, local, out_send, out_recv, slices, table_send, table_recv,
@@ -1314,7 +1316,7 @@
 
 
 def attend(
-    tokens, w_qkv, table, gain_q, gain_k, tables, doc_col, doc_row, out_part, w_gate, back, count
+    tokens, w_qkv, table, gains, tables, doc_col, doc_row, out_part, w_gate, back, count
 ):
     f32, bf16 = jnp.float32, jnp.bfloat16
     (length, width), part = tokens.shape, w_qkv.shape[1] // 3
@@ -1323,7 +1325,7 @@
     maps = shape((LANES, width), bf16)
     return pl.pallas_call(
         functools.partial(attend_kernel, back=back),
-        in_specs=[VMEM] * 7 + [ANY] * 4,
+        in_specs=[VMEM] * 6 + [ANY] * 4,
         out_specs=[VMEM] * 10 + [ANY] * 6,
         out_shape=[
             low, shape((length, LANES), bf16), shape((length, LANES), f32), maps,
@@ -1340,10 +1342,10 @@
             pltpu.VMEM((length, part), bf16), pltpu.VMEM((length, part), bf16),
             pltpu.VMEM((length, part), bf16), pltpu.VMEM((length, 2 * part), f32), DMA((4,)),
         ],
-        input_output_aliases={10: 15},
+        input_output_aliases={9: 15},
         name="attend",
         compiler_params=params(2, vmem_limit_bytes=VMEM_BYTES),
-    )(table, gain_q, gain_k, *tables, doc_col, doc_row, tokens, w_qkv, out_part, w_gate)
+    )(table, gains, *tables, doc_col, doc_row, tokens, w_qkv, out_part, w_gate)
 
 
 class Grads:
@@ -1416,23 +1418,36 @@
 
 
 def branch_kernel(
-    attended, w_out, ao, gain, bo, every_token, _up, branch, hidden, mid_out, hidden_low,
-    every, w_up, *refs,
+    ao, gains, bo, all_attended, out_weight, every_token, _up, branch, hidden, mid_out,
+    hidden_low, every, w_up, *refs,
 ):
     place, column = here()
     scatter = Scatter(refs[:SCATTER_REFS], place, column)
-    wa_send, wa_recv, ring_send, ring_recv, local, tokens, token_sem = refs[SCATTER_REFS:]
-    load = pltpu.make_async_copy(every_token.at[scatter.quarter], tokens, token_sem)
-    load.start()
+    (
+        wa_send, wa_recv, ring_send, ring_recv, local, tokens, load_sem, attended, w_out,
+    ) = refs[SCATTER_REFS:]
+    gain = gains.at[pl.ds(2, 1)]
+    loads = [
+        pltpu.make_async_copy(source, target, load_sem.at[i])
+        for i, (source, target) in enumerate(
+            (
+                (all_attended, attended), (out_weight, w_out),
+                (every_token.at[scatter.quarter], tokens),
+            )
+        )
+    ]
+    for load in loads:
+        load.start()
     greet(wa_peers(place, column)[:2] + ring_peers(place, column, w_up.shape[0]), 4)
     rings = Pair(w_up, ring_send, ring_recv, 0, place, column)
     gather = WaGather(every, wa_send, wa_recv, place, column, PIECES, hidden_low)
     lefts = [(attended, w_out, False, ao)]
     rings.step(0)
     rings.step(1)
+    for load in loads:
+        load.wait()
     scatter.outward(lefts)
     scatter.inward(lefts)
-    load.wait()
     for i in range(PIECES):
         if i % 2 == 0:
             rings.step(2 + i // 2)
@@ -1457,14 +1472,14 @@
     keep.wait()
 
 
-def out_branch(attended, w_out, ao, gain, bo, tokens, w_up):
+def out_branch(ao, gains, bo, attended, w_out, tokens, w_up):
     f32, bf16 = jnp.float32, jnp.bfloat16
     _, rows, width = tokens.shape
     count = w_up.shape[0]
     shape = jax.ShapeDtypeStruct
     return pl.pallas_call(
         branch_kernel,
-        in_specs=[VMEM] * 5 + [ANY] * 2,
+        in_specs=[VMEM] * 3 + [ANY] * 4,
         out_specs=[VMEM] * 4 + [ANY] * 2,
         out_shape=[
             shape((rows, width), f32), shape((rows, width), f32), shape((rows, LANES), bf16),
@@ -1473,16 +1488,17 @@
         scratch_shapes=scatter_scratch(rows, width)
         + [
             DMA((3, PIECES)), DMA((3, PIECES)), DMA((2, 2, count - 1)), DMA((2, 2, count - 1)),
-            DMA(()), pltpu.VMEM((rows, width), bf16), DMA(()),
+            DMA(()), pltpu.VMEM((rows, width), bf16), DMA((3,)),
+            pltpu.VMEM(attended.shape, bf16), pltpu.VMEM(w_out.shape, bf16),
         ],
         input_output_aliases={6: 5},
         name="out_branch",
         compiler_params=params(3, vmem_limit_bytes=VMEM_BYTES),
-    )(attended, w_out, ao, gain, bo, tokens, w_up)
+    )(ao, gains, bo, attended, w_out, tokens, w_up)
 
 
 def ffn_kernel(
-    full, bg, bu, ad, gain, every_row, every_hidden, home_cotangent, w_gate, w_up, down,
+    full, bg, bu, ad, gains, every_row, every_hidden, home_cotangent, w_gate, w_up, down,
     middle, layer_out, d_ffn, mid_down, my_cotangent, gate_out, up_out, mixed_out, w_down, *refs,
 ):
     place, column = here()
@@ -1491,6 +1507,7 @@
         ring_send, ring_recv, local, first_w, second_w, rows_in, hidden, home_send, home_recv,
         gate_low, up_low, mixed, write_sem,
     ) = refs[SCATTER_REFS:]
+    gain = gains.at[pl.ds(3, 1)]
     count = w_up.shape[0]
     local_len = home_cotangent.shape[1]
     level, parity = place // 2, place % 2
@@ -1556,7 +1573,17 @@
         rings.step(2 + q)
     rings.step(6)
     keep_down.wait()
+
+    def load_slabs(aways):
+        slab = down.shape[0]
+        for away in aways:
+            owner = ring_owner(rings.rings[0].spot + away, count)
+            rows_at = pl.ds(pl.multiple_of(owner * slab, slab), slab)
+            pltpu.make_async_copy(w_down.at[owner], first_w.at[rows_at], local.at[1]).start()
+
+    load_slabs(range(-2, 3))
     rings.finish()
+    load_slabs((-3, 3, 4))
     moves = [
         remote(
             home_cotangent.at[b, pl.ds(i * scatter.size, scatter.size)],
@@ -1568,7 +1595,6 @@
     ]
     for move in moves:
         move.start()
-    load(w_down, first_w, local.at[1])
     loaded(first_w, local.at[1])
     lefts = [(mixed, first_w, False, ad)]
     scatter.outward(lefts)
@@ -1596,7 +1622,7 @@
         write.wait()
 
 
-def feed_forward(rows_in, full, bg, bu, ad, hidden, cotangent, gain, w_gate, w_up, down):
+def feed_forward(rows_in, full, bg, bu, ad, hidden, cotangent, gains, w_gate, w_up, down):
     bf16 = jnp.bfloat16
     rows, width = hidden.shape
     length = rows_in.shape[0]
@@ -1623,11 +1649,11 @@
         ],
         name="feed_forward",
         compiler_params=params(4, vmem_limit_bytes=VMEM_BYTES),
-    )(full, bg, bu, ad, gain, rows_in, hidden, cotangent, w_gate, w_up, down)
+    )(full, bg, bu, ad, gains, rows_in, hidden, cotangent, w_gate, w_up, down)
 
 
 def ffn_back_kernel(
-    bg, bu, ad, cotangent, branch, gain, full, mid_gu, mid_down, own_d_ffn, gate_low, up_low,
+    bg, bu, ad, gains, full, mid_gu, mid_down, own_cotangent, own_branch, own_d_ffn, gate_low, up_low,
     gate_weight, up_weight, down_weight, all_mixed, all_hidden, layer_out,
     d_hidden, d_branch, grad_table, out_home, *refs,
 ):
@@ -1636,8 +1662,9 @@
     grads = Grads(refs[SCATTER_REFS : SCATTER_REFS + GRADS_REFS], 4, place, column)
     (
         wa_send, wa_recv, load_sem, every, d_gate, d_up, w_gate, w_up, w_down, d_mid_down,
-        home_send, home_recv,
+        home_send, home_recv, cotangent, branch,
     ) = refs[SCATTER_REFS + GRADS_REFS :]
+    gain = gains.at[pl.ds(2, 1)]
     rows, width = d_hidden.shape
     units, step = d_gate.shape[1], 1024
     quarter, far = scatter.quarter, scatter.far
@@ -1711,6 +1738,8 @@
     late = [
         pltpu.make_async_copy(all_mixed, w_down.at[pl.ds(0, length)], load_sem.at[3, 0]),
         pltpu.make_async_copy(all_hidden, w_down.at[pl.ds(length, length)], load_sem.at[3, 1]),
+        pltpu.make_async_copy(own_cotangent, cotangent, load_sem.at[3, 2]),
+        pltpu.make_async_copy(own_branch, branch, load_sem.at[3, 3]),
     ]
     for load in late:
         load.start()
@@ -1761,8 +1790,8 @@
 
 def ffn_back(near, far):
     f32, bf16 = jnp.float32, jnp.bfloat16
-    rows, width = near[4].shape
-    length, units = far[1].shape
+    rows, width = far[0].shape
+    length, units = far[3].shape
     shape = jax.ShapeDtypeStruct
     return pl.pallas_call(
         ffn_back_kernel,
@@ -1780,6 +1809,7 @@
             pltpu.VMEM((length, units), bf16), pltpu.VMEM((width, units), bf16),
             pltpu.VMEM((width, units), bf16), pltpu.VMEM((units, width), bf16),
             pltpu.VMEM((length, LANES), bf16), DMA((2, 1)), DMA((2, 1)),
+            pltpu.VMEM((rows, width), bf16), pltpu.VMEM((rows, width), f32),
         ],
         name="ffn_back",
         compiler_params=params(5, vmem_limit_bytes=VMEM_BYTES),
@@ -1787,12 +1817,13 @@
 
 
 def attend_back_kernel(
-    w_out, full, ao, query, key, value, qkv_raw, scales, gain_q, gain_k, cosine, sine,
-    doc_col, doc_row, b_qkv, mid_qkv, mid_out, table, own_branch, qkv_weight, all_hidden,
-    all_tokens, all_attended, grad_home, tables, own_tables, *refs, back,
+    full, ao, scales, gains, cosine, sine, doc_col, doc_row, b_qkv, mid_qkv, mid_out, shared, table,
+    own_branch, qkv_weight, all_hidden, all_tokens, all_attended, out_weight, all_query, all_key,
+    all_value, all_raw, own_total, grad_home, tables, *refs, back,
 ):
     place, column = here()
-    count = tables.shape[0]
+    gain_q, gain_k = (gains.at[pl.ds(i, 1)] for i in (0, 1))
+    count = shared.shape[0]
     scatter = Scatter(refs[:SCATTER_REFS], place, column)
     sums = RowSums(refs[SCATTER_REFS : SCATTER_REFS + ROW_SUMS_REFS], place, column)
     at = SCATTER_REFS + ROW_SUMS_REFS
@@ -1800,27 +1831,28 @@
     (
         ring_send, ring_recv, home_send, home_recv, local, grad, t_rows, dk_sum, dv_sum, my_grad,
         d_qkv, d_mid_out, own_table, load_sem, w_qkv, d_hidden, tokens, attended, d_rows, wa_send,
-        wa_recv,
+        wa_recv, w_out, query, key, value, qkv_raw, own_tables,
     ) = refs[at + GRADS_REFS :]
     quarter, far = scatter.quarter, scatter.far
-    own = pltpu.make_async_copy(own_branch, d_rows.at[quarter], load_sem.at[4])
+    own = pltpu.make_async_copy(own_branch, d_rows.at[quarter], load_sem.at[9])
     own.start()
     loads = [
         pltpu.make_async_copy(source, target, load_sem.at[i])
         for i, (source, target) in enumerate(
             (
-                (all_attended, attended), (qkv_weight, w_qkv), (all_tokens, tokens),
-                (all_hidden, d_hidden),
+                (out_weight, w_out), (all_query, query), (all_key, key), (all_value, value),
+                (all_attended, attended), (all_raw, qkv_raw), (qkv_weight, w_qkv),
+                (all_tokens, tokens), (all_hidden, d_hidden),
             )
         )
     ]
-    for load in loads:
-        load.start()
     home = Home(my_grad, grad_home, home_send, home_recv, place, column)
     greet(wa_peers(place, column) + ring_peers(place, column, count) + home.sources(), 7)
     gather = WaGather(d_rows, wa_send, wa_recv, place, column, PIECES, own_branch)
     for i in range(PIECES):
         gather.own(i)
+    for load in loads:
+        load.start()
     ring = Ring(tables, ring_send.at[0], ring_recv.at[0], place, column, table)
     own_ring = Ring(own_tables, ring_send.at[1], ring_recv.at[1], place, column, own_table)
     ring.step(0)
@@ -1830,7 +1862,6 @@
     f32, bf16 = jnp.float32, jnp.bfloat16
     length, part = query.shape
     rows, width = my_grad.shape
-    span = min(length, rows + back)
     scale = 1.0 / math.sqrt(HEAD_DIM)
     sums.columns[...] = jnp.zeros_like(sums.columns)
     dk_sum[...] = jnp.zeros_like(dk_sum)
@@ -1840,18 +1871,21 @@
         low = turned_grad.astype(bf16).astype(f32)
         return (low * cosine_part + pltpu.roll(low * sine_part, HEAD_DIM // 2, 1)) * gain
 
-    def attend_rows(which):
-        row = pl.multiple_of(which * rows, rows)
-        first = pl.multiple_of(jnp.maximum(row + rows - span, 0), rows)
-        at, seen = pl.ds(row, rows), pl.ds(first, span)
-        d_mid_out[at, :] = times_t(d_rows[which], full[...]).astype(bf16)
-        total = times_t(d_rows[which], w_out[...]) + low_dot(d_mid_out[at, :], ao[...])
+    def attend_rows(which, part_at=0, parts=1):
+        size = rows // parts
+        span = min(length, size + back)
+        row = pl.multiple_of(which * rows + part_at * size, size)
+        first = pl.multiple_of(jnp.maximum(row + size - span, 0), size)
+        at, seen = pl.ds(row, size), pl.ds(first, span)
+        given = d_rows[which, part_at * size : (part_at + 1) * size, :]
+        d_mid_out[at, :] = times_t(given, full[...]).astype(bf16)
+        total = times_t(given, w_out[...]) + low_dot(d_mid_out[at, :], ao[...])
         grad[at, :] = total.astype(bf16)
         bias = seen_bias(doc_col[at, :], doc_row[:, seen], row, first)
 
         def head(h, carry):
             cols = lanes(h, HEAD_DIM)
-            lane = lax.broadcasted_iota(jnp.int32, (rows, LANES), 1)
+            lane = lax.broadcasted_iota(jnp.int32, (size, LANES), 1)
             log_total = jnp.sum(
                 jnp.where(lane == 2 + h, scales[at, :], 0.0), axis=1, keepdims=True
             )
@@ -1875,19 +1909,21 @@
         lax.fori_loop(0, part // HEAD_DIM, head, 0)
 
     own.wait()
-    loads[0].wait()
+    for load in loads[:6]:
+        load.wait()
     attend_rows(quarter)
     gather.near_here()
     ring.step(2)
     attend_rows(flip(quarter, 2))
     ring.step(3)
-    for i in range(PIECES):
-        gather.forward(i)
-    ring.step(4)
-    attend_rows(far)
-    gather.last_here()
-    ring.step(5)
-    attend_rows(flip(far, 2))
+    for half in (0, 1):
+        pieces = [half * PIECES // 2 + i for i in range(PIECES // 2)]
+        for i in pieces:
+            gather.forward(i)
+        attend_rows(far, half, 2)
+        gather.last_here(pieces)
+        attend_rows(flip(far, 2), half, 2)
+        ring.step(4 + half)
     ring.step(6)
 
     def key_head(h, carry):
@@ -1923,7 +1959,7 @@
     for q in range(4):
         scatter.adapt(q, lefts)
     scatter.adapted = True
-    for load in loads[1:]:
+    for load in loads[6:]:
         load.wait()
     scatter.product(flip(far, 2), lefts)
     scatter.give(0)
@@ -1966,6 +2002,7 @@
     own_ring.step(4)
     own_ring.step(5)
     scatter.take()
+
     for i in range(PIECES):
         at, total, mid = scatter.piece(i)
         my_grad[at, :] = (d_hidden[at, :] + total + low_dot(mid, full[...])).astype(bf16)
@@ -1973,28 +2010,33 @@
         if i == 0:
             own_ring.step(6)
     gather.sent()
+    own_ring.finish()
+    keep_own.wait()
+    total = None
+    for g in range(count):
+        term = own_tables[g].astype(f32) * shared[g : g + 1, 0:1]
+        total = term if total is None else total + term
+    own_total[...] = total
+    keep.wait()
     ring.finish()
-    own_ring.finish()
     scatter.finish()
     home.finish(PIECES // 2)
     sums.finish()
     grads.finish()
-    keep.wait()
-    keep_own.wait()
 
 
 def attention_back(near, table, far, back, count):
     f32, bf16 = jnp.float32, jnp.bfloat16
-    length, part = near[3].shape
+    length, part = far[6].shape
     rows, width = length // 4, near[0].shape[1]
     shape = jax.ShapeDtypeStruct
     return pl.pallas_call(
         functools.partial(attend_back_kernel, back=back),
         in_specs=[VMEM] * len(near) + [ANY] * (1 + len(far)),
-        out_specs=[ANY] * 3,
+        out_specs=[VMEM] + [ANY] * 2,
         out_shape=[
-            shape((2, rows // 2, width), bf16), shape((count, *table.shape), bf16),
-            shape((count, 32, width), bf16),
+            shape((32, width), f32), shape((2, rows // 2, width), bf16),
+            shape((count, *table.shape), bf16),
         ],
         scratch_shapes=scatter_scratch(rows, width)
         + row_sums_scratch(length)
@@ -2004,10 +2046,13 @@
             DMA((2, PIECES // 2)), DMA((2,)), pltpu.VMEM((length, part), bf16), pltpu.VMEM((length, 2 * part), f32),
             pltpu.VMEM((length, part), f32), pltpu.VMEM((length, part), f32),
             pltpu.VMEM((rows, width), bf16), pltpu.VMEM((length, 3 * part), bf16),
-            pltpu.VMEM((length, LANES), bf16), pltpu.VMEM((32, width), bf16), DMA((5,)),
+            pltpu.VMEM((length, LANES), bf16), pltpu.VMEM((32, width), bf16), DMA((10,)),
             pltpu.VMEM((width, 3 * part), bf16), pltpu.VMEM((rows, width), f32),
             pltpu.VMEM((length, width), bf16), pltpu.VMEM((length, part), bf16),
             pltpu.VMEM((4, rows, width), bf16), DMA((3, PIECES)), DMA((3, PIECES)),
+            pltpu.VMEM((part, width), bf16), pltpu.VMEM((length, part), bf16),
+            pltpu.VMEM((length, part), bf16), pltpu.VMEM((length, part), bf16),
+            pltpu.VMEM((length, 2 * part), f32), pltpu.VMEM((count, 32, width), bf16),
         ],
         name="attend_back",
         compiler_params=params(6, vmem_limit_bytes=VMEM_BYTES),
@@ -2050,10 +2095,9 @@
     half = wa // 2
     own_rows = ADAPTER_RANK // wa
 
-    gain_q = query_norm_gain[None]
-    gain_k = key_norm_gain[None]
-    gain_a = attention_norm_gain[None]
-    gain_f = feedforward_norm_gain[None]
+    gains = jnp.stack(
+        [query_norm_gain, key_norm_gain, attention_norm_gain, feedforward_norm_gain]
+    ).astype(f32)
 
     numbers = jnp.concatenate(
         [
@@ -2091,18 +2135,18 @@
         attended, mid_qkv, scales, full, b_qkv, b_out, b_gate, b_up, b_down, w_out, query, key,
         value, qkv_raw, _, gate_slabs,
     ) = attend(
-        seq_tokens, w_qkv, table, gain_q, gain_k, rope, doc_col, doc_row, output_weight,
+        seq_tokens, w_qkv, table, gains, rope, doc_col, doc_row, output_weight,
         gate_slabs, window, groups,
     )
     w_out = w_out.reshape(slice_width, width)
     branch, hidden, mid_out, _, seq_hidden, up_slabs = out_branch(
-        attended, w_out, b_out, gain_a, full, every_token, up_slabs
+        b_out, gains, full, attended, w_out, every_token, up_slabs
     )
     seq_hidden = seq_hidden.reshape(length, width)
     (
         mid_gu, layer_out, d_ffn, mid_down, my_cotangent, gate, up_value, mixed, down_slabs,
     ) = feed_forward(
-        seq_hidden, full, b_gate, b_up, b_down, hidden, low_cotangent, gain_f, gate_slabs,
+        seq_hidden, full, b_gate, b_up, b_down, hidden, low_cotangent, gains, gate_slabs,
         up_slabs, down_weight,
     )
     w_gate = gate_slabs.reshape(width, slice_units)
@@ -2110,27 +2154,31 @@
     w_down = down_slabs.reshape(slice_units, width)
 
     d_hidden, d_branch, ffn_table, out_home = ffn_back(
-        (b_gate, b_up, b_down, my_cotangent, branch, gain_a, full, mid_gu, mid_down),
-        (d_ffn, gate, up_value, w_gate, w_up, w_down, mixed, seq_hidden, layer_out),
-    )
-    grad_home, ffn_tables, attn_tables = attention_back(
+        (b_gate, b_up, b_down, gains, full, mid_gu, mid_down),
+        (my_cotangent, branch, d_ffn, gate, up_value, w_gate, w_up, w_down, mixed, seq_hidden, layer_out),
+    )
+    shared = (adapter_of == place).astype(f32)
+    attn_total, grad_home, ffn_tables = attention_back(
         (
-            w_out, full, b_out, query, key, value, qkv_raw, scales, gain_q, gain_k, *rope,
-            doc_col, doc_row, b_qkv, mid_qkv, mid_out,
+            full, b_out, scales, gains, *rope, doc_col, doc_row, b_qkv, mid_qkv, mid_out,
+            jnp.broadcast_to(shared[:, None], (groups, LANES)),
         ),
-        ffn_table, (d_branch, w_qkv, d_hidden, seq_tokens, attended), window, groups,
-    )
-
-    shared = (adapter_of == place)[:, None, None]
-
-    def over_groups(every):
-        total = jnp.sum(jnp.where(shared, every.astype(f32), 0.0), axis=0)
+        ffn_table,
+        (
+            d_branch, w_qkv, d_hidden, seq_tokens, attended, w_out, query, key, value, qkv_raw,
+        ),
+        window, groups,
+    )
+
+    ffn_total = jnp.sum(ffn_tables.astype(f32) * shared[:, None, None], axis=0)
+
+    def parts(total):
         return total[:16].reshape(4, own_rows, width), total[16:]
 
-    attn_full, attn_cut = over_groups(attn_tables)
+    attn_full, attn_cut = parts(attn_total)
     attn_cut = attn_cut.reshape(4, own_rows, half, 2, slice_heads, HEAD_DIM)
     attn_cut = jnp.transpose(attn_cut, (0, 1, 3, 4, 2, 5)).reshape(4, own_rows, width)
-    ffn_full, ffn_cut = over_groups(ffn_tables)
+    ffn_full, ffn_cut = parts(ffn_total)
     ffn_cut = ffn_cut.reshape(wa, 4, own_rows, groups, unit_block)
     ffn_cut = jnp.transpose(ffn_cut, (1, 2, 3, 0, 4)).reshape(4, own_rows, hidden_units)
     return (

time: 690 us -> 680 us (0.986)
  Pallas kernels: 659 us -> 651 us
where the time goes in v6:
time: 680 us; the launch traced here: 676 us
  Pallas kernels  651 us (96%)
  local copies, waits for them, and re-layouts  13 us (2%)
  other arithmetic  7.94 us (1%)
    pallas_call x1, Pallas kernels, feed_forward(): pl.pallas_call(ffn_kernel, in_specs=[VMEM] * 5 + [ANY] * 6, out_specs=[VM...  137 us
    pallas_call x1, Pallas kernels, fetch(): pl.pallas_call(fetch_kernel, in_specs=[VMEM] * 15, out_specs=[ANY] * 6 +...  120 us
    pallas_call x1, Pallas kernels, attend(): pl.pallas_call(functools.partial(attend_kernel, back=back), in_specs=[VME...  118 us
    pallas_call x1, Pallas kernels, attention_back(): pl.pallas_call(functools.partial(attend_back_kernel, back=back), in_specs...  107 us
    pallas_call x1, Pallas kernels, out_branch(): pl.pallas_call(branch_kernel, in_specs=[VMEM] * 3 + [ANY] * 4, out_specs=...  85.9 us
    pallas_call x1, Pallas kernels, ffn_back(): pl.pallas_call(ffn_back_kernel, in_specs=[VMEM] * len(near) + [ANY] * len...  83.5 us

profile of v6, /device:TPU:6, one launch (start us, length us, event | category | flops | bytes accessed | tf_op | source)
XLA Modules:
  0.0 675.7 jit_solution(15133275952927471266)
XLA Ops:
  0.7 0.7 convert_bitcast_fusion.4
  1.4 0.7 convert_bitcast_fusion.3
  2.1 0.6 fusion.4.numbers
  2.7 120.4 %fetch.1 = (bf16[4,256,2048]{2,1,0:T(8,128)(2,1)}, bf16[8,256,1536]{2,1,0:T(8,128)(2,1)}, bf16[8,256,2048]{2,1,0:T(8,128)(2,1)}, bf16[8,256,2048]{2,1,0:T(8,128)...) custom-call(bf16[2,128,2048]{2,1,0:T(8,128)(2,1)} %tokens.1, ...), custom_call_target="tpu_custom_call" | custom-call | tf_op jit(solution)/shard_map/fetch/pallas_call | solution.py:1094
  123.1 1.0 slice.62
  124.0 0.6 convert_bitcast_fusion
  124.7 1.0 copy.40.doc_col
  125.7 0.1 copy.38
  126.0 0.1 copy.39
  126.2 0.6 dynamic_slice.11
  128.7 1.8 dynamic-slice_bitcast_fusion.table
  130.6 0.7 maximum_convert_fusion.gains
  131.2 118.0 %attend.1 = (bf16[1024,512]{1,0:T(8,128)(2,1)}, bf16[1024,128]{1,0:T(8,128)(2,1)}, f32[1024,128]{1,0:T(8,128)}, bf16[128,2048]{1,0:T(8,128)(2,1)}, bf16[128,1536...) custom-call(bf16[96,2048]{1,0:T(8,128)(2,1)} %dynamic-slice_bitcast_, ...), custom_call_target="tpu_custom_call", output_to_operand_aliasing={{15}: (9, {})} | custom-call | tf_op jit(solution)/shard_map/attend/pallas_call | solution.py:1326
  249.3 85.9 %out_branch.1 = (f32[256,2048]{1,0:T(8,128)}, f32[256,2048]{1,0:T(8,128)}, bf16[256,128]{1,0:T(8,128)(2,1)}, bf16[256,2048]{1,0:T(8,128)(2,1)}, bf16[4,256,2048]...) custom-call(bf16[128,512]{1,0:T(8,128)(2,1)} %get-tuple-element.64.ao, ...), custom_call_target="tpu_custom_call", output_to_operand_aliasing={{5}: (6, {})} | custom-call | tf_op jit(solution)/shard_map/out_branch/pallas_call | solution.py:1480
  335.2 137.0 %feed_forward.1 = (bf16[1024,128]{1,0:T(8,128)(2,1)}, bf16[256,2048]{1,0:T(8,128)(2,1)}, bf16[256,2048]{1,0:T(8,128)(2,1)}, bf16[256,128]{1,0:T(8,128)(2,1)}, bf...) custom-call(bf16[128,2048]{1,0:T(8,128)(2,1)} %get-tuple-element.63., ...), custom_call_target="tpu_custom_call" | custom-call | tf_op jit(solution)/shard_map/feed_forward/pallas_call | solution.py:1633
  472.2 83.5 %ffn_back.1 = (f32[256,2048]{1,0:T(8,128)}, bf16[256,2048]{1,0:T(8,128)(2,1)}, bf16[80,2048]{1,0:T(8,128)(2,1)}, bf16[2,128,2048]{2,1,0:T(8,128)(2,1)}) custom-call(bf16[128,2048]{1,0:T(8,128)(2,1)} %get-tuple-element.60.bg, bf16[128,2048]{1,0:T(8,128)(2,1)} %get-tuple-element.61.bu, bf16[128,2048]{1,0:T(8,128)(2,1)} %get-tuple-element.62.ad, ...), custom_call_target="tpu_custom_call" | custom-call | tf_op jit(solution)/shard_map/ffn_back/pallas_call | solution.py:1796
  555.7 0.7 broadcast_in_dim.2.shared
  556.4 106.6 %attend_back.1 = (f32[32,2048]{1,0:T(8,128)}, bf16[2,128,2048]{2,1,0:T(8,128)(2,1)}, bf16[8,80,2048]{2,1,0:T(8,128)(2,1)}) custom-call(bf16[128,2048]{1,0:T(8,128)(2,1)} %get-tuple-element.63.bo.full, bf16[128,512]{1,0:T(8,128)(2,1)} %get-tuple-element.64.ao, f32[1024,128]{1,0:T(8,128)} %get-tuple-element.84.scales, f32[4,2048]{1,0:T(4,128)} %maximum_convert_fusion.gains, ...), custom_call_target="tpu_custom_call" | custom-call | tf_op jit(solution)/shard_map/attend_back/pallas_call | solution.py:2033
  663.0 2.4 multiply_reduce_fusion
  665.5 0.2 copy.48
  665.7 0.2 copy.44
  665.8 0.9 slice.77
  666.8 0.7 squeeze.18
  667.6 0.7 slice.74
  668.2 0.6 slice.87
  668.9 0.9 slice.66
  669.8 0.1 reshape.124
  670.1 0.9 slice.64
  671.1 0.8 slice_bitcast_fusion
  671.9 0.8 pad_maximum_fusion
  672.7 1.6 convert_element_type.97
  674.3 1.0 copy.56
  (36 shorter events, 0.8 us)
Async XLA Ops:
  0.6 129.9 %copy-start.2 = (bf16[2048]{0:T(1024)(128)(2,1)S(1)}, bf16[2048]{0:T(1024)(128)(2,1)}, u32[]{:S(2)}) copy-start(bf16[2048]{0:T(1024)(128)(2,1)} %param.33) | copy-start | bytes 12292
  0.6 129.9 %copy-start.3 = (bf16[2048]{0:T(1024)(128)(2,1)S(1)}, bf16[2048]{0:T(1024)(128)(2,1)}, u32[]{:S(2)}) copy-start(bf16[2048]{0:T(1024)(128)(2,1)} %param.34) | copy-start | bytes 12292
  0.7 129.9 %copy-start.4 = (bf16[2048]{0:T(1024)(128)(2,1)S(1)}, bf16[2048]{0:T(1024)(128)(2,1)}, u32[]{:S(2)}) copy-start(bf16[2048]{0:T(1024)(128)(2,1)} %param.35) | copy-start | bytes 12292
  0.7 129.9 %copy-start.5 = (bf16[2048]{0:T(1024)(128)(2,1)S(1)}, bf16[2048]{0:T(1024)(128)(2,1)}, u32[]{:S(2)}) copy-start(bf16[2048]{0:T(1024)(128)(2,1)} %param.36) | copy-start | bytes 12292
  665.4 7.3 %copy-start = (bf16[2,128,2048]{2,1,0:T(8,128)(2,1)S(1)}, bf16[2,128,2048]{2,1,0:T(8,128)(2,1)}, u32[]{:S(2)}) copy-start(bf16[2,128,2048]{2,1,0:T(8,128)(2,1)} %get-tuple-element.95) | copy-start | bytes 3145732
  665.6 8.6 %copy-start.1 = (bf16[2,128,2048]{2,1,0:T(8,128)(2,1)S(1)}, bf16[2,128,2048]{2,1,0:T(8,128)(2,1)}, u32[]{:S(2)}) copy-start(bf16[2,128,2048]{2,1,0:T(8,128)(2,1)} %get-tuple-element.110) | copy-start | bytes 3145732

commit v7 on v6

--- a/solution.py
+++ b/solution.py
@@ -703,12 +703,10 @@
         self.pieces = PIECES
         self.size = self.rows // self.pieces
         self.sent = []
-        self.adapted = False
-
-    def product(self, which, lefts, part=0, parts=1):
+
+    def product(self, which, lefts):
         width, step = self.partial.shape[2], 1024
-        size = self.rows // parts
-        at = pl.ds(pl.multiple_of(which * self.rows + part * size, size), size)
+        at = pl.ds(pl.multiple_of(which * self.rows, self.rows), self.rows)
 
         def block(b, carry):
             cols = lanes(b, step)
@@ -719,12 +717,10 @@
                 else:
                     term = low_dot(left[at, :], weight[:, cols])
                 total = term if total is None else total + term
-            self.partial[which, part * size : (part + 1) * size, cols] = total.astype(jnp.bfloat16)
+            self.partial[which, :, cols] = total.astype(jnp.bfloat16)
             return carry
 
         lax.fori_loop(0, width // step, block, 0)
-        if not self.adapted and part == parts - 1:
-            self.adapt(which, lefts)
 
     def adapt(self, which, lefts):
         at = pl.ds(pl.multiple_of(which * self.rows, self.rows), self.rows)
@@ -761,25 +757,32 @@
         i = 4 + self.pieces
         return remote(self.chip_mid, self.last_mid, self.send.at[i], self.recv.at[i], self.across)
 
-    def pass_on(self):
+    def pass_on(self, lefts=None):
         f32, bf16 = jnp.float32, jnp.bfloat16
-        for copy in self.to_near(0, flip(self.far, 2)):
-            copy.wait_recv()
-        self.chip_mid[...] = (
-            self.middle[self.far].astype(f32) + self.first_mid[0].astype(f32)
-        ).astype(bf16)
-        self.begin(self.across_mid())
+        first, first_mid = self.to_near(0, flip(self.far, 2))
+        first.wait_recv()
         for i in range(self.pieces):
             at = pl.ds(i * self.size, self.size)
             self.chip[at] = (
                 self.partial[self.far, at, :].astype(f32) + self.first[0, at, :].astype(f32)
             ).astype(bf16)
             self.begin(self.across_copy(i))
-
-    def give(self, slot):
+            if i == 0:
+                if lefts is not None:
+                    self.adapt(self.far, lefts)
+                first_mid.wait_recv()
+                self.chip_mid[...] = (
+                    self.middle[self.far].astype(f32) + self.first_mid[0].astype(f32)
+                ).astype(bf16)
+                self.begin(self.across_mid())
+
+    def give(self, slot, lefts=None):
         which = flip(self.quarter if slot else self.far, 2)
-        for copy in self.to_near(slot, which):
-            self.begin(copy)
+        product, middle = self.to_near(slot, which)
+        self.begin(product)
+        if lefts is not None:
+            self.adapt(which, lefts)
+        self.begin(middle)
 
     def take(self):
         for copy in self.to_near(1, flip(self.quarter, 2)):
@@ -788,14 +791,15 @@
 
     def outward(self, lefts):
         self.product(flip(self.far, 2), lefts)
-        self.give(0)
+        self.give(0, lefts)
         self.product(self.far, lefts)
-        self.pass_on()
+        self.pass_on(lefts)
 
     def inward(self, lefts):
         self.product(flip(self.quarter, 2), lefts)
-        self.give(1)
+        self.give(1, lefts)
         self.product(self.quarter, lefts)
+        self.adapt(self.quarter, lefts)
         self.take()
 
     def piece(self, i):
@@ -924,12 +928,20 @@
 
 
 def fetch_kernel(
-    tokens, query_w, key_w, value_w, gate, up, attn_down, attn_up, ffn_down, ffn_up, down_down,
-    down_up, numbers, cotangent, frequencies,
+    tokens, query_w, key_w, value_w, all_gate, all_up, attn_down, attn_up, ffn_down, ffn_up,
+    down_down, down_up, numbers, all_cotangent, frequencies,
     all_tokens, w_qkv, w_gate, w_up, tables, marks, low_cotangent, cosine, sine,
     home_send, home_recv, part_send, part_recv, wa_send, wa_recv, mark_send, mark_recv,
-    ring_send, ring_recv, local, qkv_parts, wide_table, table,
+    ring_send, ring_recv, local, qkv_parts, wide_table, table, gate, up, cotangent, load_sem,
 ):
+    loads = [
+        pltpu.make_async_copy(source, target, load_sem.at[i])
+        for i, (source, target) in enumerate(
+            ((all_gate, gate), (all_up, up), (all_cotangent, cotangent))
+        )
+    ]
+    for load in loads:
+        load.start()
     place, column = here()
     count = w_qkv.shape[0]
     local_len = tokens.shape[1]
@@ -1021,6 +1033,7 @@
         region = gather.region(quarter, i)
         remote(region, region, home_send.at[i], home_recv.at[i], home_from[i]).wait_recv()
         gather.own(i)
+    loads[2].wait()
     low_cotangent[...] = cotangent[...].astype(bf16)
     length = cosine.shape[0]
     for row in range(0, length, 256):
@@ -1035,6 +1048,7 @@
     qkv_ring.step(3)
     table_ring.step(6)
     for t, (source, buffer) in enumerate(((gate, w_gate), (up, w_up))):
+        loads[t].wait()
         for piece, target in slices(source, buffer, column):
             pltpu.make_async_copy(piece, target, local.at[2 + t]).start()
         for k, peer in enumerate(near_far):
@@ -1093,7 +1107,7 @@
     frequencies = jnp.asarray(np.concatenate([frequencies, frequencies])[None])
     return pl.pallas_call(
         fetch_kernel,
-        in_specs=[VMEM] * 15,
+        in_specs=[VMEM] * 4 + [ANY] * 2 + [VMEM] * 7 + [ANY, VMEM],
         out_specs=[ANY] * 6 + [VMEM] * 3,
         out_shape=[
             shape(4, 2 * tokens.shape[1], width), shape(count, 4 * rows, part),
@@ -1105,7 +1119,8 @@
             DMA((2,)), DMA((2,)), DMA((3, 3)), DMA((3, 3)), DMA((3, 2)), DMA((3, 2)),
             DMA((3,)), DMA((3,)), DMA((2, 2, count - 1)), DMA((2, 2, count - 1)), DMA((5,)),
             pltpu.VMEM((4, rows, part), bf16), pltpu.VMEM((SLICES + 64, width), f32),
-            pltpu.VMEM((SLICES + 64, width), bf16),
+            pltpu.VMEM((SLICES + 64, width), bf16), pltpu.VMEM(gate.shape, bf16),
+            pltpu.VMEM(up.shape, bf16), pltpu.VMEM(cotangent.shape, f32), DMA((3,)),
         ],
         name="fetch",
         compiler_params=params(1, vmem_limit_bytes=VMEM_BYTES),
@@ -1722,17 +1737,18 @@
         load.wait()
     gather.forward(0)
     scatter.product(flip(quarter, 2), lefts)
-    scatter.give(1)
+    scatter.give(1, lefts)
     for i in (1, 2):
         gather.forward(i)
     scatter.product(quarter, lefts)
+    scatter.adapt(quarter, lefts)
     gather.forward(3)
     gather.last_here()
     for i in (0, 1):
         home.copy(i).start()
     stage(flip(far, 2))
     scatter.product(flip(far, 2), lefts)
-    scatter.give(0)
+    scatter.give(0, lefts)
     stage(far)
     length = d_gate.shape[0]
     late = [
@@ -1744,7 +1760,7 @@
     for load in late:
         load.start()
     scatter.product(far, lefts)
-    scatter.pass_on()
+    scatter.pass_on(lefts)
     scatter.take()
     for load in late:
         load.wait()
@@ -1954,15 +1970,17 @@
             ).astype(bf16)
         return carry
 
-    lax.fori_loop(0, length // rows, raw_rows, 0)
     lefts = [(d_qkv, w_qkv, True, b_qkv)]
-    for q in range(4):
-        scatter.adapt(q, lefts)
-    scatter.adapted = True
+    for which in (flip(far, 2), far):
+        raw_rows(which, 0)
     for load in loads[6:]:
         load.wait()
     scatter.product(flip(far, 2), lefts)
-    scatter.give(0)
+    scatter.give(0, lefts)
+    for which in (quarter, flip(quarter, 2)):
+        raw_rows(which, 0)
+    for which in (far, quarter, flip(quarter, 2)):
+        scatter.adapt(which, lefts)
     step = 512
     quarter_rows = scatter.rows
 

time: 680 us -> 679 us (level)
  no operation moved by 1% of the time
where the time goes in v7:
time: 679 us; the launch traced here: 675 us
  Pallas kernels  651 us (96%)
  local copies, waits for them, and re-layouts  13 us (2%)
  other arithmetic  7.94 us (1%)
    pallas_call x1, Pallas kernels, feed_forward(): pl.pallas_call(ffn_kernel, in_specs=[VMEM] * 5 + [ANY] * 6, out_specs=[VM...  137 us
    pallas_call x1, Pallas kernels, fetch(): pl.pallas_call(fetch_kernel, in_specs=[VMEM] * 4 + [ANY] * 2 + [VMEM] * 7...  119 us
    pallas_call x1, Pallas kernels, attend(): pl.pallas_call(functools.partial(attend_kernel, back=back), in_specs=[VME...  118 us
    pallas_call x1, Pallas kernels, attention_back(): pl.pallas_call(functools.partial(attend_back_kernel, back=back), in_specs...  107 us
    pallas_call x1, Pallas kernels, out_branch(): pl.pallas_call(branch_kernel, in_specs=[VMEM] * 3 + [ANY] * 4, out_specs=...  85.9 us
    pallas_call x1, Pallas kernels, ffn_back(): pl.pallas_call(ffn_back_kernel, in_specs=[VMEM] * len(near) + [ANY] * len...  83.5 us

profile of v7, /device:TPU:6, one launch (start us, length us, event | category | flops | bytes accessed | tf_op | source)
XLA Modules:
  0.0 674.7 jit_solution(10221255121614918439)
XLA Ops:
  0.7 0.7 convert_bitcast_fusion.4
  1.4 0.7 convert_bitcast_fusion.3
  2.1 0.6 fusion.4.numbers
  2.7 119.1 %fetch.1 = (bf16[4,256,2048]{2,1,0:T(8,128)(2,1)}, bf16[8,256,1536]{2,1,0:T(8,128)(2,1)}, bf16[8,256,2048]{2,1,0:T(8,128)(2,1)}, bf16[8,256,2048]{2,1,0:T(8,128)...) custom-call(bf16[2,128,2048]{2,1,0:T(8,128)(2,1)} %tokens.1, ...), custom_call_target="tpu_custom_call" | custom-call | tf_op jit(solution)/shard_map/fetch/pallas_call | solution.py:1108
  121.8 1.0 slice.62
  122.8 0.6 convert_bitcast_fusion
  123.4 1.0 copy.40.doc_col
  124.4 0.1 copy.38
  124.7 0.1 copy.39
  124.9 0.6 dynamic_slice.11
  127.5 1.8 dynamic-slice_bitcast_fusion.table
  129.3 0.7 maximum_convert_fusion.gains
  130.0 118.1 %attend.1 = (bf16[1024,512]{1,0:T(8,128)(2,1)}, bf16[1024,128]{1,0:T(8,128)(2,1)}, f32[1024,128]{1,0:T(8,128)}, bf16[128,2048]{1,0:T(8,128)(2,1)}, bf16[128,1536...) custom-call(bf16[96,2048]{1,0:T(8,128)(2,1)} %dynamic-slice_bitcast_, ...), custom_call_target="tpu_custom_call", output_to_operand_aliasing={{15}: (9, {})} | custom-call | tf_op jit(solution)/shard_map/attend/pallas_call | solution.py:1341
  248.1 85.9 %out_branch.1 = (f32[256,2048]{1,0:T(8,128)}, f32[256,2048]{1,0:T(8,128)}, bf16[256,128]{1,0:T(8,128)(2,1)}, bf16[256,2048]{1,0:T(8,128)(2,1)}, bf16[4,256,2048]...) custom-call(bf16[128,512]{1,0:T(8,128)(2,1)} %get-tuple-element.64.ao, ...), custom_call_target="tpu_custom_call", output_to_operand_aliasing={{5}: (6, {})} | custom-call | tf_op jit(solution)/shard_map/out_branch/pallas_call | solution.py:1495
  334.0 137.0 %feed_forward.1 = (bf16[1024,128]{1,0:T(8,128)(2,1)}, bf16[256,2048]{1,0:T(8,128)(2,1)}, bf16[256,2048]{1,0:T(8,128)(2,1)}, bf16[256,128]{1,0:T(8,128)(2,1)}, bf...) custom-call(bf16[128,2048]{1,0:T(8,128)(2,1)} %get-tuple-element.63., ...), custom_call_target="tpu_custom_call" | custom-call | tf_op jit(solution)/shard_map/feed_forward/pallas_call | solution.py:1648
  471.0 83.5 %ffn_back.1 = (f32[256,2048]{1,0:T(8,128)}, bf16[256,2048]{1,0:T(8,128)(2,1)}, bf16[80,2048]{1,0:T(8,128)(2,1)}, bf16[2,128,2048]{2,1,0:T(8,128)(2,1)}) custom-call(bf16[128,2048]{1,0:T(8,128)(2,1)} %get-tuple-element.60.bg, bf16[128,2048]{1,0:T(8,128)(2,1)} %get-tuple-element.61.bu, bf16[128,2048]{1,0:T(8,128)(2,1)} %get-tuple-element.62.ad, ...), custom_call_target="tpu_custom_call" | custom-call | tf_op jit(solution)/shard_map/ffn_back/pallas_call | solution.py:1812
  554.5 0.7 broadcast_in_dim.2.shared
  555.2 107.1 %attend_back.1 = (f32[32,2048]{1,0:T(8,128)}, bf16[2,128,2048]{2,1,0:T(8,128)(2,1)}, bf16[8,80,2048]{2,1,0:T(8,128)(2,1)}) custom-call(bf16[128,2048]{1,0:T(8,128)(2,1)} %get-tuple-element.63.bo.full, bf16[128,512]{1,0:T(8,128)(2,1)} %get-tuple-element.64.ao, f32[1024,128]{1,0:T(8,128)} %get-tuple-element.84.scales, f32[4,2048]{1,0:T(4,128)} %maximum_convert_fusion.gains, ...), custom_call_target="tpu_custom_call" | custom-call | tf_op jit(solution)/shard_map/attend_back/pallas_call | solution.py:2051
  662.2 2.4 multiply_reduce_fusion
  664.7 0.2 copy.48
  664.9 0.2 copy.44
  665.1 0.9 slice.77
  666.1 0.7 squeeze.18
  666.8 0.7 slice.74
  667.5 0.6 slice.87
  668.1 0.9 slice.66
  669.0 0.1 reshape.124
  669.4 0.9 slice.64
  670.3 0.8 slice_bitcast_fusion
  671.2 0.8 pad_maximum_fusion
  671.9 1.6 convert_element_type.97
  673.5 1.0 copy.56
  (36 shorter events, 0.8 us)
Async XLA Ops:
  0.6 128.6 %copy-start.2 = (bf16[2048]{0:T(1024)(128)(2,1)S(1)}, bf16[2048]{0:T(1024)(128)(2,1)}, u32[]{:S(2)}) copy-start(bf16[2048]{0:T(1024)(128)(2,1)} %param.33) | copy-start | bytes 12292
  0.6 128.6 %copy-start.3 = (bf16[2048]{0:T(1024)(128)(2,1)S(1)}, bf16[2048]{0:T(1024)(128)(2,1)}, u32[]{:S(2)}) copy-start(bf16[2048]{0:T(1024)(128)(2,1)} %param.34) | copy-start | bytes 12292
  0.7 128.6 %copy-start.4 = (bf16[2048]{0:T(1024)(128)(2,1)S(1)}, bf16[2048]{0:T(1024)(128)(2,1)}, u32[]{:S(2)}) copy-start(bf16[2048]{0:T(1024)(128)(2,1)} %param.35) | copy-start | bytes 12292
  0.7 128.6 %copy-start.5 = (bf16[2048]{0:T(1024)(128)(2,1)S(1)}, bf16[2048]{0:T(1024)(128)(2,1)}, u32[]{:S(2)}) copy-start(bf16[2048]{0:T(1024)(128)(2,1)} %param.36) | copy-start | bytes 12292
  664.6 7.3 %copy-start = (bf16[2,128,2048]{2,1,0:T(8,128)(2,1)S(1)}, bf16[2,128,2048]{2,1,0:T(8,128)(2,1)}, u32[]{:S(2)}) copy-start(bf16[2,128,2048]{2,1,0:T(8,128)(2,1)} %get-tuple-element.95) | copy-start | bytes 3145732
  664.9 8.6 %copy-start.1 = (bf16[2,128,2048]{2,1,0:T(8,128)(2,1)S(1)}, bf16[2,128,2048]{2,1,0:T(8,128)(2,1)}, u32[]{:S(2)}) copy-start(bf16[2,128,2048]{2,1,0:T(8,128)(2,1)} %get-tuple-element.110) | copy-start | bytes 3145732
